TPU v7x, 32 devices: a whole 2x2x4 slice. The times are simulated.
32 devices in a mesh: space: 8 (over z, y), segment: 4 (over x, core).
Axes of the slice: x: 2, y: 2, z: 4, core: 2. Of those that a mesh axis runs over, the one named last changes fastest.
Arguments:
- saved_inputs: bfloat16 [4, 1048576], P('segment', 'space'), may hold values from -5.5 to 5.5
- conv_weights: bfloat16 [4, 221184], P('segment'), may hold values from -0.4375 to 0.4375
- top_gradient: bfloat16 [128, 8, 2, 32], P(None, 'space'), may hold values from -6 to 6
Outputs:
- weight_grads: float32 [4, 221184], P('segment')
All inputs are finite; a program needn't handle non-finite values.
Results may differ from a plain program's by a relative error of at most 0.0023.
Values may be sent and summed in bfloat16 or wider, within the bound.
No kernel may reach another device: no remote copies, remote signals or barrier semaphores. Data moves between devices by JAX's collectives and lax.ppermute only.
A program may use at most 64 MiB of HBM per device.

v0:
```python
import math

import jax
import jax.numpy as jnp
from jax import lax
from jax.sharding import PartitionSpec as P

C0 = 4
C1 = 16
C2 = 32
C3 = 64
C4 = 128
CZ = 4
CY = 8
CX = 128


slope_negative = 0.3
tap_offsets = [
    (tap_z, tap_y, tap_x) for tap_z in range(3) for tap_y in range(3) for tap_x in range(3)
]
parity_terms = [(0, 0, 0), (0, 2, -1), (1, 1, 0)]


def as_sent(x):

    def short(part):
        return part.astype(jnp.bfloat16) if part.dtype == jnp.float32 else part

    return jax.tree.map(short, x)


def with_halo(cells, sides, width):
    for axis, dim in sides:
        count = lax.axis_size(axis)
        ends = count - 1
        head = lax.slice_in_dim(cells, 0, width, axis=dim)
        tail = lax.slice_in_dim(cells, cells.shape[dim] - width, cells.shape[dim], axis=dim)
        cells = jnp.concatenate(
            [
                lax.ppermute(tail, axis, [(i, (i + 1) % count) for i in range(ends)]),
                cells,
                lax.ppermute(head, axis, [((i + 1) % count, i) for i in range(ends)]),
            ],
            axis=dim,
        )
    return cells


def passed_along(block, axis, distance):
    devices = range(lax.axis_size(axis))
    route = [(i - distance, i) for i in devices if i - distance in devices]
    return lax.ppermute(block, axis, route)


def section_table():
    return [
        (C0, C1, 1, CZ, CY, CX),
        (C1, C2, 1, CZ, CY, CX),
        (C2, C3, 2, CZ, CY, CX),
        (C3, C4, 2, CZ // 2, CY // 2, CX // 2),
    ]


def extend_fine(volume):
    return with_halo(as_sent(volume), (("space", 1),), 1).astype(volume.dtype)


def send_back(message):
    return jax.tree.map(
        lambda part, own: part.astype(own.dtype),
        passed_along(as_sent(message), "segment", -1),
        message,
    )


def pad_cross(volume, low_side, high_side):
    return jnp.pad(volume, ((0, 0), (0, 0), (low_side, high_side), (low_side, high_side)))


def fine_weight_grad(act_ext, upstream):
    padded = pad_cross(act_ext, 1, 1)
    out_z, out_y, out_x = (upstream.shape[1], upstream.shape[2], upstream.shape[3])
    results = []
    for tap_z, tap_y, tap_x in tap_offsets:
        window = padded[:, tap_z : tap_z + out_z, tap_y : tap_y + out_y, tap_x : tap_x + out_x]
        results.append(
            jnp.einsum("dzyx,czyx->dc", upstream, window, preferred_element_type=jnp.float32)
        )
    return jnp.stack(results)


def coarse_weight_grad(act_ext, upstream):
    padded = pad_cross(act_ext, 0, 1)
    out_z, out_y, out_x = (upstream.shape[1], upstream.shape[2], upstream.shape[3])
    results = []
    for tap_z, tap_y, tap_x in tap_offsets:
        window = padded[
            :,
            tap_z : tap_z + 2 * out_z : 2,
            tap_y : tap_y + 2 * out_y : 2,
            tap_x : tap_x + 2 * out_x : 2,
        ]
        results.append(
            jnp.einsum("dzyx,czyx->dc", upstream, window, preferred_element_type=jnp.float32)
        )
    return jnp.stack(results)


def fine_input_grad(weights, delta_ext):
    padded = pad_cross(delta_ext, 1, 1)
    size_z, size_y, size_x = (delta_ext.shape[1] - 2, delta_ext.shape[2], delta_ext.shape[3])
    summed = jnp.zeros((weights.shape[2], size_z, size_y, size_x), jnp.float32)
    for position, (tap_z, tap_y, tap_x) in enumerate(tap_offsets):
        window = padded[
            :,
            2 - tap_z : 2 - tap_z + size_z,
            2 - tap_y : 2 - tap_y + size_y,
            2 - tap_x : 2 - tap_x + size_x,
        ]
        summed = summed + jnp.einsum(
            "dc,dzyx->czyx", weights[position], window, preferred_element_type=jnp.float32
        )
    return summed


def coarse_input_grad(weights, delta_ext):
    padded = pad_cross(delta_ext, 1, 0)
    out_z, out_y, out_x = (delta_ext.shape[1] - 1, delta_ext.shape[2], delta_ext.shape[3])
    parity_sums = {}
    for rest_z, tap_z, step_z in parity_terms:
        for rest_y, tap_y, step_y in parity_terms:
            for rest_x, tap_x, step_x in parity_terms:
                window = padded[
                    :,
                    1 + step_z : 1 + step_z + out_z,
                    1 + step_y : 1 + step_y + out_y,
                    1 + step_x : 1 + step_x + out_x,
                ]
                contribution = jnp.einsum(
                    "dc,dzyx->czyx",
                    weights[9 * tap_z + 3 * tap_y + tap_x],
                    window,
                    preferred_element_type=jnp.float32,
                )
                parity = (rest_z, rest_y, rest_x)
                parity_sums[parity] = (
                    parity_sums[parity] + contribution if parity in parity_sums else contribution
                )
    stacked = jnp.stack(
        [
            jnp.stack(
                [
                    jnp.stack([parity_sums[rest_z, rest_y, rest_x] for rest_x in (0, 1)])
                    for rest_y in (0, 1)
                ]
            )
            for rest_z in (0, 1)
        ]
    )
    channels = weights.shape[2]
    return jnp.transpose(stacked, (3, 4, 0, 5, 1, 6, 2)).reshape(
        channels, 2 * out_z, 2 * out_y, 2 * out_x
    )


def weight_term(act_ext, upstream, stride_size, scale_factor):
    if stride_size == 1:
        return fine_weight_grad(act_ext, upstream) * scale_factor
    return coarse_weight_grad(act_ext, upstream) * scale_factor


def message_term(weights, delta_ext, activation, stride_size):
    if stride_size == 1:
        backward = fine_input_grad(weights, delta_ext)
    else:
        backward = coarse_input_grad(weights, delta_ext)
    return (backward * jnp.where(activation > 0, 1.0, slope_negative)).astype(jnp.bfloat16)


def shards(saved_inputs, conv_weights, top_gradient):
    segment_index = lax.axis_index("segment")
    space_count = lax.axis_size("space")
    own_row = saved_inputs[0]
    own_weights = conv_weights[0]
    weight_room = conv_weights.shape[1]
    upstream = top_gradient
    collected = jnp.zeros((weight_room,), jnp.float32)
    for section in (3, 2, 1, 0):
        chan_in, chan_out, stride_size, depth_cells, height, breadth = section_table()[section]
        activation = own_row[: chan_in * depth_cells * height * breadth].reshape(
            chan_in, depth_cells, height, breadth
        )
        weights = own_weights[: 27 * chan_out * chan_in].reshape(27, chan_out, chan_in)
        active = segment_index == section
        scale_factor = 1.0 / math.sqrt(
            space_count * upstream.shape[1] * upstream.shape[2] * upstream.shape[3]
        )
        if stride_size == 1:
            if section > 0:
                joined = extend_fine(jnp.concatenate([activation, upstream], 0))
                act_ext = joined[:chan_in]
                delta_ext = joined[chan_in:]
            else:
                act_ext = extend_fine(activation)
                delta_ext = upstream
        else:
            upper_plane = passed_along(activation[:, :1], "space", -1)
            lower_plane = passed_along(as_sent(upstream[:, -1:]), "space", 1)
            act_ext = jnp.concatenate([activation, upper_plane], 1)
            delta_ext = jnp.concatenate([lower_plane, upstream], 1)
        grad_shape = (27, chan_out, chan_in)
        message_shape = activation.shape

        def weight_branch(act_ext, upstream, stride_size=stride_size, scale_factor=scale_factor):
            return weight_term(act_ext, upstream, stride_size, scale_factor)

        def weight_skip(act_ext, upstream, grad_shape=grad_shape):
            return jnp.zeros(grad_shape, jnp.float32)

        def both_branch(
            weights,
            delta_ext,
            activation,
            act_ext,
            upstream,
            stride_size=stride_size,
            scale_factor=scale_factor,
        ):
            return (
                weight_term(act_ext, upstream, stride_size, scale_factor),
                message_term(weights, delta_ext, activation, stride_size),
            )

        def both_skip(
            weights,
            delta_ext,
            activation,
            act_ext,
            upstream,
            grad_shape=grad_shape,
            message_shape=message_shape,
        ):
            return (jnp.zeros(grad_shape, jnp.float32), jnp.zeros(message_shape, jnp.bfloat16))

        if section > 0:
            local_grad, message = lax.cond(
                active, both_branch, both_skip, weights, delta_ext, activation, act_ext, upstream
            )
            passed = send_back(message)
        else:
            local_grad = lax.cond(active, weight_branch, weight_skip, act_ext, upstream)
        local_grad = lax.psum(local_grad, "space")
        flat_grad = local_grad.reshape(-1)
        collected = jnp.where(
            active, jnp.pad(flat_grad, (0, weight_room - flat_grad.shape[0])), collected
        )
        if section > 0:
            upstream = passed
    return collected[None]


def solution(mesh):
    return jax.shard_map(
        shards,
        mesh=mesh,
        in_specs=(P("segment", "space"), P("segment", None), P(None, "space", None, None)),
        out_specs=P("segment", None),
        check_vma=False,
    )
```

profile of v0, /device:TPU:2, one launch (start us, length us, event | category | flops | bytes accessed | tf_op | source)
XLA Modules:
  0.0 221.2 jit_solution(12516245438822264180)
XLA Ops:
  6.5 3.4 %collective-permute-start.4 = (bf16[128,1,2,32]{0,3,2,1:T(8,128)(2,1)}, bf16[128,1,2,32]{0,3,2,1:T(8,128)(2,1)S(1)}, u32[]{:S(2)}, u32[]{:S(2)}) collective-permute-start(bf16[128,1,2,32]{0,3,2,1:T(8,128)(2,1)} %param.13), channel_id=1, source_target_pairs={{0,4},{4,8},{8,12},{12,16},{16,20},{20,24},{24,28},{1,5},{5,9},{9,... | collective-permute-start | bytes 49160 | tf_op jit(solution)/shard_map/ppermute | solution.py:53
  13.4 4.1 %collective-permute-done.3 = bf16[64,1,4,64]{3,2,1,0:T(4,128)(2,1)S(1)} collective-permute-done((bf16[64,1,4,64]{3,2,1,0:T(4,128)(2,1)S(1)}, bf16[64,1,4,64]{3,2,1,0:T(4,128)(2,1)S(1)}, u32[]{:S(2)}, u32[]{:S(2)}) %collective-permute-start.3) | collective-permute-done | bytes 32800 | tf_op jit(solution)/shard_map/ppermute | solution.py:53
  20.4 1.9 collective-permute-start.5
  22.4 1.6 reduce.83
  24.0 1.3 collective-permute-start.2
  25.3 21.8 %collective-permute-done.5 = bf16[64,2,4,64]{3,0,1,2:T(8,128)(2,1)S(1)} collective-permute-done((bf16[64,2,4,64]{3,0,1,2:T(8,128)(2,1)S(1)}, bf16[64,2,4,64]{3,0,1,2:T(8,128)(2,1)S(1)}, u32[]{:S(2)}, u32[]{:S(2)}) %collective-permute-start.5) | collective-permute-done | bytes 65568 | tf_op jit(solution)/shard_map/ppermute | solution.py:53
  47.1 4.3 %collective-permute-start.6 = (bf16[64,1,4,64]{3,0,2,1:T(8,128)(2,1)S(1)}, bf16[64,1,4,64]{3,0,2,1:T(8,128)(2,1)S(1)}, u32[]{:S(2)}, u32[]{:S(2)}) collective-permute-start(bf16[64,1,4,64]{3,0,2,1:T(8,128)(2,1)S(1)} %copy.463), channel_id=1, source_target_pairs={{0,4},{4,8},{8,12},{12,16},{16,20},{20,24},{24,28},{1,5},{5,9},{9,... | collective-permute-start | bytes 98312 | tf_op jit(solution)/shard_map/ppermute | solution.py:53
  53.4 69.0 %conditional.5 = (f32[27,64,32]{1,2,0:T(8,128)}, bf16[32,4,8,128]{0,3,2,1:T(8,128)(2,1)}) conditional(s32[]{:T(128)} %convert_element_type.43, () %tuple.37, (bf16[32,5,8,128]{3,2,1,0:T(8,128)(2,1)}, bf16[64,2,4,64]{3,0,1,2:T(8,128)(2,1)S(1)}, bf16[1,221184]{1,0:T(2,128)(2,1)}, bf16[64,3,4,64]{3,0,2,1:T(8,128)(2,1)S(1)}, ...), branch_computations={%region_2.3_spmd, %region_3.4_spmd} | conditional | flops 114530304 | bytes 23321454 | solution.py:247
  56.7 1.3 slice_reduce_fusion.46
  66.1 1.4 multiply_convert_fusion.1
  67.6 1.8 slice.780
  69.5 1.8 slice.781
  71.5 1.8 slice.782
  73.4 1.8 slice.783
  75.4 1.8 slice.784
  77.3 1.8 slice.785
  79.3 1.8 slice.786
  81.2 1.8 slice.787
  83.2 1.8 slice.788
  85.1 1.8 slice.789
  87.1 1.8 slice.790
  89.0 1.8 slice.791
  91.0 1.8 slice.792
  92.9 1.8 slice.793
  94.9 1.8 slice.794
  96.8 1.8 slice.795
  98.8 1.8 slice.796
  100.7 1.8 slice.797
  102.7 1.9 slice.798
  104.7 1.9 slice.799
  106.8 1.9 slice.800
  108.9 1.9 slice.801
  111.0 1.9 slice.802
  113.1 1.9 slice.803
  115.2 1.9 slice.804
  117.3 1.9 slice.805
  119.4 1.9 slice.806
  122.3 1.6 copy.210
  123.9 1.9 collective-permute-start.7
  125.8 1.7 slice_reduce_fusion.81
  127.6 1.3 copy.217
  130.0 4.3 %collective-permute-start.8 = (bf16[48,1,8,128]{3,0,1,2:T(8,128)(2,1)S(1)}, bf16[48,1,8,128]{3,0,1,2:T(8,128)(2,1)S(1)}, u32[]{:S(2)}, u32[]{:S(2)}) collective-permute-start(bf16[48,1,8,128]{3,0,1,2:T(8,128)(2,1)S(1)} %get-tuple-element.206), channel_id=1, source_target_pairs={{0,4},{4,8},{8,12},{12,16},{16,20},{20,24},{24,28},{1,5},{5,9},{9,... | collective-permute-start | bytes 294920 | tf_op jit(solution)/shard_map/ppermute | solution.py:41
  137.1 6.2 %collective-permute-done.9 = bf16[48,1,8,128]{3,0,1,2:T(8,128)(2,1)S(1)} collective-permute-done((bf16[48,1,8,128]{3,0,1,2:T(8,128)(2,1)S(1)}, bf16[48,1,8,128]{3,0,1,2:T(8,128)(2,1)S(1)}, u32[]{:S(2)}, u32[]{:S(2)}) %collective-permute-start.9) | collective-permute-done | bytes 98336 | tf_op jit(solution)/shard_map/ppermute | solution.py:43
  143.7 20.0 %collective-permute-start.10 = (bf16[16,4,8,128]{3,0,1,2:T(8,128)(2,1)S(1)}, bf16[16,4,8,128]{3,0,1,2:T(8,128)(2,1)S(1)}, u32[]{:S(2)}, u32[]{:S(2)}) collective-permute-start(bf16[16,4,8,128]{3,0,1,2:T(8,128)(2,1)S(1)} %copy.213), channel_id=1, source_target_pairs={{1,0},{2,1},{3,2},{5,4},{6,5},{7,6},{9,8},{10,9},{11,10},{13,12},{... | collective-permute-start | bytes 393224 | tf_op jit(solution)/shard_map/ppermute | solution.py:53
  163.7 5.5 %collective-permute-start = (bf16[4,1,8,128]{3,2,1,0:T(8,128)(2,1)S(1)}, bf16[4,1,8,128]{3,2,1,0:T(8,128)(2,1)S(1)}, u32[]{:S(2)}, u32[]{:S(2)}) collective-permute-start(bf16[4,1,8,128]{3,2,1,0:T(8,128)(2,1)S(1)} %get-tuple-element.208), channel_id=1, source_target_pairs={{0,4},{4,8},{8,12},{12,16},{16,20},{20,24},{24,28},{1,5},{5,9},{9,... | collective-permute-start | bytes 24584 | tf_op jit(solution)/shard_map/ppermute | solution.py:41
  170.6 4.2 %collective-permute-done.1 = bf16[4,1,8,128]{3,2,1,0:T(8,128)(2,1)S(1)} collective-permute-done((bf16[4,1,8,128]{3,2,1,0:T(8,128)(2,1)S(1)}, bf16[4,1,8,128]{3,2,1,0:T(8,128)(2,1)S(1)}, u32[]{:S(2)}, u32[]{:S(2)}) %collective-permute-start.1) | collective-permute-done | bytes 8224 | tf_op jit(solution)/shard_map/ppermute | solution.py:43
  175.6 34.7 %all-reduce.10 = (f32[13824]{0:T(1024)S(1)}, f32[1728]{0:T(1024)S(1)}) all-reduce(f32[13824]{0:T(1024)S(1)} %reshape.415, f32[1728]{0:T(1024)S(1)} %reshape.414), channel_id=1, replica_groups=mesh['space'=8,'segment'=4] {'space'}, use_global_device_ids=true, to_apply=%region_9.10 | all-reduce | flops 15552 | bytes 124416 | tf_op jit(solution)/shard_map/psum | solution.py:253
  210.3 2.1 all-reduce.14.cloned.1.call-done
  (148 shorter events, 33.3 us)
Async XLA Ops:
  6.5 205.8 %all-reduce.14.cloned.1.call-start = ((), (), s32[]{:S(2)}) async-start(), calls=%async_computation | async-start | bytes 2211840 | tf_op jit(solution)/shard_map/psum | solution.py:253
  6.5 6.2 %collective-permute-start.4 = (bf16[128,1,2,32]{0,3,2,1:T(8,128)(2,1)}, bf16[128,1,2,32]{0,3,2,1:T(8,128)(2,1)S(1)}, u32[]{:S(2)}, u32[]{:S(2)}) collective-permute-start(bf16[128,1,2,32]{0,3,2,1:T(8,128)(2,1)} %param.13), channel_id=1, source_target_pairs={{0,4},{4,8},{8,12},{12,16},{16,20},{20,24},{24,28},{1,5},{5,9},{9,... | collective-permute-start | bytes 49160 | tf_op jit(solution)/shard_map/ppermute | solution.py:53
  11.4 6.2 %collective-permute-start.3 = (bf16[64,1,4,64]{3,2,1,0:T(4,128)(2,1)S(1)}, bf16[64,1,4,64]{3,2,1,0:T(4,128)(2,1)S(1)}, u32[]{:S(2)}, u32[]{:S(2)}) collective-permute-start(bf16[64,1,4,64]{3,2,1,0:T(4,128)(2,1)S(1)} %slice.982), channel_id=1, source_target_pairs={{4,0},{8,4},{12,8},{16,12},{20,16},{24,20},{28,24},{5,1},{9,5},{13... | collective-permute-start | bytes 98312 | tf_op jit(solution)/shard_map/ppermute | solution.py:53
  17.7 4.7 %copy-start.2 = (bf16[1,131072]{1,0:T(2,128)(2,1)S(1)}, bf16[1,131072]{1,0:T(2,128)(2,1)}, u32[]{:S(2)}) copy-start(bf16[1,131072]{1,0:T(2,128)(2,1)} %param.11) | copy-start | bytes 786436
  18.5 0.9 copy-start.1
  20.4 26.7 %collective-permute-start.5 = (bf16[64,2,4,64]{3,0,1,2:T(8,128)(2,1)S(1)}, bf16[64,2,4,64]{3,0,1,2:T(8,128)(2,1)S(1)}, u32[]{:S(2)}, u32[]{:S(2)}) collective-permute-start(bf16[64,2,4,64]{3,0,1,2:T(8,128)(2,1)S(1)} %copy.205), channel_id=1, source_target_pairs={{1,0},{2,1},{3,2},{5,4},{6,5},{7,6},{9,8},{10,9},{11,10},{13,12},{... | collective-permute-start | bytes 196616 | tf_op jit(solution)/shard_map/ppermute | solution.py:53
  24.0 27.5 %collective-permute-start.2 = (bf16[32,1,8,128]{3,2,1,0:T(8,128)(2,1)S(1)}, bf16[32,1,8,128]{3,2,1,0:T(8,128)(2,1)S(1)}, u32[]{:S(2)}, u32[]{:S(2)}) collective-permute-start(bf16[32,1,8,128]{3,2,1,0:T(8,128)(2,1)S(1)} %slice.981), channel_id=1, source_target_pairs={{4,0},{8,4},{12,8},{16,12},{20,16},{24,20},{28,24},{5,1},{9,5},{13... | collective-permute-start | bytes 196616 | tf_op jit(solution)/shard_map/ppermute | solution.py:53
  47.1 6.2 %collective-permute-start.6 = (bf16[64,1,4,64]{3,0,2,1:T(8,128)(2,1)S(1)}, bf16[64,1,4,64]{3,0,2,1:T(8,128)(2,1)S(1)}, u32[]{:S(2)}, u32[]{:S(2)}) collective-permute-start(bf16[64,1,4,64]{3,0,2,1:T(8,128)(2,1)S(1)} %copy.463), channel_id=1, source_target_pairs={{0,4},{4,8},{8,12},{12,16},{16,20},{20,24},{24,28},{1,5},{5,9},{9,... | collective-permute-start | bytes 98312 | tf_op jit(solution)/shard_map/ppermute | solution.py:53
  66.1 1.4 copy-start.4
  123.9 6.0 %collective-permute-start.7 = (bf16[32,4,8,128]{3,0,1,2:T(8,128)(2,1)S(1)}, bf16[32,4,8,128]{3,0,1,2:T(8,128)(2,1)S(1)}, u32[]{:S(2)}, u32[]{:S(2)}) collective-permute-start(bf16[32,4,8,128]{3,0,1,2:T(8,128)(2,1)S(1)} %copy.210), channel_id=1, source_target_pairs={{1,0},{2,1},{3,2},{5,4},{6,5},{7,6},{9,8},{10,9},{11,10},{13,12},{... | collective-permute-start | bytes 786440 | tf_op jit(solution)/shard_map/ppermute | solution.py:53
  130.0 7.1 %collective-permute-start.8 = (bf16[48,1,8,128]{3,0,1,2:T(8,128)(2,1)S(1)}, bf16[48,1,8,128]{3,0,1,2:T(8,128)(2,1)S(1)}, u32[]{:S(2)}, u32[]{:S(2)}) collective-permute-start(bf16[48,1,8,128]{3,0,1,2:T(8,128)(2,1)S(1)} %get-tuple-element.206), channel_id=1, source_target_pairs={{0,4},{4,8},{8,12},{12,16},{16,20},{20,24},{24,28},{1,5},{5,9},{9,... | collective-permute-start | bytes 294920 | tf_op jit(solution)/shard_map/ppermute | solution.py:41
  134.3 9.0 %collective-permute-start.9 = (bf16[48,1,8,128]{3,0,1,2:T(8,128)(2,1)S(1)}, bf16[48,1,8,128]{3,0,1,2:T(8,128)(2,1)S(1)}, u32[]{:S(2)}, u32[]{:S(2)}) collective-permute-start(bf16[48,1,8,128]{3,0,1,2:T(8,128)(2,1)S(1)} %get-tuple-element.207), channel_id=1, source_target_pairs={{4,0},{8,4},{12,8},{16,12},{20,16},{24,20},{28,24},{5,1},{9,5},{13... | collective-permute-start | bytes 294920 | tf_op jit(solution)/shard_map/ppermute | solution.py:43
  143.7 31.5 %collective-permute-start.10 = (bf16[16,4,8,128]{3,0,1,2:T(8,128)(2,1)S(1)}, bf16[16,4,8,128]{3,0,1,2:T(8,128)(2,1)S(1)}, u32[]{:S(2)}, u32[]{:S(2)}) collective-permute-start(bf16[16,4,8,128]{3,0,1,2:T(8,128)(2,1)S(1)} %copy.213), channel_id=1, source_target_pairs={{1,0},{2,1},{3,2},{5,4},{6,5},{7,6},{9,8},{10,9},{11,10},{13,12},{... | collective-permute-start | bytes 393224 | tf_op jit(solution)/shard_map/ppermute | solution.py:53
  163.7 6.9 %collective-permute-start = (bf16[4,1,8,128]{3,2,1,0:T(8,128)(2,1)S(1)}, bf16[4,1,8,128]{3,2,1,0:T(8,128)(2,1)S(1)}, u32[]{:S(2)}, u32[]{:S(2)}) collective-permute-start(bf16[4,1,8,128]{3,2,1,0:T(8,128)(2,1)S(1)} %get-tuple-element.208), channel_id=1, source_target_pairs={{0,4},{4,8},{8,12},{12,16},{16,20},{20,24},{24,28},{1,5},{5,9},{9,... | collective-permute-start | bytes 24584 | tf_op jit(solution)/shard_map/ppermute | solution.py:41
  169.2 5.5 %collective-permute-start.1 = (bf16[4,1,8,128]{3,2,1,0:T(8,128)(2,1)S(1)}, bf16[4,1,8,128]{3,2,1,0:T(8,128)(2,1)S(1)}, u32[]{:S(2)}, u32[]{:S(2)}) collective-permute-start(bf16[4,1,8,128]{3,2,1,0:T(8,128)(2,1)S(1)} %get-tuple-element.209), channel_id=1, source_target_pairs={{4,0},{8,4},{12,8},{16,12},{20,16},{24,20},{28,24},{5,1},{9,5},{13... | collective-permute-start | bytes 24584 | tf_op jit(solution)/shard_map/ppermute | solution.py:43
  212.4 0.9 copy-start.5
Sparse Core Ops, SparseCore 0:
  130.0 82.3 all-reduce.13
where the time goes:
time: 224 us; the launch traced here: 221 us
  local copies, waits for them, and re-layouts  68.7 us (31%)
  starting transfers between devices  46.5 us (21%)
  waiting for transfers between devices  40.1 us (18%)
  blocking collectives  34.7 us (15%)
  between operations  13.7 us (6%)
  matrix products  9.64 us (4%)
  other arithmetic  6.92 us (3%)
    slice x27, local copies, waits for them, and re-layouts, coarse_weight_grad(): padded[:, tap_z:tap_z + 2 * out_z:2, tap_y:tap_y + 2 * out_y:2, tap_x:tap...  49.8 us
    psum x1, blocking collectives, shards(): local_grad = lax.psum(local_grad, 'space')  34.7 us
    ppermute x7, starting transfers between devices, passed_along(): return lax.ppermute(block, axis, route)  34.1 us
    ppermute x7, waiting for transfers between devices, passed_along(): return lax.ppermute(block, axis, route)  27 us
    ppermute x2, waiting for transfers between devices, with_halo(): lax.ppermute(head, axis, [((i + 1) % count, i) for i in range(ends)])  10.4 us
    ppermute x2, starting transfers between devices, with_halo(): lax.ppermute(tail, axis, [(i, (i + 1) % count) for i in range(ends)])  9.78 us
    dot_general x27, matrix products, coarse_input_grad(): jnp.einsum('dc,dzyx->czyx', weights[9 * tap_z + 3 * tap_y + tap_x], windo...  5.8 us
  transfers between devices with their start and end apart: 12, of which 7 were waited for; matrix products, arithmetic and copies ran while one was open for 5% of the time, Pallas kernels for 0%

commit v1 on v0

v1 whole, which is shorter than its diff:
```python
import functools
import math

import jax
import jax.numpy as jnp
from jax import lax
from jax.experimental import pallas as pl
from jax.experimental.pallas import tpu as pltpu
from jax.sharding import PartitionSpec as P

C0, C1, C2, C3, C4 = 4, 16, 32, 64, 128
LANES = 128
SLOPE = 0.3
BF16 = jnp.bfloat16
F32 = jnp.float32
GATHER_LIMIT = 8
VMEM_LIMIT = 48 * 1024 * 1024


def on_segment(index):
    return lax.axis_index("segment") == index


def is_last_block():
    return lax.axis_index("space") == lax.axis_size("space") - 1


def cols(row, count=1):
    return slice(LANES * row, LANES * (row + count))


def moved_lanes(block, distance):
    lane = lax.broadcasted_iota(jnp.int32, block.shape, 1)
    rolled = pltpu.roll(block.astype(F32), distance % LANES, 1)
    kept = lane >= distance if distance > 0 else lane < LANES + distance
    return jnp.where(kept, rolled, 0.0).astype(BF16)


def stack_moved(read, target, chans, rows, distances):
    for row in range(rows):
        block = read(row)
        for place, distance in enumerate(distances):
            moved = moved_lanes(block, distance) if distance else block
            target[place * chans : (place + 1) * chans, cols(row)] = moved


def spread(rows_in, rows_out, source, bound):
    entry = lax.broadcasted_iota(jnp.int32, (rows_in, rows_out), 0)
    place = lax.broadcasted_iota(jnp.int32, (rows_in, rows_out), 1)
    return jnp.where((place == source(entry)) & bound(entry), 1.0, 0.0).astype(BF16)


def taps_of(cell, low, high):
    if cell % 2:
        pairs = [(1, (cell - 1) // 2)]
    else:
        pairs = [(0, cell // 2), (2, cell // 2 - 1)]
    return [(tap, place) for tap, place in pairs if low <= place <= high]


def dot_rows(left, right):
    return lax.dot_general(left, right, (((1,), (1,)), ((), ())), preferred_element_type=F32)


def dot(left, right):
    return jnp.dot(left, right, preferred_element_type=F32)


def sloped(total, activation):
    return (total * jnp.where(activation > 0, 1.0, SLOPE)).astype(BF16)


def half_row(block, odd):
    lane = lax.broadcasted_iota(jnp.int32, block.shape, 1)
    wide = block.astype(F32)
    if odd:
        wide = pltpu.roll(wide, LANES // 2, 1)
    return jnp.where(lane < LANES // 2, wide, 0.0)


def plane_of_message(ref, chans, row):
    return ref[32 * (row // 4) : 32 * (row // 4) + chans, cols(row % 4)]


def spread_top(block, half):
    unit = spread(
        LANES,
        2 * LANES,
        lambda e: LANES * ((e % 64) // 32) + 2 * (e % 32),
        lambda e: (e // 64) == half,
    )
    return dot(block, unit).astype(BF16)


def section3_kernel(top_ref, up_ref, down_ref, own_ref, weights_ref, out_ref, wide, stacked, terms):
    @pl.when(on_segment(3))
    def _():
        planes = [up_ref[:, 256:384], top_ref[...], down_ref[:, 256:384]]
        for place, block in enumerate(planes):
            for half in range(2):
                wide[64 * half : 64 * half + 64, cols(2 * place, 2)] = spread_top(block, half)
        stack_moved(lambda row: wide[:, cols(row)], stacked, C4, 6, (0, 1, 2))
        terms[...] = dot(weights_ref[...], stacked[...])
        unit = spread(LANES, LANES, lambda e: 2 * e, lambda e: e < 64)
        last = is_last_block()
        for cell_z in range(-1, 3):
            for cell_y in range(4):
                total = None
                for tap_z, place_z in taps_of(cell_z, -1, 1):
                    for tap_y, place_y in taps_of(cell_y, 0, 1):
                        first = C3 * (3 * tap_z + tap_y)
                        part = terms[first : first + C3, cols(2 * (place_z + 1) + place_y)]
                        total = part if total is None else total + part
                if cell_z == -1:
                    mask = up_ref[:, cols(cell_y // 2)]
                elif cell_z == 2:
                    mask = down_ref[:, cols(cell_y // 2)]
                else:
                    mask = own_ref[:, cols(2 * cell_z + cell_y // 2)]
                result = sloped(total, half_row(mask, cell_y % 2))
                if cell_z == 2:
                    result = jnp.where(last, jnp.zeros_like(result), result)
                out_ref[:, cols(4 * (cell_z + 1) + cell_y)] = dot(result, unit).astype(BF16)


def section2_kernel(grad_ref, up_ref, down_ref, own_ref, weights_ref, out_ref, stacked, terms):
    @pl.when(on_segment(2))
    def _():
        stack_moved(lambda row: grad_ref[:, cols(row)], stacked, C3, 16, (0, 1, 2))
        terms[...] = dot(weights_ref[:288, :192], stacked[...])
        last = is_last_block()
        for cell_z in range(-1, 5):
            for cell_y in range(8):
                total = None
                for tap_z, place_z in taps_of(cell_z, -1, 2):
                    for tap_y, place_y in taps_of(cell_y, 0, 3):
                        first = C2 * (3 * tap_z + tap_y)
                        part = terms[first : first + C2, cols(4 * (place_z + 1) + place_y)]
                        total = part if total is None else total + part
                if cell_z == -1:
                    mask = plane_of_message(up_ref, C2, cell_y)
                elif cell_z == 4:
                    mask = plane_of_message(down_ref, C2, cell_y)
                else:
                    mask = own_ref[:, cols(8 * cell_z + cell_y)]
                result = sloped(total, mask.astype(F32))
                if cell_z == 4:
                    result = jnp.where(last, jnp.zeros_like(result), result)
                out_ref[:, cols(8 * (cell_z + 1) + cell_y)] = result


def weights2_kernel(scale, grad_ref, up_ref, down_ref, own_ref, out_ref, stacked, acts):
    @pl.when(on_segment(2))
    def _():
        stack_moved(lambda row: grad_ref[:, cols(4 + row)], stacked, C3, 8, (0, 1, 2))
        for tap_z in range(3):
            for tap_y in range(3):
                first = C2 * (3 * tap_z + tap_y)
                for place_z in range(2):
                    for place_y in range(4):
                        plane, row = 2 * place_z + tap_z, 2 * place_y + tap_y
                        if row == 8:
                            block = jnp.zeros((C2, LANES), BF16)
                        elif plane == 4:
                            block = plane_of_message(down_ref, C2, row)
                        else:
                            block = own_ref[:, cols(8 * plane + row)]
                        acts[first : first + C2, cols(4 * place_z + place_y)] = block
        out_ref[...] = dot_rows(stacked[...], acts[...]) * scale


def fine_acts(chans, up_ref, down_ref, own_ref, plane, row):
    if plane == -1:
        return plane_of_message(up_ref, chans, row)
    if plane == 4:
        return plane_of_message(down_ref, chans, row)
    return own_ref[:chans, cols(8 * plane + row)]


def section01_kernel(
    scale1,
    scale0,
    grad0_ref,
    grad1_ref,
    up_ref,
    down_ref,
    own_ref,
    next_own_ref,
    next_weights_ref,
    out_ref,
    stacked,
    terms,
    result,
    moved,
    acts0,
    acts1,
):
    @pl.when(on_segment(0))
    def _():
        stack_moved(lambda row: grad0_ref[:, cols(row)], stacked, C2, 48, (-1, 0, 1))
        terms[...] = dot(next_weights_ref[:144, :96], stacked[...])
        edge = jnp.zeros((C1, LANES), F32)
        for plane in range(4):
            sums = []
            for tap_y in range(3):
                total = None
                for tap_z in range(3):
                    first = C1 * (3 * tap_z + tap_y)
                    part = terms[first : first + C1, cols(8 * (plane + 2 - tap_z), 8)]
                    total = part if total is None else total + part
                sums.append(total)
            later = jnp.concatenate([sums[0][:, LANES:], edge], 1)
            earlier = jnp.concatenate([edge, sums[2][:, : 7 * LANES]], 1)
            mask = next_own_ref[:C1, cols(8 * plane, 8)].astype(F32)
            result[:, cols(8 * plane, 8)] = sloped(sums[1] + later + earlier, mask)
        none = jnp.zeros((C1, LANES), BF16)
        for place, distance in enumerate((-1, 0, 1)):
            for plane in range(4):
                for row in range(8):
                    block = result[:, cols(8 * plane + row)]
                    block = moved_lanes(block, distance) if distance else block
                    for tap_y in range(3):
                        first = C1 * (3 * tap_y + place)
                        target = row + tap_y - 1
                        if 0 <= target < 8:
                            moved[first : first + C1, cols(8 * plane + target)] = block
                    if row == 0:
                        moved[C1 * (6 + place) : C1 * (7 + place), cols(8 * plane)] = none
                    if row == 7:
                        moved[C1 * place : C1 * (place + 1), cols(8 * plane + 7)] = none
        for tap_z in range(3):
            for plane in range(4):
                for row in range(8):
                    acts0[C1 * tap_z : C1 * (tap_z + 1), cols(8 * plane + row)] = fine_acts(
                        C1, up_ref, down_ref, own_ref, plane + tap_z - 1, row
                    )
        out_ref[:48, :] = dot_rows(acts0[...], moved[...]) * scale0
        out_ref[48:, :] = jnp.zeros((48, 144), F32)

    @pl.when(on_segment(1))
    def _():
        none = jnp.zeros((C1, LANES), BF16)
        stack_moved(lambda row: grad1_ref[:, cols(8 + row)], stacked, C2, 32, (-1, 0, 1))
        for tap_z in range(3):
            for tap_y in range(3):
                first = C1 * (3 * tap_z + tap_y)
                for plane in range(4):
                    for row in range(8):
                        source = row + tap_y - 1
                        block = none
                        if 0 <= source < 8:
                            block = fine_acts(
                                C1, up_ref, down_ref, own_ref, plane + tap_z - 1, source
                            )
                        acts1[first : first + C1, cols(8 * plane + row)] = block
        out_ref[...] = dot_rows(stacked[:, :4096], acts1[...]) * scale1


def weights3_kernel(scale, places, blocks_ref, out_ref, wide, stacked, acts):
    @pl.when(on_segment(3))
    def _():
        me = lax.axis_index("space")
        count = len(places)
        for block in range(count):
            if count == 1:
                held = blocks_ref[0]
            else:
                wanted = lax.bitwise_xor(me, block)
                position = 0
                for bit, value in places_bits(places):
                    position = position + value * lax.rem(lax.div(wanted, bit), 2)
                held = blocks_ref[position]
            for half in range(2):
                wide[64 * half : 64 * half + 64, cols(2 * block, 2)] = spread_top(
                    held[:, 768:896], half
                )
            rows = [half_row(held[:, cols(r // 2)], r % 2).astype(BF16) for r in range(12)]
            for tap_z in range(3):
                for tap_y in range(3):
                    first = C3 * (3 * tap_z + tap_y)
                    for place_y in range(2):
                        row = 2 * place_y + tap_y
                        source = jnp.zeros_like(rows[0]) if row == 4 else rows[4 * tap_z + row]
                        acts[first : first + C3, cols(2 * block + place_y)] = source
        stack_moved(lambda row: wide[:, cols(row)], stacked, C4, 2 * count, (0, 1, 2))
        out_ref[...] = dot_rows(stacked[...], acts[...]) * scale


def places_bits(places):
    count = len(places)
    bits = []
    bit = 1
    while bit < count:
        bits.append((bit, places.index(bit)))
        bit *= 2
    return bits


def call(kernel, outs, scratch, *args, flops):
    shape = jax.ShapeDtypeStruct(*outs)
    moved = sum(a.size * a.dtype.itemsize for a in args) + shape.size * shape.dtype.itemsize
    return pl.pallas_call(
        kernel,
        out_shape=shape,
        scratch_shapes=[pltpu.VMEM(*entry) for entry in scratch],
        compiler_params=pltpu.CompilerParams(vmem_limit_bytes=VMEM_LIMIT),
        cost_estimate=pl.CostEstimate(flops=flops, bytes_accessed=moved, transcendentals=0),
    )(*args)


def fine_message(plane):
    return jnp.concatenate([plane[:, :512], plane[:, 512:]], 0)


def fine_layout(row, chans):
    acts = row[: chans * 4096].reshape(chans, 4096)
    return jnp.pad(acts, ((0, 32 - chans), (0, 0)))


def fine_start(row, top, chans):
    own = fine_layout(row, chans)
    up = fine_message(own[:, 3072:])
    down = fine_message(own[:, :1024])
    return up, down, jnp.zeros((64, 512), BF16), own


def deep_start(row, top):
    own = row[:32768].reshape(64, 512)
    rest = jnp.zeros((64, 128), BF16)
    up = jnp.concatenate([own[:, 256:], top, rest], 1)
    down = jnp.concatenate([own[:, :256], top, rest], 1)
    return up, down, own, jnp.zeros((32, 4096), BF16)


def by_tap(weights, chan_out, chan_in):
    taps = weights[: 27 * chan_out * chan_in].reshape(9, 3, chan_out, chan_in)
    grouped = jnp.transpose(taps, (0, 3, 1, 2)).reshape(9 * chan_in, 3 * chan_out)
    return jnp.pad(grouped, ((0, 576 - 9 * chan_in), (0, 384 - 3 * chan_out)))


def pairs_of(segments, route):
    total = lax.axis_size("segment")
    count = lax.axis_size("space")
    return [
        (a * total + s, b * total + s) for a, b in route(count) for s in segments
    ]


def over_space(block, segments, route):
    return lax.ppermute(block, ("space", "segment"), pairs_of(segments, route))


def summed(block, segments):
    count = lax.axis_size("space")
    if count & (count - 1):
        return lax.psum(block, "space")
    bit = 1
    while bit < count:
        block = block + over_space(
            block, segments, lambda n, bit=bit: [(i, i ^ bit) for i in range(n)]
        )
        bit *= 2
    return block


def flat_row(ordered, room):
    flat = ordered.reshape(-1)
    return jnp.pad(flat, (0, room - flat.shape[0]))[None]


def shards(saved_inputs, conv_weights, top_gradient):
    segment = lax.axis_index("segment")
    count = lax.axis_size("space")
    room = conv_weights.shape[1]
    row = saved_inputs[0]
    weights = conv_weights[0]
    scales = [1.0 / math.sqrt(count * cells) for cells in (4096, 4096, 512, 64)]
    top = top_gradient.reshape(C4, 64)
    top = jnp.concatenate([top[:64], top[64:]], 1)

    up, down, own3, own = lax.switch(
        segment,
        [
            functools.partial(fine_start, chans=C0),
            functools.partial(fine_start, chans=C1),
            functools.partial(fine_start, chans=C2),
            deep_start,
        ],
        row,
        top,
    )
    up = over_space(up, range(4), lambda n: [(i, i + 1) for i in range(n - 1)])
    down = over_space(down, range(4), lambda n: [(i + 1, i) for i in range(n - 1)])
    taps = lax.switch(
        segment,
        [
            lambda w: jnp.zeros((576, 384), BF16),
            lambda w: by_tap(w, C2, C1),
            lambda w: by_tap(w, C3, C2),
            lambda w: by_tap(w, C4, C3),
        ],
        weights,
    )
    next_own = lax.ppermute(own, "segment", [(1, 0)])
    next_taps = lax.ppermute(taps, "segment", [(1, 0)])

    grad2 = call(
        section3_kernel,
        ((64, 2048), BF16),
        [((128, 768), BF16), ((384, 768), BF16), ((576, 768), F32)],
        top,
        up,
        down,
        own3,
        taps,
        flops=2 * 576 * 384 * 768,
    )
    grad2 = lax.ppermute(grad2, "segment", [(3, 2)])
    grad1 = call(
        section2_kernel,
        ((32, 6144), BF16),
        [((192, 2048), BF16), ((288, 2048), F32)],
        grad2,
        up,
        down,
        own,
        taps,
        flops=2 * 288 * 192 * 2048,
    )
    grad1_first = lax.ppermute(grad1, "segment", [(2, 0)])
    local2 = call(
        functools.partial(weights2_kernel, scales[2]),
        ((192, 288), F32),
        [((192, 1024), BF16), ((288, 1024), BF16)],
        grad2,
        up,
        down,
        own,
        flops=2 * 288 * 192 * 1024,
    )
    grad1_second = lax.ppermute(grad1, "segment", [(2, 1)])
    local01 = call(
        functools.partial(section01_kernel, scales[1], scales[0]),
        ((96, 144), F32),
        [
            ((96, 6144), BF16),
            ((144, 6144), F32),
            ((16, 4096), BF16),
            ((144, 4096), BF16),
            ((48, 4096), BF16),
            ((144, 4096), BF16),
        ],
        grad1_first,
        grad1_second,
        up,
        down,
        own,
        next_own,
        next_taps,
        flops=2 * 144 * 96 * 6144,
    )

    blocks = jnp.concatenate([own3, down[:, :256], top], 1)[None]
    places = [0]
    if count <= GATHER_LIMIT and not count & (count - 1):
        bit = count // 2
        while bit:
            received = over_space(
                blocks, [3], lambda n, bit=bit: [(i, i ^ bit) for i in range(n)]
            )
            blocks = jnp.concatenate([blocks, received], 0)
            places = places + [place ^ bit for place in places]
            bit //= 2
    held = len(places)
    sum3 = call(
        functools.partial(weights3_kernel, scales[3], places),
        ((384, 576), F32),
        [((128, 256 * held), BF16), ((384, 256 * held), BF16), ((576, 256 * held), BF16)],
        blocks,
        flops=2 * 384 * 576 * 256 * held,
    )
    if held < count:
        sum3 = summed(sum3, [3])
    sum2 = summed(local2, [2])
    sum01 = summed(local01, [0, 1])

    def finish0(sum01, sum2, sum3):
        parts = sum01[:48].reshape(3, 16, 3, 3, C1)[:, :C0]
        return flat_row(jnp.transpose(parts, (0, 2, 3, 4, 1)), room)

    def finish(total, chan_out, chan_in):
        parts = total.reshape(3, chan_out, 9, chan_in)
        return flat_row(jnp.transpose(parts, (2, 0, 1, 3)), room)

    return lax.switch(
        segment,
        [
            finish0,
            lambda a, b, c: finish(a, C2, C1),
            lambda a, b, c: finish(b, C3, C2),
            lambda a, b, c: finish(c, C4, C3),
        ],
        sum01,
        sum2,
        sum3,
    )


def solution(mesh):
    return jax.shard_map(
        shards,
        mesh=mesh,
        in_specs=(P("segment", "space"), P("segment", None), P(None, "space", None, None)),
        out_specs=P("segment", None),
        check_vma=False,
    )
```

time: 224 us -> 80.4 us (0.36)
  the two profiles are of different devices: /device:TPU:2 before, /device:TPU:0 now
where the time goes in v1:
time: 80.4 us; the launch traced here: 79.6 us
  waiting for transfers between devices  44.3 us (55%)
  starting transfers between devices  21.8 us (27%)
  Pallas kernels  5.3 us (7%)
  local copies, waits for them, and re-layouts  4.01 us (5%)
  other arithmetic  3.82 us (5%)
    ppermute x1, waiting for transfers between devices, shards(): grad1_first = lax.ppermute(grad1, 'segment', [(2, 0)])  29.2 us
    ppermute x11, starting transfers between devices, over_space(): return lax.ppermute(block, ('space', 'segment'), pairs_of(segments, route))  16.6 us
    ppermute x11, waiting for transfers between devices, over_space(): return lax.ppermute(block, ('space', 'segment'), pairs_of(segments, route))  15.1 us
    pallas_call x5, Pallas kernels, call(): pl.pallas_call(kernel, out_shape=shape, scratch_shapes=[pltpu.VMEM(*entry...  5.3 us
    unnamed x1, other arithmetic  2.5 us
  transfers between devices with their start and end apart: 16, of which 6 were waited for; matrix products, arithmetic and copies ran while one was open for 2% of the time, Pallas kernels for 7%

profile of v1, /device:TPU:0, one launch (start us, length us, event | category | flops | bytes accessed | tf_op | source)
XLA Modules:
  0.0 79.6 jit_solution(14168234225623202990)
XLA Ops:
  0.0 0.9 %fusion.6 = (bf16[64,1,2,32]{0,3,2,1:T(8,128)(2,1)S(1)}, bf16[64,1,2,32]{0,3,2,1:T(8,128)(2,1)S(1)}) fusion(bf16[128,1,2,32]{0,3,2,1:T(8,128)(2,1)} %param.17), kind=kLoop, calls=%fused_computation.24 | loop fusion | bytes 32768 | tf_op jit(solution)/shard_map/slice | solution.py:379
  0.9 0.1 copy.24
  1.0 0.1 copy.25
  1.1 0.1 pad_maximum_fusion.11.top_ref
  1.2 2.5 %reduce.4 = bf16[131072]{0:T(1024)(128)(2,1)S(1)} reduce(bf16[1,131072]{1,0:T(2,128)(2,1)} %param.15, bf16[]{:T(256)} %constant.62), dimensions={0}, to_apply=%param.15.reduce_sub_computation | reduce | bytes 524290 | tf_op args[0]
  3.7 0.0 copy-start
  3.7 1.4 %conditional.3 = (bf16[64,512]{1,0:T(8,128)(2,1)S(1)}, bf16[64,512]{1,0:T(8,128)(2,1)S(1)}, bf16[64,512]{1,0:T(8,128)(2,1)}, bf16[32,4096]{1,0:T(8,128)(2,1)}) conditional(s32[]{:T(128)} %clamp.2, bf16[131072]{0:T(1024)(128)(2,1)S(1)} %reduce.4, bf16[131072]{0:T(1024)(128)(2,1)S(1)} %reduce.4, ...), branch_computations={%region_0.1_spmd, %region_1.2_spmd, %region_2.3_spmd, %region_3.4_... | conditional | flops 327680 | bytes 1638436 | solution.py:381
  3.8 0.7 pad.21
  4.5 0.6 broadcast.14
  5.1 1.3 %collective-permute-start.1 = (bf16[64,512]{1,0:T(8,128)(2,1)S(1)}, bf16[64,512]{1,0:T(8,128)(2,1)S(1)}, u32[]{:S(2)}, u32[]{:S(2)}) collective-permute-start(bf16[64,512]{1,0:T(8,128)(2,1)S(1)} %get-tuple-element.56), channel_id=1, source_target_pairs={{4,0},{5,1},{6,2},{7,3},{8,4},{9,5},{10,6},{11,7},{12,8},{13,9},{1... | collective-permute-start | bytes 196616 | tf_op jit(solution)/shard_map/ppermute | solution.py:350
  6.4 5.5 %collective-permute-start = (bf16[64,512]{1,0:T(8,128)(2,1)S(1)}, bf16[64,512]{1,0:T(8,128)(2,1)S(1)}, u32[]{:S(2)}, u32[]{:S(2)}) collective-permute-start(bf16[64,512]{1,0:T(8,128)(2,1)S(1)} %get-tuple-element.55), channel_id=1, source_target_pairs={{0,4},{1,5},{2,6},{3,7},{4,8},{5,9},{6,10},{7,11},{8,12},{9,13},{1... | collective-permute-start | bytes 196616 | tf_op jit(solution)/shard_map/ppermute | solution.py:350
  11.9 0.3 collective-permute-done.1.down_ref
  12.2 0.9 %maximum_bitcast_fusion = bf16[1,64,896]{2,1,0:T(8,128)(2,1)S(1)} fusion(bf16[64,64]{1,0:T(8,128)(2,1)S(1)} %copy.25, bf16[64,64]{1,0:T(8,128)(2,1)S(1)} %copy.24, bf16[64,256]{1,0:T(8,128)(2,1)S(1)} %slice.146, bf16[64,512]{1,0:T(8,128)(2,1)} %get-tuple-element.57.own_ref), kind=kLoop, calls=%fused_computation.18 | loop fusion | flops 458752 | bytes 229376 | tf_op jit(solution)/shard_map/broadcast_in_dim | solution.py:463
  13.1 0.7 collective-permute-start.13
  13.8 0.1 conditional.4
  13.9 0.1 collective-permute-done.up_ref
  14.0 0.8 %shard_map.52 = bf16[64,2048]{1,0:T(8,128)(2,1)S(1)} custom-call(bf16[64,128]{1,0:T(8,128)(2,1)S(1)} %pad_maximum_fusion.11.top_ref, bf16[64,512]{1,0:T(8,128)(2,1)S(1)} %collective-permute-done.up_ref, bf16[64,512]{1,0:T(8,128)(2,1)S(1)} %collective-permute-done.1.down_ref, bf16[64,512]{1,0:T(8,128)(2,1)} %get-tuple-element.57.own_ref, ...), custom_call_target="tpu_custom_call" | custom-call | flops 339738624 | bytes 917504 | tf_op jit(solution)/shard_map/pallas_call | solution.py:302
  14.8 0.7 collective-permute-start.2
  15.5 0.0 collective-permute-done.13
  15.5 0.7 collective-permute-start.14
  16.2 0.0 collective-permute-done.2.grad_ref
  16.2 1.0 %shard_map.55 = f32[192,288]{1,0:T(8,128)S(1)} custom-call(bf16[64,2048]{1,0:T(8,128)(2,1)S(1)} %collective-permute-done.2.grad_ref, bf16[64,512]{1,0:T(8,128)(2,1)S(1)} %collective-permute-done.up_ref, bf16[64,512]{1,0:T(8,128)(2,1)S(1)} %collective-permute-done.1.down_ref, bf16[32,4096]{1,0:T(8,128)(2,1)} %get-tuple-element.58.own_ref), custom_call_target="tpu_custom_call" | custom-call | flops 113246208 | bytes 876544 | tf_op jit(solution)/shard_map/pallas_call | solution.py:302
  17.2 0.7 collective-permute-start.10
  17.9 1.3 %collective-permute-start.5 = (bf16[32,4096]{1,0:T(8,128)(2,1)}, bf16[32,4096]{1,0:T(8,128)(2,1)S(1)}, u32[]{:S(2)}, u32[]{:S(2)}) collective-permute-start(bf16[32,4096]{1,0:T(8,128)(2,1)} %get-tuple-element.58.own_ref), channel_id=1, source_target_pairs={{1,0},{5,4},{9,8},{13,12},{17,16},{21,20},{25,24},{29,28}} | collective-permute-start | bytes 786440 | tf_op jit(solution)/shard_map/ppermute | solution.py:404
  19.2 1.3 %collective-permute-start.6 = (bf16[576,384]{1,0:T(8,128)(2,1)S(1)}, bf16[576,384]{1,0:T(8,128)(2,1)S(1)}, u32[]{:S(2)}, u32[]{:S(2)}) collective-permute-start(bf16[576,384]{1,0:T(8,128)(2,1)S(1)} %get-tuple-element.114.weights_ref), channel_id=1, source_target_pairs={{1,0},{5,4},{9,8},{13,12},{17,16},{21,20},{25,24},{29,28}} | collective-permute-start | bytes 1327112 | tf_op jit(solution)/shard_map/ppermute | solution.py:405
  20.5 1.0 %shard_map.53 = bf16[32,6144]{1,0:T(8,128)(2,1)S(1)} custom-call(bf16[64,2048]{1,0:T(8,128)(2,1)S(1)} %collective-permute-done.2.grad_ref, bf16[64,512]{1,0:T(8,128)(2,1)S(1)} %collective-permute-done.up_ref, bf16[64,512]{1,0:T(8,128)(2,1)S(1)} %collective-permute-done.1.down_ref, bf16[32,4096]{1,0:T(8,128)(2,1)} %get-tuple-element.58.own_ref, ...), custom_call_target="tpu_custom_call" | custom-call | flops 226492416 | bytes 1490944 | tf_op jit(solution)/shard_map/pallas_call | solution.py:302
  21.4 0.7 collective-permute-start.4
  22.1 1.3 %collective-permute-start.3 = (bf16[32,6144]{1,0:T(8,128)(2,1)S(1)}, bf16[32,6144]{1,0:T(8,128)(2,1)S(1)}, u32[]{:S(2)}, u32[]{:S(2)}) collective-permute-start(bf16[32,6144]{1,0:T(8,128)(2,1)S(1)} %shard_map.53), channel_id=1, source_target_pairs={{2,0},{6,4},{10,8},{14,12},{18,16},{22,20},{26,24},{30,28}} | collective-permute-start | bytes 1179656 | tf_op jit(solution)/shard_map/ppermute | solution.py:430
  23.4 0.1 pad_maximum_fusion.9
  23.5 0.7 collective-permute-start.15
  24.2 0.0 collective-permute-done.5.next_own_ref
  24.2 0.7 collective-permute-start.11
  24.9 0.0 collective-permute-done.6.next_weights_ref
  25.0 29.2 %collective-permute-done.3.grad0_ref = bf16[32,6144]{1,0:T(8,128)(2,1)S(1)} collective-permute-done((bf16[32,6144]{1,0:T(8,128)(2,1)S(1)}, bf16[32,6144]{1,0:T(8,128)(2,1)S(1)}, u32[]{:S(2)}, u32[]{:S(2)}) %collective-permute-start.3) | collective-permute-done | bytes 393248 | tf_op jit(solution)/shard_map/ppermute | solution.py:430
  54.2 2.5 %shard_map.54 = f32[96,144]{1,0:T(8,128)S(1)} custom-call(bf16[32,6144]{1,0:T(8,128)(2,1)S(1)} %collective-permute-done.3.grad0_ref, bf16[32,6144]{1,0:T(8,128)(2,1)S(1)} %collective-permute-done.4.grad1_ref, bf16[64,512]{1,0:T(8,128)(2,1)S(1)} %collective-permute-done.up_ref, bf16[64,512]{1,0:T(8,128)(2,1)S(1)} %collective-permute-done.1.down_ref, ...), custom_call_target="tpu_custom_call" | custom-call | flops 169869312 | bytes 1939456 | tf_op jit(solution)/shard_map/pallas_call | solution.py:302
  56.7 1.9 %collective-permute-start.7 = (f32[96,144]{1,0:T(8,128)S(1)}, f32[96,144]{1,0:T(8,128)S(1)}, u32[]{:S(2)}, u32[]{:S(2)}) collective-permute-start(f32[96,144]{1,0:T(8,128)S(1)} %shard_map.54), channel_id=1, source_target_pairs={{0,4},{1,5},{4,0},{5,1},{8,12},{9,13},{12,8},{13,9},{16,20},{17,21... | collective-permute-start | bytes 165896 | tf_op jit(solution)/shard_map/ppermute | solution.py:350
  58.6 4.6 %collective-permute-done.7 = f32[96,144]{1,0:T(8,128)S(1)} collective-permute-done((f32[96,144]{1,0:T(8,128)S(1)}, f32[96,144]{1,0:T(8,128)S(1)}, u32[]{:S(2)}, u32[]{:S(2)}) %collective-permute-start.7) | collective-permute-done | bytes 55328 | tf_op jit(solution)/shard_map/ppermute | solution.py:350
  63.2 1.9 %collective-permute-start.8 = (f32[96,144]{1,0:T(8,128)S(1)}, f32[96,144]{1,0:T(8,128)S(1)}, u32[]{:S(2)}, u32[]{:S(2)}) collective-permute-start(f32[96,144]{1,0:T(8,128)S(1)} %add.43), channel_id=1, source_target_pairs={{0,8},{1,9},{4,12},{5,13},{8,0},{9,1},{12,4},{13,5},{16,24},{17,25... | collective-permute-start | bytes 165896 | tf_op jit(solution)/shard_map/ppermute | solution.py:350
  65.2 0.7 collective-permute-start.12
  65.9 4.7 %collective-permute-done.8 = f32[96,144]{1,0:T(8,128)S(1)} collective-permute-done((f32[96,144]{1,0:T(8,128)S(1)}, f32[96,144]{1,0:T(8,128)S(1)}, u32[]{:S(2)}, u32[]{:S(2)}) %collective-permute-start.8) | collective-permute-done | bytes 55328 | tf_op jit(solution)/shard_map/ppermute | solution.py:350
  70.6 1.9 %collective-permute-start.9 = (f32[96,144]{1,0:T(8,128)S(1)}, f32[96,144]{1,0:T(8,128)S(1)}, u32[]{:S(2)}, u32[]{:S(2)}) collective-permute-start(f32[96,144]{1,0:T(8,128)S(1)} %add.44), channel_id=1, source_target_pairs={{0,16},{1,17},{4,20},{5,21},{8,24},{9,25},{12,28},{13,29},{16,0},{... | collective-permute-start | bytes 165896 | tf_op jit(solution)/shard_map/ppermute | solution.py:350
  72.6 0.1 pad_maximum_fusion.8.blocks_ref
  72.7 5.4 %collective-permute-done.9 = f32[96,144]{1,0:T(8,128)S(1)} collective-permute-done((f32[96,144]{1,0:T(8,128)S(1)}, f32[96,144]{1,0:T(8,128)S(1)}, u32[]{:S(2)}, u32[]{:S(2)}) %collective-permute-start.9) | collective-permute-done | bytes 55328 | tf_op jit(solution)/shard_map/ppermute | solution.py:350
  78.1 1.6 %conditional.5 = (f32[1,221184]{1,0:T(1,128)}) conditional(s32[]{:T(128)} %clamp.2, (f32[96,144]{1,0:T(8,128)S(1)}, f32[96,144]{1,0:T(8,128)S(1)}) %tuple.50, (f32[96,144]{1,0:T(8,128)S(1)}, f32[96,144]{1,0:T(8,128)S(1)}) %tuple.50, (f32[192,288]{1,0:T(8,128)S(1)}, f32[192,288]{1,0:T(8,128)S(1)}) %tuple.51, ...), branch_computations={%region_8.9_spmd, %region_9.10_spmd, %region_10.11_spmd, %region_1... | conditional | flops 55296 | bytes 7077896 | solution.py:495
  78.1 0.2 reshape.69
  78.3 0.2 copy.20
  78.5 0.1 reshape.70
  78.7 1.0 %pad.25 = f32[221184]{0:T(1024)} pad(f32[1728]{0:T(1024)S(1)} %reshape.70, f32[]{:T(128)} %constant.26.clone), padding=0_219456 | pad | bytes 891652 | tf_op jit(solution)/shard_map/cond/branch_0_fun/jit(_pad)/pad | solution.py:368
  (21 shorter events, 0.3 us)
Async XLA Ops:
  3.7 10.1 %copy-start = (bf16[1,221184]{1,0:T(2,128)(2,1)S(1)}, bf16[1,221184]{1,0:T(2,128)(2,1)}, u32[]{:S(2)}) copy-start(bf16[1,221184]{1,0:T(2,128)(2,1)} %param.16) | copy-start | bytes 1327108
  5.1 7.1 %collective-permute-start.1 = (bf16[64,512]{1,0:T(8,128)(2,1)S(1)}, bf16[64,512]{1,0:T(8,128)(2,1)S(1)}, u32[]{:S(2)}, u32[]{:S(2)}) collective-permute-start(bf16[64,512]{1,0:T(8,128)(2,1)S(1)} %get-tuple-element.56), channel_id=1, source_target_pairs={{4,0},{5,1},{6,2},{7,3},{8,4},{9,5},{10,6},{11,7},{12,8},{13,9},{1... | collective-permute-start | bytes 196616 | tf_op jit(solution)/shard_map/ppermute | solution.py:350
  6.4 7.6 %collective-permute-start = (bf16[64,512]{1,0:T(8,128)(2,1)S(1)}, bf16[64,512]{1,0:T(8,128)(2,1)S(1)}, u32[]{:S(2)}, u32[]{:S(2)}) collective-permute-start(bf16[64,512]{1,0:T(8,128)(2,1)S(1)} %get-tuple-element.55), channel_id=1, source_target_pairs={{0,4},{1,5},{2,6},{3,7},{4,8},{5,9},{6,10},{7,11},{8,12},{9,13},{1... | collective-permute-start | bytes 196616 | tf_op jit(solution)/shard_map/ppermute | solution.py:350
  13.1 2.4 %collective-permute-start.13 = (bf16[1,64,896]{2,1,0:T(8,128)(2,1)S(1)}, bf16[1,64,896]{2,1,0:T(8,128)(2,1)S(1)}, u32[]{:S(2)}, u32[]{:S(2)}) collective-permute-start(bf16[1,64,896]{2,1,0:T(8,128)(2,1)S(1)} %maximum_bitcast_fusion), channel_id=1, source_target_pairs={{3,19},{7,23},{11,27},{15,31},{19,3},{23,7},{27,11},{31,15}} | collective-permute-start | bytes 344072 | tf_op jit(solution)/shard_map/ppermute | solution.py:350
  14.8 1.4 %collective-permute-start.2 = (bf16[64,2048]{1,0:T(8,128)(2,1)S(1)}, bf16[64,2048]{1,0:T(8,128)(2,1)S(1)}, u32[]{:S(2)}, u32[]{:S(2)}) collective-permute-start(bf16[64,2048]{1,0:T(8,128)(2,1)S(1)} %shard_map.52), channel_id=1, source_target_pairs={{3,2},{7,6},{11,10},{15,14},{19,18},{23,22},{27,26},{31,30}} | collective-permute-start | bytes 786440 | tf_op jit(solution)/shard_map/ppermute | solution.py:418
  15.5 6.6 %collective-permute-start.14 = (bf16[2,64,896]{2,1,0:T(8,128)(2,1)S(1)}, bf16[2,64,896]{2,1,0:T(8,128)(2,1)S(1)}, u32[]{:S(2)}, u32[]{:S(2)}) collective-permute-start(bf16[2,64,896]{2,1,0:T(8,128)(2,1)S(1)} %pad_maximum_fusion.10), channel_id=1, source_target_pairs={{3,11},{7,15},{11,3},{15,7},{19,27},{23,31},{27,19},{31,23}} | collective-permute-start | bytes 688136 | tf_op jit(solution)/shard_map/ppermute | solution.py:350
  17.2 6.3 %collective-permute-start.10 = (f32[192,288]{1,0:T(8,128)S(1)}, f32[192,288]{1,0:T(8,128)S(1)}, u32[]{:S(2)}, u32[]{:S(2)}) collective-permute-start(f32[192,288]{1,0:T(8,128)S(1)} %shard_map.55), channel_id=1, source_target_pairs={{2,6},{6,2},{10,14},{14,10},{18,22},{22,18},{26,30},{30,26}} | collective-permute-start | bytes 663560 | tf_op jit(solution)/shard_map/ppermute | solution.py:350
  17.9 6.4 %collective-permute-start.5 = (bf16[32,4096]{1,0:T(8,128)(2,1)}, bf16[32,4096]{1,0:T(8,128)(2,1)S(1)}, u32[]{:S(2)}, u32[]{:S(2)}) collective-permute-start(bf16[32,4096]{1,0:T(8,128)(2,1)} %get-tuple-element.58.own_ref), channel_id=1, source_target_pairs={{1,0},{5,4},{9,8},{13,12},{17,16},{21,20},{25,24},{29,28}} | collective-permute-start | bytes 786440 | tf_op jit(solution)/shard_map/ppermute | solution.py:404
  19.2 5.8 %collective-permute-start.6 = (bf16[576,384]{1,0:T(8,128)(2,1)S(1)}, bf16[576,384]{1,0:T(8,128)(2,1)S(1)}, u32[]{:S(2)}, u32[]{:S(2)}) collective-permute-start(bf16[576,384]{1,0:T(8,128)(2,1)S(1)} %get-tuple-element.114.weights_ref), channel_id=1, source_target_pairs={{1,0},{5,4},{9,8},{13,12},{17,16},{21,20},{25,24},{29,28}} | collective-permute-start | bytes 1327112 | tf_op jit(solution)/shard_map/ppermute | solution.py:405
  21.4 3.5 %collective-permute-start.4 = (bf16[32,6144]{1,0:T(8,128)(2,1)S(1)}, bf16[32,6144]{1,0:T(8,128)(2,1)S(1)}, u32[]{:S(2)}, u32[]{:S(2)}) collective-permute-start(bf16[32,6144]{1,0:T(8,128)(2,1)S(1)} %shard_map.53), channel_id=1, source_target_pairs={{2,1},{6,5},{10,9},{14,13},{18,17},{22,21},{26,25},{30,29}} | collective-permute-start | bytes 1179656 | tf_op jit(solution)/shard_map/ppermute | solution.py:441
  22.1 32.0 %collective-permute-start.3 = (bf16[32,6144]{1,0:T(8,128)(2,1)S(1)}, bf16[32,6144]{1,0:T(8,128)(2,1)S(1)}, u32[]{:S(2)}, u32[]{:S(2)}) collective-permute-start(bf16[32,6144]{1,0:T(8,128)(2,1)S(1)} %shard_map.53), channel_id=1, source_target_pairs={{2,0},{6,4},{10,8},{14,12},{18,16},{22,20},{26,24},{30,28}} | collective-permute-start | bytes 1179656 | tf_op jit(solution)/shard_map/ppermute | solution.py:430
  23.5 49.1 %collective-permute-start.15 = (bf16[4,64,896]{2,1,0:T(8,128)(2,1)S(1)}, bf16[4,64,896]{2,1,0:T(8,128)(2,1)S(1)}, u32[]{:S(2)}, u32[]{:S(2)}) collective-permute-start(bf16[4,64,896]{2,1,0:T(8,128)(2,1)S(1)} %pad_maximum_fusion.9), channel_id=1, source_target_pairs={{3,7},{7,3},{11,15},{15,11},{19,23},{23,19},{27,31},{31,27}} | collective-permute-start | bytes 1376264 | tf_op jit(solution)/shard_map/ppermute | solution.py:350
  24.2 40.9 %collective-permute-start.11 = (f32[192,288]{1,0:T(8,128)S(1)}, f32[192,288]{1,0:T(8,128)S(1)}, u32[]{:S(2)}, u32[]{:S(2)}) collective-permute-start(f32[192,288]{1,0:T(8,128)S(1)} %add.45), channel_id=1, source_target_pairs={{2,10},{6,14},{10,2},{14,6},{18,26},{22,30},{26,18},{30,22}} | collective-permute-start | bytes 663560 | tf_op jit(solution)/shard_map/ppermute | solution.py:350
  56.7 6.5 %collective-permute-start.7 = (f32[96,144]{1,0:T(8,128)S(1)}, f32[96,144]{1,0:T(8,128)S(1)}, u32[]{:S(2)}, u32[]{:S(2)}) collective-permute-start(f32[96,144]{1,0:T(8,128)S(1)} %shard_map.54), channel_id=1, source_target_pairs={{0,4},{1,5},{4,0},{5,1},{8,12},{9,13},{12,8},{13,9},{16,20},{17,21... | collective-permute-start | bytes 165896 | tf_op jit(solution)/shard_map/ppermute | solution.py:350
  63.2 7.4 %collective-permute-start.8 = (f32[96,144]{1,0:T(8,128)S(1)}, f32[96,144]{1,0:T(8,128)S(1)}, u32[]{:S(2)}, u32[]{:S(2)}) collective-permute-start(f32[96,144]{1,0:T(8,128)S(1)} %add.43), channel_id=1, source_target_pairs={{0,8},{1,9},{4,12},{5,13},{8,0},{9,1},{12,4},{13,5},{16,24},{17,25... | collective-permute-start | bytes 165896 | tf_op jit(solution)/shard_map/ppermute | solution.py:350
  65.2 12.9 %collective-permute-start.12 = (f32[192,288]{1,0:T(8,128)S(1)}, f32[192,288]{1,0:T(8,128)S(1)}, u32[]{:S(2)}, u32[]{:S(2)}) collective-permute-start(f32[192,288]{1,0:T(8,128)S(1)} %add.46), channel_id=1, source_target_pairs={{2,18},{6,22},{10,26},{14,30},{18,2},{22,6},{26,10},{30,14}} | collective-permute-start | bytes 663560 | tf_op jit(solution)/shard_map/ppermute | solution.py:350
  70.6 7.4 %collective-permute-start.9 = (f32[96,144]{1,0:T(8,128)S(1)}, f32[96,144]{1,0:T(8,128)S(1)}, u32[]{:S(2)}, u32[]{:S(2)}) collective-permute-start(f32[96,144]{1,0:T(8,128)S(1)} %add.44), channel_id=1, source_target_pairs={{0,16},{1,17},{4,20},{5,21},{8,24},{9,25},{12,28},{13,29},{16,0},{... | collective-permute-start | bytes 165896 | tf_op jit(solution)/shard_map/ppermute | solution.py:350

commit v2 on v1

v2 whole, which is shorter than its diff:
```python
import functools
import math

import jax
import jax.numpy as jnp
from jax import lax
from jax.experimental import pallas as pl
from jax.experimental.pallas import tpu as pltpu
from jax.sharding import PartitionSpec as P

C0, C1, C2, C3, C4 = 4, 16, 32, 64, 128
LANES = 128
SLOPE = 0.3
BF16 = jnp.bfloat16
F32 = jnp.float32
GATHER_LIMIT = 8
VMEM_LIMIT = 48 * 1024 * 1024


def on_segment(index):
    return lax.axis_index("segment") == index


def is_last_block():
    return lax.axis_index("space") == lax.axis_size("space") - 1


def cols(row, count=1):
    return slice(LANES * row, LANES * (row + count))


def moved_lanes(block, distance):
    lane = lax.broadcasted_iota(jnp.int32, block.shape, 1)
    rolled = pltpu.roll(block.astype(F32), distance % LANES, 1)
    kept = lane >= distance if distance > 0 else lane < LANES + distance
    return jnp.where(kept, rolled, 0.0).astype(BF16)


def stack_moved(read, target, chans, rows, distances):
    for row in range(rows):
        block = read(row)
        for place, distance in enumerate(distances):
            moved = moved_lanes(block, distance) if distance else block
            target[place * chans : (place + 1) * chans, cols(row)] = moved


def spread(rows_in, rows_out, source, bound):
    entry = lax.broadcasted_iota(jnp.int32, (rows_in, rows_out), 0)
    place = lax.broadcasted_iota(jnp.int32, (rows_in, rows_out), 1)
    return jnp.where((place == source(entry)) & bound(entry), 1.0, 0.0).astype(BF16)


def taps_of(cell, low, high):
    if cell % 2:
        pairs = [(1, (cell - 1) // 2)]
    else:
        pairs = [(0, cell // 2), (2, cell // 2 - 1)]
    return [(tap, place) for tap, place in pairs if low <= place <= high]


def dot_rows(left, right):
    return lax.dot_general(left, right, (((1,), (1,)), ((), ())), preferred_element_type=F32)


def dot(left, right):
    return jnp.dot(left, right, preferred_element_type=F32)


def sloped(total, activation):
    return (total * jnp.where(activation > 0, 1.0, SLOPE)).astype(BF16)


def half_row(block, odd):
    lane = lax.broadcasted_iota(jnp.int32, block.shape, 1)
    wide = block.astype(F32)
    if odd:
        wide = pltpu.roll(wide, LANES // 2, 1)
    return jnp.where(lane < LANES // 2, wide, 0.0)


def plane_of_message(ref, chans, row):
    return ref[32 * (row // 4) : 32 * (row // 4) + chans, cols(row % 4)]


def spread_top(block):
    unit = spread(64, 2 * LANES, lambda e: LANES * (e // 32) + 2 * (e % 32), lambda e: e >= 0)
    turned = (((0,), (0,)), ((), ()))
    return lax.dot_general(block, unit, turned, preferred_element_type=F32).astype(BF16)


def section3_kernel(own_ref, up_ref, down_ref, weights_ref, out_ref, wide, stacked, terms):
    @pl.when(on_segment(3))
    def _():
        for place, ref in enumerate((up_ref, own_ref, down_ref)):
            wide[:, cols(2 * place, 2)] = spread_top(ref[:, cols(4)])
        stack_moved(lambda row: wide[:, cols(row)], stacked, C4, 6, (0, 1, 2))
        terms[...] = dot(weights_ref[...], stacked[...])
        unit = spread(LANES, LANES, lambda e: 2 * e, lambda e: e < 64)
        last = is_last_block()
        for cell_z in range(-1, 3):
            for cell_y in range(4):
                total = None
                for tap_z, place_z in taps_of(cell_z, -1, 1):
                    for tap_y, place_y in taps_of(cell_y, 0, 1):
                        first = C3 * (3 * tap_z + tap_y)
                        part = terms[first : first + C3, cols(2 * (place_z + 1) + place_y)]
                        total = part if total is None else total + part
                if cell_z == -1:
                    mask = up_ref[:, cols(2 + cell_y // 2)]
                elif cell_z == 2:
                    mask = down_ref[:, cols(cell_y // 2)]
                else:
                    mask = own_ref[:, cols(2 * cell_z + cell_y // 2)]
                result = sloped(total, half_row(mask, cell_y % 2))
                if cell_z == 2:
                    result = jnp.where(last, jnp.zeros_like(result), result)
                out_ref[:, cols(4 * (cell_z + 1) + cell_y)] = dot(result, unit).astype(BF16)


def section21_kernel(
    grad_ref,
    up_ref,
    down_ref,
    own_ref,
    weights_ref,
    next_own_ref,
    next_weights_ref,
    out1_ref,
    out0_ref,
    stacked,
    terms,
    middle,
    next_stacked,
    next_terms,
):
    @pl.when(on_segment(2))
    def _():
        stack_moved(lambda row: grad_ref[:, cols(row)], stacked, C3, 16, (0, 1, 2))
        terms[...] = dot(weights_ref[:288, :192], stacked[...])
        last = is_last_block()
        for cell_z in range(-1, 5):
            for cell_y in range(8):
                total = None
                for tap_z, place_z in taps_of(cell_z, -1, 2):
                    for tap_y, place_y in taps_of(cell_y, 0, 3):
                        first = C2 * (3 * tap_z + tap_y)
                        part = terms[first : first + C2, cols(4 * (place_z + 1) + place_y)]
                        total = part if total is None else total + part
                if cell_z == -1:
                    mask = plane_of_message(up_ref, C2, cell_y)
                elif cell_z == 4:
                    mask = plane_of_message(down_ref, C2, cell_y)
                else:
                    mask = own_ref[:, cols(8 * cell_z + cell_y)]
                result = sloped(total, mask.astype(F32))
                if cell_z == 4:
                    result = jnp.where(last, jnp.zeros_like(result), result)
                middle[:, cols(8 * (cell_z + 1) + cell_y)] = result
                if 0 <= cell_z < 4:
                    out1_ref[:, cols(8 * cell_z + cell_y)] = result
        stack_moved(lambda row: middle[:, cols(row)], next_stacked, C2, 48, (-1, 0, 1))
        next_terms[...] = dot(next_weights_ref[:, :96], next_stacked[...])
        edge = jnp.zeros((C1, LANES), F32)
        for plane in range(4):
            sums = []
            for tap_y in range(3):
                total = None
                for tap_z in range(3):
                    first = C1 * (3 * tap_z + tap_y)
                    part = next_terms[first : first + C1, cols(8 * (plane + 2 - tap_z), 8)]
                    total = part if total is None else total + part
                sums.append(total)
            later = jnp.concatenate([sums[0][:, LANES:], edge], 1)
            earlier = jnp.concatenate([edge, sums[2][:, : 7 * LANES]], 1)
            mask = next_own_ref[:, cols(8 * plane, 8)].astype(F32)
            out0_ref[:, cols(8 * plane, 8)] = sloped(sums[1] + later + earlier, mask)


def weights2_kernel(scale, grad_ref, up_ref, down_ref, own_ref, out_ref, stacked, acts):
    @pl.when(on_segment(2))
    def _():
        stack_moved(lambda row: grad_ref[:, cols(4 + row)], stacked, C3, 8, (0, 1, 2))
        for tap_z in range(3):
            for tap_y in range(3):
                first = C2 * (3 * tap_z + tap_y)
                for place_z in range(2):
                    for place_y in range(4):
                        plane, row = 2 * place_z + tap_z, 2 * place_y + tap_y
                        if row == 8:
                            block = jnp.zeros((C2, LANES), BF16)
                        elif plane == 4:
                            block = plane_of_message(down_ref, C2, row)
                        else:
                            block = own_ref[:, cols(8 * plane + row)]
                        acts[first : first + C2, cols(4 * place_z + place_y)] = block
        out_ref[:288, :] = dot_rows(acts[...], stacked[:128, :]) * scale
        out_ref[288:, :64] = dot_rows(acts[:144, :], stacked[128:, :]) * scale
        out_ref[288:, 64:] = dot_rows(acts[144:, :], stacked[128:, :]) * scale


def fine_acts(chans, up_ref, down_ref, own_ref, plane, row):
    if plane == -1:
        return plane_of_message(up_ref, chans, row)
    if plane == 4:
        return plane_of_message(down_ref, chans, row)
    return own_ref[:chans, cols(8 * plane + row)]


def weights01_kernel(
    scale1, scale0, grad0_ref, grad1_ref, up_ref, down_ref, own_ref, out_ref, stacked, acts
):
    none = jnp.zeros((C1, LANES), BF16)

    @pl.when(on_segment(0))
    def _():
        for place, distance in enumerate((-1, 0, 1)):
            for plane in range(4):
                for row in range(8):
                    block = grad0_ref[:, cols(8 * plane + row)]
                    block = moved_lanes(block, distance) if distance else block
                    for tap_y in range(3):
                        first = C1 * (3 * tap_y + place)
                        target = row + tap_y - 1
                        if 0 <= target < 8:
                            acts[first : first + C1, cols(8 * plane + target)] = block
                    if row == 0:
                        acts[C1 * (6 + place) : C1 * (7 + place), cols(8 * plane)] = none
                    if row == 7:
                        acts[C1 * place : C1 * (place + 1), cols(8 * plane + 7)] = none
        for tap_z in range(3):
            for plane in range(4):
                for row in range(8):
                    stacked[C1 * tap_z : C1 * (tap_z + 1), cols(8 * plane + row)] = fine_acts(
                        C1, up_ref, down_ref, own_ref, plane + tap_z - 1, row
                    )
        out_ref[:, :48] = dot_rows(acts[...], stacked[:48, :]) * scale0
        out_ref[:, 48:] = jnp.zeros((144, 80), F32)

    @pl.when(on_segment(1))
    def _():
        stack_moved(lambda row: grad1_ref[:, cols(row)], stacked, C2, 32, (-1, 0, 1))
        for tap_z in range(3):
            for tap_y in range(3):
                first = C1 * (3 * tap_z + tap_y)
                for plane in range(4):
                    for row in range(8):
                        source = row + tap_y - 1
                        block = none
                        if 0 <= source < 8:
                            block = fine_acts(
                                C1, up_ref, down_ref, own_ref, plane + tap_z - 1, source
                            )
                        acts[first : first + C1, cols(8 * plane + row)] = block
        out_ref[:, :96] = dot_rows(acts[...], stacked[...]) * scale1
        out_ref[:, 96:] = jnp.zeros((144, 32), F32)


def weights3_kernel(scale, places, blocks_ref, down_ref, out_ref, wide, stacked, acts):
    @pl.when(on_segment(3))
    def _():
        me = lax.axis_index("space")
        count = len(places)

        def held(block):
            wanted = lax.bitwise_xor(me, block)
            position = 0
            for bit, value in places_bits(places):
                position = position + value * lax.rem(lax.div(wanted, bit), 2)
            return blocks_ref[position]

        zero = jnp.zeros((64, LANES), BF16)
        for block in range(count):
            here = blocks_ref[0] if count == 1 else held(block)
            wide[:, cols(2 * block, 2)] = spread_top(here[:, cols(4)])
            rows = [half_row(here[:, cols(r // 2)], r % 2).astype(BF16) for r in range(8)]
            if count == 1:
                after = down_ref[:, : 2 * LANES]
            elif block + 1 < count:
                after = held(block + 1)[:, : 2 * LANES]
            else:
                after = None
            for r in range(4):
                rows.append(
                    zero if after is None else half_row(after[:, cols(r // 2)], r % 2).astype(BF16)
                )
            for tap_z in range(3):
                for tap_y in range(3):
                    first = C3 * (3 * tap_z + tap_y)
                    for place_y in range(2):
                        row = 2 * place_y + tap_y
                        source = zero if row == 4 else rows[4 * tap_z + row]
                        acts[first : first + C3, cols(2 * block + place_y)] = source
        stack_moved(lambda row: wide[:, cols(row)], stacked, C4, 2 * count, (0, 1, 2))
        out_ref[...] = dot_rows(stacked[...], acts[...]) * scale


def places_bits(places):
    count = len(places)
    bits = []
    bit = 1
    while bit < count:
        bits.append((bit, places.index(bit)))
        bit *= 2
    return bits


def call(kernel, outs, scratch, *args, flops):
    shapes = [jax.ShapeDtypeStruct(*entry) for entry in outs]
    moved = sum(a.size * a.dtype.itemsize for a in [*args, *shapes])
    return pl.pallas_call(
        kernel,
        out_shape=shapes,
        scratch_shapes=[pltpu.VMEM(*entry) for entry in scratch],
        compiler_params=pltpu.CompilerParams(vmem_limit_bytes=VMEM_LIMIT),
        cost_estimate=pl.CostEstimate(flops=flops, bytes_accessed=moved, transcendentals=0),
    )(*args)


def padded(block, rows, columns):
    return jnp.pad(block, ((0, rows - block.shape[0]), (0, columns - block.shape[1])))


def fine_message(plane):
    plane = padded(plane, 32, 1024)
    return jnp.concatenate([plane[:, :512], plane[:, 512:]], 0)


def by_tap(weights, chan_out, chan_in):
    groups = []
    size = 9 * chan_out * chan_in
    for tap_z in range(3):
        taps = weights[0, tap_z * size : (tap_z + 1) * size].reshape(3, 3, chan_out, chan_in)
        groups.append(jnp.transpose(taps, (0, 3, 1, 2)).reshape(3 * chan_in, 3 * chan_out))
    return jnp.concatenate(groups, 0)


def prepared(section, saved, weights):
    deep_taps = jnp.zeros((576, 384), BF16)
    fine_taps = jnp.zeros((144, 128), BF16)
    own2 = jnp.zeros((32, 4096), BF16)
    own01 = jnp.zeros((16, 4096), BF16)
    up = down = jnp.zeros((64, 512), BF16)
    if section == 3:
        deep_taps = by_tap(weights, C4, C3)
    else:
        chans = (C0, C1, C2)[section]
        own = saved[0, : chans * 4096].reshape(chans, 4096)
        up, down = fine_message(own[:, 3072:]), fine_message(own[:, :1024])
        if section == 2:
            own2 = own
            deep_taps = padded(by_tap(weights, C3, C2), 576, 384)
        else:
            own01 = padded(own, 16, 4096)
        if section == 1:
            fine_taps = padded(by_tap(weights, C2, C1), 144, 128)
    return deep_taps, fine_taps, own2, own01, up, down


def pairs_of(segments, route):
    total = lax.axis_size("segment")
    count = lax.axis_size("space")
    return [
        (a * total + s, b * total + s) for a, b in route(count) for s in segments
    ]


def over_space(block, segments, route):
    return lax.ppermute(block, ("space", "segment"), pairs_of(segments, route))


def summed(block, segments):
    count = lax.axis_size("space")
    if count & (count - 1):
        return lax.psum(block, "space")
    bit = 1
    while bit < count:
        block = block + over_space(
            block, segments, lambda n, bit=bit: [(i, i ^ bit) for i in range(n)]
        )
        bit *= 2
    return block


def flat_row(ordered, room):
    flat = ordered.reshape(-1)
    return jnp.pad(flat, (0, room - flat.shape[0]))[None]


def shards(saved_inputs, conv_weights, top_gradient):
    segment = lax.axis_index("segment")
    count = lax.axis_size("space")
    room = conv_weights.shape[1]
    scales = [1.0 / math.sqrt(count * cells) for cells in (4096, 4096, 512, 64)]

    def later(n):
        return [(i, i + 1) for i in range(n - 1)]

    def sooner(n):
        return [(i + 1, i) for i in range(n - 1)]

    top = jnp.transpose(top_gradient[:, 0], (1, 2, 0)).reshape(64, C4)
    deep = jnp.concatenate([saved_inputs[0, :32768].reshape(64, 512), top], 1)
    deep_up = over_space(deep, [3], later)
    deep_down = over_space(deep, [3], sooner)
    deep_taps, fine_taps, own2, own01, up, down = lax.switch(
        segment,
        [functools.partial(prepared, section) for section in range(4)],
        saved_inputs,
        conv_weights,
    )
    up = over_space(up, [0, 1, 2], later)
    down = over_space(down, [0, 1, 2], sooner)
    next_own = lax.ppermute(own01, "segment", [(1, 2)])
    next_taps = lax.ppermute(fine_taps, "segment", [(1, 2)])

    (grad2,) = call(
        section3_kernel,
        [((64, 2048), BF16)],
        [((128, 768), BF16), ((384, 768), BF16), ((576, 768), F32)],
        deep,
        deep_up,
        deep_down,
        deep_taps,
        flops=2 * 576 * 384 * 768,
    )
    grad2 = lax.ppermute(grad2, "segment", [(3, 2)])
    grad1, grad0 = call(
        section21_kernel,
        [((32, 4096), BF16), ((16, 4096), BF16)],
        [
            ((192, 2048), BF16),
            ((288, 2048), F32),
            ((32, 6144), BF16),
            ((96, 6144), BF16),
            ((144, 6144), F32),
        ],
        grad2,
        up,
        down,
        own2,
        deep_taps,
        next_own,
        next_taps,
        flops=2 * 288 * 192 * 2048,
    )
    grad0 = lax.ppermute(grad0, "segment", [(2, 0)])
    grad1 = lax.ppermute(grad1, "segment", [(2, 1)])
    (local2,) = call(
        functools.partial(weights2_kernel, scales[2]),
        [((432, 128), F32)],
        [((192, 1024), BF16), ((288, 1024), BF16)],
        grad2,
        up,
        down,
        own2,
        flops=2 * 288 * 192 * 1024,
    )
    (local01,) = call(
        functools.partial(weights01_kernel, scales[1], scales[0]),
        [((144, 128), F32)],
        [((96, 4096), BF16), ((144, 4096), BF16)],
        grad0,
        grad1,
        up,
        down,
        own01,
        flops=2 * 144 * 96 * 6144,
    )

    blocks = deep[None]
    places = [0]
    if count <= GATHER_LIMIT and not count & (count - 1):
        bit = count // 2
        while bit:
            received = over_space(
                blocks, [3], lambda n, bit=bit: [(i, i ^ bit) for i in range(n)]
            )
            blocks = jnp.concatenate([blocks, received], 0)
            places = places + [place ^ bit for place in places]
            bit //= 2
    held = len(places)
    (sum3,) = call(
        functools.partial(weights3_kernel, scales[3], places),
        [((384, 576), F32)],
        [((128, 256 * held), BF16), ((384, 256 * held), BF16), ((576, 256 * held), BF16)],
        blocks,
        deep_down,
        flops=2 * 384 * 576 * 256 * held,
    )
    if held < count:
        sum3 = summed(sum3, [3])
    sum2 = summed(local2, [2])
    sum01 = summed(local01, [0, 1])

    def finish0(sum01, sum2, sum3):
        parts = sum01[:, :48].reshape(3, 3, C1, 3, 16)[..., :C0]
        return flat_row(jnp.transpose(parts, (3, 0, 1, 2, 4)), room)

    def finish1(sum01, sum2, sum3):
        parts = sum01[:, :96].reshape(9, C1, 3, C2)
        return flat_row(jnp.transpose(parts, (0, 2, 3, 1)), room)

    def finish2(sum01, sum2, sum3):
        two = sum2[:288].reshape(9, C2, 2, C3)
        one = jnp.transpose(sum2[288:].reshape(144, 2, C3), (1, 0, 2)).reshape(9, C2, 1, C3)
        return flat_row(jnp.transpose(jnp.concatenate([two, one], 2), (0, 2, 3, 1)), room)

    def finish3(sum01, sum2, sum3):
        parts = sum3.reshape(3, C4, 9, C3)
        return flat_row(jnp.transpose(parts, (2, 0, 1, 3)), room)

    return lax.switch(segment, [finish0, finish1, finish2, finish3], sum01, sum2, sum3)


def solution(mesh):
    return jax.shard_map(
        shards,
        mesh=mesh,
        in_specs=(P("segment", "space"), P("segment", None), P(None, "space", None, None)),
        out_specs=P("segment", None),
        check_vma=False,
    )
```

time: 80.4 us -> 70 us (0.87)
  waiting for transfers between devices: 44.3 us -> 31.8 us
  starting transfers between devices: 21.8 us -> 27.2 us
  other arithmetic: 3.82 us -> 0.98 us
  Pallas kernels: 5.3 us -> 3.41 us
  local copies, waits for them, and re-layouts: 4.01 us -> 5.54 us
    ppermute x4, waiting for transfers between devices: 29.2 us -> 18.9 us  [the longest x1 18.9 us: shards(): grad0 = lax.ppermute(grad0, 'segment', [(2, 0)])]
    ppermute x11 -> x13, starting transfers between devices: 16.6 us -> 23.3 us  [over_space(): return lax.ppermute(block, ('space', 'segment'), pairs_of(segments, route))]
    unnamed x1 -> x0, other arithmetic: 2.5 us -> none
    ppermute x11 -> x13, waiting for transfers between devices: 15.1 us -> 13 us  [over_space(): return lax.ppermute(block, ('space', 'segment'), pairs_of(segments, route))]
    pallas_call x5, Pallas kernels: 5.3 us -> 3.41 us  [call(): pl.pallas_call(kernel, out_shape=shapes, scratch_shapes=[pltpu.VMEM(*entr...]
    ppermute x4, starting transfers between devices: 4.55 us -> 3.28 us  [the longest x1 1.29 us: shards(): grad0 = lax.ppermute(grad0, 'segment', [(2, 0)])]
    slice x6 -> x3, local copies, waits for them, and re-layouts: 1.08 us -> 2.31 us  [the longest x1 1.28 us: shards(): deep = jnp.concatenate([saved_inputs[0, :32768].reshape(64, 512), top], 1)]
  transfers between devices with their start and end apart: 16 -> 18, of which waited for: 6 -> 6; matrix products, arithmetic and copies ran while one was open for 2% -> 4% of each run, Pallas kernels for 7% -> 5%
where the time goes in v2:
time: 70 us; the launch traced here: 69.4 us
  waiting for transfers between devices  31.8 us (45%)
  starting transfers between devices  27.2 us (39%)
  local copies, waits for them, and re-layouts  5.54 us (8%)
  Pallas kernels  3.41 us (5%)
  other arithmetic  0.98 us (1%)
    ppermute x13, starting transfers between devices, over_space(): return lax.ppermute(block, ('space', 'segment'), pairs_of(segments, route))  23.3 us
    ppermute x1, waiting for transfers between devices, shards(): grad0 = lax.ppermute(grad0, 'segment', [(2, 0)])  18.9 us
    ppermute x13, waiting for transfers between devices, over_space(): return lax.ppermute(block, ('space', 'segment'), pairs_of(segments, route))  13 us
    pallas_call x5, Pallas kernels, call(): pl.pallas_call(kernel, out_shape=shapes, scratch_shapes=[pltpu.VMEM(*entr...  3.41 us
  transfers between devices with their start and end apart: 18, of which 6 were waited for; matrix products, arithmetic and copies ran while one was open for 4% of the time, Pallas kernels for 5%

profile of v2, /device:TPU:0, one launch (start us, length us, event | category | flops | bytes accessed | tf_op | source)
XLA Modules:
  0.0 69.4 jit_solution(17043476459392292079)
XLA Ops:
  0.0 1.3 %slice_reduce_fusion.11 = bf16[32768]{0:T(1024)(128)(2,1)S(1)} fusion(bf16[1,131072]{1,0:T(2,128)(2,1)} %param.11), kind=kLoop, calls=%fused_computation.53 | loop fusion | bytes 131072 | tf_op jit(solution)/shard_map/slice | solution.py:402
  1.3 0.1 reshape_squeeze.3
  1.3 0.7 %fusion.14 = (bf16[1,64,640]{2,1,0:T(8,128)(2,1)S(1)}, bf16[64,640]{1,0:T(8,128)(2,1)S(1)}) fusion(bf16[64,128]{1,0:T(8,128)(2,1)} %bitcast.69, bf16[64,512]{1,0:T(8,128)(2,1)S(1)} %reshape_squeeze.3), kind=kLoop, calls=%fused_computation.55 | loop fusion | flops 163840 | bytes 245760 | tf_op jit(solution)/shard_map/broadcast_in_dim | solution.py:470
  2.1 0.7 collective-permute-start.1
  2.8 0.7 collective-permute-start
  3.4 0.7 collective-permute-start.15
  4.1 2.6 %conditional.2 = (bf16[576,384]{1,0:T(8,128)(2,1)S(1)}, bf16[144,128]{1,0:T(8,128)(2,1)S(1)}, bf16[32,4096]{1,0:T(8,128)(2,1)}, bf16[16,4096]{1,0:T(8,128)(2,1)}...) conditional(s32[]{:T(128)} %clamp.4, ...), branch_computations={%region_0.1_spmd, %region_1.2_spmd, %region_2.3_spmd, %region_3.4_... | conditional | flops 3579904 | bytes 4984890 | solution.py:405
  4.1 1.0 %slice_reduce_fusion = bf16[16384]{0:T(1024)(128)(2,1)S(1)} fusion(bf16[1,131072]{1,0:T(2,128)(2,1)} %param), kind=kLoop, calls=%fused_computation.10 | loop fusion | bytes 65536 | tf_op jit(solution)/shard_map/cond/branch_0_fun/slice | solution.py:347
  5.2 0.7 pad.28
  5.9 0.7 %broadcast.24 = bf16[32,4096]{1,0:T(8,128)(2,1)} broadcast(bf16[]{:T(256)} %constant.7.clone), dimensions={} | broadcast | bytes 262146 | tf_op jit(solution)/shard_map/broadcast.3
  6.7 0.0 collective-permute-done.up_ref
  6.7 0.7 collective-permute-start.2
  7.4 0.7 collective-permute-start.16
  8.1 0.7 collective-permute-start.5
  8.8 4.9 %collective-permute-start.3 = (bf16[64,512]{1,0:T(8,128)(2,1)S(1)}, bf16[64,512]{1,0:T(8,128)(2,1)S(1)}, u32[]{:S(2)}, u32[]{:S(2)}) collective-permute-start(bf16[64,512]{1,0:T(8,128)(2,1)S(1)} %get-tuple-element.55), channel_id=1, source_target_pairs={{0,4},{1,5},{2,6},{4,8},{5,9},{6,10},{8,12},{9,13},{10,14},{12,16}... | collective-permute-start | bytes 196616 | tf_op jit(solution)/shard_map/ppermute | solution.py:368
  13.7 1.3 %collective-permute-start.4 = (bf16[64,512]{1,0:T(8,128)(2,1)S(1)}, bf16[64,512]{1,0:T(8,128)(2,1)S(1)}, u32[]{:S(2)}, u32[]{:S(2)}) collective-permute-start(bf16[64,512]{1,0:T(8,128)(2,1)S(1)} %get-tuple-element.56), channel_id=1, source_target_pairs={{4,0},{5,1},{6,2},{8,4},{9,5},{10,6},{12,8},{13,9},{14,10},{16,12}... | collective-permute-start | bytes 196616 | tf_op jit(solution)/shard_map/ppermute | solution.py:368
  15.0 0.6 collective-permute-done.3.up_ref
  15.6 0.7 collective-permute-start.6
  16.2 3.6 %collective-permute-done.4.down_ref = bf16[64,512]{1,0:T(8,128)(2,1)S(1)} collective-permute-done((bf16[64,512]{1,0:T(8,128)(2,1)S(1)}, bf16[64,512]{1,0:T(8,128)(2,1)S(1)}, u32[]{:S(2)}, u32[]{:S(2)}) %collective-permute-start.4) | collective-permute-done | bytes 65568 | tf_op jit(solution)/shard_map/ppermute | solution.py:368
  19.8 1.0 %shard_map.50 = f32[432,128]{1,0:T(8,128)S(1)} custom-call(bf16[64,2048]{1,0:T(8,128)(2,1)S(1)} %collective-permute-done.2.grad_ref, bf16[64,512]{1,0:T(8,128)(2,1)S(1)} %collective-permute-done.3.up_ref, bf16[64,512]{1,0:T(8,128)(2,1)S(1)} %collective-permute-done.4.down_ref, bf16[32,4096]{1,0:T(8,128)(2,1)} %get-tuple-element.57.own_ref), custom_call_target="tpu_custom_call" | custom-call | flops 113246208 | bytes 876544 | tf_op jit(solution)/shard_map/pallas_call | solution.py:310
  20.8 0.7 collective-permute-start.12
  21.5 0.0 collective-permute-done.6.next_weights_ref
  21.5 0.0 collective-permute-done.5.next_own_ref
  21.5 1.0 %shard_map.48 = (bf16[32,4096]{1,0:T(8,128)(2,1)S(1)}, bf16[16,4096]{1,0:T(8,128)(2,1)S(1)}) custom-call(bf16[64,2048]{1,0:T(8,128)(2,1)S(1)} %collective-permute-done.2.grad_ref, bf16[64,512]{1,0:T(8,128)(2,1)S(1)} %collective-permute-done.3.up_ref, bf16[64,512]{1,0:T(8,128)(2,1)S(1)} %collective-permute-done.4.down_ref, ...), custom_call_target="tpu_custom_call" | custom-call | flops 226492416 | bytes 1658880 | tf_op jit(solution)/shard_map/pallas_call | solution.py:310
  22.4 0.7 collective-permute-start.8
  23.1 0.0 collective-permute-done.16
  23.2 0.7 collective-permute-start.17
  23.9 0.0 collective-permute-done.12
  23.9 0.7 collective-permute-start.13
  24.6 1.3 %collective-permute-start.7 = (bf16[16,4096]{1,0:T(8,128)(2,1)S(1)}, bf16[16,4096]{1,0:T(8,128)(2,1)S(1)}, u32[]{:S(2)}, u32[]{:S(2)}) collective-permute-start(bf16[16,4096]{1,0:T(8,128)(2,1)S(1)} %get-tuple-element.60), channel_id=1, source_target_pairs={{2,0},{6,4},{10,8},{14,12},{18,16},{22,20},{26,24},{30,28}} | collective-permute-start | bytes 393224 | tf_op jit(solution)/shard_map/ppermute | solution.py:446
  25.9 18.9 %collective-permute-done.7.grad0_ref = bf16[16,4096]{1,0:T(8,128)(2,1)S(1)} collective-permute-done((bf16[16,4096]{1,0:T(8,128)(2,1)S(1)}, bf16[16,4096]{1,0:T(8,128)(2,1)S(1)}, u32[]{:S(2)}, u32[]{:S(2)}) %collective-permute-start.7) | collective-permute-done | bytes 131104 | tf_op jit(solution)/shard_map/ppermute | solution.py:446
  44.7 0.0 collective-permute-done.8.grad1_ref
  44.7 1.5 %shard_map.49 = f32[144,128]{1,0:T(8,128)S(1)} custom-call(bf16[16,4096]{1,0:T(8,128)(2,1)S(1)} %collective-permute-done.7.grad0_ref, bf16[32,4096]{1,0:T(8,128)(2,1)S(1)} %collective-permute-done.8.grad1_ref, bf16[64,512]{1,0:T(8,128)(2,1)S(1)} %collective-permute-done.3.up_ref, bf16[64,512]{1,0:T(8,128)(2,1)S(1)} %collective-permute-done.4.down_ref, ...), custom_call_target="tpu_custom_call" | custom-call | flops 169869312 | bytes 729088 | tf_op jit(solution)/shard_map/pallas_call | solution.py:310
  46.2 3.8 %collective-permute-start.9 = (f32[144,128]{1,0:T(8,128)S(1)}, f32[144,128]{1,0:T(8,128)S(1)}, u32[]{:S(2)}, u32[]{:S(2)}) collective-permute-start(f32[144,128]{1,0:T(8,128)S(1)} %shard_map.49), channel_id=1, source_target_pairs={{0,4},{1,5},{4,0},{5,1},{8,12},{9,13},{12,8},{13,9},{16,20},{17,21... | collective-permute-start | bytes 221192 | tf_op jit(solution)/shard_map/ppermute | solution.py:368
  50.1 0.7 collective-permute-start.14
  50.8 1.7 %collective-permute-done.9 = f32[144,128]{1,0:T(8,128)S(1)} collective-permute-done((f32[144,128]{1,0:T(8,128)S(1)}, f32[144,128]{1,0:T(8,128)S(1)}, u32[]{:S(2)}, u32[]{:S(2)}) %collective-permute-start.9) | collective-permute-done | bytes 73760 | tf_op jit(solution)/shard_map/ppermute | solution.py:368
  52.5 2.8 %collective-permute-start.10 = (f32[144,128]{1,0:T(8,128)S(1)}, f32[144,128]{1,0:T(8,128)S(1)}, u32[]{:S(2)}, u32[]{:S(2)}) collective-permute-start(f32[144,128]{1,0:T(8,128)S(1)} %add.49), channel_id=1, source_target_pairs={{0,8},{1,9},{4,12},{5,13},{8,0},{9,1},{12,4},{13,5},{16,24},{17,25... | collective-permute-start | bytes 221192 | tf_op jit(solution)/shard_map/ppermute | solution.py:368
  55.3 0.1 pad_maximum_fusion.7.blocks_ref
  55.4 4.0 %collective-permute-done.10 = f32[144,128]{1,0:T(8,128)S(1)} collective-permute-done((f32[144,128]{1,0:T(8,128)S(1)}, f32[144,128]{1,0:T(8,128)S(1)}, u32[]{:S(2)}, u32[]{:S(2)}) %collective-permute-start.10) | collective-permute-done | bytes 73760 | tf_op jit(solution)/shard_map/ppermute | solution.py:368
  59.4 5.1 %collective-permute-start.11 = (f32[144,128]{1,0:T(8,128)S(1)}, f32[144,128]{1,0:T(8,128)S(1)}, u32[]{:S(2)}, u32[]{:S(2)}) collective-permute-start(f32[144,128]{1,0:T(8,128)S(1)} %add.50), channel_id=1, source_target_pairs={{0,16},{1,17},{4,20},{5,21},{8,24},{9,25},{12,28},{13,29},{16,0},{... | collective-permute-start | bytes 221192 | tf_op jit(solution)/shard_map/ppermute | solution.py:368
  64.5 3.1 %collective-permute-done.11 = f32[144,128]{1,0:T(8,128)S(1)} collective-permute-done((f32[144,128]{1,0:T(8,128)S(1)}, f32[144,128]{1,0:T(8,128)S(1)}, u32[]{:S(2)}, u32[]{:S(2)}) %collective-permute-start.11) | collective-permute-done | bytes 73760 | tf_op jit(solution)/shard_map/ppermute | solution.py:368
  67.6 1.8 %conditional.3 = (f32[1,221184]{1,0:T(1,128)}) conditional(s32[]{:T(128)} %clamp.4, (f32[144,128]{1,0:T(8,128)S(1)}, f32[144,128]{1,0:T(8,128)S(1)}) %tuple.37, (f32[144,128]{1,0:T(8,128)S(1)}, f32[144,128]{1,0:T(8,128)S(1)}) %tuple.37, (f32[432,128]{1,0:T(8,128)S(1)}, f32[432,128]{1,0:T(8,128)S(1)}) %tuple.38, ...), branch_computations={%region_4.5_spmd, %region_5.6_spmd, %region_6.7_spmd, %region_7.8_... | conditional | flops 110592 | bytes 7077896 | solution.py:512
  67.6 0.1 copy.34
  67.7 0.1 copy.33
  67.8 0.2 reshape.49
  68.0 0.2 copy.27
  68.3 0.1 reshape.50
  68.4 1.0 %pad.35 = f32[221184]{0:T(1024)} pad(f32[1728]{0:T(1024)S(1)} %reshape.50, f32[]{:T(128)} %constant.18.clone), padding=0_219456 | pad | bytes 891652 | tf_op jit(solution)/shard_map/cond/branch_0_fun/jit(_pad)/pad | solution.py:386
  (23 shorter events, 0.3 us)
Async XLA Ops:
  2.1 4.6 %collective-permute-start.1 = (bf16[64,640]{1,0:T(8,128)(2,1)S(1)}, bf16[64,640]{1,0:T(8,128)(2,1)S(1)}, u32[]{:S(2)}, u32[]{:S(2)}) collective-permute-start(bf16[64,640]{1,0:T(8,128)(2,1)S(1)} %get-tuple-element.99.own_ref), channel_id=1, source_target_pairs={{7,3},{11,7},{15,11},{19,15},{23,19},{27,23},{31,27}} | collective-permute-start | bytes 245768 | tf_op jit(solution)/shard_map/ppermute | solution.py:368
  2.8 3.9 %collective-permute-start = (bf16[64,640]{1,0:T(8,128)(2,1)S(1)}, bf16[64,640]{1,0:T(8,128)(2,1)S(1)}, u32[]{:S(2)}, u32[]{:S(2)}) collective-permute-start(bf16[64,640]{1,0:T(8,128)(2,1)S(1)} %get-tuple-element.99.own_ref), channel_id=1, source_target_pairs={{3,7},{7,11},{11,15},{15,19},{19,23},{23,27},{27,31}} | collective-permute-start | bytes 245768 | tf_op jit(solution)/shard_map/ppermute | solution.py:368
  3.4 4.0 %collective-permute-start.15 = (bf16[1,64,640]{2,1,0:T(8,128)(2,1)S(1)}, bf16[1,64,640]{2,1,0:T(8,128)(2,1)S(1)}, u32[]{:S(2)}, u32[]{:S(2)}) collective-permute-start(bf16[1,64,640]{2,1,0:T(8,128)(2,1)S(1)} %get-tuple-element.98), channel_id=1, source_target_pairs={{3,19},{7,23},{11,27},{15,31},{19,3},{23,7},{27,11},{31,15}} | collective-permute-start | bytes 245768 | tf_op jit(solution)/shard_map/ppermute | solution.py:368
  6.7 13.1 %collective-permute-start.2 = (bf16[64,2048]{1,0:T(8,128)(2,1)S(1)}, bf16[64,2048]{1,0:T(8,128)(2,1)S(1)}, u32[]{:S(2)}, u32[]{:S(2)}) collective-permute-start(bf16[64,2048]{1,0:T(8,128)(2,1)S(1)} %shard_map.47), channel_id=1, source_target_pairs={{3,2},{7,6},{11,10},{15,14},{19,18},{23,22},{27,26},{31,30}} | collective-permute-start | bytes 786440 | tf_op jit(solution)/shard_map/ppermute | solution.py:426
  7.4 15.7 %collective-permute-start.16 = (bf16[2,64,640]{2,1,0:T(8,128)(2,1)S(1)}, bf16[2,64,640]{2,1,0:T(8,128)(2,1)S(1)}, u32[]{:S(2)}, u32[]{:S(2)}) collective-permute-start(bf16[2,64,640]{2,1,0:T(8,128)(2,1)S(1)} %pad_maximum_fusion.9), channel_id=1, source_target_pairs={{3,11},{7,15},{11,3},{15,7},{19,27},{23,31},{27,19},{31,23}} | collective-permute-start | bytes 491528 | tf_op jit(solution)/shard_map/ppermute | solution.py:368
  8.1 13.4 %collective-permute-start.5 = (bf16[16,4096]{1,0:T(8,128)(2,1)}, bf16[16,4096]{1,0:T(8,128)(2,1)S(1)}, u32[]{:S(2)}, u32[]{:S(2)}) collective-permute-start(bf16[16,4096]{1,0:T(8,128)(2,1)} %get-tuple-element.58.own_ref), channel_id=1, source_target_pairs={{1,2},{5,6},{9,10},{13,14},{17,18},{21,22},{25,26},{29,30}} | collective-permute-start | bytes 393224 | tf_op jit(solution)/shard_map/ppermute | solution.py:413
  8.8 6.8 %collective-permute-start.3 = (bf16[64,512]{1,0:T(8,128)(2,1)S(1)}, bf16[64,512]{1,0:T(8,128)(2,1)S(1)}, u32[]{:S(2)}, u32[]{:S(2)}) collective-permute-start(bf16[64,512]{1,0:T(8,128)(2,1)S(1)} %get-tuple-element.55), channel_id=1, source_target_pairs={{0,4},{1,5},{2,6},{4,8},{5,9},{6,10},{8,12},{9,13},{10,14},{12,16}... | collective-permute-start | bytes 196616 | tf_op jit(solution)/shard_map/ppermute | solution.py:368
  13.7 6.2 %collective-permute-start.4 = (bf16[64,512]{1,0:T(8,128)(2,1)S(1)}, bf16[64,512]{1,0:T(8,128)(2,1)S(1)}, u32[]{:S(2)}, u32[]{:S(2)}) collective-permute-start(bf16[64,512]{1,0:T(8,128)(2,1)S(1)} %get-tuple-element.56), channel_id=1, source_target_pairs={{4,0},{5,1},{6,2},{8,4},{9,5},{10,6},{12,8},{13,9},{14,10},{16,12}... | collective-permute-start | bytes 196616 | tf_op jit(solution)/shard_map/ppermute | solution.py:368
  15.6 5.9 %collective-permute-start.6 = (bf16[144,128]{1,0:T(8,128)(2,1)S(1)}, bf16[144,128]{1,0:T(8,128)(2,1)S(1)}, u32[]{:S(2)}, u32[]{:S(2)}) collective-permute-start(bf16[144,128]{1,0:T(8,128)(2,1)S(1)} %get-tuple-element.59), channel_id=1, source_target_pairs={{1,2},{5,6},{9,10},{13,14},{17,18},{21,22},{25,26},{29,30}} | collective-permute-start | bytes 110600 | tf_op jit(solution)/shard_map/ppermute | solution.py:414
  20.8 3.1 %collective-permute-start.12 = (f32[432,128]{1,0:T(8,128)S(1)}, f32[432,128]{1,0:T(8,128)S(1)}, u32[]{:S(2)}, u32[]{:S(2)}) collective-permute-start(f32[432,128]{1,0:T(8,128)S(1)} %shard_map.50), channel_id=1, source_target_pairs={{2,6},{6,2},{10,14},{14,10},{18,22},{22,18},{26,30},{30,26}} | collective-permute-start | bytes 663560 | tf_op jit(solution)/shard_map/ppermute | solution.py:368
  22.4 22.3 %collective-permute-start.8 = (bf16[32,4096]{1,0:T(8,128)(2,1)S(1)}, bf16[32,4096]{1,0:T(8,128)(2,1)S(1)}, u32[]{:S(2)}, u32[]{:S(2)}) collective-permute-start(bf16[32,4096]{1,0:T(8,128)(2,1)S(1)} %get-tuple-element.61), channel_id=1, source_target_pairs={{2,1},{6,5},{10,9},{14,13},{18,17},{22,21},{26,25},{30,29}} | collective-permute-start | bytes 786440 | tf_op jit(solution)/shard_map/ppermute | solution.py:447
  23.2 32.1 %collective-permute-start.17 = (bf16[4,64,640]{2,1,0:T(8,128)(2,1)S(1)}, bf16[4,64,640]{2,1,0:T(8,128)(2,1)S(1)}, u32[]{:S(2)}, u32[]{:S(2)}) collective-permute-start(bf16[4,64,640]{2,1,0:T(8,128)(2,1)S(1)} %pad_maximum_fusion.8), channel_id=1, source_target_pairs={{3,7},{7,3},{11,15},{15,11},{19,23},{23,19},{27,31},{31,27}} | collective-permute-start | bytes 983048 | tf_op jit(solution)/shard_map/ppermute | solution.py:368
  23.9 26.2 %collective-permute-start.13 = (f32[432,128]{1,0:T(8,128)S(1)}, f32[432,128]{1,0:T(8,128)S(1)}, u32[]{:S(2)}, u32[]{:S(2)}) collective-permute-start(f32[432,128]{1,0:T(8,128)S(1)} %add.51), channel_id=1, source_target_pairs={{2,10},{6,14},{10,2},{14,6},{18,26},{22,30},{26,18},{30,22}} | collective-permute-start | bytes 663560 | tf_op jit(solution)/shard_map/ppermute | solution.py:368
  24.6 20.2 %collective-permute-start.7 = (bf16[16,4096]{1,0:T(8,128)(2,1)S(1)}, bf16[16,4096]{1,0:T(8,128)(2,1)S(1)}, u32[]{:S(2)}, u32[]{:S(2)}) collective-permute-start(bf16[16,4096]{1,0:T(8,128)(2,1)S(1)} %get-tuple-element.60), channel_id=1, source_target_pairs={{2,0},{6,4},{10,8},{14,12},{18,16},{22,20},{26,24},{30,28}} | collective-permute-start | bytes 393224 | tf_op jit(solution)/shard_map/ppermute | solution.py:446
  46.2 6.2 %collective-permute-start.9 = (f32[144,128]{1,0:T(8,128)S(1)}, f32[144,128]{1,0:T(8,128)S(1)}, u32[]{:S(2)}, u32[]{:S(2)}) collective-permute-start(f32[144,128]{1,0:T(8,128)S(1)} %shard_map.49), channel_id=1, source_target_pairs={{0,4},{1,5},{4,0},{5,1},{8,12},{9,13},{12,8},{13,9},{16,20},{17,21... | collective-permute-start | bytes 221192 | tf_op jit(solution)/shard_map/ppermute | solution.py:368
  50.1 17.5 %collective-permute-start.14 = (f32[432,128]{1,0:T(8,128)S(1)}, f32[432,128]{1,0:T(8,128)S(1)}, u32[]{:S(2)}, u32[]{:S(2)}) collective-permute-start(f32[432,128]{1,0:T(8,128)S(1)} %add.52), channel_id=1, source_target_pairs={{2,18},{6,22},{10,26},{14,30},{18,2},{22,6},{26,10},{30,14}} | collective-permute-start | bytes 663560 | tf_op jit(solution)/shard_map/ppermute | solution.py:368
  52.5 6.9 %collective-permute-start.10 = (f32[144,128]{1,0:T(8,128)S(1)}, f32[144,128]{1,0:T(8,128)S(1)}, u32[]{:S(2)}, u32[]{:S(2)}) collective-permute-start(f32[144,128]{1,0:T(8,128)S(1)} %add.49), channel_id=1, source_target_pairs={{0,8},{1,9},{4,12},{5,13},{8,0},{9,1},{12,4},{13,5},{16,24},{17,25... | collective-permute-start | bytes 221192 | tf_op jit(solution)/shard_map/ppermute | solution.py:368
  59.4 8.2 %collective-permute-start.11 = (f32[144,128]{1,0:T(8,128)S(1)}, f32[144,128]{1,0:T(8,128)S(1)}, u32[]{:S(2)}, u32[]{:S(2)}) collective-permute-start(f32[144,128]{1,0:T(8,128)S(1)} %add.50), channel_id=1, source_target_pairs={{0,16},{1,17},{4,20},{5,21},{8,24},{9,25},{12,28},{13,29},{16,0},{... | collective-permute-start | bytes 221192 | tf_op jit(solution)/shard_map/ppermute | solution.py:368

commit v3 on v2

--- a/solution.py
+++ b/solution.py
@@ -86,6 +86,41 @@
     unit = spread(64, 2 * LANES, lambda e: LANES * (e // 32) + 2 * (e % 32), lambda e: e >= 0)
     turned = (((0,), (0,)), ((), ()))
     return lax.dot_general(block, unit, turned, preferred_element_type=F32).astype(BF16)
+
+
+def copy_rows(saved_ref, wide, chans, width):
+    for chan in range(chans):
+        source = saved_ref[:, chan * width : (chan + 1) * width]
+        wide[chan : chan + 1, :width] = source.astype(F32)
+
+
+def layout_kernel(saved_ref, top_ref, up_ref, down_ref, own2_ref, own01_ref, wide):
+    def send(chans, place, plane, target_ref):
+        for half in range(2):
+            target_ref[32 * half : 32 * half + place, :512] = wide[
+                :place, cols(8 * plane + 4 * half, 4)
+            ].astype(BF16)
+
+    @pl.when(on_segment(3))
+    def _():
+        copy_rows(saved_ref, wide, C3, 512)
+        block = wide[:, :512].astype(BF16)
+        for ref in (up_ref, down_ref):
+            ref[:, :512] = block
+            ref[:, 512:] = top_ref[...]
+
+    for section, chans in enumerate((C0, C1, C2)):
+
+        @pl.when(on_segment(section))
+        def _(section=section, chans=chans):
+            if section == 0:
+                wide[:C1, :] = jnp.zeros((C1, 4096), F32)
+            copy_rows(saved_ref, wide, chans, 4096)
+            place = max(chans, C1)
+            own_ref = own2_ref if section == 2 else own01_ref
+            own_ref[...] = wide[:place, :].astype(BF16)
+            send(chans, place, 3, up_ref)
+            send(chans, place, 0, down_ref)
 
 
 def section3_kernel(own_ref, up_ref, down_ref, weights_ref, out_ref, wide, stacked, terms):
@@ -320,11 +355,6 @@
     return jnp.pad(block, ((0, rows - block.shape[0]), (0, columns - block.shape[1])))
 
 
-def fine_message(plane):
-    plane = padded(plane, 32, 1024)
-    return jnp.concatenate([plane[:, :512], plane[:, 512:]], 0)
-
-
 def by_tap(weights, chan_out, chan_in):
     groups = []
     size = 9 * chan_out * chan_in
@@ -334,26 +364,16 @@
     return jnp.concatenate(groups, 0)
 
 
-def prepared(section, saved, weights):
+def tap_layouts(section, weights):
     deep_taps = jnp.zeros((576, 384), BF16)
     fine_taps = jnp.zeros((144, 128), BF16)
-    own2 = jnp.zeros((32, 4096), BF16)
-    own01 = jnp.zeros((16, 4096), BF16)
-    up = down = jnp.zeros((64, 512), BF16)
     if section == 3:
         deep_taps = by_tap(weights, C4, C3)
-    else:
-        chans = (C0, C1, C2)[section]
-        own = saved[0, : chans * 4096].reshape(chans, 4096)
-        up, down = fine_message(own[:, 3072:]), fine_message(own[:, :1024])
-        if section == 2:
-            own2 = own
-            deep_taps = padded(by_tap(weights, C3, C2), 576, 384)
-        else:
-            own01 = padded(own, 16, 4096)
-        if section == 1:
-            fine_taps = padded(by_tap(weights, C2, C1), 144, 128)
-    return deep_taps, fine_taps, own2, own01, up, down
+    if section == 2:
+        deep_taps = padded(by_tap(weights, C3, C2), 576, 384)
+    if section == 1:
+        fine_taps = padded(by_tap(weights, C2, C1), 144, 128)
+    return deep_taps, fine_taps
 
 
 def pairs_of(segments, route):
@@ -368,19 +388,6 @@
     return lax.ppermute(block, ("space", "segment"), pairs_of(segments, route))
 
 
-def summed(block, segments):
-    count = lax.axis_size("space")
-    if count & (count - 1):
-        return lax.psum(block, "space")
-    bit = 1
-    while bit < count:
-        block = block + over_space(
-            block, segments, lambda n, bit=bit: [(i, i ^ bit) for i in range(n)]
-        )
-        bit *= 2
-    return block
-
-
 def flat_row(ordered, room):
     flat = ordered.reshape(-1)
     return jnp.pad(flat, (0, room - flat.shape[0]))[None]
@@ -399,17 +406,22 @@
         return [(i + 1, i) for i in range(n - 1)]
 
     top = jnp.transpose(top_gradient[:, 0], (1, 2, 0)).reshape(64, C4)
-    deep = jnp.concatenate([saved_inputs[0, :32768].reshape(64, 512), top], 1)
-    deep_up = over_space(deep, [3], later)
-    deep_down = over_space(deep, [3], sooner)
-    deep_taps, fine_taps, own2, own01, up, down = lax.switch(
+    to_later, to_sooner, own2, own01 = call(
+        layout_kernel,
+        [((64, 640), BF16), ((64, 640), BF16), ((32, 4096), BF16), ((16, 4096), BF16)],
+        [((64, 4096), F32)],
+        saved_inputs,
+        top,
+        flops=0,
+    )
+    deep = to_later
+    up = over_space(to_later, range(4), later)
+    down = over_space(to_sooner, range(4), sooner)
+    deep_taps, fine_taps = lax.switch(
         segment,
-        [functools.partial(prepared, section) for section in range(4)],
-        saved_inputs,
+        [functools.partial(tap_layouts, section) for section in range(4)],
         conv_weights,
     )
-    up = over_space(up, [0, 1, 2], later)
-    down = over_space(down, [0, 1, 2], sooner)
     next_own = lax.ppermute(own01, "segment", [(1, 2)])
     next_taps = lax.ppermute(fine_taps, "segment", [(1, 2)])
 
@@ -418,8 +430,8 @@
         [((64, 2048), BF16)],
         [((128, 768), BF16), ((384, 768), BF16), ((576, 768), F32)],
         deep,
-        deep_up,
-        deep_down,
+        up,
+        down,
         deep_taps,
         flops=2 * 576 * 384 * 768,
     )
@@ -445,16 +457,6 @@
     )
     grad0 = lax.ppermute(grad0, "segment", [(2, 0)])
     grad1 = lax.ppermute(grad1, "segment", [(2, 1)])
-    (local2,) = call(
-        functools.partial(weights2_kernel, scales[2]),
-        [((432, 128), F32)],
-        [((192, 1024), BF16), ((288, 1024), BF16)],
-        grad2,
-        up,
-        down,
-        own2,
-        flops=2 * 288 * 192 * 1024,
-    )
     (local01,) = call(
         functools.partial(weights01_kernel, scales[1], scales[0]),
         [((144, 128), F32)],
@@ -466,31 +468,59 @@
         own01,
         flops=2 * 144 * 96 * 6144,
     )
-
-    blocks = deep[None]
+    def swap(block, segments, bit):
+        return over_space(block, segments, lambda n: [(i, i ^ bit) for i in range(n)])
+
+    def behind(values, leader):
+        return lax.optimization_barrier((*values, leader))[:-1]
+
+    def kernel_gradient2(grad2):
+        (local2,) = call(
+            functools.partial(weights2_kernel, scales[2]),
+            [((432, 128), F32)],
+            [((192, 1024), BF16), ((288, 1024), BF16)],
+            grad2,
+            up,
+            down,
+            own2,
+            flops=2 * 288 * 192 * 1024,
+        )
+        return local2
+
+    sum01 = local01
+    grad2, blocks = behind((grad2, deep[None]), sum01)
     places = [0]
-    if count <= GATHER_LIMIT and not count & (count - 1):
-        bit = count // 2
-        while bit:
-            received = over_space(
-                blocks, [3], lambda n, bit=bit: [(i, i ^ bit) for i in range(n)]
-            )
-            blocks = jnp.concatenate([blocks, received], 0)
-            places = places + [place ^ bit for place in places]
-            bit //= 2
+    even = not count & (count - 1)
+    gathers = even and count <= GATHER_LIMIT
+    if even:
+        bits = [1 << power for power in range(count.bit_length() - 1)]
+        sum2 = None
+        for bit, place_bit in zip(bits, reversed(bits)):
+            received01 = swap(sum01, [0, 1], bit)
+            if sum2 is None:
+                sum2 = kernel_gradient2(grad2)
+            received2 = swap(sum2, [2], bit)
+            if gathers:
+                blocks = jnp.concatenate([blocks, swap(blocks, [3], place_bit)], 0)
+                places = places + [place ^ place_bit for place in places]
+            sum01 = sum01 + received01
+            sum2 = sum2 + received2
+            if bit != bits[-1]:
+                sum2, blocks = behind((sum2, blocks), sum01)
+    else:
+        sum2 = lax.psum(kernel_gradient2(grad2), "space")
+        sum01 = lax.psum(sum01, "space")
     held = len(places)
     (sum3,) = call(
         functools.partial(weights3_kernel, scales[3], places),
         [((384, 576), F32)],
         [((128, 256 * held), BF16), ((384, 256 * held), BF16), ((576, 256 * held), BF16)],
         blocks,
-        deep_down,
+        down,
         flops=2 * 384 * 576 * 256 * held,
     )
     if held < count:
-        sum3 = summed(sum3, [3])
-    sum2 = summed(local2, [2])
-    sum01 = summed(local01, [0, 1])
+        sum3 = lax.psum(sum3, "space")
 
     def finish0(sum01, sum2, sum3):
         parts = sum01[:, :48].reshape(3, 3, C1, 3, 16)[..., :C0]

time: 70 us -> 60.8 us (0.87)
  the two profiles are of different devices: /device:TPU:0 before, /device:TPU:2 now
where the time goes in v3:
time: 60.8 us; the launch traced here: 60.3 us
  starting transfers between devices  31.3 us (51%)
  waiting for transfers between devices  19.5 us (32%)
  local copies, waits for them, and re-layouts  6.46 us (11%)
  Pallas kernels  2.19 us (4%)
    ppermute x11, starting transfers between devices, over_space(): return lax.ppermute(block, ('space', 'segment'), pairs_of(segments, route))  24.8 us
    ppermute x11, waiting for transfers between devices, over_space(): return lax.ppermute(block, ('space', 'segment'), pairs_of(segments, route))  11.5 us
    ppermute x1, waiting for transfers between devices, shards(): next_taps = lax.ppermute(fine_taps, 'segment', [(1, 2)])  4.08 us
    ppermute x1, waiting for transfers between devices, shards(): grad0 = lax.ppermute(grad0, 'segment', [(2, 0)])  3.96 us
    unnamed x6, local copies, waits for them, and re-layouts  2.66 us
    pallas_call x6, Pallas kernels, call(): pl.pallas_call(kernel, out_shape=shapes, scratch_shapes=[pltpu.VMEM(*entr...  2.19 us
    slice x1, local copies, waits for them, and re-layouts, by_tap(): weights[0, tap_z * size:(tap_z + 1) * size].reshape(3, 3, chan_out, chan_in)  1.59 us
    ppermute x1, starting transfers between devices, shards(): grad1 = lax.ppermute(grad1, 'segment', [(2, 1)])  1.31 us
  transfers between devices with their start and end apart: 16, of which 5 were waited for; matrix products, arithmetic and copies ran while one was open for 5% of the time, Pallas kernels for 0%

profile of v3, /device:TPU:2, one launch (start us, length us, event | category | flops | bytes accessed | tf_op | source)
XLA Modules:
  0.0 60.3 jit_solution(4279061684288665228)
XLA Ops:
  0.0 1.0 %copy-done = bf16[1,131072]{1,0:T(2,128)(2,1)S(1)} copy-done((bf16[1,131072]{1,0:T(2,128)(2,1)S(1)}, bf16[1,131072]{1,0:T(2,128)(2,1)}, u32[]{:S(2)}) %copy-start) | copy-done | bytes 262168
  1.0 0.7 %copy-done.1 = bf16[128,1,2,32]{0,3,2,1:T(8,128)(2,1)S(1)} copy-done((bf16[128,1,2,32]{0,3,2,1:T(8,128)(2,1)S(1)}, bf16[128,1,2,32]{0,3,2,1:T(8,128)(2,1)}, u32[]{:S(2)}) %copy-start.1) | copy-done | bytes 16408
  1.8 0.1 shard_map.53
  1.9 1.3 %collective-permute-start.1 = (bf16[64,640]{1,0:T(8,128)(2,1)S(1)}, bf16[64,640]{1,0:T(8,128)(2,1)S(1)}, u32[]{:S(2)}, u32[]{:S(2)}) collective-permute-start(bf16[64,640]{1,0:T(8,128)(2,1)S(1)} %get-tuple-element.50), channel_id=1, source_target_pairs={{4,0},{5,1},{6,2},{7,3},{8,4},{9,5},{10,6},{11,7},{12,8},{13,9},{1... | collective-permute-start | bytes 245768 | tf_op jit(solution)/shard_map/ppermute | solution.py:388
  3.2 4.6 %collective-permute-start = (bf16[64,640]{1,0:T(8,128)(2,1)S(1)}, bf16[64,640]{1,0:T(8,128)(2,1)S(1)}, u32[]{:S(2)}, u32[]{:S(2)}) collective-permute-start(bf16[64,640]{1,0:T(8,128)(2,1)S(1)} %get-tuple-element.49.own_ref), channel_id=1, source_target_pairs={{0,4},{1,5},{2,6},{3,7},{4,8},{5,9},{6,10},{7,11},{8,12},{9,13},{1... | collective-permute-start | bytes 245768 | tf_op jit(solution)/shard_map/ppermute | solution.py:388
  7.8 2.9 %conditional.2 = (bf16[576,384]{1,0:T(8,128)(2,1)S(1)}, bf16[144,128]{1,0:T(8,128)(2,1)S(1)}) conditional(s32[]{:T(128)} %clamp.4, () %tuple.39, (bf16[1,221184]{1,0:T(2,128)(2,1)}) %tuple.45, (bf16[1,221184]{1,0:T(2,128)(2,1)}) %tuple.45, (bf16[1,221184]{1,0:T(2,128)(2,1)}) %tuple.45), branch_computations={%region_0.0_spmd, %region_1.2_spmd, %region_2.3_spmd, %region_3.4_... | conditional | flops 3317760 | bytes 4460562 | solution.py:420
  7.8 1.6 %slice_reduce_fusion.5 = (bf16[18432]{0:T(1024)(128)(2,1)S(1)}, bf16[18432]{0:T(1024)(128)(2,1)S(1)}, bf16[18432]{0:T(1024)(128)(2,1)S(1)}) fusion(bf16[1,221184]{1,0:T(2,128)(2,1)} %get-tuple-element.67), kind=kLoop, calls=%fused_computation.26 | loop fusion | bytes 221184 | tf_op jit(solution)/shard_map/cond/branch_2_fun/slice | solution.py:362
  9.4 0.1 squeeze.23
  9.5 0.1 copy.24
  9.6 0.1 reshape.43
  9.8 0.1 squeeze.24
  9.9 0.1 copy.25
  10.0 0.1 reshape.44
  10.2 0.1 squeeze.25
  10.3 0.1 copy.26
  10.4 0.1 reshape.45
  10.7 1.3 %collective-permute-start.2 = (bf16[64,2048]{1,0:T(8,128)(2,1)S(1)}, bf16[64,2048]{1,0:T(8,128)(2,1)S(1)}, u32[]{:S(2)}, u32[]{:S(2)}) collective-permute-start(bf16[64,2048]{1,0:T(8,128)(2,1)S(1)} %shard_map.54), channel_id=1, source_target_pairs={{3,2},{7,6},{11,10},{15,14},{19,18},{23,22},{27,26},{31,30}} | collective-permute-start | bytes 786440 | tf_op jit(solution)/shard_map/ppermute | solution.py:438
  12.0 1.3 %collective-permute-start.3 = (bf16[16,4096]{1,0:T(8,128)(2,1)S(1)}, bf16[16,4096]{1,0:T(8,128)(2,1)S(1)}, u32[]{:S(2)}, u32[]{:S(2)}) collective-permute-start(bf16[16,4096]{1,0:T(8,128)(2,1)S(1)} %get-tuple-element.53.own_ref), channel_id=1, source_target_pairs={{1,2},{5,6},{9,10},{13,14},{17,18},{21,22},{25,26},{29,30}} | collective-permute-start | bytes 393224 | tf_op jit(solution)/shard_map/ppermute | solution.py:425
  13.3 1.3 %collective-permute-start.4 = (bf16[144,128]{1,0:T(8,128)(2,1)S(1)}, bf16[144,128]{1,0:T(8,128)(2,1)S(1)}, u32[]{:S(2)}, u32[]{:S(2)}) collective-permute-start(bf16[144,128]{1,0:T(8,128)(2,1)S(1)} %get-tuple-element.54), channel_id=1, source_target_pairs={{1,2},{5,6},{9,10},{13,14},{17,18},{21,22},{25,26},{29,30}} | collective-permute-start | bytes 110600 | tf_op jit(solution)/shard_map/ppermute | solution.py:426
  14.6 4.1 %collective-permute-done.4.next_weights_ref = bf16[144,128]{1,0:T(8,128)(2,1)S(1)} collective-permute-done((bf16[144,128]{1,0:T(8,128)(2,1)S(1)}, bf16[144,128]{1,0:T(8,128)(2,1)S(1)}, u32[]{:S(2)}, u32[]{:S(2)}) %collective-permute-start.4) | collective-permute-done | bytes 36896 | tf_op jit(solution)/shard_map/ppermute | solution.py:426
  18.7 1.2 %shard_map.55 = (bf16[32,4096]{1,0:T(8,128)(2,1)S(1)}, bf16[16,4096]{1,0:T(8,128)(2,1)S(1)}) custom-call(bf16[64,2048]{1,0:T(8,128)(2,1)S(1)} %collective-permute-done.2.grad_ref, bf16[64,640]{1,0:T(8,128)(2,1)S(1)} %collective-permute-done.up_ref, bf16[64,640]{1,0:T(8,128)(2,1)S(1)} %collective-permute-done.1.down_ref, ...), custom_call_target="tpu_custom_call" | custom-call | flops 226492416 | bytes 1691648 | tf_op jit(solution)/shard_map/pallas_call | solution.py:345
  19.9 1.3 %collective-permute-start.6 = (bf16[32,4096]{1,0:T(8,128)(2,1)S(1)}, bf16[32,4096]{1,0:T(8,128)(2,1)S(1)}, u32[]{:S(2)}, u32[]{:S(2)}) collective-permute-start(bf16[32,4096]{1,0:T(8,128)(2,1)S(1)} %get-tuple-element.56), channel_id=1, source_target_pairs={{2,1},{6,5},{10,9},{14,13},{18,17},{22,21},{26,25},{30,29}} | collective-permute-start | bytes 786440 | tf_op jit(solution)/shard_map/ppermute | solution.py:459
  21.2 1.3 %collective-permute-start.5 = (bf16[16,4096]{1,0:T(8,128)(2,1)S(1)}, bf16[16,4096]{1,0:T(8,128)(2,1)S(1)}, u32[]{:S(2)}, u32[]{:S(2)}) collective-permute-start(bf16[16,4096]{1,0:T(8,128)(2,1)S(1)} %get-tuple-element.55), channel_id=1, source_target_pairs={{2,0},{6,4},{10,8},{14,12},{18,16},{22,20},{26,24},{30,28}} | collective-permute-start | bytes 393224 | tf_op jit(solution)/shard_map/ppermute | solution.py:458
  22.5 4.0 %collective-permute-done.5.grad0_ref = bf16[16,4096]{1,0:T(8,128)(2,1)S(1)} collective-permute-done((bf16[16,4096]{1,0:T(8,128)(2,1)S(1)}, bf16[16,4096]{1,0:T(8,128)(2,1)S(1)}, u32[]{:S(2)}, u32[]{:S(2)}) %collective-permute-start.5) | collective-permute-done | bytes 131104 | tf_op jit(solution)/shard_map/ppermute | solution.py:458
  26.5 0.6 %shard_map.57 = f32[432,128]{1,0:T(8,128)S(1)} custom-call(bf16[64,2048]{1,0:T(8,128)(2,1)S(1)} %collective-permute-done.2.grad_ref, bf16[64,640]{1,0:T(8,128)(2,1)S(1)} %collective-permute-done.up_ref, bf16[64,640]{1,0:T(8,128)(2,1)S(1)} %collective-permute-done.1.down_ref, bf16[32,4096]{1,0:T(8,128)(2,1)S(1)} %get-tuple-element.52.own_ref), custom_call_target="tpu_custom_call" | custom-call | flops 113246208 | bytes 909312 | tf_op jit(solution)/shard_map/pallas_call | solution.py:345
  27.1 4.3 %collective-permute-start.10 = (f32[432,128]{1,0:T(8,128)S(1)}, f32[432,128]{1,0:T(8,128)S(1)}, u32[]{:S(2)}, u32[]{:S(2)}) collective-permute-start(f32[432,128]{1,0:T(8,128)S(1)} %shard_map.57), channel_id=1, source_target_pairs={{2,6},{6,2},{10,14},{14,10},{18,22},{22,18},{26,30},{30,26}} | collective-permute-start | bytes 663560 | tf_op jit(solution)/shard_map/ppermute | solution.py:388
  31.5 0.7 %collective-permute-start.11 = (bf16[1,64,640]{2,1,0:T(8,128)(2,1)S(1)}, bf16[1,64,640]{2,1,0:T(8,128)(2,1)S(1)}, u32[]{:S(2)}, u32[]{:S(2)}) collective-permute-start(bf16[1,64,640]{2,1,0:T(8,128)(2,1)S(1)} %bitcast.51), channel_id=1, source_target_pairs={{3,19},{7,23},{11,27},{15,31},{19,3},{23,7},{27,11},{31,15}} | collective-permute-start | bytes 245768 | tf_op jit(solution)/shard_map/ppermute | solution.py:388
  32.1 0.7 %collective-permute-start.7 = (f32[144,128]{1,0:T(8,128)S(1)}, f32[144,128]{1,0:T(8,128)S(1)}, u32[]{:S(2)}, u32[]{:S(2)}) collective-permute-start(f32[144,128]{1,0:T(8,128)S(1)} %shard_map.56), channel_id=1, source_target_pairs={{0,4},{1,5},{4,0},{5,1},{8,12},{9,13},{12,8},{13,9},{16,20},{17,21... | collective-permute-start | bytes 221192 | tf_op jit(solution)/shard_map/ppermute | solution.py:388
  32.9 2.5 %collective-permute-done.10 = f32[432,128]{1,0:T(8,128)S(1)} collective-permute-done((f32[432,128]{1,0:T(8,128)S(1)}, f32[432,128]{1,0:T(8,128)S(1)}, u32[]{:S(2)}, u32[]{:S(2)}) %collective-permute-start.10) | collective-permute-done | bytes 221216 | tf_op jit(solution)/shard_map/ppermute | solution.py:388
  35.4 0.7 %collective-permute-start.13 = (bf16[2,64,640]{2,1,0:T(8,128)(2,1)S(1)}, bf16[2,64,640]{2,1,0:T(8,128)(2,1)S(1)}, u32[]{:S(2)}, u32[]{:S(2)}) collective-permute-start(bf16[2,64,640]{2,1,0:T(8,128)(2,1)S(1)} %pad_maximum_fusion.3), channel_id=1, source_target_pairs={{3,11},{7,15},{11,3},{15,7},{19,27},{23,31},{27,19},{31,23}} | collective-permute-start | bytes 491528 | tf_op jit(solution)/shard_map/ppermute | solution.py:388
  36.1 6.1 %collective-permute-start.12 = (f32[432,128]{1,0:T(8,128)S(1)}, f32[432,128]{1,0:T(8,128)S(1)}, u32[]{:S(2)}, u32[]{:S(2)}) collective-permute-start(f32[432,128]{1,0:T(8,128)S(1)} %add.41), channel_id=1, source_target_pairs={{2,10},{6,14},{10,2},{14,6},{18,26},{22,30},{26,18},{30,22}} | collective-permute-start | bytes 663560 | tf_op jit(solution)/shard_map/ppermute | solution.py:388
  42.1 0.7 %collective-permute-start.8 = (f32[144,128]{1,0:T(8,128)S(1)}, f32[144,128]{1,0:T(8,128)S(1)}, u32[]{:S(2)}, u32[]{:S(2)}) collective-permute-start(f32[144,128]{1,0:T(8,128)S(1)} %add.39), channel_id=1, source_target_pairs={{0,8},{1,9},{4,12},{5,13},{8,0},{9,1},{12,4},{13,5},{16,24},{17,25... | collective-permute-start | bytes 221192 | tf_op jit(solution)/shard_map/ppermute | solution.py:388
  42.9 3.1 %collective-permute-done.12 = f32[432,128]{1,0:T(8,128)S(1)} collective-permute-done((f32[432,128]{1,0:T(8,128)S(1)}, f32[432,128]{1,0:T(8,128)S(1)}, u32[]{:S(2)}, u32[]{:S(2)}) %collective-permute-start.12) | collective-permute-done | bytes 221216 | tf_op jit(solution)/shard_map/ppermute | solution.py:388
  46.1 0.7 %collective-permute-start.15 = (bf16[4,64,640]{2,1,0:T(8,128)(2,1)S(1)}, bf16[4,64,640]{2,1,0:T(8,128)(2,1)S(1)}, u32[]{:S(2)}, u32[]{:S(2)}) collective-permute-start(bf16[4,64,640]{2,1,0:T(8,128)(2,1)S(1)} %pad_maximum_fusion.2), channel_id=1, source_target_pairs={{3,7},{7,3},{11,15},{15,11},{19,23},{23,19},{27,31},{31,27}} | collective-permute-start | bytes 983048 | tf_op jit(solution)/shard_map/ppermute | solution.py:388
  46.7 4.6 %collective-permute-start.14 = (f32[432,128]{1,0:T(8,128)S(1)}, f32[432,128]{1,0:T(8,128)S(1)}, u32[]{:S(2)}, u32[]{:S(2)}) collective-permute-start(f32[432,128]{1,0:T(8,128)S(1)} %add.42), channel_id=1, source_target_pairs={{2,18},{6,22},{10,26},{14,30},{18,2},{22,6},{26,10},{30,14}} | collective-permute-start | bytes 663560 | tf_op jit(solution)/shard_map/ppermute | solution.py:388
  51.3 0.7 %collective-permute-start.9 = (f32[144,128]{1,0:T(8,128)S(1)}, f32[144,128]{1,0:T(8,128)S(1)}, u32[]{:S(2)}, u32[]{:S(2)}) collective-permute-start(f32[144,128]{1,0:T(8,128)S(1)} %add.40), channel_id=1, source_target_pairs={{0,16},{1,17},{4,20},{5,21},{8,24},{9,25},{12,28},{13,29},{16,0},{... | collective-permute-start | bytes 221192 | tf_op jit(solution)/shard_map/ppermute | solution.py:388
  52.0 5.8 %collective-permute-done.14 = f32[432,128]{1,0:T(8,128)S(1)} collective-permute-done((f32[432,128]{1,0:T(8,128)S(1)}, f32[432,128]{1,0:T(8,128)S(1)}, u32[]{:S(2)}, u32[]{:S(2)}) %collective-permute-start.14) | collective-permute-done | bytes 221216 | tf_op jit(solution)/shard_map/ppermute | solution.py:388
  57.8 0.1 pad_maximum_fusion.1.blocks_ref
  57.9 0.2 shard_map.58
  58.1 1.3 %conditional.3 = (f32[1,221184]{1,0:T(1,128)S(1)}) conditional(s32[]{:T(128)} %clamp.4, (f32[144,128]{1,0:T(8,128)S(1)}, f32[144,128]{1,0:T(8,128)S(1)}) %tuple.40, (f32[144,128]{1,0:T(8,128)S(1)}, f32[144,128]{1,0:T(8,128)S(1)}) %tuple.40, (f32[432,128]{1,0:T(8,128)S(1)}, f32[432,128]{1,0:T(8,128)S(1)}) %tuple.44, ...), branch_computations={%region_4.5_spmd, %region_5.6_spmd, %region_6.7_spmd, %region_7.8_... | conditional | flops 110592 | bytes 7077896 | solution.py:542
  58.2 0.1 reshape.54
  58.4 0.2 copy.34
  58.5 0.2 reshape.53
  58.7 0.2 copy.33
  59.0 0.1 maximum_bitcast_fusion
  59.1 0.2 reshape.56
  59.3 0.1 pad.19
  59.4 0.9 %copy-done.2 = f32[1,221184]{1,0:T(1,128)} copy-done((f32[1,221184]{1,0:T(1,128)}, f32[1,221184]{1,0:T(1,128)S(1)}, u32[]{:S(2)}) %copy-start.2) | copy-done | bytes 884760
  (28 shorter events, 0.3 us)
Async XLA Ops:
  0.0 1.0 %copy-start = (bf16[1,131072]{1,0:T(2,128)(2,1)S(1)}, bf16[1,131072]{1,0:T(2,128)(2,1)}, u32[]{:S(2)}) copy-start(bf16[1,131072]{1,0:T(2,128)(2,1)} %saved_ref.1) | copy-start | bytes 786436
  1.0 0.7 %copy-start.1 = (bf16[128,1,2,32]{0,3,2,1:T(8,128)(2,1)S(1)}, bf16[128,1,2,32]{0,3,2,1:T(8,128)(2,1)}, u32[]{:S(2)}) copy-start(bf16[128,1,2,32]{0,3,2,1:T(8,128)(2,1)} %param.13) | copy-start | bytes 49156
  1.9 8.8 %collective-permute-start.1 = (bf16[64,640]{1,0:T(8,128)(2,1)S(1)}, bf16[64,640]{1,0:T(8,128)(2,1)S(1)}, u32[]{:S(2)}, u32[]{:S(2)}) collective-permute-start(bf16[64,640]{1,0:T(8,128)(2,1)S(1)} %get-tuple-element.50), channel_id=1, source_target_pairs={{4,0},{5,1},{6,2},{7,3},{8,4},{9,5},{10,6},{11,7},{12,8},{13,9},{1... | collective-permute-start | bytes 245768 | tf_op jit(solution)/shard_map/ppermute | solution.py:388
  3.2 7.5 %collective-permute-start = (bf16[64,640]{1,0:T(8,128)(2,1)S(1)}, bf16[64,640]{1,0:T(8,128)(2,1)S(1)}, u32[]{:S(2)}, u32[]{:S(2)}) collective-permute-start(bf16[64,640]{1,0:T(8,128)(2,1)S(1)} %get-tuple-element.49.own_ref), channel_id=1, source_target_pairs={{0,4},{1,5},{2,6},{3,7},{4,8},{5,9},{6,10},{7,11},{8,12},{9,13},{1... | collective-permute-start | bytes 245768 | tf_op jit(solution)/shard_map/ppermute | solution.py:388
  10.7 8.0 %collective-permute-start.2 = (bf16[64,2048]{1,0:T(8,128)(2,1)S(1)}, bf16[64,2048]{1,0:T(8,128)(2,1)S(1)}, u32[]{:S(2)}, u32[]{:S(2)}) collective-permute-start(bf16[64,2048]{1,0:T(8,128)(2,1)S(1)} %shard_map.54), channel_id=1, source_target_pairs={{3,2},{7,6},{11,10},{15,14},{19,18},{23,22},{27,26},{31,30}} | collective-permute-start | bytes 786440 | tf_op jit(solution)/shard_map/ppermute | solution.py:438
  12.0 6.7 %collective-permute-start.3 = (bf16[16,4096]{1,0:T(8,128)(2,1)S(1)}, bf16[16,4096]{1,0:T(8,128)(2,1)S(1)}, u32[]{:S(2)}, u32[]{:S(2)}) collective-permute-start(bf16[16,4096]{1,0:T(8,128)(2,1)S(1)} %get-tuple-element.53.own_ref), channel_id=1, source_target_pairs={{1,2},{5,6},{9,10},{13,14},{17,18},{21,22},{25,26},{29,30}} | collective-permute-start | bytes 393224 | tf_op jit(solution)/shard_map/ppermute | solution.py:425
  13.3 5.4 %collective-permute-start.4 = (bf16[144,128]{1,0:T(8,128)(2,1)S(1)}, bf16[144,128]{1,0:T(8,128)(2,1)S(1)}, u32[]{:S(2)}, u32[]{:S(2)}) collective-permute-start(bf16[144,128]{1,0:T(8,128)(2,1)S(1)} %get-tuple-element.54), channel_id=1, source_target_pairs={{1,2},{5,6},{9,10},{13,14},{17,18},{21,22},{25,26},{29,30}} | collective-permute-start | bytes 110600 | tf_op jit(solution)/shard_map/ppermute | solution.py:426
  19.9 6.6 %collective-permute-start.6 = (bf16[32,4096]{1,0:T(8,128)(2,1)S(1)}, bf16[32,4096]{1,0:T(8,128)(2,1)S(1)}, u32[]{:S(2)}, u32[]{:S(2)}) collective-permute-start(bf16[32,4096]{1,0:T(8,128)(2,1)S(1)} %get-tuple-element.56), channel_id=1, source_target_pairs={{2,1},{6,5},{10,9},{14,13},{18,17},{22,21},{26,25},{30,29}} | collective-permute-start | bytes 786440 | tf_op jit(solution)/shard_map/ppermute | solution.py:459
  21.2 5.3 %collective-permute-start.5 = (bf16[16,4096]{1,0:T(8,128)(2,1)S(1)}, bf16[16,4096]{1,0:T(8,128)(2,1)S(1)}, u32[]{:S(2)}, u32[]{:S(2)}) collective-permute-start(bf16[16,4096]{1,0:T(8,128)(2,1)S(1)} %get-tuple-element.55), channel_id=1, source_target_pairs={{2,0},{6,4},{10,8},{14,12},{18,16},{22,20},{26,24},{30,28}} | collective-permute-start | bytes 393224 | tf_op jit(solution)/shard_map/ppermute | solution.py:458
  27.1 8.2 %collective-permute-start.10 = (f32[432,128]{1,0:T(8,128)S(1)}, f32[432,128]{1,0:T(8,128)S(1)}, u32[]{:S(2)}, u32[]{:S(2)}) collective-permute-start(f32[432,128]{1,0:T(8,128)S(1)} %shard_map.57), channel_id=1, source_target_pairs={{2,6},{6,2},{10,14},{14,10},{18,22},{22,18},{26,30},{30,26}} | collective-permute-start | bytes 663560 | tf_op jit(solution)/shard_map/ppermute | solution.py:388
  31.5 1.4 %collective-permute-start.11 = (bf16[1,64,640]{2,1,0:T(8,128)(2,1)S(1)}, bf16[1,64,640]{2,1,0:T(8,128)(2,1)S(1)}, u32[]{:S(2)}, u32[]{:S(2)}) collective-permute-start(bf16[1,64,640]{2,1,0:T(8,128)(2,1)S(1)} %bitcast.51), channel_id=1, source_target_pairs={{3,19},{7,23},{11,27},{15,31},{19,3},{23,7},{27,11},{31,15}} | collective-permute-start | bytes 245768 | tf_op jit(solution)/shard_map/ppermute | solution.py:388
  32.1 0.7 %collective-permute-start.7 = (f32[144,128]{1,0:T(8,128)S(1)}, f32[144,128]{1,0:T(8,128)S(1)}, u32[]{:S(2)}, u32[]{:S(2)}) collective-permute-start(f32[144,128]{1,0:T(8,128)S(1)} %shard_map.56), channel_id=1, source_target_pairs={{0,4},{1,5},{4,0},{5,1},{8,12},{9,13},{12,8},{13,9},{16,20},{17,21... | collective-permute-start | bytes 221192 | tf_op jit(solution)/shard_map/ppermute | solution.py:388
  35.4 7.5 %collective-permute-start.13 = (bf16[2,64,640]{2,1,0:T(8,128)(2,1)S(1)}, bf16[2,64,640]{2,1,0:T(8,128)(2,1)S(1)}, u32[]{:S(2)}, u32[]{:S(2)}) collective-permute-start(bf16[2,64,640]{2,1,0:T(8,128)(2,1)S(1)} %pad_maximum_fusion.3), channel_id=1, source_target_pairs={{3,11},{7,15},{11,3},{15,7},{19,27},{23,31},{27,19},{31,23}} | collective-permute-start | bytes 491528 | tf_op jit(solution)/shard_map/ppermute | solution.py:388
  36.1 10.0 %collective-permute-start.12 = (f32[432,128]{1,0:T(8,128)S(1)}, f32[432,128]{1,0:T(8,128)S(1)}, u32[]{:S(2)}, u32[]{:S(2)}) collective-permute-start(f32[432,128]{1,0:T(8,128)S(1)} %add.41), channel_id=1, source_target_pairs={{2,10},{6,14},{10,2},{14,6},{18,26},{22,30},{26,18},{30,22}} | collective-permute-start | bytes 663560 | tf_op jit(solution)/shard_map/ppermute | solution.py:388
  42.1 0.7 %collective-permute-start.8 = (f32[144,128]{1,0:T(8,128)S(1)}, f32[144,128]{1,0:T(8,128)S(1)}, u32[]{:S(2)}, u32[]{:S(2)}) collective-permute-start(f32[144,128]{1,0:T(8,128)S(1)} %add.39), channel_id=1, source_target_pairs={{0,8},{1,9},{4,12},{5,13},{8,0},{9,1},{12,4},{13,5},{16,24},{17,25... | collective-permute-start | bytes 221192 | tf_op jit(solution)/shard_map/ppermute | solution.py:388
  46.1 11.8 %collective-permute-start.15 = (bf16[4,64,640]{2,1,0:T(8,128)(2,1)S(1)}, bf16[4,64,640]{2,1,0:T(8,128)(2,1)S(1)}, u32[]{:S(2)}, u32[]{:S(2)}) collective-permute-start(bf16[4,64,640]{2,1,0:T(8,128)(2,1)S(1)} %pad_maximum_fusion.2), channel_id=1, source_target_pairs={{3,7},{7,3},{11,15},{15,11},{19,23},{23,19},{27,31},{31,27}} | collective-permute-start | bytes 983048 | tf_op jit(solution)/shard_map/ppermute | solution.py:388
  46.7 11.1 %collective-permute-start.14 = (f32[432,128]{1,0:T(8,128)S(1)}, f32[432,128]{1,0:T(8,128)S(1)}, u32[]{:S(2)}, u32[]{:S(2)}) collective-permute-start(f32[432,128]{1,0:T(8,128)S(1)} %add.42), channel_id=1, source_target_pairs={{2,18},{6,22},{10,26},{14,30},{18,2},{22,6},{26,10},{30,14}} | collective-permute-start | bytes 663560 | tf_op jit(solution)/shard_map/ppermute | solution.py:388
  51.3 0.7 %collective-permute-start.9 = (f32[144,128]{1,0:T(8,128)S(1)}, f32[144,128]{1,0:T(8,128)S(1)}, u32[]{:S(2)}, u32[]{:S(2)}) collective-permute-start(f32[144,128]{1,0:T(8,128)S(1)} %add.40), channel_id=1, source_target_pairs={{0,16},{1,17},{4,20},{5,21},{8,24},{9,25},{12,28},{13,29},{16,0},{... | collective-permute-start | bytes 221192 | tf_op jit(solution)/shard_map/ppermute | solution.py:388
  59.4 0.9 %copy-start.2 = (f32[1,221184]{1,0:T(1,128)}, f32[1,221184]{1,0:T(1,128)S(1)}, u32[]{:S(2)}) copy-start(f32[1,221184]{1,0:T(1,128)S(1)} %get-tuple-element.112) | copy-start | bytes 2654212

commit v4 on v3

--- a/solution.py
+++ b/solution.py
@@ -15,6 +15,7 @@
 F32 = jnp.float32
 GATHER_LIMIT = 8
 VMEM_LIMIT = 48 * 1024 * 1024
+LONG = 20_000_000_000
 
 
 def on_segment(index):
@@ -94,8 +95,17 @@
         wide[chan : chan + 1, :width] = source.astype(F32)
 
 
-def layout_kernel(saved_ref, top_ref, up_ref, down_ref, own2_ref, own01_ref, wide):
-    def send(chans, place, plane, target_ref):
+def layout_kernel(
+    saved_ref, top_ref, taps_ref, up_ref, down_ref, own2_ref, own01_ref, held, wide, arrived
+):
+    def fetch(size):
+        copy = pltpu.make_async_copy(
+            saved_ref.at[:, pl.ds(0, size)], held.at[:, pl.ds(0, size)], arrived
+        )
+        copy.start()
+        copy.wait()
+
+    def send(place, plane, target_ref):
         for half in range(2):
             target_ref[32 * half : 32 * half + place, :512] = wide[
                 :place, cols(8 * plane + 4 * half, 4)
@@ -103,7 +113,8 @@
 
     @pl.when(on_segment(3))
     def _():
-        copy_rows(saved_ref, wide, C3, 512)
+        fetch(C3 * 512)
+        copy_rows(held, wide, C3, 512)
         block = wide[:, :512].astype(BF16)
         for ref in (up_ref, down_ref):
             ref[:, :512] = block
@@ -115,12 +126,16 @@
         def _(section=section, chans=chans):
             if section == 0:
                 wide[:C1, :] = jnp.zeros((C1, 4096), F32)
-            copy_rows(saved_ref, wide, chans, 4096)
+            fetch(chans * 4096)
+            copy_rows(held, wide, chans, 4096)
             place = max(chans, C1)
             own_ref = own2_ref if section == 2 else own01_ref
-            own_ref[...] = wide[:place, :].astype(BF16)
-            send(chans, place, 3, up_ref)
-            send(chans, place, 0, down_ref)
+            own_ref[:, :4096] = wide[:place, :].astype(BF16)
+            if section == 1:
+                for tap in range(9):
+                    own01_ref[:, cols(32 + tap)] = taps_ref[C1 * tap : C1 * (tap + 1), :]
+            send(place, 3, up_ref)
+            send(place, 0, down_ref)
 
 
 def section3_kernel(own_ref, up_ref, down_ref, weights_ref, out_ref, wide, stacked, terms):
@@ -158,13 +173,13 @@
     down_ref,
     own_ref,
     weights_ref,
-    next_own_ref,
-    next_weights_ref,
+    next_ref,
     out1_ref,
     out0_ref,
     stacked,
     terms,
     middle,
+    next_weights,
     next_stacked,
     next_terms,
 ):
@@ -194,7 +209,9 @@
                 if 0 <= cell_z < 4:
                     out1_ref[:, cols(8 * cell_z + cell_y)] = result
         stack_moved(lambda row: middle[:, cols(row)], next_stacked, C2, 48, (-1, 0, 1))
-        next_terms[...] = dot(next_weights_ref[:, :96], next_stacked[...])
+        for tap in range(9):
+            next_weights[C1 * tap : C1 * (tap + 1), :] = next_ref[:, cols(32 + tap)]
+        next_terms[...] = dot(next_weights[:, :96], next_stacked[...])
         edge = jnp.zeros((C1, LANES), F32)
         for plane in range(4):
             sums = []
@@ -207,7 +224,7 @@
                 sums.append(total)
             later = jnp.concatenate([sums[0][:, LANES:], edge], 1)
             earlier = jnp.concatenate([edge, sums[2][:, : 7 * LANES]], 1)
-            mask = next_own_ref[:, cols(8 * plane, 8)].astype(F32)
+            mask = next_ref[:, cols(8 * plane, 8)].astype(F32)
             out0_ref[:, cols(8 * plane, 8)] = sloped(sums[1] + later + earlier, mask)
 
 
@@ -339,13 +356,18 @@
     return bits
 
 
-def call(kernel, outs, scratch, *args, flops):
+def call(kernel, outs, scratch, *args, flops, far=()):
     shapes = [jax.ShapeDtypeStruct(*entry) for entry in outs]
     moved = sum(a.size * a.dtype.itemsize for a in [*args, *shapes])
+    near_spec = pl.BlockSpec(memory_space=pltpu.VMEM)
+    far_spec = pl.BlockSpec(memory_space=pltpu.HBM)
     return pl.pallas_call(
         kernel,
         out_shape=shapes,
-        scratch_shapes=[pltpu.VMEM(*entry) for entry in scratch],
+        in_specs=[far_spec if place in far else near_spec for place in range(len(args))],
+        scratch_shapes=[
+            pltpu.VMEM(*entry) if isinstance(entry, tuple) else entry for entry in scratch
+        ],
         compiler_params=pltpu.CompilerParams(vmem_limit_bytes=VMEM_LIMIT),
         cost_estimate=pl.CostEstimate(flops=flops, bytes_accessed=moved, transcendentals=0),
     )(*args)
@@ -405,25 +427,31 @@
     def sooner(n):
         return [(i + 1, i) for i in range(n - 1)]
 
-    top = jnp.transpose(top_gradient[:, 0], (1, 2, 0)).reshape(64, C4)
-    to_later, to_sooner, own2, own01 = call(
-        layout_kernel,
-        [((64, 640), BF16), ((64, 640), BF16), ((32, 4096), BF16), ((16, 4096), BF16)],
-        [((64, 4096), F32)],
-        saved_inputs,
-        top,
-        flops=0,
-    )
-    deep = to_later
-    up = over_space(to_later, range(4), later)
-    down = over_space(to_sooner, range(4), sooner)
+    def behind(values, *leaders):
+        return lax.optimization_barrier((*values, *leaders))[: len(values)]
+
     deep_taps, fine_taps = lax.switch(
         segment,
         [functools.partial(tap_layouts, section) for section in range(4)],
         conv_weights,
     )
+    top = jnp.transpose(top_gradient[:, 0], (1, 2, 0)).reshape(64, C4)
+    top, fine_taps = behind((top, fine_taps), deep_taps)
+    to_later, to_sooner, own2, own01 = call(
+        layout_kernel,
+        [((64, 640), BF16), ((64, 640), BF16), ((32, 4096), BF16), ((16, 5248), BF16)],
+        [((1, 131072), BF16), ((64, 4096), F32), pltpu.SemaphoreType.DMA],
+        saved_inputs,
+        top,
+        fine_taps,
+        flops=0,
+        far=(0,),
+    )
+    deep = to_later
+    up = over_space(to_later, range(4), later)
+    down = over_space(to_sooner, range(4), sooner)
     next_own = lax.ppermute(own01, "segment", [(1, 2)])
-    next_taps = lax.ppermute(fine_taps, "segment", [(1, 2)])
+    (deep_taps,) = behind((deep_taps,), next_own)
 
     (grad2,) = call(
         section3_kernel,
@@ -443,6 +471,7 @@
             ((192, 2048), BF16),
             ((288, 2048), F32),
             ((32, 6144), BF16),
+            ((144, 128), BF16),
             ((96, 6144), BF16),
             ((144, 6144), F32),
         ],
@@ -452,12 +481,38 @@
         own2,
         deep_taps,
         next_own,
-        next_taps,
         flops=2 * 288 * 192 * 2048,
     )
+    def swap(block, segments, bit):
+        return over_space(block, segments, lambda n: [(i, i ^ bit) for i in range(n)])
+
+    grad2, blocks = behind((grad2, deep[None]), grad1)
     grad0 = lax.ppermute(grad0, "segment", [(2, 0)])
     grad1 = lax.ppermute(grad1, "segment", [(2, 1)])
-    (local01,) = call(
+    (sum2,) = call(
+        functools.partial(weights2_kernel, scales[2]),
+        [((432, 128), F32)],
+        [((192, 1024), BF16), ((288, 1024), BF16)],
+        grad2,
+        up,
+        down,
+        own2,
+        flops=LONG,
+    )
+    places = [0]
+    even = not count & (count - 1)
+    gathers = even and count <= GATHER_LIMIT
+    bits = [1 << power for power in range(count.bit_length() - 1)] if even else []
+
+    def gathered(blocks, bit):
+        return jnp.concatenate([blocks, swap(blocks, [3], bit)], 0)
+
+    if gathers:
+        for bit in bits[:0:-1]:
+            blocks = gathered(blocks, bit)
+            places = places + [place ^ bit for place in places]
+    grad0, grad1 = behind((grad0, grad1), sum2, blocks)
+    (sum01,) = call(
         functools.partial(weights01_kernel, scales[1], scales[0]),
         [((144, 128), F32)],
         [((96, 4096), BF16), ((144, 4096), BF16)],
@@ -468,48 +523,16 @@
         own01,
         flops=2 * 144 * 96 * 6144,
     )
-    def swap(block, segments, bit):
-        return over_space(block, segments, lambda n: [(i, i ^ bit) for i in range(n)])
-
-    def behind(values, leader):
-        return lax.optimization_barrier((*values, leader))[:-1]
-
-    def kernel_gradient2(grad2):
-        (local2,) = call(
-            functools.partial(weights2_kernel, scales[2]),
-            [((432, 128), F32)],
-            [((192, 1024), BF16), ((288, 1024), BF16)],
-            grad2,
-            up,
-            down,
-            own2,
-            flops=2 * 288 * 192 * 1024,
-        )
-        return local2
-
-    sum01 = local01
-    grad2, blocks = behind((grad2, deep[None]), sum01)
-    places = [0]
-    even = not count & (count - 1)
-    gathers = even and count <= GATHER_LIMIT
-    if even:
-        bits = [1 << power for power in range(count.bit_length() - 1)]
-        sum2 = None
-        for bit, place_bit in zip(bits, reversed(bits)):
-            received01 = swap(sum01, [0, 1], bit)
-            if sum2 is None:
-                sum2 = kernel_gradient2(grad2)
-            received2 = swap(sum2, [2], bit)
-            if gathers:
-                blocks = jnp.concatenate([blocks, swap(blocks, [3], place_bit)], 0)
-                places = places + [place ^ place_bit for place in places]
-            sum01 = sum01 + received01
-            sum2 = sum2 + received2
-            if bit != bits[-1]:
-                sum2, blocks = behind((sum2, blocks), sum01)
-    else:
-        sum2 = lax.psum(kernel_gradient2(grad2), "space")
+    for bit in bits:
+        sum2 = sum2 + swap(sum2, [2], bit)
+    if not even:
+        sum2 = lax.psum(sum2, "space")
         sum01 = lax.psum(sum01, "space")
+    if gathers:
+        blocks = gathered(blocks, bits[0])
+        places = places + [place ^ bits[0] for place in places]
+    for bit in bits:
+        sum01 = sum01 + swap(sum01, [0, 1], bit)
     held = len(places)
     (sum3,) = call(
         functools.partial(weights3_kernel, scales[3], places),
@@ -517,7 +540,7 @@
         [((128, 256 * held), BF16), ((384, 256 * held), BF16), ((576, 256 * held), BF16)],
         blocks,
         down,
-        flops=2 * 384 * 576 * 256 * held,
+        flops=LONG,
     )
     if held < count:
         sum3 = lax.psum(sum3, "space")

time: 60.8 us -> 55.2 us (0.908)
  waiting for transfers between devices: 19.5 us -> 16.9 us
  local copies, waits for them, and re-layouts: 6.46 us -> 4.81 us
  starting transfers between devices: 31.3 us -> 29.9 us
    ppermute x1 -> x0, waiting for transfers between devices: 4.08 us -> none  [shards(): next_taps = lax.ppermute(fine_taps, 'segment', [(1, 2)])]
    ppermute x1, waiting for transfers between devices: 3.96 us -> 0.01 us  [shards(): grad0 = lax.ppermute(grad0, 'segment', [(2, 0)])]
    ppermute x11, waiting for transfers between devices: 11.5 us -> 14.6 us  [over_space(): return lax.ppermute(block, ('space', 'segment'), pairs_of(segments, route))]
    ppermute x1, waiting for transfers between devices: 0.01 us -> 2.22 us  [shards(): grad2 = lax.ppermute(grad2, 'segment', [(3, 2)])]
    unnamed x6 -> x8, local copies, waits for them, and re-layouts: 2.66 us -> 0.94 us
    ppermute x1 -> x0, starting transfers between devices: 1.29 us -> none  [shards(): next_taps = lax.ppermute(fine_taps, 'segment', [(1, 2)])]
  transfers between devices with their start and end apart: 16 -> 15, of which waited for: 5 -> 6; matrix products, arithmetic and copies ran while one was open for 5% -> 0% of each run, Pallas kernels for 0% -> 2%
where the time goes in v4:
time: 55.2 us; the launch traced here: 54.6 us
  starting transfers between devices  29.9 us (54%)
  waiting for transfers between devices  16.9 us (31%)
  local copies, waits for them, and re-layouts  4.81 us (9%)
  Pallas kernels  2.28 us (4%)
    ppermute x11, starting transfers between devices, over_space(): return lax.ppermute(block, ('space', 'segment'), pairs_of(segments, route))  24.7 us
    ppermute x11, waiting for transfers between devices, over_space(): return lax.ppermute(block, ('space', 'segment'), pairs_of(segments, route))  14.6 us
    pallas_call x6, Pallas kernels, call(): pl.pallas_call(kernel, out_shape=shapes, in_specs=[far_spec if place in f...  2.28 us
    ppermute x1, waiting for transfers between devices, shards(): grad2 = lax.ppermute(grad2, 'segment', [(3, 2)])  2.22 us
    slice x1, local copies, waits for them, and re-layouts, by_tap(): weights[0, tap_z * size:(tap_z + 1) * size].reshape(3, 3, chan_out, chan_in)  1.64 us
    ppermute x1, starting transfers between devices, shards(): grad1 = lax.ppermute(grad1, 'segment', [(2, 1)])  1.31 us
    ppermute x1, starting transfers between devices, shards(): grad0 = lax.ppermute(grad0, 'segment', [(2, 0)])  1.3 us
    ppermute x1, starting transfers between devices, shards(): next_own = lax.ppermute(own01, 'segment', [(1, 2)])  1.29 us
  transfers between devices with their start and end apart: 15, of which 6 were waited for; matrix products, arithmetic and copies ran while one was open for 0% of the time, Pallas kernels for 2%

profile of v4, /device:TPU:2, one launch (start us, length us, event | category | flops | bytes accessed | tf_op | source)
XLA Modules:
  0.0 54.6 jit_solution(14734222792077258758)
XLA Ops:
  0.0 2.9 %conditional.2 = (bf16[576,384]{1,0:T(8,128)(2,1)S(1)}, bf16[144,128]{1,0:T(8,128)(2,1)S(1)}) conditional(s32[]{:T(128)} %clamp.4, () %tuple.40, (bf16[1,221184]{1,0:T(2,128)(2,1)}) %tuple.47, (bf16[1,221184]{1,0:T(2,128)(2,1)}) %tuple.47, (bf16[1,221184]{1,0:T(2,128)(2,1)}) %tuple.47), branch_computations={%region_0.0_spmd, %region_1.2_spmd, %region_2.3_spmd, %region_3.4_... | conditional | flops 3317760 | bytes 4460562 | solution.py:433
  0.0 1.6 %slice_reduce_fusion.5 = (bf16[18432]{0:T(1024)(128)(2,1)S(1)}, bf16[18432]{0:T(1024)(128)(2,1)S(1)}, bf16[18432]{0:T(1024)(128)(2,1)S(1)}) fusion(bf16[1,221184]{1,0:T(2,128)(2,1)} %get-tuple-element.69), kind=kLoop, calls=%fused_computation.26 | loop fusion | bytes 221184 | tf_op jit(solution)/shard_map/cond/branch_2_fun/slice | solution.py:384
  1.6 0.1 squeeze.23
  1.8 0.1 copy.24
  1.9 0.1 reshape.43
  2.0 0.1 squeeze.24
  2.2 0.1 copy.25
  2.3 0.1 reshape.44
  2.4 0.1 squeeze.25
  2.6 0.1 copy.26
  2.7 0.1 reshape.45
  2.8 0.1 fusion.13
  2.9 0.2 shard_map.53
  3.1 1.3 %collective-permute-start.2 = (bf16[16,5248]{1,0:T(8,128)(2,1)S(1)}, bf16[16,5248]{1,0:T(8,128)(2,1)S(1)}, u32[]{:S(2)}, u32[]{:S(2)}) collective-permute-start(bf16[16,5248]{1,0:T(8,128)(2,1)S(1)} %get-tuple-element.56.own_ref), channel_id=1, source_target_pairs={{1,2},{5,6},{9,10},{13,14},{17,18},{21,22},{25,26},{29,30}} | collective-permute-start | bytes 503816 | tf_op jit(solution)/shard_map/ppermute | solution.py:453
  4.4 1.3 %collective-permute-start.1 = (bf16[64,640]{1,0:T(8,128)(2,1)S(1)}, bf16[64,640]{1,0:T(8,128)(2,1)S(1)}, u32[]{:S(2)}, u32[]{:S(2)}) collective-permute-start(bf16[64,640]{1,0:T(8,128)(2,1)S(1)} %get-tuple-element.55), channel_id=1, source_target_pairs={{4,0},{5,1},{6,2},{7,3},{8,4},{9,5},{10,6},{11,7},{12,8},{13,9},{1... | collective-permute-start | bytes 245768 | tf_op jit(solution)/shard_map/ppermute | solution.py:410
  5.7 4.6 %collective-permute-start = (bf16[64,640]{1,0:T(8,128)(2,1)S(1)}, bf16[64,640]{1,0:T(8,128)(2,1)S(1)}, u32[]{:S(2)}, u32[]{:S(2)}) collective-permute-start(bf16[64,640]{1,0:T(8,128)(2,1)S(1)} %get-tuple-element.54.own_ref), channel_id=1, source_target_pairs={{0,4},{1,5},{2,6},{3,7},{4,8},{5,9},{6,10},{7,11},{8,12},{9,13},{1... | collective-permute-start | bytes 245768 | tf_op jit(solution)/shard_map/ppermute | solution.py:410
  10.3 1.0 %collective-permute-done.1.down_ref = bf16[64,640]{1,0:T(8,128)(2,1)S(1)} collective-permute-done((bf16[64,640]{1,0:T(8,128)(2,1)S(1)}, bf16[64,640]{1,0:T(8,128)(2,1)S(1)}, u32[]{:S(2)}, u32[]{:S(2)}) %collective-permute-start.1) | collective-permute-done | bytes 81952 | tf_op jit(solution)/shard_map/ppermute | solution.py:410
  11.3 2.0 %collective-permute-done.up_ref = bf16[64,640]{1,0:T(8,128)(2,1)S(1)} collective-permute-done((bf16[64,640]{1,0:T(8,128)(2,1)S(1)}, bf16[64,640]{1,0:T(8,128)(2,1)S(1)}, u32[]{:S(2)}, u32[]{:S(2)}) %collective-permute-start) | collective-permute-done | bytes 81952 | tf_op jit(solution)/shard_map/ppermute | solution.py:410
  13.3 1.3 %collective-permute-start.3 = (bf16[64,2048]{1,0:T(8,128)(2,1)S(1)}, bf16[64,2048]{1,0:T(8,128)(2,1)S(1)}, u32[]{:S(2)}, u32[]{:S(2)}) collective-permute-start(bf16[64,2048]{1,0:T(8,128)(2,1)S(1)} %shard_map.54), channel_id=1, source_target_pairs={{3,2},{7,6},{11,10},{15,14},{19,18},{23,22},{27,26},{31,30}} | collective-permute-start | bytes 786440 | tf_op jit(solution)/shard_map/ppermute | solution.py:466
  14.6 2.2 %collective-permute-done.3.grad_ref = bf16[64,2048]{1,0:T(8,128)(2,1)S(1)} collective-permute-done((bf16[64,2048]{1,0:T(8,128)(2,1)S(1)}, bf16[64,2048]{1,0:T(8,128)(2,1)S(1)}, u32[]{:S(2)}, u32[]{:S(2)}) %collective-permute-start.3) | collective-permute-done | bytes 262176 | tf_op jit(solution)/shard_map/ppermute | solution.py:466
  16.9 1.2 %shard_map.55 = (bf16[32,4096]{1,0:T(8,128)(2,1)S(1)}, bf16[16,4096]{1,0:T(8,128)(2,1)S(1)}) custom-call(bf16[64,2048]{1,0:T(8,128)(2,1)S(1)} %collective-permute-done.3.grad_ref, bf16[64,640]{1,0:T(8,128)(2,1)S(1)} %collective-permute-done.up_ref, bf16[64,640]{1,0:T(8,128)(2,1)S(1)} %collective-permute-done.1.down_ref, ...), custom_call_target="tpu_custom_call" | custom-call | flops 226492416 | bytes 1691648 | tf_op jit(solution)/shard_map/pallas_call | solution.py:364
  18.1 1.3 %collective-permute-start.5 = (bf16[32,4096]{1,0:T(8,128)(2,1)S(1)}, bf16[32,4096]{1,0:T(8,128)(2,1)S(1)}, u32[]{:S(2)}, u32[]{:S(2)}) collective-permute-start(bf16[32,4096]{1,0:T(8,128)(2,1)S(1)} %get-tuple-element.60), channel_id=1, source_target_pairs={{2,1},{6,5},{10,9},{14,13},{18,17},{22,21},{26,25},{30,29}} | collective-permute-start | bytes 786440 | tf_op jit(solution)/shard_map/ppermute | solution.py:491
  19.4 0.7 %collective-permute-start.6 = (bf16[1,64,640]{2,1,0:T(8,128)(2,1)S(1)}, bf16[1,64,640]{2,1,0:T(8,128)(2,1)S(1)}, u32[]{:S(2)}, u32[]{:S(2)}) collective-permute-start(bf16[1,64,640]{2,1,0:T(8,128)(2,1)S(1)} %bitcast.51), channel_id=1, source_target_pairs={{3,19},{7,23},{11,27},{15,31},{19,3},{23,7},{27,11},{31,15}} | collective-permute-start | bytes 245768 | tf_op jit(solution)/shard_map/ppermute | solution.py:410
  20.1 1.3 %collective-permute-start.4 = (bf16[16,4096]{1,0:T(8,128)(2,1)S(1)}, bf16[16,4096]{1,0:T(8,128)(2,1)S(1)}, u32[]{:S(2)}, u32[]{:S(2)}) collective-permute-start(bf16[16,4096]{1,0:T(8,128)(2,1)S(1)} %get-tuple-element.59), channel_id=1, source_target_pairs={{2,0},{6,4},{10,8},{14,12},{18,16},{22,20},{26,24},{30,28}} | collective-permute-start | bytes 393224 | tf_op jit(solution)/shard_map/ppermute | solution.py:490
  21.5 0.7 %collective-permute-start.7 = (bf16[2,64,640]{2,1,0:T(8,128)(2,1)S(1)}, bf16[2,64,640]{2,1,0:T(8,128)(2,1)S(1)}, u32[]{:S(2)}, u32[]{:S(2)}) collective-permute-start(bf16[2,64,640]{2,1,0:T(8,128)(2,1)S(1)} %pad_maximum_fusion.2), channel_id=1, source_target_pairs={{3,11},{7,15},{11,3},{15,7},{19,27},{23,31},{27,19},{31,23}} | collective-permute-start | bytes 491528 | tf_op jit(solution)/shard_map/ppermute | solution.py:410
  22.1 0.6 %shard_map.56 = f32[432,128]{1,0:T(8,128)S(1)} custom-call(bf16[64,2048]{1,0:T(8,128)(2,1)S(1)} %collective-permute-done.3.grad_ref, bf16[64,640]{1,0:T(8,128)(2,1)S(1)} %collective-permute-done.up_ref, bf16[64,640]{1,0:T(8,128)(2,1)S(1)} %collective-permute-done.1.down_ref, bf16[32,4096]{1,0:T(8,128)(2,1)S(1)} %get-tuple-element.58.own_ref), custom_call_target="tpu_custom_call" | custom-call | flops 20000000000 | bytes 909312 | tf_op jit(solution)/shard_map/pallas_call | solution.py:364
  22.8 4.4 %collective-permute-start.11 = (f32[432,128]{1,0:T(8,128)S(1)}, f32[432,128]{1,0:T(8,128)S(1)}, u32[]{:S(2)}, u32[]{:S(2)}) collective-permute-start(f32[432,128]{1,0:T(8,128)S(1)} %shard_map.56), channel_id=1, source_target_pairs={{2,6},{6,2},{10,14},{14,10},{18,22},{22,18},{26,30},{30,26}} | collective-permute-start | bytes 663560 | tf_op jit(solution)/shard_map/ppermute | solution.py:410
  27.2 0.7 %collective-permute-start.14 = (bf16[4,64,640]{2,1,0:T(8,128)(2,1)S(1)}, bf16[4,64,640]{2,1,0:T(8,128)(2,1)S(1)}, u32[]{:S(2)}, u32[]{:S(2)}) collective-permute-start(bf16[4,64,640]{2,1,0:T(8,128)(2,1)S(1)} %constant_dynamic-update-slice_fusion), channel_id=1, source_target_pairs={{3,7},{7,3},{11,15},{15,11},{19,23},{23,19},{27,31},{31,27}} | collective-permute-start | bytes 983048 | tf_op jit(solution)/shard_map/ppermute | solution.py:410
  27.9 3.1 %collective-permute-done.11 = f32[432,128]{1,0:T(8,128)S(1)} collective-permute-done((f32[432,128]{1,0:T(8,128)S(1)}, f32[432,128]{1,0:T(8,128)S(1)}, u32[]{:S(2)}, u32[]{:S(2)}) %collective-permute-start.11) | collective-permute-done | bytes 221216 | tf_op jit(solution)/shard_map/ppermute | solution.py:410
  31.1 0.7 %collective-permute-start.8 = (f32[144,128]{1,0:T(8,128)S(1)}, f32[144,128]{1,0:T(8,128)S(1)}, u32[]{:S(2)}, u32[]{:S(2)}) collective-permute-start(f32[144,128]{1,0:T(8,128)S(1)} %shard_map.57), channel_id=1, source_target_pairs={{0,4},{1,5},{4,0},{5,1},{8,12},{9,13},{12,8},{13,9},{16,20},{17,21... | collective-permute-start | bytes 221192 | tf_op jit(solution)/shard_map/ppermute | solution.py:410
  31.8 5.5 %collective-permute-start.12 = (f32[432,128]{1,0:T(8,128)S(1)}, f32[432,128]{1,0:T(8,128)S(1)}, u32[]{:S(2)}, u32[]{:S(2)}) collective-permute-start(f32[432,128]{1,0:T(8,128)S(1)} %add.41), channel_id=1, source_target_pairs={{2,10},{6,14},{10,2},{14,6},{18,26},{22,30},{26,18},{30,22}} | collective-permute-start | bytes 663560 | tf_op jit(solution)/shard_map/ppermute | solution.py:410
  37.4 0.7 %collective-permute-start.9 = (f32[144,128]{1,0:T(8,128)S(1)}, f32[144,128]{1,0:T(8,128)S(1)}, u32[]{:S(2)}, u32[]{:S(2)}) collective-permute-start(f32[144,128]{1,0:T(8,128)S(1)} %add.39), channel_id=1, source_target_pairs={{0,8},{1,9},{4,12},{5,13},{8,0},{9,1},{12,4},{13,5},{16,24},{17,25... | collective-permute-start | bytes 221192 | tf_op jit(solution)/shard_map/ppermute | solution.py:410
  38.1 0.7 %collective-permute-start.10 = (f32[144,128]{1,0:T(8,128)S(1)}, f32[144,128]{1,0:T(8,128)S(1)}, u32[]{:S(2)}, u32[]{:S(2)}) collective-permute-start(f32[144,128]{1,0:T(8,128)S(1)} %add.40), channel_id=1, source_target_pairs={{0,16},{1,17},{4,20},{5,21},{8,24},{9,25},{12,28},{13,29},{16,0},{... | collective-permute-start | bytes 221192 | tf_op jit(solution)/shard_map/ppermute | solution.py:410
  38.7 2.5 %collective-permute-done.12 = f32[432,128]{1,0:T(8,128)S(1)} collective-permute-done((f32[432,128]{1,0:T(8,128)S(1)}, f32[432,128]{1,0:T(8,128)S(1)}, u32[]{:S(2)}, u32[]{:S(2)}) %collective-permute-start.12) | collective-permute-done | bytes 221216 | tf_op jit(solution)/shard_map/ppermute | solution.py:410
  41.3 4.9 %collective-permute-start.13 = (f32[432,128]{1,0:T(8,128)S(1)}, f32[432,128]{1,0:T(8,128)S(1)}, u32[]{:S(2)}, u32[]{:S(2)}) collective-permute-start(f32[432,128]{1,0:T(8,128)S(1)} %add.42), channel_id=1, source_target_pairs={{2,18},{6,22},{10,26},{14,30},{18,2},{22,6},{26,10},{30,14}} | collective-permute-start | bytes 663560 | tf_op jit(solution)/shard_map/ppermute | solution.py:410
  46.2 0.1 pad_maximum_fusion.1.blocks_ref
  46.3 0.2 shard_map.58
  46.5 5.9 %collective-permute-done.13 = f32[432,128]{1,0:T(8,128)S(1)} collective-permute-done((f32[432,128]{1,0:T(8,128)S(1)}, f32[432,128]{1,0:T(8,128)S(1)}, u32[]{:S(2)}, u32[]{:S(2)}) %collective-permute-start.13) | collective-permute-done | bytes 221216 | tf_op jit(solution)/shard_map/ppermute | solution.py:410
  52.5 1.2 %conditional.3 = (f32[1,221184]{1,0:T(1,128)S(1)}) conditional(s32[]{:T(128)} %clamp.4, (f32[144,128]{1,0:T(8,128)S(1)}, f32[144,128]{1,0:T(8,128)S(1)}) %tuple.45, (f32[144,128]{1,0:T(8,128)S(1)}, f32[144,128]{1,0:T(8,128)S(1)}) %tuple.45, (f32[432,128]{1,0:T(8,128)S(1)}, f32[432,128]{1,0:T(8,128)S(1)}) %tuple.46, ...), branch_computations={%region_4.5_spmd, %region_5.6_spmd, %region_6.7_spmd, %region_7.8_... | conditional | flops 110592 | bytes 7077896 | solution.py:565
  52.5 0.1 reshape.54
  52.7 0.2 copy.34
  52.8 0.2 reshape.53
  53.1 0.2 copy.33
  53.3 0.1 maximum_bitcast_fusion
  53.4 0.2 reshape.56
  53.6 0.1 pad.19
  53.7 0.0 copy-start.2
  53.7 0.9 %copy-done.2 = f32[1,221184]{1,0:T(1,128)} copy-done((f32[1,221184]{1,0:T(1,128)}, f32[1,221184]{1,0:T(1,128)S(1)}, u32[]{:S(2)}) %copy-start.2) | copy-done | bytes 884760
  (28 shorter events, 0.3 us)
Async XLA Ops:
  0.0 2.9 %copy-start = (bf16[1,131072]{1,0:T(2,128)(2,1)S(1)}, bf16[1,131072]{1,0:T(2,128)(2,1)}, u32[]{:S(2)}) copy-start(bf16[1,131072]{1,0:T(2,128)(2,1)} %saved_ref.1) | copy-start | bytes 786436
  0.0 2.9 %copy-start.1 = (bf16[128,1,2,32]{0,3,2,1:T(8,128)(2,1)S(1)}, bf16[128,1,2,32]{0,3,2,1:T(8,128)(2,1)}, u32[]{:S(2)}) copy-start(bf16[128,1,2,32]{0,3,2,1:T(8,128)(2,1)} %param.13) | copy-start | bytes 49156
  3.1 7.2 %collective-permute-start.2 = (bf16[16,5248]{1,0:T(8,128)(2,1)S(1)}, bf16[16,5248]{1,0:T(8,128)(2,1)S(1)}, u32[]{:S(2)}, u32[]{:S(2)}) collective-permute-start(bf16[16,5248]{1,0:T(8,128)(2,1)S(1)} %get-tuple-element.56.own_ref), channel_id=1, source_target_pairs={{1,2},{5,6},{9,10},{13,14},{17,18},{21,22},{25,26},{29,30}} | collective-permute-start | bytes 503816 | tf_op jit(solution)/shard_map/ppermute | solution.py:453
  4.4 6.9 %collective-permute-start.1 = (bf16[64,640]{1,0:T(8,128)(2,1)S(1)}, bf16[64,640]{1,0:T(8,128)(2,1)S(1)}, u32[]{:S(2)}, u32[]{:S(2)}) collective-permute-start(bf16[64,640]{1,0:T(8,128)(2,1)S(1)} %get-tuple-element.55), channel_id=1, source_target_pairs={{4,0},{5,1},{6,2},{7,3},{8,4},{9,5},{10,6},{11,7},{12,8},{13,9},{1... | collective-permute-start | bytes 245768 | tf_op jit(solution)/shard_map/ppermute | solution.py:410
  5.7 7.6 %collective-permute-start = (bf16[64,640]{1,0:T(8,128)(2,1)S(1)}, bf16[64,640]{1,0:T(8,128)(2,1)S(1)}, u32[]{:S(2)}, u32[]{:S(2)}) collective-permute-start(bf16[64,640]{1,0:T(8,128)(2,1)S(1)} %get-tuple-element.54.own_ref), channel_id=1, source_target_pairs={{0,4},{1,5},{2,6},{3,7},{4,8},{5,9},{6,10},{7,11},{8,12},{9,13},{1... | collective-permute-start | bytes 245768 | tf_op jit(solution)/shard_map/ppermute | solution.py:410
  13.3 3.5 %collective-permute-start.3 = (bf16[64,2048]{1,0:T(8,128)(2,1)S(1)}, bf16[64,2048]{1,0:T(8,128)(2,1)S(1)}, u32[]{:S(2)}, u32[]{:S(2)}) collective-permute-start(bf16[64,2048]{1,0:T(8,128)(2,1)S(1)} %shard_map.54), channel_id=1, source_target_pairs={{3,2},{7,6},{11,10},{15,14},{19,18},{23,22},{27,26},{31,30}} | collective-permute-start | bytes 786440 | tf_op jit(solution)/shard_map/ppermute | solution.py:466
  18.1 13.0 %collective-permute-start.5 = (bf16[32,4096]{1,0:T(8,128)(2,1)S(1)}, bf16[32,4096]{1,0:T(8,128)(2,1)S(1)}, u32[]{:S(2)}, u32[]{:S(2)}) collective-permute-start(bf16[32,4096]{1,0:T(8,128)(2,1)S(1)} %get-tuple-element.60), channel_id=1, source_target_pairs={{2,1},{6,5},{10,9},{14,13},{18,17},{22,21},{26,25},{30,29}} | collective-permute-start | bytes 786440 | tf_op jit(solution)/shard_map/ppermute | solution.py:491
  19.4 2.0 %collective-permute-start.6 = (bf16[1,64,640]{2,1,0:T(8,128)(2,1)S(1)}, bf16[1,64,640]{2,1,0:T(8,128)(2,1)S(1)}, u32[]{:S(2)}, u32[]{:S(2)}) collective-permute-start(bf16[1,64,640]{2,1,0:T(8,128)(2,1)S(1)} %bitcast.51), channel_id=1, source_target_pairs={{3,19},{7,23},{11,27},{15,31},{19,3},{23,7},{27,11},{31,15}} | collective-permute-start | bytes 245768 | tf_op jit(solution)/shard_map/ppermute | solution.py:410
  20.1 11.0 %collective-permute-start.4 = (bf16[16,4096]{1,0:T(8,128)(2,1)S(1)}, bf16[16,4096]{1,0:T(8,128)(2,1)S(1)}, u32[]{:S(2)}, u32[]{:S(2)}) collective-permute-start(bf16[16,4096]{1,0:T(8,128)(2,1)S(1)} %get-tuple-element.59), channel_id=1, source_target_pairs={{2,0},{6,4},{10,8},{14,12},{18,16},{22,20},{26,24},{30,28}} | collective-permute-start | bytes 393224 | tf_op jit(solution)/shard_map/ppermute | solution.py:490
  21.5 5.7 %collective-permute-start.7 = (bf16[2,64,640]{2,1,0:T(8,128)(2,1)S(1)}, bf16[2,64,640]{2,1,0:T(8,128)(2,1)S(1)}, u32[]{:S(2)}, u32[]{:S(2)}) collective-permute-start(bf16[2,64,640]{2,1,0:T(8,128)(2,1)S(1)} %pad_maximum_fusion.2), channel_id=1, source_target_pairs={{3,11},{7,15},{11,3},{15,7},{19,27},{23,31},{27,19},{31,23}} | collective-permute-start | bytes 491528 | tf_op jit(solution)/shard_map/ppermute | solution.py:410
  22.8 8.3 %collective-permute-start.11 = (f32[432,128]{1,0:T(8,128)S(1)}, f32[432,128]{1,0:T(8,128)S(1)}, u32[]{:S(2)}, u32[]{:S(2)}) collective-permute-start(f32[432,128]{1,0:T(8,128)S(1)} %shard_map.56), channel_id=1, source_target_pairs={{2,6},{6,2},{10,14},{14,10},{18,22},{22,18},{26,30},{30,26}} | collective-permute-start | bytes 663560 | tf_op jit(solution)/shard_map/ppermute | solution.py:410
  27.2 19.0 %collective-permute-start.14 = (bf16[4,64,640]{2,1,0:T(8,128)(2,1)S(1)}, bf16[4,64,640]{2,1,0:T(8,128)(2,1)S(1)}, u32[]{:S(2)}, u32[]{:S(2)}) collective-permute-start(bf16[4,64,640]{2,1,0:T(8,128)(2,1)S(1)} %constant_dynamic-update-slice_fusion), channel_id=1, source_target_pairs={{3,7},{7,3},{11,15},{15,11},{19,23},{23,19},{27,31},{31,27}} | collective-permute-start | bytes 983048 | tf_op jit(solution)/shard_map/ppermute | solution.py:410
  31.1 6.2 %collective-permute-start.8 = (f32[144,128]{1,0:T(8,128)S(1)}, f32[144,128]{1,0:T(8,128)S(1)}, u32[]{:S(2)}, u32[]{:S(2)}) collective-permute-start(f32[144,128]{1,0:T(8,128)S(1)} %shard_map.57), channel_id=1, source_target_pairs={{0,4},{1,5},{4,0},{5,1},{8,12},{9,13},{12,8},{13,9},{16,20},{17,21... | collective-permute-start | bytes 221192 | tf_op jit(solution)/shard_map/ppermute | solution.py:410
  31.8 9.4 %collective-permute-start.12 = (f32[432,128]{1,0:T(8,128)S(1)}, f32[432,128]{1,0:T(8,128)S(1)}, u32[]{:S(2)}, u32[]{:S(2)}) collective-permute-start(f32[432,128]{1,0:T(8,128)S(1)} %add.41), channel_id=1, source_target_pairs={{2,10},{6,14},{10,2},{14,6},{18,26},{22,30},{26,18},{30,22}} | collective-permute-start | bytes 663560 | tf_op jit(solution)/shard_map/ppermute | solution.py:410
  37.4 0.7 %collective-permute-start.9 = (f32[144,128]{1,0:T(8,128)S(1)}, f32[144,128]{1,0:T(8,128)S(1)}, u32[]{:S(2)}, u32[]{:S(2)}) collective-permute-start(f32[144,128]{1,0:T(8,128)S(1)} %add.39), channel_id=1, source_target_pairs={{0,8},{1,9},{4,12},{5,13},{8,0},{9,1},{12,4},{13,5},{16,24},{17,25... | collective-permute-start | bytes 221192 | tf_op jit(solution)/shard_map/ppermute | solution.py:410
  38.1 8.1 %collective-permute-start.10 = (f32[144,128]{1,0:T(8,128)S(1)}, f32[144,128]{1,0:T(8,128)S(1)}, u32[]{:S(2)}, u32[]{:S(2)}) collective-permute-start(f32[144,128]{1,0:T(8,128)S(1)} %add.40), channel_id=1, source_target_pairs={{0,16},{1,17},{4,20},{5,21},{8,24},{9,25},{12,28},{13,29},{16,0},{... | collective-permute-start | bytes 221192 | tf_op jit(solution)/shard_map/ppermute | solution.py:410
  41.3 11.2 %collective-permute-start.13 = (f32[432,128]{1,0:T(8,128)S(1)}, f32[432,128]{1,0:T(8,128)S(1)}, u32[]{:S(2)}, u32[]{:S(2)}) collective-permute-start(f32[432,128]{1,0:T(8,128)S(1)} %add.42), channel_id=1, source_target_pairs={{2,18},{6,22},{10,26},{14,30},{18,2},{22,6},{26,10},{30,14}} | collective-permute-start | bytes 663560 | tf_op jit(solution)/shard_map/ppermute | solution.py:410
  53.7 0.9 %copy-start.2 = (f32[1,221184]{1,0:T(1,128)}, f32[1,221184]{1,0:T(1,128)S(1)}, u32[]{:S(2)}) copy-start(f32[1,221184]{1,0:T(1,128)S(1)} %get-tuple-element.112) | copy-start | bytes 2654212

commit v5 on v4

--- a/solution.py
+++ b/solution.py
@@ -96,7 +96,17 @@
 
 
 def layout_kernel(
-    saved_ref, top_ref, taps_ref, up_ref, down_ref, own2_ref, own01_ref, held, wide, arrived
+    saved_ref,
+    top_ref,
+    taps_ref,
+    deep_ref,
+    up_ref,
+    down_ref,
+    own2_ref,
+    own01_ref,
+    held,
+    wide,
+    arrived,
 ):
     def fetch(size):
         copy = pltpu.make_async_copy(
@@ -107,7 +117,7 @@
 
     def send(place, plane, target_ref):
         for half in range(2):
-            target_ref[32 * half : 32 * half + place, :512] = wide[
+            target_ref[32 * half : 32 * half + place, :] = wide[
                 :place, cols(8 * plane + 4 * half, 4)
             ].astype(BF16)
 
@@ -116,9 +126,13 @@
         fetch(C3 * 512)
         copy_rows(held, wide, C3, 512)
         block = wide[:, :512].astype(BF16)
-        for ref in (up_ref, down_ref):
-            ref[:, :512] = block
-            ref[:, 512:] = top_ref[...]
+        top = top_ref[...]
+        deep_ref[:, :512] = block
+        deep_ref[:, 512:] = top
+        for ref, half in ((up_ref, block[:, 256:]), (down_ref, block[:, :256])):
+            ref[:, :256] = half
+            ref[:, 256:384] = top
+            ref[:, 384:] = jnp.zeros((64, LANES), BF16)
 
     for section, chans in enumerate((C0, C1, C2)):
 
@@ -141,8 +155,8 @@
 def section3_kernel(own_ref, up_ref, down_ref, weights_ref, out_ref, wide, stacked, terms):
     @pl.when(on_segment(3))
     def _():
-        for place, ref in enumerate((up_ref, own_ref, down_ref)):
-            wide[:, cols(2 * place, 2)] = spread_top(ref[:, cols(4)])
+        for place, (ref, first) in enumerate(((up_ref, 2), (own_ref, 4), (down_ref, 2))):
+            wide[:, cols(2 * place, 2)] = spread_top(ref[:, cols(first)])
         stack_moved(lambda row: wide[:, cols(row)], stacked, C4, 6, (0, 1, 2))
         terms[...] = dot(weights_ref[...], stacked[...])
         unit = spread(LANES, LANES, lambda e: 2 * e, lambda e: e < 64)
@@ -156,7 +170,7 @@
                         part = terms[first : first + C3, cols(2 * (place_z + 1) + place_y)]
                         total = part if total is None else total + part
                 if cell_z == -1:
-                    mask = up_ref[:, cols(2 + cell_y // 2)]
+                    mask = up_ref[:, cols(cell_y // 2)]
                 elif cell_z == 2:
                     mask = down_ref[:, cols(cell_y // 2)]
                 else:
@@ -386,16 +400,18 @@
     return jnp.concatenate(groups, 0)
 
 
-def tap_layouts(section, weights):
-    deep_taps = jnp.zeros((576, 384), BF16)
-    fine_taps = jnp.zeros((144, 128), BF16)
+def deep_layout(section, weights):
     if section == 3:
-        deep_taps = by_tap(weights, C4, C3)
+        return by_tap(weights, C4, C3)
     if section == 2:
-        deep_taps = padded(by_tap(weights, C3, C2), 576, 384)
+        return padded(by_tap(weights, C3, C2), 576, 384)
+    return jnp.zeros((576, 384), BF16)
+
+
+def fine_layout(section, weights):
     if section == 1:
-        fine_taps = padded(by_tap(weights, C2, C1), 144, 128)
-    return deep_taps, fine_taps
+        return padded(by_tap(weights, C2, C1), 144, 128)
+    return jnp.zeros((144, 128), BF16)
 
 
 def pairs_of(segments, route):
@@ -430,27 +446,34 @@
     def behind(values, *leaders):
         return lax.optimization_barrier((*values, *leaders))[: len(values)]
 
-    deep_taps, fine_taps = lax.switch(
-        segment,
-        [functools.partial(tap_layouts, section) for section in range(4)],
-        conv_weights,
-    )
+    def for_section(layout):
+        branches = [functools.partial(layout, section) for section in range(4)]
+        return lax.switch(segment, branches, conv_weights)
+
     top = jnp.transpose(top_gradient[:, 0], (1, 2, 0)).reshape(64, C4)
-    top, fine_taps = behind((top, fine_taps), deep_taps)
-    to_later, to_sooner, own2, own01 = call(
+    deep, up, down, own2, own01 = call(
         layout_kernel,
-        [((64, 640), BF16), ((64, 640), BF16), ((32, 4096), BF16), ((16, 5248), BF16)],
+        [
+            ((64, 640), BF16),
+            ((64, 512), BF16),
+            ((64, 512), BF16),
+            ((32, 4096), BF16),
+            ((16, 5248), BF16),
+        ],
         [((1, 131072), BF16), ((64, 4096), F32), pltpu.SemaphoreType.DMA],
         saved_inputs,
         top,
-        fine_taps,
+        for_section(fine_layout),
         flops=0,
         far=(0,),
     )
-    deep = to_later
-    up = over_space(to_later, range(4), later)
-    down = over_space(to_sooner, range(4), sooner)
+    up = over_space(up, range(4), later)
+    down = over_space(down, range(4), sooner)
     next_own = lax.ppermute(own01, "segment", [(1, 2)])
+    (weights,) = behind((conv_weights,), deep)
+    deep_taps = lax.switch(
+        segment, [functools.partial(deep_layout, section) for section in range(4)], weights
+    )
     (deep_taps,) = behind((deep_taps,), next_own)
 
     (grad2,) = call(

time: 55.2 us -> 53.3 us (0.966)
  starting transfers between devices: 29.9 us -> 27 us
  local copies, waits for them, and re-layouts: 4.81 us -> 6.51 us
  waiting for transfers between devices: 16.9 us -> 15.8 us
    ppermute x11, starting transfers between devices: 24.7 us -> 21.8 us  [over_space(): return lax.ppermute(block, ('space', 'segment'), pairs_of(segments, route))]
    ppermute x11, waiting for transfers between devices: 14.6 us -> 13.6 us  [over_space(): return lax.ppermute(block, ('space', 'segment'), pairs_of(segments, route))]
    pad x1, local copies, waits for them, and re-layouts: 0.06 us -> 0.97 us  [flat_row(): return jnp.pad(flat, (0, room - flat.shape[0]))[None]]
    unnamed x8 -> x6, local copies, waits for them, and re-layouts: 0.94 us -> 1.78 us
  transfers between devices with their start and end apart: 15 -> 15, of which waited for: 6 -> 5; matrix products, arithmetic and copies ran while one was open for 0% -> 6% of each run, Pallas kernels for 2% -> 2%
where the time goes in v5:
time: 53.3 us; the launch traced here: 52.3 us
  starting transfers between devices  27 us (51%)
  waiting for transfers between devices  15.8 us (30%)
  local copies, waits for them, and re-layouts  6.51 us (12%)
  Pallas kernels  2.27 us (4%)
    ppermute x11, starting transfers between devices, over_space(): return lax.ppermute(block, ('space', 'segment'), pairs_of(segments, route))  21.8 us
    ppermute x11, waiting for transfers between devices, over_space(): return lax.ppermute(block, ('space', 'segment'), pairs_of(segments, route))  13.6 us
    pallas_call x6, Pallas kernels, call(): pl.pallas_call(kernel, out_shape=shapes, in_specs=[far_spec if place in f...  2.27 us
    ppermute x1, waiting for transfers between devices, shards(): grad2 = lax.ppermute(grad2, 'segment', [(3, 2)])  2.13 us
    unnamed x6, local copies, waits for them, and re-layouts  1.78 us
    slice x1, local copies, waits for them, and re-layouts, by_tap(): weights[0, tap_z * size:(tap_z + 1) * size].reshape(3, 3, chan_out, chan_in)  1.59 us
    ppermute x1, starting transfers between devices, shards(): grad1 = lax.ppermute(grad1, 'segment', [(2, 1)])  1.31 us
    ppermute x1, starting transfers between devices, shards(): grad0 = lax.ppermute(grad0, 'segment', [(2, 0)])  1.3 us
  transfers between devices with their start and end apart: 15, of which 5 were waited for; matrix products, arithmetic and copies ran while one was open for 6% of the time, Pallas kernels for 2%

profile of v5, /device:TPU:2, one launch (start us, length us, event | category | flops | bytes accessed | tf_op | source)
XLA Modules:
  0.0 52.3 jit_solution(3140280206135939191)
XLA Ops:
  0.0 0.0 copy-start
  0.0 1.0 %copy-done = bf16[1,131072]{1,0:T(2,128)(2,1)S(1)} copy-done((bf16[1,131072]{1,0:T(2,128)(2,1)S(1)}, bf16[1,131072]{1,0:T(2,128)(2,1)}, u32[]{:S(2)}) %copy-start) | copy-done | bytes 262168
  1.1 0.7 %copy-done.1 = bf16[128,1,2,32]{0,3,2,1:T(8,128)(2,1)S(1)} copy-done((bf16[128,1,2,32]{0,3,2,1:T(8,128)(2,1)S(1)}, bf16[128,1,2,32]{0,3,2,1:T(8,128)(2,1)}, u32[]{:S(2)}) %copy-start.1) | copy-done | bytes 16408
  1.8 0.2 shard_map.44
  2.0 1.3 %collective-permute-start.2 = (bf16[16,5248]{1,0:T(8,128)(2,1)S(1)}, bf16[16,5248]{1,0:T(8,128)(2,1)S(1)}, u32[]{:S(2)}, u32[]{:S(2)}) collective-permute-start(bf16[16,5248]{1,0:T(8,128)(2,1)S(1)} %get-tuple-element.62.own_ref), channel_id=1, source_target_pairs={{1,2},{5,6},{9,10},{13,14},{17,18},{21,22},{25,26},{29,30}} | collective-permute-start | bytes 503816 | tf_op jit(solution)/shard_map/ppermute | solution.py:472
  3.3 3.4 %collective-permute-start = (bf16[64,512]{1,0:T(8,128)(2,1)S(1)}, bf16[64,512]{1,0:T(8,128)(2,1)S(1)}, u32[]{:S(2)}, u32[]{:S(2)}) collective-permute-start(bf16[64,512]{1,0:T(8,128)(2,1)S(1)} %get-tuple-element.59), channel_id=1, source_target_pairs={{0,4},{1,5},{2,6},{3,7},{4,8},{5,9},{6,10},{7,11},{8,12},{9,13},{1... | collective-permute-start | bytes 196616 | tf_op jit(solution)/shard_map/ppermute | solution.py:426
  6.7 1.3 %collective-permute-start.1 = (bf16[64,512]{1,0:T(8,128)(2,1)S(1)}, bf16[64,512]{1,0:T(8,128)(2,1)S(1)}, u32[]{:S(2)}, u32[]{:S(2)}) collective-permute-start(bf16[64,512]{1,0:T(8,128)(2,1)S(1)} %get-tuple-element.60), channel_id=1, source_target_pairs={{4,0},{5,1},{6,2},{7,3},{8,4},{9,5},{10,6},{11,7},{12,8},{13,9},{1... | collective-permute-start | bytes 196616 | tf_op jit(solution)/shard_map/ppermute | solution.py:426
  8.0 2.9 %conditional.4 = (bf16[576,384]{1,0:T(8,128)(2,1)S(1)}) conditional(s32[]{:T(128)} %clamp.2, () %tuple.51, () %tuple.52, bf16[1,221184]{1,0:T(2,128)(2,1)} %param.16, bf16[1,221184]{1,0:T(2,128)(2,1)} %param.16), branch_computations={%region_4.5_spmd, %region_5.6_spmd, %region_6.7_spmd, %region_7.8_... | conditional | flops 3317760 | bytes 4423688 | solution.py:474
  8.0 1.6 %slice_reduce_fusion.5 = (bf16[18432]{0:T(1024)(128)(2,1)S(1)}, bf16[18432]{0:T(1024)(128)(2,1)S(1)}, bf16[18432]{0:T(1024)(128)(2,1)S(1)}) fusion(bf16[1,221184]{1,0:T(2,128)(2,1)} %param.6), kind=kLoop, calls=%fused_computation.26 | loop fusion | bytes 221184 | tf_op jit(solution)/shard_map/cond/branch_2_fun/slice | solution.py:398
  9.6 0.1 squeeze.23
  9.7 0.1 copy.21
  9.9 0.1 reshape.43
  10.0 0.1 squeeze.25
  10.1 0.1 copy.23
  10.3 0.1 reshape.45
  10.4 0.1 squeeze.24
  10.5 0.1 copy.22
  10.7 0.1 reshape.44
  10.8 0.1 fusion.13
  10.9 2.0 %collective-permute-done.1.down_ref = bf16[64,512]{1,0:T(8,128)(2,1)S(1)} collective-permute-done((bf16[64,512]{1,0:T(8,128)(2,1)S(1)}, bf16[64,512]{1,0:T(8,128)(2,1)S(1)}, u32[]{:S(2)}, u32[]{:S(2)}) %collective-permute-start.1) | collective-permute-done | bytes 65568 | tf_op jit(solution)/shard_map/ppermute | solution.py:426
  12.9 1.3 %collective-permute-start.3 = (bf16[64,2048]{1,0:T(8,128)(2,1)S(1)}, bf16[64,2048]{1,0:T(8,128)(2,1)S(1)}, u32[]{:S(2)}, u32[]{:S(2)}) collective-permute-start(bf16[64,2048]{1,0:T(8,128)(2,1)S(1)} %shard_map.45), channel_id=1, source_target_pairs={{3,2},{7,6},{11,10},{15,14},{19,18},{23,22},{27,26},{31,30}} | collective-permute-start | bytes 786440 | tf_op jit(solution)/shard_map/ppermute | solution.py:489
  14.1 2.1 %collective-permute-done.3.grad_ref = bf16[64,2048]{1,0:T(8,128)(2,1)S(1)} collective-permute-done((bf16[64,2048]{1,0:T(8,128)(2,1)S(1)}, bf16[64,2048]{1,0:T(8,128)(2,1)S(1)}, u32[]{:S(2)}, u32[]{:S(2)}) %collective-permute-start.3) | collective-permute-done | bytes 262176 | tf_op jit(solution)/shard_map/ppermute | solution.py:489
  16.3 1.3 %shard_map.46 = (bf16[32,4096]{1,0:T(8,128)(2,1)S(1)}, bf16[16,4096]{1,0:T(8,128)(2,1)S(1)}) custom-call(bf16[64,2048]{1,0:T(8,128)(2,1)S(1)} %collective-permute-done.3.grad_ref, bf16[64,512]{1,0:T(8,128)(2,1)S(1)} %collective-permute-done.up_ref, bf16[64,512]{1,0:T(8,128)(2,1)S(1)} %collective-permute-done.1.down_ref, ...), custom_call_target="tpu_custom_call" | custom-call | flops 226492416 | bytes 1658880 | tf_op jit(solution)/shard_map/pallas_call | solution.py:378
  17.5 1.3 %collective-permute-start.5 = (bf16[32,4096]{1,0:T(8,128)(2,1)S(1)}, bf16[32,4096]{1,0:T(8,128)(2,1)S(1)}, u32[]{:S(2)}, u32[]{:S(2)}) collective-permute-start(bf16[32,4096]{1,0:T(8,128)(2,1)S(1)} %get-tuple-element.66), channel_id=1, source_target_pairs={{2,1},{6,5},{10,9},{14,13},{18,17},{22,21},{26,25},{30,29}} | collective-permute-start | bytes 786440 | tf_op jit(solution)/shard_map/ppermute | solution.py:514
  18.8 0.7 %collective-permute-start.6 = (bf16[1,64,640]{2,1,0:T(8,128)(2,1)S(1)}, bf16[1,64,640]{2,1,0:T(8,128)(2,1)S(1)}, u32[]{:S(2)}, u32[]{:S(2)}) collective-permute-start(bf16[1,64,640]{2,1,0:T(8,128)(2,1)S(1)} %bitcast.51), channel_id=1, source_target_pairs={{3,19},{7,23},{11,27},{15,31},{19,3},{23,7},{27,11},{31,15}} | collective-permute-start | bytes 245768 | tf_op jit(solution)/shard_map/ppermute | solution.py:426
  19.5 1.3 %collective-permute-start.4 = (bf16[16,4096]{1,0:T(8,128)(2,1)S(1)}, bf16[16,4096]{1,0:T(8,128)(2,1)S(1)}, u32[]{:S(2)}, u32[]{:S(2)}) collective-permute-start(bf16[16,4096]{1,0:T(8,128)(2,1)S(1)} %get-tuple-element.65), channel_id=1, source_target_pairs={{2,0},{6,4},{10,8},{14,12},{18,16},{22,20},{26,24},{30,28}} | collective-permute-start | bytes 393224 | tf_op jit(solution)/shard_map/ppermute | solution.py:513
  20.9 0.7 %collective-permute-start.7 = (bf16[2,64,640]{2,1,0:T(8,128)(2,1)S(1)}, bf16[2,64,640]{2,1,0:T(8,128)(2,1)S(1)}, u32[]{:S(2)}, u32[]{:S(2)}) collective-permute-start(bf16[2,64,640]{2,1,0:T(8,128)(2,1)S(1)} %pad_maximum_fusion.2), channel_id=1, source_target_pairs={{3,11},{7,15},{11,3},{15,7},{19,27},{23,31},{27,19},{31,23}} | collective-permute-start | bytes 491528 | tf_op jit(solution)/shard_map/ppermute | solution.py:426
  21.6 0.6 %shard_map.47 = f32[432,128]{1,0:T(8,128)S(1)} custom-call(bf16[64,2048]{1,0:T(8,128)(2,1)S(1)} %collective-permute-done.3.grad_ref, bf16[64,512]{1,0:T(8,128)(2,1)S(1)} %collective-permute-done.up_ref, bf16[64,512]{1,0:T(8,128)(2,1)S(1)} %collective-permute-done.1.down_ref, bf16[32,4096]{1,0:T(8,128)(2,1)S(1)} %get-tuple-element.64.own_ref), custom_call_target="tpu_custom_call" | custom-call | flops 20000000000 | bytes 876544 | tf_op jit(solution)/shard_map/pallas_call | solution.py:378
  22.2 4.3 %collective-permute-start.11 = (f32[432,128]{1,0:T(8,128)S(1)}, f32[432,128]{1,0:T(8,128)S(1)}, u32[]{:S(2)}, u32[]{:S(2)}) collective-permute-start(f32[432,128]{1,0:T(8,128)S(1)} %shard_map.47), channel_id=1, source_target_pairs={{2,6},{6,2},{10,14},{14,10},{18,22},{22,18},{26,30},{30,26}} | collective-permute-start | bytes 663560 | tf_op jit(solution)/shard_map/ppermute | solution.py:426
  26.6 0.7 %collective-permute-start.14 = (bf16[4,64,640]{2,1,0:T(8,128)(2,1)S(1)}, bf16[4,64,640]{2,1,0:T(8,128)(2,1)S(1)}, u32[]{:S(2)}, u32[]{:S(2)}) collective-permute-start(bf16[4,64,640]{2,1,0:T(8,128)(2,1)S(1)} %constant_dynamic-update-slice_fusion), channel_id=1, source_target_pairs={{3,7},{7,3},{11,15},{15,11},{19,23},{23,19},{27,31},{31,27}} | collective-permute-start | bytes 983048 | tf_op jit(solution)/shard_map/ppermute | solution.py:426
  27.3 3.1 %collective-permute-done.11 = f32[432,128]{1,0:T(8,128)S(1)} collective-permute-done((f32[432,128]{1,0:T(8,128)S(1)}, f32[432,128]{1,0:T(8,128)S(1)}, u32[]{:S(2)}, u32[]{:S(2)}) %collective-permute-start.11) | collective-permute-done | bytes 221216 | tf_op jit(solution)/shard_map/ppermute | solution.py:426
  30.5 0.7 %collective-permute-start.8 = (f32[144,128]{1,0:T(8,128)S(1)}, f32[144,128]{1,0:T(8,128)S(1)}, u32[]{:S(2)}, u32[]{:S(2)}) collective-permute-start(f32[144,128]{1,0:T(8,128)S(1)} %shard_map.48), channel_id=1, source_target_pairs={{0,4},{1,5},{4,0},{5,1},{8,12},{9,13},{12,8},{13,9},{16,20},{17,21... | collective-permute-start | bytes 221192 | tf_op jit(solution)/shard_map/ppermute | solution.py:426
  31.2 3.9 %collective-permute-start.12 = (f32[432,128]{1,0:T(8,128)S(1)}, f32[432,128]{1,0:T(8,128)S(1)}, u32[]{:S(2)}, u32[]{:S(2)}) collective-permute-start(f32[432,128]{1,0:T(8,128)S(1)} %add.41), channel_id=1, source_target_pairs={{2,10},{6,14},{10,2},{14,6},{18,26},{22,30},{26,18},{30,22}} | collective-permute-start | bytes 663560 | tf_op jit(solution)/shard_map/ppermute | solution.py:426
  35.1 0.7 %collective-permute-start.9 = (f32[144,128]{1,0:T(8,128)S(1)}, f32[144,128]{1,0:T(8,128)S(1)}, u32[]{:S(2)}, u32[]{:S(2)}) collective-permute-start(f32[144,128]{1,0:T(8,128)S(1)} %add.39), channel_id=1, source_target_pairs={{0,8},{1,9},{4,12},{5,13},{8,0},{9,1},{12,4},{13,5},{16,24},{17,25... | collective-permute-start | bytes 221192 | tf_op jit(solution)/shard_map/ppermute | solution.py:426
  35.8 0.7 %collective-permute-start.10 = (f32[144,128]{1,0:T(8,128)S(1)}, f32[144,128]{1,0:T(8,128)S(1)}, u32[]{:S(2)}, u32[]{:S(2)}) collective-permute-start(f32[144,128]{1,0:T(8,128)S(1)} %add.40), channel_id=1, source_target_pairs={{0,16},{1,17},{4,20},{5,21},{8,24},{9,25},{12,28},{13,29},{16,0},{... | collective-permute-start | bytes 221192 | tf_op jit(solution)/shard_map/ppermute | solution.py:426
  36.5 2.6 %collective-permute-done.12 = f32[432,128]{1,0:T(8,128)S(1)} collective-permute-done((f32[432,128]{1,0:T(8,128)S(1)}, f32[432,128]{1,0:T(8,128)S(1)}, u32[]{:S(2)}, u32[]{:S(2)}) %collective-permute-start.12) | collective-permute-done | bytes 221216 | tf_op jit(solution)/shard_map/ppermute | solution.py:426
  39.0 4.9 %collective-permute-start.13 = (f32[432,128]{1,0:T(8,128)S(1)}, f32[432,128]{1,0:T(8,128)S(1)}, u32[]{:S(2)}, u32[]{:S(2)}) collective-permute-start(f32[432,128]{1,0:T(8,128)S(1)} %add.42), channel_id=1, source_target_pairs={{2,18},{6,22},{10,26},{14,30},{18,2},{22,6},{26,10},{30,14}} | collective-permute-start | bytes 663560 | tf_op jit(solution)/shard_map/ppermute | solution.py:426
  43.9 0.1 pad_maximum_fusion.1.blocks_ref
  44.0 0.2 shard_map.49
  44.2 5.9 %collective-permute-done.13 = f32[432,128]{1,0:T(8,128)S(1)} collective-permute-done((f32[432,128]{1,0:T(8,128)S(1)}, f32[432,128]{1,0:T(8,128)S(1)}, u32[]{:S(2)}, u32[]{:S(2)}) %collective-permute-start.13) | collective-permute-done | bytes 221216 | tf_op jit(solution)/shard_map/ppermute | solution.py:426
  50.2 2.1 %conditional.5 = (f32[1,221184]{1,0:T(1,128)}) conditional(s32[]{:T(128)} %clamp.2, (f32[144,128]{1,0:T(8,128)S(1)}, f32[144,128]{1,0:T(8,128)S(1)}) %tuple.57, (f32[144,128]{1,0:T(8,128)S(1)}, f32[144,128]{1,0:T(8,128)S(1)}) %tuple.57, (f32[432,128]{1,0:T(8,128)S(1)}, f32[432,128]{1,0:T(8,128)S(1)}) %tuple.58, ...), branch_computations={%region_8.9_spmd, %region_9.10_spmd, %region_10.11_spmd, %region_1... | conditional | flops 110592 | bytes 7077896 | solution.py:588
  50.3 0.1 reshape.54
  50.4 0.2 copy.31
  50.6 0.2 reshape.53
  50.8 0.2 copy.30
  51.0 0.1 maximum_bitcast_fusion
  51.1 0.2 reshape.56
  51.4 1.0 %pad.19 = f32[221184]{0:T(1024)} pad(f32[55296]{0:T(1024)S(1)} %reshape.56, f32[]{:T(128)} %constant.30.clone), padding=0_165888 | pad | bytes 1105924 | tf_op jit(solution)/shard_map/cond/branch_2_fun/jit(_pad)/pad | solution.py:431
  (27 shorter events, 0.3 us)
Async XLA Ops:
  0.0 1.0 %copy-start = (bf16[1,131072]{1,0:T(2,128)(2,1)S(1)}, bf16[1,131072]{1,0:T(2,128)(2,1)}, u32[]{:S(2)}) copy-start(bf16[1,131072]{1,0:T(2,128)(2,1)} %saved_ref.1) | copy-start | bytes 786436
  1.1 0.7 %copy-start.1 = (bf16[128,1,2,32]{0,3,2,1:T(8,128)(2,1)S(1)}, bf16[128,1,2,32]{0,3,2,1:T(8,128)(2,1)}, u32[]{:S(2)}) copy-start(bf16[128,1,2,32]{0,3,2,1:T(8,128)(2,1)} %param.17) | copy-start | bytes 49156
  2.0 8.9 %collective-permute-start.2 = (bf16[16,5248]{1,0:T(8,128)(2,1)S(1)}, bf16[16,5248]{1,0:T(8,128)(2,1)S(1)}, u32[]{:S(2)}, u32[]{:S(2)}) collective-permute-start(bf16[16,5248]{1,0:T(8,128)(2,1)S(1)} %get-tuple-element.62.own_ref), channel_id=1, source_target_pairs={{1,2},{5,6},{9,10},{13,14},{17,18},{21,22},{25,26},{29,30}} | collective-permute-start | bytes 503816 | tf_op jit(solution)/shard_map/ppermute | solution.py:472
  3.3 7.6 %collective-permute-start = (bf16[64,512]{1,0:T(8,128)(2,1)S(1)}, bf16[64,512]{1,0:T(8,128)(2,1)S(1)}, u32[]{:S(2)}, u32[]{:S(2)}) collective-permute-start(bf16[64,512]{1,0:T(8,128)(2,1)S(1)} %get-tuple-element.59), channel_id=1, source_target_pairs={{0,4},{1,5},{2,6},{3,7},{4,8},{5,9},{6,10},{7,11},{8,12},{9,13},{1... | collective-permute-start | bytes 196616 | tf_op jit(solution)/shard_map/ppermute | solution.py:426
  6.7 6.2 %collective-permute-start.1 = (bf16[64,512]{1,0:T(8,128)(2,1)S(1)}, bf16[64,512]{1,0:T(8,128)(2,1)S(1)}, u32[]{:S(2)}, u32[]{:S(2)}) collective-permute-start(bf16[64,512]{1,0:T(8,128)(2,1)S(1)} %get-tuple-element.60), channel_id=1, source_target_pairs={{4,0},{5,1},{6,2},{7,3},{8,4},{9,5},{10,6},{11,7},{12,8},{13,9},{1... | collective-permute-start | bytes 196616 | tf_op jit(solution)/shard_map/ppermute | solution.py:426
  12.9 3.4 %collective-permute-start.3 = (bf16[64,2048]{1,0:T(8,128)(2,1)S(1)}, bf16[64,2048]{1,0:T(8,128)(2,1)S(1)}, u32[]{:S(2)}, u32[]{:S(2)}) collective-permute-start(bf16[64,2048]{1,0:T(8,128)(2,1)S(1)} %shard_map.45), channel_id=1, source_target_pairs={{3,2},{7,6},{11,10},{15,14},{19,18},{23,22},{27,26},{31,30}} | collective-permute-start | bytes 786440 | tf_op jit(solution)/shard_map/ppermute | solution.py:489
  17.5 12.9 %collective-permute-start.5 = (bf16[32,4096]{1,0:T(8,128)(2,1)S(1)}, bf16[32,4096]{1,0:T(8,128)(2,1)S(1)}, u32[]{:S(2)}, u32[]{:S(2)}) collective-permute-start(bf16[32,4096]{1,0:T(8,128)(2,1)S(1)} %get-tuple-element.66), channel_id=1, source_target_pairs={{2,1},{6,5},{10,9},{14,13},{18,17},{22,21},{26,25},{30,29}} | collective-permute-start | bytes 786440 | tf_op jit(solution)/shard_map/ppermute | solution.py:514
  18.8 2.0 %collective-permute-start.6 = (bf16[1,64,640]{2,1,0:T(8,128)(2,1)S(1)}, bf16[1,64,640]{2,1,0:T(8,128)(2,1)S(1)}, u32[]{:S(2)}, u32[]{:S(2)}) collective-permute-start(bf16[1,64,640]{2,1,0:T(8,128)(2,1)S(1)} %bitcast.51), channel_id=1, source_target_pairs={{3,19},{7,23},{11,27},{15,31},{19,3},{23,7},{27,11},{31,15}} | collective-permute-start | bytes 245768 | tf_op jit(solution)/shard_map/ppermute | solution.py:426
  19.5 10.9 %collective-permute-start.4 = (bf16[16,4096]{1,0:T(8,128)(2,1)S(1)}, bf16[16,4096]{1,0:T(8,128)(2,1)S(1)}, u32[]{:S(2)}, u32[]{:S(2)}) collective-permute-start(bf16[16,4096]{1,0:T(8,128)(2,1)S(1)} %get-tuple-element.65), channel_id=1, source_target_pairs={{2,0},{6,4},{10,8},{14,12},{18,16},{22,20},{26,24},{30,28}} | collective-permute-start | bytes 393224 | tf_op jit(solution)/shard_map/ppermute | solution.py:513
  20.9 5.7 %collective-permute-start.7 = (bf16[2,64,640]{2,1,0:T(8,128)(2,1)S(1)}, bf16[2,64,640]{2,1,0:T(8,128)(2,1)S(1)}, u32[]{:S(2)}, u32[]{:S(2)}) collective-permute-start(bf16[2,64,640]{2,1,0:T(8,128)(2,1)S(1)} %pad_maximum_fusion.2), channel_id=1, source_target_pairs={{3,11},{7,15},{11,3},{15,7},{19,27},{23,31},{27,19},{31,23}} | collective-permute-start | bytes 491528 | tf_op jit(solution)/shard_map/ppermute | solution.py:426
  22.2 8.2 %collective-permute-start.11 = (f32[432,128]{1,0:T(8,128)S(1)}, f32[432,128]{1,0:T(8,128)S(1)}, u32[]{:S(2)}, u32[]{:S(2)}) collective-permute-start(f32[432,128]{1,0:T(8,128)S(1)} %shard_map.47), channel_id=1, source_target_pairs={{2,6},{6,2},{10,14},{14,10},{18,22},{22,18},{26,30},{30,26}} | collective-permute-start | bytes 663560 | tf_op jit(solution)/shard_map/ppermute | solution.py:426
  26.6 17.3 %collective-permute-start.14 = (bf16[4,64,640]{2,1,0:T(8,128)(2,1)S(1)}, bf16[4,64,640]{2,1,0:T(8,128)(2,1)S(1)}, u32[]{:S(2)}, u32[]{:S(2)}) collective-permute-start(bf16[4,64,640]{2,1,0:T(8,128)(2,1)S(1)} %constant_dynamic-update-slice_fusion), channel_id=1, source_target_pairs={{3,7},{7,3},{11,15},{15,11},{19,23},{23,19},{27,31},{31,27}} | collective-permute-start | bytes 983048 | tf_op jit(solution)/shard_map/ppermute | solution.py:426
  30.5 4.5 %collective-permute-start.8 = (f32[144,128]{1,0:T(8,128)S(1)}, f32[144,128]{1,0:T(8,128)S(1)}, u32[]{:S(2)}, u32[]{:S(2)}) collective-permute-start(f32[144,128]{1,0:T(8,128)S(1)} %shard_map.48), channel_id=1, source_target_pairs={{0,4},{1,5},{4,0},{5,1},{8,12},{9,13},{12,8},{13,9},{16,20},{17,21... | collective-permute-start | bytes 221192 | tf_op jit(solution)/shard_map/ppermute | solution.py:426
  31.2 7.8 %collective-permute-start.12 = (f32[432,128]{1,0:T(8,128)S(1)}, f32[432,128]{1,0:T(8,128)S(1)}, u32[]{:S(2)}, u32[]{:S(2)}) collective-permute-start(f32[432,128]{1,0:T(8,128)S(1)} %add.41), channel_id=1, source_target_pairs={{2,10},{6,14},{10,2},{14,6},{18,26},{22,30},{26,18},{30,22}} | collective-permute-start | bytes 663560 | tf_op jit(solution)/shard_map/ppermute | solution.py:426
  35.1 0.7 %collective-permute-start.9 = (f32[144,128]{1,0:T(8,128)S(1)}, f32[144,128]{1,0:T(8,128)S(1)}, u32[]{:S(2)}, u32[]{:S(2)}) collective-permute-start(f32[144,128]{1,0:T(8,128)S(1)} %add.39), channel_id=1, source_target_pairs={{0,8},{1,9},{4,12},{5,13},{8,0},{9,1},{12,4},{13,5},{16,24},{17,25... | collective-permute-start | bytes 221192 | tf_op jit(solution)/shard_map/ppermute | solution.py:426
  35.8 8.1 %collective-permute-start.10 = (f32[144,128]{1,0:T(8,128)S(1)}, f32[144,128]{1,0:T(8,128)S(1)}, u32[]{:S(2)}, u32[]{:S(2)}) collective-permute-start(f32[144,128]{1,0:T(8,128)S(1)} %add.40), channel_id=1, source_target_pairs={{0,16},{1,17},{4,20},{5,21},{8,24},{9,25},{12,28},{13,29},{16,0},{... | collective-permute-start | bytes 221192 | tf_op jit(solution)/shard_map/ppermute | solution.py:426
  39.0 11.2 %collective-permute-start.13 = (f32[432,128]{1,0:T(8,128)S(1)}, f32[432,128]{1,0:T(8,128)S(1)}, u32[]{:S(2)}, u32[]{:S(2)}) collective-permute-start(f32[432,128]{1,0:T(8,128)S(1)} %add.42), channel_id=1, source_target_pairs={{2,18},{6,22},{10,26},{14,30},{18,2},{22,6},{26,10},{30,14}} | collective-permute-start | bytes 663560 | tf_op jit(solution)/shard_map/ppermute | solution.py:426

commit v6 on v5

--- a/solution.py
+++ b/solution.py
@@ -84,6 +84,7 @@
 
 
 def spread_top(block):
+    block = dot(block, halves_of(C4, 2)).astype(BF16)
     unit = spread(64, 2 * LANES, lambda e: LANES * (e // 32) + 2 * (e % 32), lambda e: e >= 0)
     turned = (((0,), (0,)), ((), ()))
     return lax.dot_general(block, unit, turned, preferred_element_type=F32).astype(BF16)
@@ -152,12 +153,39 @@
             send(place, 0, down_ref)
 
 
+def weights_layout_kernel(weights_ref, out_ref, wide):
+    @pl.when(on_segment(3))
+    def _():
+        for tap in range(27):
+            first = 8192 * tap
+            wide[64 * tap : 64 * tap + 64, :] = (
+                weights_ref[:, first : first + 8192].astype(F32).reshape(64, LANES)
+            )
+        for group in range(9):
+            turned = jnp.transpose(wide[192 * group : 192 * group + 192, :]).astype(BF16)
+            rows = slice(C3 * group, C3 * group + C3)
+            out_ref[rows, :192] = turned[:64]
+            out_ref[rows, 192:] = turned[64:]
+
+
+def halves_of(channels, parts):
+    size = channels // parts
+    return spread(channels, channels, lambda e: (e % parts) * size + e // parts, lambda e: e >= 0)
+
+
 def section3_kernel(own_ref, up_ref, down_ref, weights_ref, out_ref, wide, stacked, terms):
     @pl.when(on_segment(3))
     def _():
         for place, (ref, first) in enumerate(((up_ref, 2), (own_ref, 4), (down_ref, 2))):
             wide[:, cols(2 * place, 2)] = spread_top(ref[:, cols(first)])
-        stack_moved(lambda row: wide[:, cols(row)], stacked, C4, 6, (0, 1, 2))
+        for half in range(2):
+            stack_moved(
+                lambda row: wide[64 * half : 64 * half + 64, cols(row)],
+                stacked.at[192 * half : 192 * half + 192],
+                64,
+                6,
+                (0, 1, 2),
+            )
         terms[...] = dot(weights_ref[...], stacked[...])
         unit = spread(LANES, LANES, lambda e: 2 * e, lambda e: e < 64)
         last = is_last_block()
@@ -200,7 +228,7 @@
     @pl.when(on_segment(2))
     def _():
         stack_moved(lambda row: grad_ref[:, cols(row)], stacked, C3, 16, (0, 1, 2))
-        terms[...] = dot(weights_ref[:288, :192], stacked[...])
+        terms[...] = dot(weights_ref[...], stacked[...])
         last = is_last_block()
         for cell_z in range(-1, 5):
             for cell_y in range(8):
@@ -245,7 +273,13 @@
 def weights2_kernel(scale, grad_ref, up_ref, down_ref, own_ref, out_ref, stacked, acts):
     @pl.when(on_segment(2))
     def _():
-        stack_moved(lambda row: grad_ref[:, cols(4 + row)], stacked, C3, 8, (0, 1, 2))
+        ordered = lax.dot_general(
+            halves_of(C3, 4),
+            grad_ref[:, cols(4, 8)],
+            (((0,), (0,)), ((), ())),
+            preferred_element_type=F32,
+        ).astype(BF16)
+        stack_moved(lambda row: ordered[:, cols(row)], stacked, C3, 8, (0, 1, 2))
         for tap_z in range(3):
             for tap_y in range(3):
                 first = C2 * (3 * tap_z + tap_y)
@@ -259,9 +293,15 @@
                         else:
                             block = own_ref[:, cols(8 * plane + row)]
                         acts[first : first + C2, cols(4 * place_z + place_y)] = block
-        out_ref[:288, :] = dot_rows(acts[...], stacked[:128, :]) * scale
-        out_ref[288:, :64] = dot_rows(acts[:144, :], stacked[128:, :]) * scale
-        out_ref[288:, 64:] = dot_rows(acts[144:, :], stacked[128:, :]) * scale
+        total = dot_rows(stacked[...], acts[...]) * scale
+        for group in range(9):
+            for tap_x in range(3):
+                first = 16 * (3 * group + tap_x)
+                for part in range(4):
+                    row = C3 * tap_x + 16 * part
+                    out_ref[first : first + 16, 32 * part : 32 * part + 32] = total[
+                        row : row + 16, 32 * group : 32 * group + 32
+                    ]
 
 
 def fine_acts(chans, up_ref, down_ref, own_ref, plane, row):
@@ -357,7 +397,15 @@
                         source = zero if row == 4 else rows[4 * tap_z + row]
                         acts[first : first + C3, cols(2 * block + place_y)] = source
         stack_moved(lambda row: wide[:, cols(row)], stacked, C4, 2 * count, (0, 1, 2))
-        out_ref[...] = dot_rows(stacked[...], acts[...]) * scale
+        total = dot_rows(stacked[...], acts[...]) * scale
+        for group in range(9):
+            for tap_x in range(3):
+                first = 64 * (3 * group + tap_x)
+                for part in range(2):
+                    row = C4 * tap_x + 64 * part
+                    out_ref[first : first + 64, 64 * part : 64 * part + 64] = total[
+                        row : row + 64, C3 * group : C3 * group + C3
+                    ]
 
 
 def places_bits(places):
@@ -400,12 +448,10 @@
     return jnp.concatenate(groups, 0)
 
 
-def deep_layout(section, weights):
-    if section == 3:
-        return by_tap(weights, C4, C3)
+def middle_layout(section, weights):
     if section == 2:
-        return padded(by_tap(weights, C3, C2), 576, 384)
-    return jnp.zeros((576, 384), BF16)
+        return by_tap(weights, C3, C2)
+    return jnp.zeros((288, 192), BF16)
 
 
 def fine_layout(section, weights):
@@ -426,9 +472,12 @@
     return lax.ppermute(block, ("space", "segment"), pairs_of(segments, route))
 
 
-def flat_row(ordered, room):
-    flat = ordered.reshape(-1)
-    return jnp.pad(flat, (0, room - flat.shape[0]))[None]
+def filled(ordered):
+    rows = ordered.reshape(-1, LANES) if ordered.size % LANES == 0 else None
+    if rows is None:
+        flat = ordered.reshape(-1)
+        rows = jnp.pad(flat, (0, -flat.shape[0] % LANES)).reshape(-1, LANES)
+    return rows
 
 
 def shards(saved_inputs, conv_weights, top_gradient):
@@ -470,11 +519,18 @@
     up = over_space(up, range(4), later)
     down = over_space(down, range(4), sooner)
     next_own = lax.ppermute(own01, "segment", [(1, 2)])
+    (taps3,) = call(
+        weights_layout_kernel,
+        [((576, 384), BF16)],
+        [((1728, 128), F32)],
+        conv_weights,
+        flops=LONG,
+    )
     (weights,) = behind((conv_weights,), deep)
-    deep_taps = lax.switch(
-        segment, [functools.partial(deep_layout, section) for section in range(4)], weights
-    )
-    (deep_taps,) = behind((deep_taps,), next_own)
+    taps2 = lax.switch(
+        segment, [functools.partial(middle_layout, section) for section in range(4)], weights
+    )
+    taps3, taps2 = behind((taps3, taps2), next_own)
 
     (grad2,) = call(
         section3_kernel,
@@ -483,7 +539,7 @@
         deep,
         up,
         down,
-        deep_taps,
+        taps3,
         flops=2 * 576 * 384 * 768,
     )
     grad2 = lax.ppermute(grad2, "segment", [(3, 2)])
@@ -502,7 +558,7 @@
         up,
         down,
         own2,
-        deep_taps,
+        taps2,
         next_own,
         flops=2 * 288 * 192 * 2048,
     )
@@ -559,7 +615,7 @@
     held = len(places)
     (sum3,) = call(
         functools.partial(weights3_kernel, scales[3], places),
-        [((384, 576), F32)],
+        [((1728, 128), F32)],
         [((128, 256 * held), BF16), ((384, 256 * held), BF16), ((576, 256 * held), BF16)],
         blocks,
         down,
@@ -570,22 +626,22 @@
 
     def finish0(sum01, sum2, sum3):
         parts = sum01[:, :48].reshape(3, 3, C1, 3, 16)[..., :C0]
-        return flat_row(jnp.transpose(parts, (3, 0, 1, 2, 4)), room)
+        return filled(jnp.transpose(parts, (3, 0, 1, 2, 4)))
 
     def finish1(sum01, sum2, sum3):
         parts = sum01[:, :96].reshape(9, C1, 3, C2)
-        return flat_row(jnp.transpose(parts, (0, 2, 3, 1)), room)
-
-    def finish2(sum01, sum2, sum3):
-        two = sum2[:288].reshape(9, C2, 2, C3)
-        one = jnp.transpose(sum2[288:].reshape(144, 2, C3), (1, 0, 2)).reshape(9, C2, 1, C3)
-        return flat_row(jnp.transpose(jnp.concatenate([two, one], 2), (0, 2, 3, 1)), room)
-
-    def finish3(sum01, sum2, sum3):
-        parts = sum3.reshape(3, C4, 9, C3)
-        return flat_row(jnp.transpose(parts, (2, 0, 1, 3)), room)
-
-    return lax.switch(segment, [finish0, finish1, finish2, finish3], sum01, sum2, sum3)
+        return filled(jnp.transpose(parts, (0, 2, 3, 1)))
+
+    def whole(finish):
+        def branch(*sums):
+            rows = finish(*sums)
+            return jnp.pad(rows, ((0, room // LANES - rows.shape[0]), (0, 0)))
+
+        return branch
+
+    ends = [finish0, finish1, lambda a, b, c: b, lambda a, b, c: c]
+    rows = lax.switch(segment, [whole(end) for end in ends], sum01, sum2, sum3)
+    return rows.reshape(1, room)
 
 
 def solution(mesh):

time: 53.3 us -> 53.1 us (level)
  local copies, waits for them, and re-layouts: 6.51 us -> 4.78 us
  starting transfers between devices: 27 us -> 28.3 us
  Pallas kernels: 2.27 us -> 3.47 us
    ppermute x11, waiting for transfers between devices: 13.6 us -> 11.8 us  [over_space(): return lax.ppermute(block, ('space', 'segment'), pairs_of(segments, route))]
    ppermute x1, waiting for transfers between devices: 0.01 us -> 1.4 us  [shards(): next_own = lax.ppermute(own01, 'segment', [(1, 2)])]
    ppermute x11, starting transfers between devices: 21.8 us -> 23.1 us  [over_space(): return lax.ppermute(block, ('space', 'segment'), pairs_of(segments, route))]
    pallas_call x6 -> x7, Pallas kernels: 2.27 us -> 3.47 us  [call(): pl.pallas_call(kernel, out_shape=shapes, in_specs=[far_spec if place in f...]
    reshape x5 -> x0, local copies, waits for them, and re-layouts: 0.96 us -> none  [the longest x2 0.43 us: finish2(): two = sum2[:288].reshape(9, C2, 2, C3)]
    pad x1, local copies, waits for them, and re-layouts: 0.97 us -> 0.06 us  [branch(): return jnp.pad(rows, ((0, room // LANES - rows.shape[0]), (0, 0)))]
    unnamed x6 -> x8, local copies, waits for them, and re-layouts: 1.78 us -> 1.95 us
  transfers between devices with their start and end apart: 15 -> 15, of which waited for: 5 -> 5; matrix products, arithmetic and copies ran while one was open for 6% -> 6% of each run, Pallas kernels for 2% -> 4%
where the time goes in v6:
time: 53.1 us; the launch traced here: 52.5 us
  starting transfers between devices  28.3 us (53%)
  waiting for transfers between devices  15.3 us (29%)
  local copies, waits for them, and re-layouts  4.78 us (9%)
  Pallas kernels  3.47 us (7%)
    ppermute x11, starting transfers between devices, over_space(): return lax.ppermute(block, ('space', 'segment'), pairs_of(segments, route))  23.1 us
    ppermute x11, waiting for transfers between devices, over_space(): return lax.ppermute(block, ('space', 'segment'), pairs_of(segments, route))  11.8 us
    pallas_call x7, Pallas kernels, call(): pl.pallas_call(kernel, out_shape=shapes, in_specs=[far_spec if place in f...  3.47 us
    ppermute x1, waiting for transfers between devices, shards(): grad2 = lax.ppermute(grad2, 'segment', [(3, 2)])  2.13 us
    unnamed x8, local copies, waits for them, and re-layouts  1.95 us
    slice x1, local copies, waits for them, and re-layouts, by_tap(): weights[0, tap_z * size:(tap_z + 1) * size].reshape(3, 3, chan_out, chan_in)  1.59 us
    ppermute x1, waiting for transfers between devices, shards(): next_own = lax.ppermute(own01, 'segment', [(1, 2)])  1.4 us
    ppermute x1, starting transfers between devices, shards(): grad1 = lax.ppermute(grad1, 'segment', [(2, 1)])  1.31 us
  transfers between devices with their start and end apart: 15, of which 5 were waited for; matrix products, arithmetic and copies ran while one was open for 6% of the time, Pallas kernels for 4%

profile of v6, /device:TPU:2, one launch (start us, length us, event | category | flops | bytes accessed | tf_op | source)
XLA Modules:
  0.0 52.5 jit_solution(16529834942873804666)
XLA Ops:
  0.0 1.0 %copy-done = bf16[1,131072]{1,0:T(2,128)(2,1)S(1)} copy-done((bf16[1,131072]{1,0:T(2,128)(2,1)S(1)}, bf16[1,131072]{1,0:T(2,128)(2,1)}, u32[]{:S(2)}) %copy-start) | copy-done | bytes 262168
  1.0 0.2 shard_map.44
  1.2 3.4 %collective-permute-start = (bf16[64,512]{1,0:T(8,128)(2,1)S(1)}, bf16[64,512]{1,0:T(8,128)(2,1)S(1)}, u32[]{:S(2)}, u32[]{:S(2)}) collective-permute-start(bf16[64,512]{1,0:T(8,128)(2,1)S(1)} %get-tuple-element.61), channel_id=1, source_target_pairs={{0,4},{1,5},{2,6},{3,7},{4,8},{5,9},{6,10},{7,11},{8,12},{9,13},{1... | collective-permute-start | bytes 196616 | tf_op jit(solution)/shard_map/ppermute | solution.py:472
  4.7 1.3 %collective-permute-start.1 = (bf16[64,512]{1,0:T(8,128)(2,1)S(1)}, bf16[64,512]{1,0:T(8,128)(2,1)S(1)}, u32[]{:S(2)}, u32[]{:S(2)}) collective-permute-start(bf16[64,512]{1,0:T(8,128)(2,1)S(1)} %get-tuple-element.62), channel_id=1, source_target_pairs={{4,0},{5,1},{6,2},{7,3},{8,4},{9,5},{10,6},{11,7},{12,8},{13,9},{1... | collective-permute-start | bytes 196616 | tf_op jit(solution)/shard_map/ppermute | solution.py:472
  6.0 1.3 %collective-permute-start.2 = (bf16[16,5248]{1,0:T(8,128)(2,1)S(1)}, bf16[16,5248]{1,0:T(8,128)(2,1)S(1)}, u32[]{:S(2)}, u32[]{:S(2)}) collective-permute-start(bf16[16,5248]{1,0:T(8,128)(2,1)S(1)} %get-tuple-element.64.own_ref), channel_id=1, source_target_pairs={{1,2},{5,6},{9,10},{13,14},{17,18},{21,22},{25,26},{29,30}} | collective-permute-start | bytes 503816 | tf_op jit(solution)/shard_map/ppermute | solution.py:521
  7.3 1.2 %shard_map.45.weights_ref = bf16[576,384]{1,0:T(8,128)(2,1)S(1)} custom-call(bf16[1,221184]{1,0:T(2,128)(2,1)} %weights_ref.1), custom_call_target="tpu_custom_call" | custom-call | flops 20000000000 | bytes 884736 | tf_op jit(solution)/shard_map/pallas_call | solution.py:426
  8.4 2.8 %conditional.4 = (bf16[288,192]{1,0:T(8,128)(2,1)S(1)}) conditional(s32[]{:T(128)} %clamp.2, () %tuple.55, () %tuple.56, bf16[1,221184]{1,0:T(2,128)(2,1)} %weights_ref.1, () %tuple.58), branch_computations={%region_4.5_spmd, %region_5.6_spmd, %region_6.7_spmd, %region_7.8_... | conditional | flops 331776 | bytes 1105928 | solution.py:530
  8.4 1.6 %slice_reduce_fusion.5 = (bf16[18432]{0:T(1024)(128)(2,1)S(1)}, bf16[18432]{0:T(1024)(128)(2,1)S(1)}, bf16[18432]{0:T(1024)(128)(2,1)S(1)}) fusion(bf16[1,221184]{1,0:T(2,128)(2,1)} %param.6), kind=kLoop, calls=%fused_computation.16 | loop fusion | bytes 221184 | tf_op jit(solution)/shard_map/cond/branch_2_fun/slice | solution.py:446
  10.0 0.1 squeeze.17
  10.1 0.1 copy.18
  10.3 0.1 reshape.36
  10.4 0.1 squeeze.19
  10.5 0.1 copy.20
  10.7 0.1 reshape.38
  10.8 0.1 squeeze.18
  10.9 0.1 copy.19
  11.1 0.1 reshape.37
  11.2 1.4 %collective-permute-done.2.next_ref = bf16[16,5248]{1,0:T(8,128)(2,1)S(1)} collective-permute-done((bf16[16,5248]{1,0:T(8,128)(2,1)S(1)}, bf16[16,5248]{1,0:T(8,128)(2,1)S(1)}, u32[]{:S(2)}, u32[]{:S(2)}) %collective-permute-start.2) | collective-permute-done | bytes 167968 | tf_op jit(solution)/shard_map/ppermute | solution.py:521
  12.6 0.0 collective-permute-done.up_ref
  12.6 0.0 collective-permute-done.1.down_ref
  12.6 1.3 %collective-permute-start.3 = (bf16[64,2048]{1,0:T(8,128)(2,1)S(1)}, bf16[64,2048]{1,0:T(8,128)(2,1)S(1)}, u32[]{:S(2)}, u32[]{:S(2)}) collective-permute-start(bf16[64,2048]{1,0:T(8,128)(2,1)S(1)} %shard_map.46), channel_id=1, source_target_pairs={{3,2},{7,6},{11,10},{15,14},{19,18},{23,22},{27,26},{31,30}} | collective-permute-start | bytes 786440 | tf_op jit(solution)/shard_map/ppermute | solution.py:545
  13.9 2.1 %collective-permute-done.3.grad_ref = bf16[64,2048]{1,0:T(8,128)(2,1)S(1)} collective-permute-done((bf16[64,2048]{1,0:T(8,128)(2,1)S(1)}, bf16[64,2048]{1,0:T(8,128)(2,1)S(1)}, u32[]{:S(2)}, u32[]{:S(2)}) %collective-permute-start.3) | collective-permute-done | bytes 262176 | tf_op jit(solution)/shard_map/ppermute | solution.py:545
  16.1 1.2 %shard_map.47 = (bf16[32,4096]{1,0:T(8,128)(2,1)S(1)}, bf16[16,4096]{1,0:T(8,128)(2,1)S(1)}) custom-call(bf16[64,2048]{1,0:T(8,128)(2,1)S(1)} %collective-permute-done.3.grad_ref, bf16[64,512]{1,0:T(8,128)(2,1)S(1)} %collective-permute-done.up_ref, bf16[64,512]{1,0:T(8,128)(2,1)S(1)} %collective-permute-done.1.down_ref, ...), custom_call_target="tpu_custom_call" | custom-call | flops 226492416 | bytes 1327104 | tf_op jit(solution)/shard_map/pallas_call | solution.py:426
  17.3 1.3 %collective-permute-start.5 = (bf16[32,4096]{1,0:T(8,128)(2,1)S(1)}, bf16[32,4096]{1,0:T(8,128)(2,1)S(1)}, u32[]{:S(2)}, u32[]{:S(2)}) collective-permute-start(bf16[32,4096]{1,0:T(8,128)(2,1)S(1)} %get-tuple-element.69), channel_id=1, source_target_pairs={{2,1},{6,5},{10,9},{14,13},{18,17},{22,21},{26,25},{30,29}} | collective-permute-start | bytes 786440 | tf_op jit(solution)/shard_map/ppermute | solution.py:570
  18.6 0.7 %collective-permute-start.6 = (bf16[1,64,640]{2,1,0:T(8,128)(2,1)S(1)}, bf16[1,64,640]{2,1,0:T(8,128)(2,1)S(1)}, u32[]{:S(2)}, u32[]{:S(2)}) collective-permute-start(bf16[1,64,640]{2,1,0:T(8,128)(2,1)S(1)} %bitcast.27), channel_id=1, source_target_pairs={{3,19},{7,23},{11,27},{15,31},{19,3},{23,7},{27,11},{31,15}} | collective-permute-start | bytes 245768 | tf_op jit(solution)/shard_map/ppermute | solution.py:472
  19.3 1.3 %collective-permute-start.4 = (bf16[16,4096]{1,0:T(8,128)(2,1)S(1)}, bf16[16,4096]{1,0:T(8,128)(2,1)S(1)}, u32[]{:S(2)}, u32[]{:S(2)}) collective-permute-start(bf16[16,4096]{1,0:T(8,128)(2,1)S(1)} %get-tuple-element.68), channel_id=1, source_target_pairs={{2,0},{6,4},{10,8},{14,12},{18,16},{22,20},{26,24},{30,28}} | collective-permute-start | bytes 393224 | tf_op jit(solution)/shard_map/ppermute | solution.py:569
  20.6 0.0 collective-permute-done.6
  20.7 0.7 %collective-permute-start.7 = (bf16[2,64,640]{2,1,0:T(8,128)(2,1)S(1)}, bf16[2,64,640]{2,1,0:T(8,128)(2,1)S(1)}, u32[]{:S(2)}, u32[]{:S(2)}) collective-permute-start(bf16[2,64,640]{2,1,0:T(8,128)(2,1)S(1)} %pad_maximum_fusion.2), channel_id=1, source_target_pairs={{3,11},{7,15},{11,3},{15,7},{19,27},{23,31},{27,19},{31,23}} | collective-permute-start | bytes 491528 | tf_op jit(solution)/shard_map/ppermute | solution.py:472
  21.4 0.8 %shard_map.48 = f32[432,128]{1,0:T(8,128)S(1)} custom-call(bf16[64,2048]{1,0:T(8,128)(2,1)S(1)} %collective-permute-done.3.grad_ref, bf16[64,512]{1,0:T(8,128)(2,1)S(1)} %collective-permute-done.up_ref, bf16[64,512]{1,0:T(8,128)(2,1)S(1)} %collective-permute-done.1.down_ref, bf16[32,4096]{1,0:T(8,128)(2,1)S(1)} %get-tuple-element.66.own_ref), custom_call_target="tpu_custom_call" | custom-call | flops 20000000000 | bytes 876544 | tf_op jit(solution)/shard_map/pallas_call | solution.py:426
  22.2 4.6 %collective-permute-start.11 = (f32[432,128]{1,0:T(8,128)S(1)}, f32[432,128]{1,0:T(8,128)S(1)}, u32[]{:S(2)}, u32[]{:S(2)}) collective-permute-start(f32[432,128]{1,0:T(8,128)S(1)} %shard_map.48), channel_id=1, source_target_pairs={{2,6},{6,2},{10,14},{14,10},{18,22},{22,18},{26,30},{30,26}} | collective-permute-start | bytes 663560 | tf_op jit(solution)/shard_map/ppermute | solution.py:472
  26.8 0.0 collective-permute-done.7
  26.8 0.7 %collective-permute-start.14 = (bf16[4,64,640]{2,1,0:T(8,128)(2,1)S(1)}, bf16[4,64,640]{2,1,0:T(8,128)(2,1)S(1)}, u32[]{:S(2)}, u32[]{:S(2)}) collective-permute-start(bf16[4,64,640]{2,1,0:T(8,128)(2,1)S(1)} %constant_dynamic-update-slice_fusion), channel_id=1, source_target_pairs={{3,7},{7,3},{11,15},{15,11},{19,23},{23,19},{27,31},{31,27}} | collective-permute-start | bytes 983048 | tf_op jit(solution)/shard_map/ppermute | solution.py:472
  27.5 3.1 %collective-permute-done.11 = f32[432,128]{1,0:T(8,128)S(1)} collective-permute-done((f32[432,128]{1,0:T(8,128)S(1)}, f32[432,128]{1,0:T(8,128)S(1)}, u32[]{:S(2)}, u32[]{:S(2)}) %collective-permute-start.11) | collective-permute-done | bytes 221216 | tf_op jit(solution)/shard_map/ppermute | solution.py:472
  30.7 0.0 collective-permute-done.4.grad0_ref
  30.7 0.7 %collective-permute-start.8 = (f32[144,128]{1,0:T(8,128)S(1)}, f32[144,128]{1,0:T(8,128)S(1)}, u32[]{:S(2)}, u32[]{:S(2)}) collective-permute-start(f32[144,128]{1,0:T(8,128)S(1)} %shard_map.49), channel_id=1, source_target_pairs={{0,4},{1,5},{4,0},{5,1},{8,12},{9,13},{12,8},{13,9},{16,20},{17,21... | collective-permute-start | bytes 221192 | tf_op jit(solution)/shard_map/ppermute | solution.py:472
  31.4 4.9 %collective-permute-start.12 = (f32[432,128]{1,0:T(8,128)S(1)}, f32[432,128]{1,0:T(8,128)S(1)}, u32[]{:S(2)}, u32[]{:S(2)}) collective-permute-start(f32[432,128]{1,0:T(8,128)S(1)} %add.41), channel_id=1, source_target_pairs={{2,10},{6,14},{10,2},{14,6},{18,26},{22,30},{26,18},{30,22}} | collective-permute-start | bytes 663560 | tf_op jit(solution)/shard_map/ppermute | solution.py:472
  36.3 0.0 collective-permute-done.8
  36.3 0.7 %collective-permute-start.9 = (f32[144,128]{1,0:T(8,128)S(1)}, f32[144,128]{1,0:T(8,128)S(1)}, u32[]{:S(2)}, u32[]{:S(2)}) collective-permute-start(f32[144,128]{1,0:T(8,128)S(1)} %add.39), channel_id=1, source_target_pairs={{0,8},{1,9},{4,12},{5,13},{8,0},{9,1},{12,4},{13,5},{16,24},{17,25... | collective-permute-start | bytes 221192 | tf_op jit(solution)/shard_map/ppermute | solution.py:472
  37.0 0.7 %collective-permute-start.10 = (f32[144,128]{1,0:T(8,128)S(1)}, f32[144,128]{1,0:T(8,128)S(1)}, u32[]{:S(2)}, u32[]{:S(2)}) collective-permute-start(f32[144,128]{1,0:T(8,128)S(1)} %add.40), channel_id=1, source_target_pairs={{0,16},{1,17},{4,20},{5,21},{8,24},{9,25},{12,28},{13,29},{16,0},{... | collective-permute-start | bytes 221192 | tf_op jit(solution)/shard_map/ppermute | solution.py:472
  37.7 2.5 %collective-permute-done.12 = f32[432,128]{1,0:T(8,128)S(1)} collective-permute-done((f32[432,128]{1,0:T(8,128)S(1)}, f32[432,128]{1,0:T(8,128)S(1)}, u32[]{:S(2)}, u32[]{:S(2)}) %collective-permute-start.12) | collective-permute-done | bytes 221216 | tf_op jit(solution)/shard_map/ppermute | solution.py:472
  40.2 4.9 %collective-permute-start.13 = (f32[432,128]{1,0:T(8,128)S(1)}, f32[432,128]{1,0:T(8,128)S(1)}, u32[]{:S(2)}, u32[]{:S(2)}) collective-permute-start(f32[432,128]{1,0:T(8,128)S(1)} %add.42), channel_id=1, source_target_pairs={{2,18},{6,22},{10,26},{14,30},{18,2},{22,6},{26,10},{30,14}} | collective-permute-start | bytes 663560 | tf_op jit(solution)/shard_map/ppermute | solution.py:472
  45.2 0.0 collective-permute-done.14
  45.2 0.1 pad_maximum_fusion.1.blocks_ref
  45.3 6.1 %collective-permute-done.13 = f32[432,128]{1,0:T(8,128)S(1)} collective-permute-done((f32[432,128]{1,0:T(8,128)S(1)}, f32[432,128]{1,0:T(8,128)S(1)}, u32[]{:S(2)}, u32[]{:S(2)}) %collective-permute-start.13) | collective-permute-done | bytes 221216 | tf_op jit(solution)/shard_map/ppermute | solution.py:472
  51.4 0.1 conditional.5
  51.5 0.1 pad.19
  51.6 0.0 copy-start.2
  51.6 0.9 %copy-done.2 = f32[1,221184]{1,0:T(1,128)} copy-done((f32[1,221184]{1,0:T(1,128)}, f32[1,221184]{1,0:T(1,128)S(1)}, u32[]{:S(2)}) %copy-start.2) | copy-done | bytes 884760
  (21 shorter events, 0.3 us)
Async XLA Ops:
  0.0 1.0 %copy-start = (bf16[1,131072]{1,0:T(2,128)(2,1)S(1)}, bf16[1,131072]{1,0:T(2,128)(2,1)}, u32[]{:S(2)}) copy-start(bf16[1,131072]{1,0:T(2,128)(2,1)} %saved_ref.1) | copy-start | bytes 786436
  0.0 1.0 %copy-start.1 = (bf16[128,1,2,32]{0,3,2,1:T(8,128)(2,1)S(1)}, bf16[128,1,2,32]{0,3,2,1:T(8,128)(2,1)}, u32[]{:S(2)}) copy-start(bf16[128,1,2,32]{0,3,2,1:T(8,128)(2,1)} %param.17) | copy-start | bytes 49156
  1.2 11.4 %collective-permute-start = (bf16[64,512]{1,0:T(8,128)(2,1)S(1)}, bf16[64,512]{1,0:T(8,128)(2,1)S(1)}, u32[]{:S(2)}, u32[]{:S(2)}) collective-permute-start(bf16[64,512]{1,0:T(8,128)(2,1)S(1)} %get-tuple-element.61), channel_id=1, source_target_pairs={{0,4},{1,5},{2,6},{3,7},{4,8},{5,9},{6,10},{7,11},{8,12},{9,13},{1... | collective-permute-start | bytes 196616 | tf_op jit(solution)/shard_map/ppermute | solution.py:472
  4.7 8.0 %collective-permute-start.1 = (bf16[64,512]{1,0:T(8,128)(2,1)S(1)}, bf16[64,512]{1,0:T(8,128)(2,1)S(1)}, u32[]{:S(2)}, u32[]{:S(2)}) collective-permute-start(bf16[64,512]{1,0:T(8,128)(2,1)S(1)} %get-tuple-element.62), channel_id=1, source_target_pairs={{4,0},{5,1},{6,2},{7,3},{8,4},{9,5},{10,6},{11,7},{12,8},{13,9},{1... | collective-permute-start | bytes 196616 | tf_op jit(solution)/shard_map/ppermute | solution.py:472
  6.0 6.7 %collective-permute-start.2 = (bf16[16,5248]{1,0:T(8,128)(2,1)S(1)}, bf16[16,5248]{1,0:T(8,128)(2,1)S(1)}, u32[]{:S(2)}, u32[]{:S(2)}) collective-permute-start(bf16[16,5248]{1,0:T(8,128)(2,1)S(1)} %get-tuple-element.64.own_ref), channel_id=1, source_target_pairs={{1,2},{5,6},{9,10},{13,14},{17,18},{21,22},{25,26},{29,30}} | collective-permute-start | bytes 503816 | tf_op jit(solution)/shard_map/ppermute | solution.py:521
  12.6 3.4 %collective-permute-start.3 = (bf16[64,2048]{1,0:T(8,128)(2,1)S(1)}, bf16[64,2048]{1,0:T(8,128)(2,1)S(1)}, u32[]{:S(2)}, u32[]{:S(2)}) collective-permute-start(bf16[64,2048]{1,0:T(8,128)(2,1)S(1)} %shard_map.46), channel_id=1, source_target_pairs={{3,2},{7,6},{11,10},{15,14},{19,18},{23,22},{27,26},{31,30}} | collective-permute-start | bytes 786440 | tf_op jit(solution)/shard_map/ppermute | solution.py:545
  17.3 13.4 %collective-permute-start.5 = (bf16[32,4096]{1,0:T(8,128)(2,1)S(1)}, bf16[32,4096]{1,0:T(8,128)(2,1)S(1)}, u32[]{:S(2)}, u32[]{:S(2)}) collective-permute-start(bf16[32,4096]{1,0:T(8,128)(2,1)S(1)} %get-tuple-element.69), channel_id=1, source_target_pairs={{2,1},{6,5},{10,9},{14,13},{18,17},{22,21},{26,25},{30,29}} | collective-permute-start | bytes 786440 | tf_op jit(solution)/shard_map/ppermute | solution.py:570
  18.6 2.0 %collective-permute-start.6 = (bf16[1,64,640]{2,1,0:T(8,128)(2,1)S(1)}, bf16[1,64,640]{2,1,0:T(8,128)(2,1)S(1)}, u32[]{:S(2)}, u32[]{:S(2)}) collective-permute-start(bf16[1,64,640]{2,1,0:T(8,128)(2,1)S(1)} %bitcast.27), channel_id=1, source_target_pairs={{3,19},{7,23},{11,27},{15,31},{19,3},{23,7},{27,11},{31,15}} | collective-permute-start | bytes 245768 | tf_op jit(solution)/shard_map/ppermute | solution.py:472
  19.3 11.4 %collective-permute-start.4 = (bf16[16,4096]{1,0:T(8,128)(2,1)S(1)}, bf16[16,4096]{1,0:T(8,128)(2,1)S(1)}, u32[]{:S(2)}, u32[]{:S(2)}) collective-permute-start(bf16[16,4096]{1,0:T(8,128)(2,1)S(1)} %get-tuple-element.68), channel_id=1, source_target_pairs={{2,0},{6,4},{10,8},{14,12},{18,16},{22,20},{26,24},{30,28}} | collective-permute-start | bytes 393224 | tf_op jit(solution)/shard_map/ppermute | solution.py:569
  20.7 6.1 %collective-permute-start.7 = (bf16[2,64,640]{2,1,0:T(8,128)(2,1)S(1)}, bf16[2,64,640]{2,1,0:T(8,128)(2,1)S(1)}, u32[]{:S(2)}, u32[]{:S(2)}) collective-permute-start(bf16[2,64,640]{2,1,0:T(8,128)(2,1)S(1)} %pad_maximum_fusion.2), channel_id=1, source_target_pairs={{3,11},{7,15},{11,3},{15,7},{19,27},{23,31},{27,19},{31,23}} | collective-permute-start | bytes 491528 | tf_op jit(solution)/shard_map/ppermute | solution.py:472
  22.2 8.5 %collective-permute-start.11 = (f32[432,128]{1,0:T(8,128)S(1)}, f32[432,128]{1,0:T(8,128)S(1)}, u32[]{:S(2)}, u32[]{:S(2)}) collective-permute-start(f32[432,128]{1,0:T(8,128)S(1)} %shard_map.48), channel_id=1, source_target_pairs={{2,6},{6,2},{10,14},{14,10},{18,22},{22,18},{26,30},{30,26}} | collective-permute-start | bytes 663560 | tf_op jit(solution)/shard_map/ppermute | solution.py:472
  26.8 18.4 %collective-permute-start.14 = (bf16[4,64,640]{2,1,0:T(8,128)(2,1)S(1)}, bf16[4,64,640]{2,1,0:T(8,128)(2,1)S(1)}, u32[]{:S(2)}, u32[]{:S(2)}) collective-permute-start(bf16[4,64,640]{2,1,0:T(8,128)(2,1)S(1)} %constant_dynamic-update-slice_fusion), channel_id=1, source_target_pairs={{3,7},{7,3},{11,15},{15,11},{19,23},{23,19},{27,31},{31,27}} | collective-permute-start | bytes 983048 | tf_op jit(solution)/shard_map/ppermute | solution.py:472
  30.7 5.6 %collective-permute-start.8 = (f32[144,128]{1,0:T(8,128)S(1)}, f32[144,128]{1,0:T(8,128)S(1)}, u32[]{:S(2)}, u32[]{:S(2)}) collective-permute-start(f32[144,128]{1,0:T(8,128)S(1)} %shard_map.49), channel_id=1, source_target_pairs={{0,4},{1,5},{4,0},{5,1},{8,12},{9,13},{12,8},{13,9},{16,20},{17,21... | collective-permute-start | bytes 221192 | tf_op jit(solution)/shard_map/ppermute | solution.py:472
  31.4 8.8 %collective-permute-start.12 = (f32[432,128]{1,0:T(8,128)S(1)}, f32[432,128]{1,0:T(8,128)S(1)}, u32[]{:S(2)}, u32[]{:S(2)}) collective-permute-start(f32[432,128]{1,0:T(8,128)S(1)} %add.41), channel_id=1, source_target_pairs={{2,10},{6,14},{10,2},{14,6},{18,26},{22,30},{26,18},{30,22}} | collective-permute-start | bytes 663560 | tf_op jit(solution)/shard_map/ppermute | solution.py:472
  36.3 0.7 %collective-permute-start.9 = (f32[144,128]{1,0:T(8,128)S(1)}, f32[144,128]{1,0:T(8,128)S(1)}, u32[]{:S(2)}, u32[]{:S(2)}) collective-permute-start(f32[144,128]{1,0:T(8,128)S(1)} %add.39), channel_id=1, source_target_pairs={{0,8},{1,9},{4,12},{5,13},{8,0},{9,1},{12,4},{13,5},{16,24},{17,25... | collective-permute-start | bytes 221192 | tf_op jit(solution)/shard_map/ppermute | solution.py:472
  37.0 8.1 %collective-permute-start.10 = (f32[144,128]{1,0:T(8,128)S(1)}, f32[144,128]{1,0:T(8,128)S(1)}, u32[]{:S(2)}, u32[]{:S(2)}) collective-permute-start(f32[144,128]{1,0:T(8,128)S(1)} %add.40), channel_id=1, source_target_pairs={{0,16},{1,17},{4,20},{5,21},{8,24},{9,25},{12,28},{13,29},{16,0},{... | collective-permute-start | bytes 221192 | tf_op jit(solution)/shard_map/ppermute | solution.py:472
  40.2 11.2 %collective-permute-start.13 = (f32[432,128]{1,0:T(8,128)S(1)}, f32[432,128]{1,0:T(8,128)S(1)}, u32[]{:S(2)}, u32[]{:S(2)}) collective-permute-start(f32[432,128]{1,0:T(8,128)S(1)} %add.42), channel_id=1, source_target_pairs={{2,18},{6,22},{10,26},{14,30},{18,2},{22,6},{26,10},{30,14}} | collective-permute-start | bytes 663560 | tf_op jit(solution)/shard_map/ppermute | solution.py:472
  51.6 0.9 %copy-start.2 = (f32[1,221184]{1,0:T(1,128)}, f32[1,221184]{1,0:T(1,128)S(1)}, u32[]{:S(2)}) copy-start(f32[1,221184]{1,0:T(1,128)S(1)} %get-tuple-element.119) | copy-start | bytes 2654212

commit v7 on v6

--- a/solution.py
+++ b/solution.py
@@ -96,25 +96,41 @@
         wide[chan : chan + 1, :width] = source.astype(F32)
 
 
+def fetched(far_ref, near_ref, size, arrived):
+    part = pl.ds(0, size)
+    copy = pltpu.make_async_copy(far_ref.at[:, part], near_ref.at[:, part], arrived)
+    copy.start()
+    copy.wait()
+
+
+def weight_rows(held, wide, rows):
+    for tap in range(27):
+        first = LANES * rows * tap
+        wide[rows * tap : rows * tap + rows, :] = (
+            held[:, first : first + LANES * rows].astype(F32).reshape(rows, LANES)
+        )
+
+
 def layout_kernel(
     saved_ref,
+    weights_ref,
     top_ref,
-    taps_ref,
     deep_ref,
     up_ref,
     down_ref,
     own2_ref,
     own01_ref,
     held,
+    held_weights,
     wide,
+    wide_weights,
+    mixed,
+    held_top,
     arrived,
+    arrived_top,
 ):
     def fetch(size):
-        copy = pltpu.make_async_copy(
-            saved_ref.at[:, pl.ds(0, size)], held.at[:, pl.ds(0, size)], arrived
-        )
-        copy.start()
-        copy.wait()
+        fetched(saved_ref, held, size, arrived)
 
     def send(place, plane, target_ref):
         for half in range(2):
@@ -124,10 +140,13 @@
 
     @pl.when(on_segment(3))
     def _():
+        copy = pltpu.make_async_copy(top_ref, held_top, arrived_top)
+        copy.start()
         fetch(C3 * 512)
         copy_rows(held, wide, C3, 512)
         block = wide[:, :512].astype(BF16)
-        top = top_ref[...]
+        copy.wait()
+        top = held_top[...]
         deep_ref[:, :512] = block
         deep_ref[:, 512:] = top
         for ref, half in ((up_ref, block[:, 256:]), (down_ref, block[:, :256])):
@@ -147,30 +166,59 @@
             own_ref = own2_ref if section == 2 else own01_ref
             own_ref[:, :4096] = wide[:place, :].astype(BF16)
             if section == 1:
-                for tap in range(9):
-                    own01_ref[:, cols(32 + tap)] = taps_ref[C1 * tap : C1 * (tap + 1), :]
+                fetched(weights_ref, held_weights, 27 * C1 * C2, arrived)
+                weight_rows(held_weights, wide_weights, 4)
+                turned = jnp.transpose(wide_weights[...])
+                mixed[...] = jnp.zeros((144, LANES), F32)
+                for group in range(9):
+                    for part in range(8):
+                        mixed[16 * group : 16 * group + 16, 12 * part : 12 * part + 12] = turned[
+                            16 * part : 16 * part + 16, 12 * group : 12 * group + 12
+                        ]
+                ordered = spread(
+                    LANES,
+                    LANES,
+                    lambda e: 32 * ((e % 12) // 4) + 8 * (e % 4) + e // 12,
+                    lambda e: e < 96,
+                )
+                taps = dot(mixed[...].astype(BF16), ordered).astype(BF16)
+                for group in range(9):
+                    own01_ref[:, cols(32 + group)] = taps[16 * group : 16 * group + 16, :]
             send(place, 3, up_ref)
             send(place, 0, down_ref)
 
 
-def weights_layout_kernel(weights_ref, out_ref, wide):
+def weights_layout_kernel(weights_ref, out3_ref, out2_ref, held, wide, arrived):
     @pl.when(on_segment(3))
     def _():
-        for tap in range(27):
-            first = 8192 * tap
-            wide[64 * tap : 64 * tap + 64, :] = (
-                weights_ref[:, first : first + 8192].astype(F32).reshape(64, LANES)
-            )
+        fetched(weights_ref, held, 27 * C3 * C4, arrived)
+        weight_rows(held, wide, 64)
         for group in range(9):
             turned = jnp.transpose(wide[192 * group : 192 * group + 192, :]).astype(BF16)
             rows = slice(C3 * group, C3 * group + C3)
-            out_ref[rows, :192] = turned[:64]
-            out_ref[rows, 192:] = turned[64:]
+            for part in range(2):
+                out3_ref[rows, 192 * part : 192 * part + 192] = turned[64 * part : 64 * part + 64]
+
+    @pl.when(on_segment(2))
+    def _():
+        fetched(weights_ref, held, 27 * C2 * C3, arrived)
+        weight_rows(held, wide, 16)
+        for group in range(9):
+            turned = jnp.transpose(wide[48 * group : 48 * group + 48, :]).astype(BF16)
+            rows = slice(C2 * group, C2 * group + C2)
+            for part in range(4):
+                out2_ref[rows, 48 * part : 48 * part + 48] = turned[32 * part : 32 * part + 32]
 
 
 def halves_of(channels, parts):
     size = channels // parts
     return spread(channels, channels, lambda e: (e % parts) * size + e // parts, lambda e: e >= 0)
+
+
+def quarters(grad):
+    turned = (((0,), (0,)), ((), ()))
+    mixed = lax.dot_general(halves_of(C3, 4), grad, turned, preferred_element_type=F32)
+    return mixed.astype(BF16)
 
 
 def section3_kernel(own_ref, up_ref, down_ref, weights_ref, out_ref, wide, stacked, terms):
@@ -227,7 +275,15 @@
 ):
     @pl.when(on_segment(2))
     def _():
-        stack_moved(lambda row: grad_ref[:, cols(row)], stacked, C3, 16, (0, 1, 2))
+        ordered = quarters(grad_ref[...])
+        for part in range(4):
+            stack_moved(
+                lambda row: ordered[16 * part : 16 * part + 16, cols(row)],
+                stacked.at[48 * part : 48 * part + 48],
+                16,
+                16,
+                (0, 1, 2),
+            )
         terms[...] = dot(weights_ref[...], stacked[...])
         last = is_last_block()
         for cell_z in range(-1, 5):
@@ -273,12 +329,7 @@
 def weights2_kernel(scale, grad_ref, up_ref, down_ref, own_ref, out_ref, stacked, acts):
     @pl.when(on_segment(2))
     def _():
-        ordered = lax.dot_general(
-            halves_of(C3, 4),
-            grad_ref[:, cols(4, 8)],
-            (((0,), (0,)), ((), ())),
-            preferred_element_type=F32,
-        ).astype(BF16)
+        ordered = quarters(grad_ref[:, cols(4, 8)])
         stack_moved(lambda row: ordered[:, cols(row)], stacked, C3, 8, (0, 1, 2))
         for tap_z in range(3):
             for tap_y in range(3):
@@ -435,31 +486,6 @@
     )(*args)
 
 
-def padded(block, rows, columns):
-    return jnp.pad(block, ((0, rows - block.shape[0]), (0, columns - block.shape[1])))
-
-
-def by_tap(weights, chan_out, chan_in):
-    groups = []
-    size = 9 * chan_out * chan_in
-    for tap_z in range(3):
-        taps = weights[0, tap_z * size : (tap_z + 1) * size].reshape(3, 3, chan_out, chan_in)
-        groups.append(jnp.transpose(taps, (0, 3, 1, 2)).reshape(3 * chan_in, 3 * chan_out))
-    return jnp.concatenate(groups, 0)
-
-
-def middle_layout(section, weights):
-    if section == 2:
-        return by_tap(weights, C3, C2)
-    return jnp.zeros((288, 192), BF16)
-
-
-def fine_layout(section, weights):
-    if section == 1:
-        return padded(by_tap(weights, C2, C1), 144, 128)
-    return jnp.zeros((144, 128), BF16)
-
-
 def pairs_of(segments, route):
     total = lax.axis_size("segment")
     count = lax.axis_size("space")
@@ -495,11 +521,10 @@
     def behind(values, *leaders):
         return lax.optimization_barrier((*values, *leaders))[: len(values)]
 
-    def for_section(layout):
-        branches = [functools.partial(layout, section) for section in range(4)]
-        return lax.switch(segment, branches, conv_weights)
-
+    saved_inputs = pltpu.with_memory_space_constraint(saved_inputs, pltpu.HBM)
+    conv_weights = pltpu.with_memory_space_constraint(conv_weights, pltpu.HBM)
     top = jnp.transpose(top_gradient[:, 0], (1, 2, 0)).reshape(64, C4)
+    top = pltpu.with_memory_space_constraint(top, pltpu.HBM)
     deep, up, down, own2, own01 = call(
         layout_kernel,
         [
@@ -509,26 +534,33 @@
             ((32, 4096), BF16),
             ((16, 5248), BF16),
         ],
-        [((1, 131072), BF16), ((64, 4096), F32), pltpu.SemaphoreType.DMA],
+        [
+            ((1, 131072), BF16),
+            ((1, 13824), BF16),
+            ((64, 4096), F32),
+            ((128, 128), F32),
+            ((144, 128), F32),
+            ((64, 128), BF16),
+            pltpu.SemaphoreType.DMA,
+            pltpu.SemaphoreType.DMA,
+        ],
         saved_inputs,
+        conv_weights,
         top,
-        for_section(fine_layout),
         flops=0,
-        far=(0,),
+        far=(0, 1, 2),
     )
     up = over_space(up, range(4), later)
     down = over_space(down, range(4), sooner)
     next_own = lax.ppermute(own01, "segment", [(1, 2)])
-    (taps3,) = call(
+    (weights,) = behind((conv_weights,), deep)
+    taps3, taps2 = call(
         weights_layout_kernel,
-        [((576, 384), BF16)],
-        [((1728, 128), F32)],
-        conv_weights,
-        flops=LONG,
-    )
-    (weights,) = behind((conv_weights,), deep)
-    taps2 = lax.switch(
-        segment, [functools.partial(middle_layout, section) for section in range(4)], weights
+        [((576, 384), BF16), ((288, 192), BF16)],
+        [((1, 221184), BF16), ((1728, 128), F32), pltpu.SemaphoreType.DMA],
+        weights,
+        flops=0,
+        far=(0,),
     )
     taps3, taps2 = behind((taps3, taps2), next_own)
 

time: 53.1 us -> 51.7 us (0.974)
  local copies, waits for them, and re-layouts: 4.78 us -> 1.01 us
  waiting for transfers between devices: 15.3 us -> 18.3 us
  starting transfers between devices: 28.3 us -> 26.2 us
  Pallas kernels: 3.47 us -> 4.75 us
    ppermute x11, waiting for transfers between devices: 11.8 us -> 16.1 us  [over_space(): return lax.ppermute(block, ('space', 'segment'), pairs_of(segments, route))]
    ppermute x11, starting transfers between devices: 23.1 us -> 21 us  [over_space(): return lax.ppermute(block, ('space', 'segment'), pairs_of(segments, route))]
    slice x1 -> x0, local copies, waits for them, and re-layouts: 1.59 us -> none  [by_tap(): weights[0, tap_z * size:(tap_z + 1) * size].reshape(3, 3, chan_out, chan_in)]
    ppermute x1, waiting for transfers between devices: 1.4 us -> 0.01 us  [shards(): next_own = lax.ppermute(own01, 'segment', [(1, 2)])]
    pallas_call x7, Pallas kernels: 3.47 us -> 4.75 us  [call(): pl.pallas_call(kernel, out_shape=shapes, in_specs=[far_spec if place in f...]
    unnamed x8 -> x4, local copies, waits for them, and re-layouts: 1.95 us -> 0.93 us
  transfers between devices with their start and end apart: 15 -> 15, of which waited for: 5 -> 5; matrix products, arithmetic and copies ran while one was open for 6% -> 0% of each run, Pallas kernels for 4% -> 4%
where the time goes in v7:
time: 51.7 us; the launch traced here: 50.8 us
  starting transfers between devices  26.2 us (51%)
  waiting for transfers between devices  18.3 us (35%)
  Pallas kernels  4.75 us (9%)
  local copies, waits for them, and re-layouts  1.01 us (2%)
    ppermute x11, starting transfers between devices, over_space(): return lax.ppermute(block, ('space', 'segment'), pairs_of(segments, route))  21 us
    ppermute x11, waiting for transfers between devices, over_space(): return lax.ppermute(block, ('space', 'segment'), pairs_of(segments, route))  16.1 us
    pallas_call x7, Pallas kernels, call(): pl.pallas_call(kernel, out_shape=shapes, in_specs=[far_spec if place in f...  4.75 us
    ppermute x1, waiting for transfers between devices, shards(): grad2 = lax.ppermute(grad2, 'segment', [(3, 2)])  2.13 us
    ppermute x1, starting transfers between devices, shards(): grad1 = lax.ppermute(grad1, 'segment', [(2, 1)])  1.31 us
    ppermute x1, starting transfers between devices, shards(): grad0 = lax.ppermute(grad0, 'segment', [(2, 0)])  1.3 us
    ppermute x1, starting transfers between devices, shards(): next_own = lax.ppermute(own01, 'segment', [(1, 2)])  1.29 us
    ppermute x1, starting transfers between devices, shards(): grad2 = lax.ppermute(grad2, 'segment', [(3, 2)])  1.28 us
  transfers between devices with their start and end apart: 15, of which 5 were waited for; matrix products, arithmetic and copies ran while one was open for 0% of the time, Pallas kernels for 4%

profile of v7, /device:TPU:2, one launch (start us, length us, event | category | flops | bytes accessed | tf_op | source)
XLA Modules:
  0.0 50.8 jit_solution(9357886692231135567)
XLA Ops:
  0.0 1.2 %shard_map.41 = (bf16[64,640]{1,0:T(8,128)(2,1)S(1)}, bf16[64,512]{1,0:T(8,128)(2,1)S(1)}, bf16[64,512]{1,0:T(8,128)(2,1)S(1)}, bf16[32,4096]{1,0:T(8,128)(2,1)S(1)}, bf16[16,5248]{1,0:T(8,128)(2,1)S(1)}) custom-call(bf16[1,131072]{1,0:T(2,128)(2,1)} %saved_ref.1, bf16[1,221184]{1,0:T(2,128)(2,1)} %weights_ref.2, bf16[64,128]{1,0:T(8,128)(2,1)} %bitcast.26), custom_call_target="tpu_custom_call" | custom-call | bytes 1363968 | tf_op jit(solution)/shard_map/pallas_call | solution.py:477
  1.2 1.3 %collective-permute-start.2 = (bf16[16,5248]{1,0:T(8,128)(2,1)S(1)}, bf16[16,5248]{1,0:T(8,128)(2,1)S(1)}, u32[]{:S(2)}, u32[]{:S(2)}) collective-permute-start(bf16[16,5248]{1,0:T(8,128)(2,1)S(1)} %get-tuple-element.56.own_ref), channel_id=1, source_target_pairs={{1,2},{5,6},{9,10},{13,14},{17,18},{21,22},{25,26},{29,30}} | collective-permute-start | bytes 503816 | tf_op jit(solution)/shard_map/ppermute | solution.py:555
  2.5 3.4 %collective-permute-start = (bf16[64,512]{1,0:T(8,128)(2,1)S(1)}, bf16[64,512]{1,0:T(8,128)(2,1)S(1)}, u32[]{:S(2)}, u32[]{:S(2)}) collective-permute-start(bf16[64,512]{1,0:T(8,128)(2,1)S(1)} %get-tuple-element.51), channel_id=1, source_target_pairs={{0,4},{1,5},{2,6},{3,7},{4,8},{5,9},{6,10},{7,11},{8,12},{9,13},{1... | collective-permute-start | bytes 196616 | tf_op jit(solution)/shard_map/ppermute | solution.py:498
  5.9 1.3 %collective-permute-start.1 = (bf16[64,512]{1,0:T(8,128)(2,1)S(1)}, bf16[64,512]{1,0:T(8,128)(2,1)S(1)}, u32[]{:S(2)}, u32[]{:S(2)}) collective-permute-start(bf16[64,512]{1,0:T(8,128)(2,1)S(1)} %get-tuple-element.52), channel_id=1, source_target_pairs={{4,0},{5,1},{6,2},{7,3},{8,4},{9,5},{10,6},{11,7},{12,8},{13,9},{1... | collective-permute-start | bytes 196616 | tf_op jit(solution)/shard_map/ppermute | solution.py:498
  7.2 1.3 %shard_map.42 = (bf16[576,384]{1,0:T(8,128)(2,1)S(1)}, bf16[288,192]{1,0:T(8,128)(2,1)S(1)}) custom-call(bf16[1,221184]{1,0:T(2,128)(2,1)} %weights_ref.2), custom_call_target="tpu_custom_call" | custom-call | bytes 995328 | tf_op jit(solution)/shard_map/pallas_call | solution.py:477
  8.5 0.0 collective-permute-done.2.next_ref
  8.5 0.0 collective-permute-done.up_ref
  8.5 3.6 %collective-permute-done.1.down_ref = bf16[64,512]{1,0:T(8,128)(2,1)S(1)} collective-permute-done((bf16[64,512]{1,0:T(8,128)(2,1)S(1)}, bf16[64,512]{1,0:T(8,128)(2,1)S(1)}, u32[]{:S(2)}, u32[]{:S(2)}) %collective-permute-start.1) | collective-permute-done | bytes 65568 | tf_op jit(solution)/shard_map/ppermute | solution.py:498
  12.1 1.3 %collective-permute-start.3 = (bf16[64,2048]{1,0:T(8,128)(2,1)S(1)}, bf16[64,2048]{1,0:T(8,128)(2,1)S(1)}, u32[]{:S(2)}, u32[]{:S(2)}) collective-permute-start(bf16[64,2048]{1,0:T(8,128)(2,1)S(1)} %shard_map.43), channel_id=1, source_target_pairs={{3,2},{7,6},{11,10},{15,14},{19,18},{23,22},{27,26},{31,30}} | collective-permute-start | bytes 786440 | tf_op jit(solution)/shard_map/ppermute | solution.py:577
  13.4 2.1 %collective-permute-done.3.grad_ref = bf16[64,2048]{1,0:T(8,128)(2,1)S(1)} collective-permute-done((bf16[64,2048]{1,0:T(8,128)(2,1)S(1)}, bf16[64,2048]{1,0:T(8,128)(2,1)S(1)}, u32[]{:S(2)}, u32[]{:S(2)}) %collective-permute-start.3) | collective-permute-done | bytes 262176 | tf_op jit(solution)/shard_map/ppermute | solution.py:577
  15.5 1.4 %shard_map.44 = (bf16[32,4096]{1,0:T(8,128)(2,1)S(1)}, bf16[16,4096]{1,0:T(8,128)(2,1)S(1)}) custom-call(bf16[64,2048]{1,0:T(8,128)(2,1)S(1)} %collective-permute-done.3.grad_ref, bf16[64,512]{1,0:T(8,128)(2,1)S(1)} %collective-permute-done.up_ref, bf16[64,512]{1,0:T(8,128)(2,1)S(1)} %collective-permute-done.1.down_ref, ...), custom_call_target="tpu_custom_call" | custom-call | flops 226492416 | bytes 1327104 | tf_op jit(solution)/shard_map/pallas_call | solution.py:477
  16.9 1.3 %collective-permute-start.5 = (bf16[32,4096]{1,0:T(8,128)(2,1)S(1)}, bf16[32,4096]{1,0:T(8,128)(2,1)S(1)}, u32[]{:S(2)}, u32[]{:S(2)}) collective-permute-start(bf16[32,4096]{1,0:T(8,128)(2,1)S(1)} %get-tuple-element.61), channel_id=1, source_target_pairs={{2,1},{6,5},{10,9},{14,13},{18,17},{22,21},{26,25},{30,29}} | collective-permute-start | bytes 786440 | tf_op jit(solution)/shard_map/ppermute | solution.py:602
  18.3 0.7 %collective-permute-start.6 = (bf16[1,64,640]{2,1,0:T(8,128)(2,1)S(1)}, bf16[1,64,640]{2,1,0:T(8,128)(2,1)S(1)}, u32[]{:S(2)}, u32[]{:S(2)}) collective-permute-start(bf16[1,64,640]{2,1,0:T(8,128)(2,1)S(1)} %bitcast.21), channel_id=1, source_target_pairs={{3,19},{7,23},{11,27},{15,31},{19,3},{23,7},{27,11},{31,15}} | collective-permute-start | bytes 245768 | tf_op jit(solution)/shard_map/ppermute | solution.py:498
  18.9 1.3 %collective-permute-start.4 = (bf16[16,4096]{1,0:T(8,128)(2,1)S(1)}, bf16[16,4096]{1,0:T(8,128)(2,1)S(1)}, u32[]{:S(2)}, u32[]{:S(2)}) collective-permute-start(bf16[16,4096]{1,0:T(8,128)(2,1)S(1)} %get-tuple-element.60), channel_id=1, source_target_pairs={{2,0},{6,4},{10,8},{14,12},{18,16},{22,20},{26,24},{30,28}} | collective-permute-start | bytes 393224 | tf_op jit(solution)/shard_map/ppermute | solution.py:601
  20.2 0.0 collective-permute-done.6
  20.3 0.7 %collective-permute-start.7 = (bf16[2,64,640]{2,1,0:T(8,128)(2,1)S(1)}, bf16[2,64,640]{2,1,0:T(8,128)(2,1)S(1)}, u32[]{:S(2)}, u32[]{:S(2)}) collective-permute-start(bf16[2,64,640]{2,1,0:T(8,128)(2,1)S(1)} %pad_maximum_fusion.1), channel_id=1, source_target_pairs={{3,11},{7,15},{11,3},{15,7},{19,27},{23,31},{27,19},{31,23}} | collective-permute-start | bytes 491528 | tf_op jit(solution)/shard_map/ppermute | solution.py:498
  21.0 0.9 %shard_map.45 = f32[432,128]{1,0:T(8,128)S(1)} custom-call(bf16[64,2048]{1,0:T(8,128)(2,1)S(1)} %collective-permute-done.3.grad_ref, bf16[64,512]{1,0:T(8,128)(2,1)S(1)} %collective-permute-done.up_ref, bf16[64,512]{1,0:T(8,128)(2,1)S(1)} %collective-permute-done.1.down_ref, bf16[32,4096]{1,0:T(8,128)(2,1)S(1)} %get-tuple-element.58.own_ref), custom_call_target="tpu_custom_call" | custom-call | flops 20000000000 | bytes 876544 | tf_op jit(solution)/shard_map/pallas_call | solution.py:477
  21.8 4.3 %collective-permute-start.11 = (f32[432,128]{1,0:T(8,128)S(1)}, f32[432,128]{1,0:T(8,128)S(1)}, u32[]{:S(2)}, u32[]{:S(2)}) collective-permute-start(f32[432,128]{1,0:T(8,128)S(1)} %shard_map.45), channel_id=1, source_target_pairs={{2,6},{6,2},{10,14},{14,10},{18,22},{22,18},{26,30},{30,26}} | collective-permute-start | bytes 663560 | tf_op jit(solution)/shard_map/ppermute | solution.py:498
  26.2 0.0 collective-permute-done.7
  26.2 0.7 %collective-permute-start.14 = (bf16[4,64,640]{2,1,0:T(8,128)(2,1)S(1)}, bf16[4,64,640]{2,1,0:T(8,128)(2,1)S(1)}, u32[]{:S(2)}, u32[]{:S(2)}) collective-permute-start(bf16[4,64,640]{2,1,0:T(8,128)(2,1)S(1)} %constant_dynamic-update-slice_fusion), channel_id=1, source_target_pairs={{3,7},{7,3},{11,15},{15,11},{19,23},{23,19},{27,31},{31,27}} | collective-permute-start | bytes 983048 | tf_op jit(solution)/shard_map/ppermute | solution.py:498
  26.9 3.1 %collective-permute-done.11 = f32[432,128]{1,0:T(8,128)S(1)} collective-permute-done((f32[432,128]{1,0:T(8,128)S(1)}, f32[432,128]{1,0:T(8,128)S(1)}, u32[]{:S(2)}, u32[]{:S(2)}) %collective-permute-start.11) | collective-permute-done | bytes 221216 | tf_op jit(solution)/shard_map/ppermute | solution.py:498
  30.1 0.0 collective-permute-done.4.grad0_ref
  30.1 0.0 collective-permute-done.5.grad1_ref
  30.1 0.7 %collective-permute-start.8 = (f32[144,128]{1,0:T(8,128)S(1)}, f32[144,128]{1,0:T(8,128)S(1)}, u32[]{:S(2)}, u32[]{:S(2)}) collective-permute-start(f32[144,128]{1,0:T(8,128)S(1)} %shard_map.46), channel_id=1, source_target_pairs={{0,4},{1,5},{4,0},{5,1},{8,12},{9,13},{12,8},{13,9},{16,20},{17,21... | collective-permute-start | bytes 221192 | tf_op jit(solution)/shard_map/ppermute | solution.py:498
  30.8 3.5 %collective-permute-start.12 = (f32[432,128]{1,0:T(8,128)S(1)}, f32[432,128]{1,0:T(8,128)S(1)}, u32[]{:S(2)}, u32[]{:S(2)}) collective-permute-start(f32[432,128]{1,0:T(8,128)S(1)} %add.39), channel_id=1, source_target_pairs={{2,10},{6,14},{10,2},{14,6},{18,26},{22,30},{26,18},{30,22}} | collective-permute-start | bytes 663560 | tf_op jit(solution)/shard_map/ppermute | solution.py:498
  34.3 0.0 collective-permute-done.8
  34.3 0.7 %collective-permute-start.9 = (f32[144,128]{1,0:T(8,128)S(1)}, f32[144,128]{1,0:T(8,128)S(1)}, u32[]{:S(2)}, u32[]{:S(2)}) collective-permute-start(f32[144,128]{1,0:T(8,128)S(1)} %add.37), channel_id=1, source_target_pairs={{0,8},{1,9},{4,12},{5,13},{8,0},{9,1},{12,4},{13,5},{16,24},{17,25... | collective-permute-start | bytes 221192 | tf_op jit(solution)/shard_map/ppermute | solution.py:498
  35.0 0.0 collective-permute-done.9
  35.0 0.7 %collective-permute-start.10 = (f32[144,128]{1,0:T(8,128)S(1)}, f32[144,128]{1,0:T(8,128)S(1)}, u32[]{:S(2)}, u32[]{:S(2)}) collective-permute-start(f32[144,128]{1,0:T(8,128)S(1)} %add.38), channel_id=1, source_target_pairs={{0,16},{1,17},{4,20},{5,21},{8,24},{9,25},{12,28},{13,29},{16,0},{... | collective-permute-start | bytes 221192 | tf_op jit(solution)/shard_map/ppermute | solution.py:498
  35.7 2.9 %collective-permute-done.12 = f32[432,128]{1,0:T(8,128)S(1)} collective-permute-done((f32[432,128]{1,0:T(8,128)S(1)}, f32[432,128]{1,0:T(8,128)S(1)}, u32[]{:S(2)}, u32[]{:S(2)}) %collective-permute-start.12) | collective-permute-done | bytes 221216 | tf_op jit(solution)/shard_map/ppermute | solution.py:498
  38.7 4.5 %collective-permute-start.13 = (f32[432,128]{1,0:T(8,128)S(1)}, f32[432,128]{1,0:T(8,128)S(1)}, u32[]{:S(2)}, u32[]{:S(2)}) collective-permute-start(f32[432,128]{1,0:T(8,128)S(1)} %add.40), channel_id=1, source_target_pairs={{2,18},{6,22},{10,26},{14,30},{18,2},{22,6},{26,10},{30,14}} | collective-permute-start | bytes 663560 | tf_op jit(solution)/shard_map/ppermute | solution.py:498
  43.2 0.0 collective-permute-done.10
  43.2 0.0 collective-permute-done.14
  43.2 0.1 pad_maximum_fusion.blocks_ref
  43.3 6.5 %collective-permute-done.13 = f32[432,128]{1,0:T(8,128)S(1)} collective-permute-done((f32[432,128]{1,0:T(8,128)S(1)}, f32[432,128]{1,0:T(8,128)S(1)}, u32[]{:S(2)}, u32[]{:S(2)}) %collective-permute-start.13) | collective-permute-done | bytes 221216 | tf_op jit(solution)/shard_map/ppermute | solution.py:498
  49.8 0.1 conditional.1
  49.8 0.1 pad.15
  49.9 0.0 copy-start
  49.9 0.9 %copy-done = f32[1,221184]{1,0:T(1,128)} copy-done((f32[1,221184]{1,0:T(1,128)}, f32[1,221184]{1,0:T(1,128)S(1)}, u32[]{:S(2)}) %copy-start) | copy-done | bytes 884760
  (12 shorter events, 0.2 us)
Async XLA Ops:
  1.2 7.3 %collective-permute-start.2 = (bf16[16,5248]{1,0:T(8,128)(2,1)S(1)}, bf16[16,5248]{1,0:T(8,128)(2,1)S(1)}, u32[]{:S(2)}, u32[]{:S(2)}) collective-permute-start(bf16[16,5248]{1,0:T(8,128)(2,1)S(1)} %get-tuple-element.56.own_ref), channel_id=1, source_target_pairs={{1,2},{5,6},{9,10},{13,14},{17,18},{21,22},{25,26},{29,30}} | collective-permute-start | bytes 503816 | tf_op jit(solution)/shard_map/ppermute | solution.py:555
  2.5 6.0 %collective-permute-start = (bf16[64,512]{1,0:T(8,128)(2,1)S(1)}, bf16[64,512]{1,0:T(8,128)(2,1)S(1)}, u32[]{:S(2)}, u32[]{:S(2)}) collective-permute-start(bf16[64,512]{1,0:T(8,128)(2,1)S(1)} %get-tuple-element.51), channel_id=1, source_target_pairs={{0,4},{1,5},{2,6},{3,7},{4,8},{5,9},{6,10},{7,11},{8,12},{9,13},{1... | collective-permute-start | bytes 196616 | tf_op jit(solution)/shard_map/ppermute | solution.py:498
  5.9 6.2 %collective-permute-start.1 = (bf16[64,512]{1,0:T(8,128)(2,1)S(1)}, bf16[64,512]{1,0:T(8,128)(2,1)S(1)}, u32[]{:S(2)}, u32[]{:S(2)}) collective-permute-start(bf16[64,512]{1,0:T(8,128)(2,1)S(1)} %get-tuple-element.52), channel_id=1, source_target_pairs={{4,0},{5,1},{6,2},{7,3},{8,4},{9,5},{10,6},{11,7},{12,8},{13,9},{1... | collective-permute-start | bytes 196616 | tf_op jit(solution)/shard_map/ppermute | solution.py:498
  12.1 3.4 %collective-permute-start.3 = (bf16[64,2048]{1,0:T(8,128)(2,1)S(1)}, bf16[64,2048]{1,0:T(8,128)(2,1)S(1)}, u32[]{:S(2)}, u32[]{:S(2)}) collective-permute-start(bf16[64,2048]{1,0:T(8,128)(2,1)S(1)} %shard_map.43), channel_id=1, source_target_pairs={{3,2},{7,6},{11,10},{15,14},{19,18},{23,22},{27,26},{31,30}} | collective-permute-start | bytes 786440 | tf_op jit(solution)/shard_map/ppermute | solution.py:577
  16.9 13.2 %collective-permute-start.5 = (bf16[32,4096]{1,0:T(8,128)(2,1)S(1)}, bf16[32,4096]{1,0:T(8,128)(2,1)S(1)}, u32[]{:S(2)}, u32[]{:S(2)}) collective-permute-start(bf16[32,4096]{1,0:T(8,128)(2,1)S(1)} %get-tuple-element.61), channel_id=1, source_target_pairs={{2,1},{6,5},{10,9},{14,13},{18,17},{22,21},{26,25},{30,29}} | collective-permute-start | bytes 786440 | tf_op jit(solution)/shard_map/ppermute | solution.py:602
  18.3 2.0 %collective-permute-start.6 = (bf16[1,64,640]{2,1,0:T(8,128)(2,1)S(1)}, bf16[1,64,640]{2,1,0:T(8,128)(2,1)S(1)}, u32[]{:S(2)}, u32[]{:S(2)}) collective-permute-start(bf16[1,64,640]{2,1,0:T(8,128)(2,1)S(1)} %bitcast.21), channel_id=1, source_target_pairs={{3,19},{7,23},{11,27},{15,31},{19,3},{23,7},{27,11},{31,15}} | collective-permute-start | bytes 245768 | tf_op jit(solution)/shard_map/ppermute | solution.py:498
  18.9 11.2 %collective-permute-start.4 = (bf16[16,4096]{1,0:T(8,128)(2,1)S(1)}, bf16[16,4096]{1,0:T(8,128)(2,1)S(1)}, u32[]{:S(2)}, u32[]{:S(2)}) collective-permute-start(bf16[16,4096]{1,0:T(8,128)(2,1)S(1)} %get-tuple-element.60), channel_id=1, source_target_pairs={{2,0},{6,4},{10,8},{14,12},{18,16},{22,20},{26,24},{30,28}} | collective-permute-start | bytes 393224 | tf_op jit(solution)/shard_map/ppermute | solution.py:601
  20.3 5.9 %collective-permute-start.7 = (bf16[2,64,640]{2,1,0:T(8,128)(2,1)S(1)}, bf16[2,64,640]{2,1,0:T(8,128)(2,1)S(1)}, u32[]{:S(2)}, u32[]{:S(2)}) collective-permute-start(bf16[2,64,640]{2,1,0:T(8,128)(2,1)S(1)} %pad_maximum_fusion.1), channel_id=1, source_target_pairs={{3,11},{7,15},{11,3},{15,7},{19,27},{23,31},{27,19},{31,23}} | collective-permute-start | bytes 491528 | tf_op jit(solution)/shard_map/ppermute | solution.py:498
  21.8 8.2 %collective-permute-start.11 = (f32[432,128]{1,0:T(8,128)S(1)}, f32[432,128]{1,0:T(8,128)S(1)}, u32[]{:S(2)}, u32[]{:S(2)}) collective-permute-start(f32[432,128]{1,0:T(8,128)S(1)} %shard_map.45), channel_id=1, source_target_pairs={{2,6},{6,2},{10,14},{14,10},{18,22},{22,18},{26,30},{30,26}} | collective-permute-start | bytes 663560 | tf_op jit(solution)/shard_map/ppermute | solution.py:498
  26.2 17.0 %collective-permute-start.14 = (bf16[4,64,640]{2,1,0:T(8,128)(2,1)S(1)}, bf16[4,64,640]{2,1,0:T(8,128)(2,1)S(1)}, u32[]{:S(2)}, u32[]{:S(2)}) collective-permute-start(bf16[4,64,640]{2,1,0:T(8,128)(2,1)S(1)} %constant_dynamic-update-slice_fusion), channel_id=1, source_target_pairs={{3,7},{7,3},{11,15},{15,11},{19,23},{23,19},{27,31},{31,27}} | collective-permute-start | bytes 983048 | tf_op jit(solution)/shard_map/ppermute | solution.py:498
  30.1 4.2 %collective-permute-start.8 = (f32[144,128]{1,0:T(8,128)S(1)}, f32[144,128]{1,0:T(8,128)S(1)}, u32[]{:S(2)}, u32[]{:S(2)}) collective-permute-start(f32[144,128]{1,0:T(8,128)S(1)} %shard_map.46), channel_id=1, source_target_pairs={{0,4},{1,5},{4,0},{5,1},{8,12},{9,13},{12,8},{13,9},{16,20},{17,21... | collective-permute-start | bytes 221192 | tf_op jit(solution)/shard_map/ppermute | solution.py:498
  30.8 7.8 %collective-permute-start.12 = (f32[432,128]{1,0:T(8,128)S(1)}, f32[432,128]{1,0:T(8,128)S(1)}, u32[]{:S(2)}, u32[]{:S(2)}) collective-permute-start(f32[432,128]{1,0:T(8,128)S(1)} %add.39), channel_id=1, source_target_pairs={{2,10},{6,14},{10,2},{14,6},{18,26},{22,30},{26,18},{30,22}} | collective-permute-start | bytes 663560 | tf_op jit(solution)/shard_map/ppermute | solution.py:498
  34.3 0.7 %collective-permute-start.9 = (f32[144,128]{1,0:T(8,128)S(1)}, f32[144,128]{1,0:T(8,128)S(1)}, u32[]{:S(2)}, u32[]{:S(2)}) collective-permute-start(f32[144,128]{1,0:T(8,128)S(1)} %add.37), channel_id=1, source_target_pairs={{0,8},{1,9},{4,12},{5,13},{8,0},{9,1},{12,4},{13,5},{16,24},{17,25... | collective-permute-start | bytes 221192 | tf_op jit(solution)/shard_map/ppermute | solution.py:498
  35.0 8.1 %collective-permute-start.10 = (f32[144,128]{1,0:T(8,128)S(1)}, f32[144,128]{1,0:T(8,128)S(1)}, u32[]{:S(2)}, u32[]{:S(2)}) collective-permute-start(f32[144,128]{1,0:T(8,128)S(1)} %add.38), channel_id=1, source_target_pairs={{0,16},{1,17},{4,20},{5,21},{8,24},{9,25},{12,28},{13,29},{16,0},{... | collective-permute-start | bytes 221192 | tf_op jit(solution)/shard_map/ppermute | solution.py:498
  38.7 11.1 %collective-permute-start.13 = (f32[432,128]{1,0:T(8,128)S(1)}, f32[432,128]{1,0:T(8,128)S(1)}, u32[]{:S(2)}, u32[]{:S(2)}) collective-permute-start(f32[432,128]{1,0:T(8,128)S(1)} %add.40), channel_id=1, source_target_pairs={{2,18},{6,22},{10,26},{14,30},{18,2},{22,6},{26,10},{30,14}} | collective-permute-start | bytes 663560 | tf_op jit(solution)/shard_map/ppermute | solution.py:498
  49.9 0.9 %copy-start = (f32[1,221184]{1,0:T(1,128)}, f32[1,221184]{1,0:T(1,128)S(1)}, u32[]{:S(2)}) copy-start(f32[1,221184]{1,0:T(1,128)S(1)} %get-tuple-element.103) | copy-start | bytes 2654212

commit v8 on v7

--- a/solution.py
+++ b/solution.py
@@ -258,20 +258,25 @@
 
 
 def section21_kernel(
+    scale2,
+    scale1,
     grad_ref,
     up_ref,
     down_ref,
     own_ref,
     weights_ref,
     next_ref,
-    out1_ref,
     out0_ref,
+    sum2_ref,
+    sum1_ref,
     stacked,
     terms,
     middle,
     next_weights,
     next_stacked,
     next_terms,
+    acts2,
+    acts1,
 ):
     @pl.when(on_segment(2))
     def _():
@@ -304,8 +309,6 @@
                 if cell_z == 4:
                     result = jnp.where(last, jnp.zeros_like(result), result)
                 middle[:, cols(8 * (cell_z + 1) + cell_y)] = result
-                if 0 <= cell_z < 4:
-                    out1_ref[:, cols(8 * cell_z + cell_y)] = result
         stack_moved(lambda row: middle[:, cols(row)], next_stacked, C2, 48, (-1, 0, 1))
         for tap in range(9):
             next_weights[C1 * tap : C1 * (tap + 1), :] = next_ref[:, cols(32 + tap)]
@@ -324,13 +327,6 @@
             earlier = jnp.concatenate([edge, sums[2][:, : 7 * LANES]], 1)
             mask = next_ref[:, cols(8 * plane, 8)].astype(F32)
             out0_ref[:, cols(8 * plane, 8)] = sloped(sums[1] + later + earlier, mask)
-
-
-def weights2_kernel(scale, grad_ref, up_ref, down_ref, own_ref, out_ref, stacked, acts):
-    @pl.when(on_segment(2))
-    def _():
-        ordered = quarters(grad_ref[:, cols(4, 8)])
-        stack_moved(lambda row: ordered[:, cols(row)], stacked, C3, 8, (0, 1, 2))
         for tap_z in range(3):
             for tap_y in range(3):
                 first = C2 * (3 * tap_z + tap_y)
@@ -343,16 +339,29 @@
                             block = plane_of_message(down_ref, C2, row)
                         else:
                             block = own_ref[:, cols(8 * plane + row)]
-                        acts[first : first + C2, cols(4 * place_z + place_y)] = block
-        total = dot_rows(stacked[...], acts[...]) * scale
+                        acts2[first : first + C2, cols(4 * place_z + place_y)] = block
+        total = dot_rows(stacked[:, 512:1536], acts2[...]) * scale2
         for group in range(9):
             for tap_x in range(3):
                 first = 16 * (3 * group + tap_x)
                 for part in range(4):
-                    row = C3 * tap_x + 16 * part
-                    out_ref[first : first + 16, 32 * part : 32 * part + 32] = total[
+                    row = 48 * part + 16 * tap_x
+                    sum2_ref[first : first + 16, 32 * part : 32 * part + 32] = total[
                         row : row + 16, 32 * group : 32 * group + 32
                     ]
+        none = jnp.zeros((C1, LANES), BF16)
+        for tap_y in range(3):
+            for plane in range(4):
+                for row in range(8):
+                    source = row + tap_y - 1
+                    inside = 0 <= source < 8
+                    acts1[C1 * tap_y : C1 * (tap_y + 1), cols(8 * plane + row)] = (
+                        next_ref[:, cols(8 * plane + source)] if inside else none
+                    )
+        for tap_z in range(3):
+            grads = next_stacked[:, cols(8 * (2 - tap_z), 32)]
+            sum1_ref[48 * tap_z : 48 * tap_z + 48, :96] = dot_rows(acts1[...], grads) * scale1
+        sum1_ref[:, 96:] = jnp.zeros((144, 32), F32)
 
 
 def fine_acts(chans, up_ref, down_ref, own_ref, plane, row):
@@ -364,7 +373,7 @@
 
 
 def weights01_kernel(
-    scale1, scale0, grad0_ref, grad1_ref, up_ref, down_ref, own_ref, out_ref, stacked, acts
+    scale, grad0_ref, sum1_ref, up_ref, down_ref, own_ref, out_ref, stacked, acts
 ):
     none = jnp.zeros((C1, LANES), BF16)
 
@@ -390,26 +399,12 @@
                     stacked[C1 * tap_z : C1 * (tap_z + 1), cols(8 * plane + row)] = fine_acts(
                         C1, up_ref, down_ref, own_ref, plane + tap_z - 1, row
                     )
-        out_ref[:, :48] = dot_rows(acts[...], stacked[:48, :]) * scale0
+        out_ref[:, :48] = dot_rows(acts[...], stacked[...]) * scale
         out_ref[:, 48:] = jnp.zeros((144, 80), F32)
 
     @pl.when(on_segment(1))
     def _():
-        stack_moved(lambda row: grad1_ref[:, cols(row)], stacked, C2, 32, (-1, 0, 1))
-        for tap_z in range(3):
-            for tap_y in range(3):
-                first = C1 * (3 * tap_z + tap_y)
-                for plane in range(4):
-                    for row in range(8):
-                        source = row + tap_y - 1
-                        block = none
-                        if 0 <= source < 8:
-                            block = fine_acts(
-                                C1, up_ref, down_ref, own_ref, plane + tap_z - 1, source
-                            )
-                        acts[first : first + C1, cols(8 * plane + row)] = block
-        out_ref[:, :96] = dot_rows(acts[...], stacked[...]) * scale1
-        out_ref[:, 96:] = jnp.zeros((144, 32), F32)
+        out_ref[...] = sum1_ref[...]
 
 
 def weights3_kernel(scale, places, blocks_ref, down_ref, out_ref, wide, stacked, acts):
@@ -575,9 +570,9 @@
         flops=2 * 576 * 384 * 768,
     )
     grad2 = lax.ppermute(grad2, "segment", [(3, 2)])
-    grad1, grad0 = call(
-        section21_kernel,
-        [((32, 4096), BF16), ((16, 4096), BF16)],
+    grad0, sum2, sum1 = call(
+        functools.partial(section21_kernel, scales[2], scales[1]),
+        [((16, 4096), BF16), ((432, 128), F32), ((144, 128), F32)],
         [
             ((192, 2048), BF16),
             ((288, 2048), F32),
@@ -585,6 +580,8 @@
             ((144, 128), BF16),
             ((96, 6144), BF16),
             ((144, 6144), F32),
+            ((288, 1024), BF16),
+            ((48, 4096), BF16),
         ],
         grad2,
         up,
@@ -597,19 +594,9 @@
     def swap(block, segments, bit):
         return over_space(block, segments, lambda n: [(i, i ^ bit) for i in range(n)])
 
-    grad2, blocks = behind((grad2, deep[None]), grad1)
+    (blocks,) = behind((deep[None],), grad0)
     grad0 = lax.ppermute(grad0, "segment", [(2, 0)])
-    grad1 = lax.ppermute(grad1, "segment", [(2, 1)])
-    (sum2,) = call(
-        functools.partial(weights2_kernel, scales[2]),
-        [((432, 128), F32)],
-        [((192, 1024), BF16), ((288, 1024), BF16)],
-        grad2,
-        up,
-        down,
-        own2,
-        flops=LONG,
-    )
+    sum1 = lax.ppermute(sum1, "segment", [(2, 1)])
     places = [0]
     even = not count & (count - 1)
     gathers = even and count <= GATHER_LIMIT
@@ -622,13 +609,13 @@
         for bit in bits[:0:-1]:
             blocks = gathered(blocks, bit)
             places = places + [place ^ bit for place in places]
-    grad0, grad1 = behind((grad0, grad1), sum2, blocks)
+    grad0, sum1 = behind((grad0, sum1), blocks)
     (sum01,) = call(
-        functools.partial(weights01_kernel, scales[1], scales[0]),
+        functools.partial(weights01_kernel, scales[0]),
         [((144, 128), F32)],
-        [((96, 4096), BF16), ((144, 4096), BF16)],
+        [((48, 4096), BF16), ((144, 4096), BF16)],
         grad0,
-        grad1,
+        sum1,
         up,
         down,
         own01,

time: 51.7 us -> 50.6 us (0.979)
  waiting for transfers between devices: 18.3 us -> 17 us
    ppermute x11, waiting for transfers between devices: 16.1 us -> 14.8 us  [over_space(): return lax.ppermute(block, ('space', 'segment'), pairs_of(segments, route))]
    pallas_call x7 -> x6, Pallas kernels: 4.75 us -> 4.97 us  [call(): pl.pallas_call(kernel, out_shape=shapes, in_specs=[far_spec if place in f...]
  transfers between devices with their start and end apart: 15 -> 15, of which waited for: 5 -> 6; matrix products, arithmetic and copies ran while one was open for 0% -> 0% of each run, Pallas kernels for 4% -> 3%
where the time goes in v8:
time: 50.6 us; the launch traced here: 49.7 us
  starting transfers between devices  26.2 us (52%)
  waiting for transfers between devices  17 us (34%)
  Pallas kernels  4.97 us (10%)
  local copies, waits for them, and re-layouts  1.01 us (2%)
    ppermute x11, starting transfers between devices, over_space(): return lax.ppermute(block, ('space', 'segment'), pairs_of(segments, route))  21 us
    ppermute x11, waiting for transfers between devices, over_space(): return lax.ppermute(block, ('space', 'segment'), pairs_of(segments, route))  14.8 us
    pallas_call x6, Pallas kernels, call(): pl.pallas_call(kernel, out_shape=shapes, in_specs=[far_spec if place in f...  4.97 us
    ppermute x1, waiting for transfers between devices, shards(): grad2 = lax.ppermute(grad2, 'segment', [(3, 2)])  2.13 us
    ppermute x1, starting transfers between devices, shards(): grad0 = lax.ppermute(grad0, 'segment', [(2, 0)])  1.3 us
    ppermute x1, starting transfers between devices, shards(): sum1 = lax.ppermute(sum1, 'segment', [(2, 1)])  1.29 us
    ppermute x1, starting transfers between devices, shards(): next_own = lax.ppermute(own01, 'segment', [(1, 2)])  1.29 us
    ppermute x1, starting transfers between devices, shards(): grad2 = lax.ppermute(grad2, 'segment', [(3, 2)])  1.28 us
  transfers between devices with their start and end apart: 15, of which 6 were waited for; matrix products, arithmetic and copies ran while one was open for 0% of the time, Pallas kernels for 3%

profile of v8, /device:TPU:2, one launch (start us, length us, event | category | flops | bytes accessed | tf_op | source)
XLA Modules:
  0.0 49.7 jit_solution(14906466734445044114)
XLA Ops:
  0.0 1.2 %shard_map.41 = (bf16[64,640]{1,0:T(8,128)(2,1)S(1)}, bf16[64,512]{1,0:T(8,128)(2,1)S(1)}, bf16[64,512]{1,0:T(8,128)(2,1)S(1)}, bf16[32,4096]{1,0:T(8,128)(2,1)S(1)}, bf16[16,5248]{1,0:T(8,128)(2,1)S(1)}) custom-call(bf16[1,131072]{1,0:T(2,128)(2,1)} %saved_ref.1, bf16[1,221184]{1,0:T(2,128)(2,1)} %weights_ref.2, bf16[64,128]{1,0:T(8,128)(2,1)} %bitcast.26), custom_call_target="tpu_custom_call" | custom-call | bytes 1363968 | tf_op jit(solution)/shard_map/pallas_call | solution.py:472
  1.2 1.3 %collective-permute-start.2 = (bf16[16,5248]{1,0:T(8,128)(2,1)S(1)}, bf16[16,5248]{1,0:T(8,128)(2,1)S(1)}, u32[]{:S(2)}, u32[]{:S(2)}) collective-permute-start(bf16[16,5248]{1,0:T(8,128)(2,1)S(1)} %get-tuple-element.56.own_ref), channel_id=1, source_target_pairs={{1,2},{5,6},{9,10},{13,14},{17,18},{21,22},{25,26},{29,30}} | collective-permute-start | bytes 503816 | tf_op jit(solution)/shard_map/ppermute | solution.py:550
  2.5 3.4 %collective-permute-start = (bf16[64,512]{1,0:T(8,128)(2,1)S(1)}, bf16[64,512]{1,0:T(8,128)(2,1)S(1)}, u32[]{:S(2)}, u32[]{:S(2)}) collective-permute-start(bf16[64,512]{1,0:T(8,128)(2,1)S(1)} %get-tuple-element.51), channel_id=1, source_target_pairs={{0,4},{1,5},{2,6},{3,7},{4,8},{5,9},{6,10},{7,11},{8,12},{9,13},{1... | collective-permute-start | bytes 196616 | tf_op jit(solution)/shard_map/ppermute | solution.py:493
  5.9 1.3 %collective-permute-start.1 = (bf16[64,512]{1,0:T(8,128)(2,1)S(1)}, bf16[64,512]{1,0:T(8,128)(2,1)S(1)}, u32[]{:S(2)}, u32[]{:S(2)}) collective-permute-start(bf16[64,512]{1,0:T(8,128)(2,1)S(1)} %get-tuple-element.52), channel_id=1, source_target_pairs={{4,0},{5,1},{6,2},{7,3},{8,4},{9,5},{10,6},{11,7},{12,8},{13,9},{1... | collective-permute-start | bytes 196616 | tf_op jit(solution)/shard_map/ppermute | solution.py:493
  7.2 1.3 %shard_map.42 = (bf16[576,384]{1,0:T(8,128)(2,1)S(1)}, bf16[288,192]{1,0:T(8,128)(2,1)S(1)}) custom-call(bf16[1,221184]{1,0:T(2,128)(2,1)} %weights_ref.2), custom_call_target="tpu_custom_call" | custom-call | bytes 995328 | tf_op jit(solution)/shard_map/pallas_call | solution.py:472
  8.5 0.0 collective-permute-done.2.next_ref
  8.5 0.0 collective-permute-done.up_ref
  8.5 3.6 %collective-permute-done.1.down_ref = bf16[64,512]{1,0:T(8,128)(2,1)S(1)} collective-permute-done((bf16[64,512]{1,0:T(8,128)(2,1)S(1)}, bf16[64,512]{1,0:T(8,128)(2,1)S(1)}, u32[]{:S(2)}, u32[]{:S(2)}) %collective-permute-start.1) | collective-permute-done | bytes 65568 | tf_op jit(solution)/shard_map/ppermute | solution.py:493
  12.1 1.3 %collective-permute-start.3 = (bf16[64,2048]{1,0:T(8,128)(2,1)S(1)}, bf16[64,2048]{1,0:T(8,128)(2,1)S(1)}, u32[]{:S(2)}, u32[]{:S(2)}) collective-permute-start(bf16[64,2048]{1,0:T(8,128)(2,1)S(1)} %shard_map.43), channel_id=1, source_target_pairs={{3,2},{7,6},{11,10},{15,14},{19,18},{23,22},{27,26},{31,30}} | collective-permute-start | bytes 786440 | tf_op jit(solution)/shard_map/ppermute | solution.py:572
  13.4 2.1 %collective-permute-done.3.grad_ref = bf16[64,2048]{1,0:T(8,128)(2,1)S(1)} collective-permute-done((bf16[64,2048]{1,0:T(8,128)(2,1)S(1)}, bf16[64,2048]{1,0:T(8,128)(2,1)S(1)}, u32[]{:S(2)}, u32[]{:S(2)}) %collective-permute-start.3) | collective-permute-done | bytes 262176 | tf_op jit(solution)/shard_map/ppermute | solution.py:572
  15.5 2.5 %shard_map.44 = (bf16[16,4096]{1,0:T(8,128)(2,1)S(1)}, f32[432,128]{1,0:T(8,128)S(1)}, f32[144,128]{1,0:T(8,128)S(1)}) custom-call(bf16[64,2048]{1,0:T(8,128)(2,1)S(1)} %collective-permute-done.3.grad_ref, bf16[64,512]{1,0:T(8,128)(2,1)S(1)} %collective-permute-done.up_ref, bf16[64,512]{1,0:T(8,128)(2,1)S(1)} %collective-permute-done.1.down_ref, ...), custom_call_target="tpu_custom_call" | custom-call | flops 226492416 | bytes 1359872 | tf_op jit(solution)/shard_map/pallas_call | solution.py:472
  18.0 0.7 %collective-permute-start.6 = (bf16[1,64,640]{2,1,0:T(8,128)(2,1)S(1)}, bf16[1,64,640]{2,1,0:T(8,128)(2,1)S(1)}, u32[]{:S(2)}, u32[]{:S(2)}) collective-permute-start(bf16[1,64,640]{2,1,0:T(8,128)(2,1)S(1)} %bitcast.21), channel_id=1, source_target_pairs={{3,19},{7,23},{11,27},{15,31},{19,3},{23,7},{27,11},{31,15}} | collective-permute-start | bytes 245768 | tf_op jit(solution)/shard_map/ppermute | solution.py:493
  18.7 1.3 %collective-permute-start.4 = (bf16[16,4096]{1,0:T(8,128)(2,1)S(1)}, bf16[16,4096]{1,0:T(8,128)(2,1)S(1)}, u32[]{:S(2)}, u32[]{:S(2)}) collective-permute-start(bf16[16,4096]{1,0:T(8,128)(2,1)S(1)} %get-tuple-element.60), channel_id=1, source_target_pairs={{2,0},{6,4},{10,8},{14,12},{18,16},{22,20},{26,24},{30,28}} | collective-permute-start | bytes 393224 | tf_op jit(solution)/shard_map/ppermute | solution.py:598
  20.0 0.0 collective-permute-done.6
  20.1 0.7 %collective-permute-start.7 = (bf16[2,64,640]{2,1,0:T(8,128)(2,1)S(1)}, bf16[2,64,640]{2,1,0:T(8,128)(2,1)S(1)}, u32[]{:S(2)}, u32[]{:S(2)}) collective-permute-start(bf16[2,64,640]{2,1,0:T(8,128)(2,1)S(1)} %pad_maximum_fusion.1), channel_id=1, source_target_pairs={{3,11},{7,15},{11,3},{15,7},{19,27},{23,31},{27,19},{31,23}} | collective-permute-start | bytes 491528 | tf_op jit(solution)/shard_map/ppermute | solution.py:493
  20.8 4.3 %collective-permute-start.11 = (f32[432,128]{1,0:T(8,128)S(1)}, f32[432,128]{1,0:T(8,128)S(1)}, u32[]{:S(2)}, u32[]{:S(2)}) collective-permute-start(f32[432,128]{1,0:T(8,128)S(1)} %get-tuple-element.65), channel_id=1, source_target_pairs={{2,6},{6,2},{10,14},{14,10},{18,22},{22,18},{26,30},{30,26}} | collective-permute-start | bytes 663560 | tf_op jit(solution)/shard_map/ppermute | solution.py:493
  25.1 0.0 collective-permute-done.7
  25.1 0.7 %collective-permute-start.14 = (bf16[4,64,640]{2,1,0:T(8,128)(2,1)S(1)}, bf16[4,64,640]{2,1,0:T(8,128)(2,1)S(1)}, u32[]{:S(2)}, u32[]{:S(2)}) collective-permute-start(bf16[4,64,640]{2,1,0:T(8,128)(2,1)S(1)} %constant_dynamic-update-slice_fusion), channel_id=1, source_target_pairs={{3,7},{7,3},{11,15},{15,11},{19,23},{23,19},{27,31},{31,27}} | collective-permute-start | bytes 983048 | tf_op jit(solution)/shard_map/ppermute | solution.py:493
  25.8 1.3 %collective-permute-start.5 = (f32[144,128]{1,0:T(8,128)S(1)}, f32[144,128]{1,0:T(8,128)S(1)}, u32[]{:S(2)}, u32[]{:S(2)}) collective-permute-start(f32[144,128]{1,0:T(8,128)S(1)} %get-tuple-element.61), channel_id=1, source_target_pairs={{2,1},{6,5},{10,9},{14,13},{18,17},{22,21},{26,25},{30,29}} | collective-permute-start | bytes 221192 | tf_op jit(solution)/shard_map/ppermute | solution.py:599
  27.1 1.8 %collective-permute-done.11 = f32[432,128]{1,0:T(8,128)S(1)} collective-permute-done((f32[432,128]{1,0:T(8,128)S(1)}, f32[432,128]{1,0:T(8,128)S(1)}, u32[]{:S(2)}, u32[]{:S(2)}) %collective-permute-start.11) | collective-permute-done | bytes 221216 | tf_op jit(solution)/shard_map/ppermute | solution.py:493
  29.0 0.1 collective-permute-done.5.sum1_ref
  29.1 0.0 collective-permute-done.4.grad0_ref
  29.1 0.7 %collective-permute-start.8 = (f32[144,128]{1,0:T(8,128)S(1)}, f32[144,128]{1,0:T(8,128)S(1)}, u32[]{:S(2)}, u32[]{:S(2)}) collective-permute-start(f32[144,128]{1,0:T(8,128)S(1)} %shard_map.45), channel_id=1, source_target_pairs={{0,4},{1,5},{4,0},{5,1},{8,12},{9,13},{12,8},{13,9},{16,20},{17,21... | collective-permute-start | bytes 221192 | tf_op jit(solution)/shard_map/ppermute | solution.py:493
  29.8 3.5 %collective-permute-start.12 = (f32[432,128]{1,0:T(8,128)S(1)}, f32[432,128]{1,0:T(8,128)S(1)}, u32[]{:S(2)}, u32[]{:S(2)}) collective-permute-start(f32[432,128]{1,0:T(8,128)S(1)} %add.39), channel_id=1, source_target_pairs={{2,10},{6,14},{10,2},{14,6},{18,26},{22,30},{26,18},{30,22}} | collective-permute-start | bytes 663560 | tf_op jit(solution)/shard_map/ppermute | solution.py:493
  33.3 0.0 collective-permute-done.8
  33.3 0.7 %collective-permute-start.9 = (f32[144,128]{1,0:T(8,128)S(1)}, f32[144,128]{1,0:T(8,128)S(1)}, u32[]{:S(2)}, u32[]{:S(2)}) collective-permute-start(f32[144,128]{1,0:T(8,128)S(1)} %add.37), channel_id=1, source_target_pairs={{0,8},{1,9},{4,12},{5,13},{8,0},{9,1},{12,4},{13,5},{16,24},{17,25... | collective-permute-start | bytes 221192 | tf_op jit(solution)/shard_map/ppermute | solution.py:493
  34.0 0.0 collective-permute-done.9
  34.0 0.7 %collective-permute-start.10 = (f32[144,128]{1,0:T(8,128)S(1)}, f32[144,128]{1,0:T(8,128)S(1)}, u32[]{:S(2)}, u32[]{:S(2)}) collective-permute-start(f32[144,128]{1,0:T(8,128)S(1)} %add.38), channel_id=1, source_target_pairs={{0,16},{1,17},{4,20},{5,21},{8,24},{9,25},{12,28},{13,29},{16,0},{... | collective-permute-start | bytes 221192 | tf_op jit(solution)/shard_map/ppermute | solution.py:493
  34.7 2.9 %collective-permute-done.12 = f32[432,128]{1,0:T(8,128)S(1)} collective-permute-done((f32[432,128]{1,0:T(8,128)S(1)}, f32[432,128]{1,0:T(8,128)S(1)}, u32[]{:S(2)}, u32[]{:S(2)}) %collective-permute-start.12) | collective-permute-done | bytes 221216 | tf_op jit(solution)/shard_map/ppermute | solution.py:493
  37.6 4.5 %collective-permute-start.13 = (f32[432,128]{1,0:T(8,128)S(1)}, f32[432,128]{1,0:T(8,128)S(1)}, u32[]{:S(2)}, u32[]{:S(2)}) collective-permute-start(f32[432,128]{1,0:T(8,128)S(1)} %add.40), channel_id=1, source_target_pairs={{2,18},{6,22},{10,26},{14,30},{18,2},{22,6},{26,10},{30,14}} | collective-permute-start | bytes 663560 | tf_op jit(solution)/shard_map/ppermute | solution.py:493
  42.1 0.0 collective-permute-done.10
  42.1 0.0 collective-permute-done.14
  42.2 0.1 pad_maximum_fusion.blocks_ref
  42.3 6.5 %collective-permute-done.13 = f32[432,128]{1,0:T(8,128)S(1)} collective-permute-done((f32[432,128]{1,0:T(8,128)S(1)}, f32[432,128]{1,0:T(8,128)S(1)}, u32[]{:S(2)}, u32[]{:S(2)}) %collective-permute-start.13) | collective-permute-done | bytes 221216 | tf_op jit(solution)/shard_map/ppermute | solution.py:493
  48.7 0.1 conditional.1
  48.8 0.1 pad.15
  48.8 0.0 copy-start
  48.8 0.9 %copy-done = f32[1,221184]{1,0:T(1,128)} copy-done((f32[1,221184]{1,0:T(1,128)}, f32[1,221184]{1,0:T(1,128)S(1)}, u32[]{:S(2)}) %copy-start) | copy-done | bytes 884760
  (12 shorter events, 0.2 us)
Async XLA Ops:
  1.2 7.3 %collective-permute-start.2 = (bf16[16,5248]{1,0:T(8,128)(2,1)S(1)}, bf16[16,5248]{1,0:T(8,128)(2,1)S(1)}, u32[]{:S(2)}, u32[]{:S(2)}) collective-permute-start(bf16[16,5248]{1,0:T(8,128)(2,1)S(1)} %get-tuple-element.56.own_ref), channel_id=1, source_target_pairs={{1,2},{5,6},{9,10},{13,14},{17,18},{21,22},{25,26},{29,30}} | collective-permute-start | bytes 503816 | tf_op jit(solution)/shard_map/ppermute | solution.py:550
  2.5 6.0 %collective-permute-start = (bf16[64,512]{1,0:T(8,128)(2,1)S(1)}, bf16[64,512]{1,0:T(8,128)(2,1)S(1)}, u32[]{:S(2)}, u32[]{:S(2)}) collective-permute-start(bf16[64,512]{1,0:T(8,128)(2,1)S(1)} %get-tuple-element.51), channel_id=1, source_target_pairs={{0,4},{1,5},{2,6},{3,7},{4,8},{5,9},{6,10},{7,11},{8,12},{9,13},{1... | collective-permute-start | bytes 196616 | tf_op jit(solution)/shard_map/ppermute | solution.py:493
  5.9 6.2 %collective-permute-start.1 = (bf16[64,512]{1,0:T(8,128)(2,1)S(1)}, bf16[64,512]{1,0:T(8,128)(2,1)S(1)}, u32[]{:S(2)}, u32[]{:S(2)}) collective-permute-start(bf16[64,512]{1,0:T(8,128)(2,1)S(1)} %get-tuple-element.52), channel_id=1, source_target_pairs={{4,0},{5,1},{6,2},{7,3},{8,4},{9,5},{10,6},{11,7},{12,8},{13,9},{1... | collective-permute-start | bytes 196616 | tf_op jit(solution)/shard_map/ppermute | solution.py:493
  12.1 3.4 %collective-permute-start.3 = (bf16[64,2048]{1,0:T(8,128)(2,1)S(1)}, bf16[64,2048]{1,0:T(8,128)(2,1)S(1)}, u32[]{:S(2)}, u32[]{:S(2)}) collective-permute-start(bf16[64,2048]{1,0:T(8,128)(2,1)S(1)} %shard_map.43), channel_id=1, source_target_pairs={{3,2},{7,6},{11,10},{15,14},{19,18},{23,22},{27,26},{31,30}} | collective-permute-start | bytes 786440 | tf_op jit(solution)/shard_map/ppermute | solution.py:572
  18.0 2.0 %collective-permute-start.6 = (bf16[1,64,640]{2,1,0:T(8,128)(2,1)S(1)}, bf16[1,64,640]{2,1,0:T(8,128)(2,1)S(1)}, u32[]{:S(2)}, u32[]{:S(2)}) collective-permute-start(bf16[1,64,640]{2,1,0:T(8,128)(2,1)S(1)} %bitcast.21), channel_id=1, source_target_pairs={{3,19},{7,23},{11,27},{15,31},{19,3},{23,7},{27,11},{31,15}} | collective-permute-start | bytes 245768 | tf_op jit(solution)/shard_map/ppermute | solution.py:493
  18.7 10.4 %collective-permute-start.4 = (bf16[16,4096]{1,0:T(8,128)(2,1)S(1)}, bf16[16,4096]{1,0:T(8,128)(2,1)S(1)}, u32[]{:S(2)}, u32[]{:S(2)}) collective-permute-start(bf16[16,4096]{1,0:T(8,128)(2,1)S(1)} %get-tuple-element.60), channel_id=1, source_target_pairs={{2,0},{6,4},{10,8},{14,12},{18,16},{22,20},{26,24},{30,28}} | collective-permute-start | bytes 393224 | tf_op jit(solution)/shard_map/ppermute | solution.py:598
  20.1 5.1 %collective-permute-start.7 = (bf16[2,64,640]{2,1,0:T(8,128)(2,1)S(1)}, bf16[2,64,640]{2,1,0:T(8,128)(2,1)S(1)}, u32[]{:S(2)}, u32[]{:S(2)}) collective-permute-start(bf16[2,64,640]{2,1,0:T(8,128)(2,1)S(1)} %pad_maximum_fusion.1), channel_id=1, source_target_pairs={{3,11},{7,15},{11,3},{15,7},{19,27},{23,31},{27,19},{31,23}} | collective-permute-start | bytes 491528 | tf_op jit(solution)/shard_map/ppermute | solution.py:493
  20.8 8.2 %collective-permute-start.11 = (f32[432,128]{1,0:T(8,128)S(1)}, f32[432,128]{1,0:T(8,128)S(1)}, u32[]{:S(2)}, u32[]{:S(2)}) collective-permute-start(f32[432,128]{1,0:T(8,128)S(1)} %get-tuple-element.65), channel_id=1, source_target_pairs={{2,6},{6,2},{10,14},{14,10},{18,22},{22,18},{26,30},{30,26}} | collective-permute-start | bytes 663560 | tf_op jit(solution)/shard_map/ppermute | solution.py:493
  25.1 17.0 %collective-permute-start.14 = (bf16[4,64,640]{2,1,0:T(8,128)(2,1)S(1)}, bf16[4,64,640]{2,1,0:T(8,128)(2,1)S(1)}, u32[]{:S(2)}, u32[]{:S(2)}) collective-permute-start(bf16[4,64,640]{2,1,0:T(8,128)(2,1)S(1)} %constant_dynamic-update-slice_fusion), channel_id=1, source_target_pairs={{3,7},{7,3},{11,15},{15,11},{19,23},{23,19},{27,31},{31,27}} | collective-permute-start | bytes 983048 | tf_op jit(solution)/shard_map/ppermute | solution.py:493
  25.8 3.3 %collective-permute-start.5 = (f32[144,128]{1,0:T(8,128)S(1)}, f32[144,128]{1,0:T(8,128)S(1)}, u32[]{:S(2)}, u32[]{:S(2)}) collective-permute-start(f32[144,128]{1,0:T(8,128)S(1)} %get-tuple-element.61), channel_id=1, source_target_pairs={{2,1},{6,5},{10,9},{14,13},{18,17},{22,21},{26,25},{30,29}} | collective-permute-start | bytes 221192 | tf_op jit(solution)/shard_map/ppermute | solution.py:599
  29.1 4.2 %collective-permute-start.8 = (f32[144,128]{1,0:T(8,128)S(1)}, f32[144,128]{1,0:T(8,128)S(1)}, u32[]{:S(2)}, u32[]{:S(2)}) collective-permute-start(f32[144,128]{1,0:T(8,128)S(1)} %shard_map.45), channel_id=1, source_target_pairs={{0,4},{1,5},{4,0},{5,1},{8,12},{9,13},{12,8},{13,9},{16,20},{17,21... | collective-permute-start | bytes 221192 | tf_op jit(solution)/shard_map/ppermute | solution.py:493
  29.8 7.8 %collective-permute-start.12 = (f32[432,128]{1,0:T(8,128)S(1)}, f32[432,128]{1,0:T(8,128)S(1)}, u32[]{:S(2)}, u32[]{:S(2)}) collective-permute-start(f32[432,128]{1,0:T(8,128)S(1)} %add.39), channel_id=1, source_target_pairs={{2,10},{6,14},{10,2},{14,6},{18,26},{22,30},{26,18},{30,22}} | collective-permute-start | bytes 663560 | tf_op jit(solution)/shard_map/ppermute | solution.py:493
  33.3 0.7 %collective-permute-start.9 = (f32[144,128]{1,0:T(8,128)S(1)}, f32[144,128]{1,0:T(8,128)S(1)}, u32[]{:S(2)}, u32[]{:S(2)}) collective-permute-start(f32[144,128]{1,0:T(8,128)S(1)} %add.37), channel_id=1, source_target_pairs={{0,8},{1,9},{4,12},{5,13},{8,0},{9,1},{12,4},{13,5},{16,24},{17,25... | collective-permute-start | bytes 221192 | tf_op jit(solution)/shard_map/ppermute | solution.py:493
  34.0 8.1 %collective-permute-start.10 = (f32[144,128]{1,0:T(8,128)S(1)}, f32[144,128]{1,0:T(8,128)S(1)}, u32[]{:S(2)}, u32[]{:S(2)}) collective-permute-start(f32[144,128]{1,0:T(8,128)S(1)} %add.38), channel_id=1, source_target_pairs={{0,16},{1,17},{4,20},{5,21},{8,24},{9,25},{12,28},{13,29},{16,0},{... | collective-permute-start | bytes 221192 | tf_op jit(solution)/shard_map/ppermute | solution.py:493
  37.6 11.1 %collective-permute-start.13 = (f32[432,128]{1,0:T(8,128)S(1)}, f32[432,128]{1,0:T(8,128)S(1)}, u32[]{:S(2)}, u32[]{:S(2)}) collective-permute-start(f32[432,128]{1,0:T(8,128)S(1)} %add.40), channel_id=1, source_target_pairs={{2,18},{6,22},{10,26},{14,30},{18,2},{22,6},{26,10},{30,14}} | collective-permute-start | bytes 663560 | tf_op jit(solution)/shard_map/ppermute | solution.py:493
  48.8 0.9 %copy-start = (f32[1,221184]{1,0:T(1,128)}, f32[1,221184]{1,0:T(1,128)S(1)}, u32[]{:S(2)}) copy-start(f32[1,221184]{1,0:T(1,128)S(1)} %get-tuple-element.103) | copy-start | bytes 2654212

commit v9 on v8

--- a/solution.py
+++ b/solution.py
@@ -258,8 +258,6 @@
 
 
 def section21_kernel(
-    scale2,
-    scale1,
     grad_ref,
     up_ref,
     down_ref,
@@ -267,16 +265,12 @@
     weights_ref,
     next_ref,
     out0_ref,
-    sum2_ref,
-    sum1_ref,
     stacked,
+    next_stacked,
     terms,
     middle,
     next_weights,
-    next_stacked,
     next_terms,
-    acts2,
-    acts1,
 ):
     @pl.when(on_segment(2))
     def _():
@@ -327,6 +321,23 @@
             earlier = jnp.concatenate([edge, sums[2][:, : 7 * LANES]], 1)
             mask = next_ref[:, cols(8 * plane, 8)].astype(F32)
             out0_ref[:, cols(8 * plane, 8)] = sloped(sums[1] + later + earlier, mask)
+
+
+def weights21_kernel(
+    scale2,
+    scale1,
+    stacked,
+    next_stacked,
+    down_ref,
+    own_ref,
+    next_ref,
+    sum2_ref,
+    sum1_ref,
+    acts2,
+    acts1,
+):
+    @pl.when(on_segment(2))
+    def _():
         for tap_z in range(3):
             for tap_y in range(3):
                 first = C2 * (3 * tap_z + tap_y)
@@ -569,19 +580,33 @@
         taps3,
         flops=2 * 576 * 384 * 768,
     )
+    places = [0]
+    even = not count & (count - 1)
+    gathers = even and count <= GATHER_LIMIT
+    bits = [1 << power for power in range(count.bit_length() - 1)] if even else []
+
+
+    def swap(block, segments, bit):
+        return over_space(block, segments, lambda n: [(i, i ^ bit) for i in range(n)])
+
+    def gathered(blocks, bit):
+        return jnp.concatenate([blocks, swap(blocks, [3], bit)], 0)
+
+    (blocks,) = behind((deep[None],), grad2)
+    if gathers:
+        for bit in bits[:0:-1][:1]:
+            blocks = gathered(blocks, bit)
+            places = places + [place ^ bit for place in places]
     grad2 = lax.ppermute(grad2, "segment", [(3, 2)])
-    grad0, sum2, sum1 = call(
-        functools.partial(section21_kernel, scales[2], scales[1]),
-        [((16, 4096), BF16), ((432, 128), F32), ((144, 128), F32)],
+    (grad2,) = behind((grad2,), blocks)
+    grad0, stacked2, stacked1 = call(
+        section21_kernel,
+        [((16, 4096), BF16), ((192, 2048), BF16), ((96, 6144), BF16)],
         [
-            ((192, 2048), BF16),
             ((288, 2048), F32),
             ((32, 6144), BF16),
             ((144, 128), BF16),
-            ((96, 6144), BF16),
             ((144, 6144), F32),
-            ((288, 1024), BF16),
-            ((48, 4096), BF16),
         ],
         grad2,
         up,
@@ -591,22 +616,22 @@
         next_own,
         flops=2 * 288 * 192 * 2048,
     )
-    def swap(block, segments, bit):
-        return over_space(block, segments, lambda n: [(i, i ^ bit) for i in range(n)])
-
-    (blocks,) = behind((deep[None],), grad0)
+    sum2, sum1 = call(
+        functools.partial(weights21_kernel, scales[2], scales[1]),
+        [((432, 128), F32), ((144, 128), F32)],
+        [((288, 1024), BF16), ((48, 4096), BF16)],
+        stacked2,
+        stacked1,
+        down,
+        own2,
+        next_own,
+        flops=LONG,
+    )
+    (blocks,) = behind((blocks,), grad0)
     grad0 = lax.ppermute(grad0, "segment", [(2, 0)])
     sum1 = lax.ppermute(sum1, "segment", [(2, 1)])
-    places = [0]
-    even = not count & (count - 1)
-    gathers = even and count <= GATHER_LIMIT
-    bits = [1 << power for power in range(count.bit_length() - 1)] if even else []
-
-    def gathered(blocks, bit):
-        return jnp.concatenate([blocks, swap(blocks, [3], bit)], 0)
-
     if gathers:
-        for bit in bits[:0:-1]:
+        for bit in bits[:0:-1][1:]:
             blocks = gathered(blocks, bit)
             places = places + [place ^ bit for place in places]
     grad0, sum1 = behind((grad0, sum1), blocks)

time: 50.6 us -> 50.1 us (level)
  the two profiles are of different devices: /device:TPU:2 before, /device:TPU:1 now
where the time goes in v9:
time: 50.1 us; the launch traced here: 49.7 us
  starting transfers between devices  23.9 us (48%)
  waiting for transfers between devices  21.4 us (43%)
  Pallas kernels  2.31 us (5%)
  local copies, waits for them, and re-layouts  1.56 us (3%)
    ppermute x11, starting transfers between devices, over_space(): return lax.ppermute(block, ('space', 'segment'), pairs_of(segments, route))  17.8 us
    ppermute x1, waiting for transfers between devices, shards(): sum1 = lax.ppermute(sum1, 'segment', [(2, 1)])  11.6 us
    ppermute x11, waiting for transfers between devices, over_space(): return lax.ppermute(block, ('space', 'segment'), pairs_of(segments, route))  9.77 us
    ppermute x1, starting transfers between devices, shards(): next_own = lax.ppermute(own01, 'segment', [(1, 2)])  3.47 us
    pallas_call x7, Pallas kernels, call(): pl.pallas_call(kernel, out_shape=shapes, in_specs=[far_spec if place in f...  2.31 us
    ppermute x1, starting transfers between devices, shards(): sum1 = lax.ppermute(sum1, 'segment', [(2, 1)])  1.29 us
  transfers between devices with their start and end apart: 15, of which 5 were waited for; matrix products, arithmetic and copies ran while one was open for 0% of the time, Pallas kernels for 0%

profile of v9, /device:TPU:1, one launch (start us, length us, event | category | flops | bytes accessed | tf_op | source)
XLA Modules:
  0.0 49.7 jit_solution(8993081807465962380)
XLA Ops:
  0.0 2.2 %shard_map.41 = (bf16[64,640]{1,0:T(8,128)(2,1)S(1)}, bf16[64,512]{1,0:T(8,128)(2,1)S(1)}, bf16[64,512]{1,0:T(8,128)(2,1)S(1)}, bf16[32,4096]{1,0:T(8,128)(2,1)S(1)}, bf16[16,5248]{1,0:T(8,128)(2,1)S(1)}) custom-call(bf16[1,131072]{1,0:T(2,128)(2,1)} %saved_ref.1, bf16[1,221184]{1,0:T(2,128)(2,1)} %weights_ref.2, bf16[64,128]{1,0:T(8,128)(2,1)} %bitcast.24), custom_call_target="tpu_custom_call" | custom-call | bytes 1363968 | tf_op jit(solution)/shard_map/pallas_call | solution.py:483
  2.2 3.5 %collective-permute-start.2 = (bf16[16,5248]{1,0:T(8,128)(2,1)S(1)}, bf16[16,5248]{1,0:T(8,128)(2,1)S(1)}, u32[]{:S(2)}, u32[]{:S(2)}) collective-permute-start(bf16[16,5248]{1,0:T(8,128)(2,1)S(1)} %get-tuple-element.60.own_ref), channel_id=1, source_target_pairs={{1,2},{5,6},{9,10},{13,14},{17,18},{21,22},{25,26},{29,30}} | collective-permute-start | bytes 503816 | tf_op jit(solution)/shard_map/ppermute | solution.py:561
  5.7 3.1 %collective-permute-start = (bf16[64,512]{1,0:T(8,128)(2,1)S(1)}, bf16[64,512]{1,0:T(8,128)(2,1)S(1)}, u32[]{:S(2)}, u32[]{:S(2)}) collective-permute-start(bf16[64,512]{1,0:T(8,128)(2,1)S(1)} %get-tuple-element.55), channel_id=1, source_target_pairs={{0,4},{1,5},{2,6},{3,7},{4,8},{5,9},{6,10},{7,11},{8,12},{9,13},{1... | collective-permute-start | bytes 196616 | tf_op jit(solution)/shard_map/ppermute | solution.py:504
  8.9 1.3 %collective-permute-start.1 = (bf16[64,512]{1,0:T(8,128)(2,1)S(1)}, bf16[64,512]{1,0:T(8,128)(2,1)S(1)}, u32[]{:S(2)}, u32[]{:S(2)}) collective-permute-start(bf16[64,512]{1,0:T(8,128)(2,1)S(1)} %get-tuple-element.56), channel_id=1, source_target_pairs={{4,0},{5,1},{6,2},{7,3},{8,4},{9,5},{10,6},{11,7},{12,8},{13,9},{1... | collective-permute-start | bytes 196616 | tf_op jit(solution)/shard_map/ppermute | solution.py:504
  10.2 0.0 collective-permute-done.2.next_ref
  10.2 0.0 collective-permute-done.up_ref
  10.2 3.7 %collective-permute-done.1.down_ref = bf16[64,512]{1,0:T(8,128)(2,1)S(1)} collective-permute-done((bf16[64,512]{1,0:T(8,128)(2,1)S(1)}, bf16[64,512]{1,0:T(8,128)(2,1)S(1)}, u32[]{:S(2)}, u32[]{:S(2)}) %collective-permute-start.1) | collective-permute-done | bytes 65568 | tf_op jit(solution)/shard_map/ppermute | solution.py:504
  13.9 0.7 %collective-permute-start.3 = (bf16[64,2048]{1,0:T(8,128)(2,1)S(1)}, bf16[64,2048]{1,0:T(8,128)(2,1)S(1)}, u32[]{:S(2)}, u32[]{:S(2)}) collective-permute-start(bf16[64,2048]{1,0:T(8,128)(2,1)S(1)} %shard_map.43), channel_id=1, source_target_pairs={{3,2},{7,6},{11,10},{15,14},{19,18},{23,22},{27,26},{31,30}} | collective-permute-start | bytes 786440 | tf_op jit(solution)/shard_map/ppermute | solution.py:600
  14.6 0.7 %collective-permute-start.4 = (bf16[1,64,640]{2,1,0:T(8,128)(2,1)S(1)}, bf16[1,64,640]{2,1,0:T(8,128)(2,1)S(1)}, u32[]{:S(2)}, u32[]{:S(2)}) collective-permute-start(bf16[1,64,640]{2,1,0:T(8,128)(2,1)S(1)} %bitcast.21), channel_id=1, source_target_pairs={{3,19},{7,23},{11,27},{15,31},{19,3},{23,7},{27,11},{31,15}} | collective-permute-start | bytes 245768 | tf_op jit(solution)/shard_map/ppermute | solution.py:504
  15.2 0.0 collective-permute-done.4
  15.3 0.0 collective-permute-done.3.grad_ref
  15.3 0.7 %collective-permute-start.5 = (bf16[16,4096]{1,0:T(8,128)(2,1)S(1)}, bf16[16,4096]{1,0:T(8,128)(2,1)S(1)}, u32[]{:S(2)}, u32[]{:S(2)}) collective-permute-start(bf16[16,4096]{1,0:T(8,128)(2,1)S(1)} %get-tuple-element.66), channel_id=1, source_target_pairs={{2,0},{6,4},{10,8},{14,12},{18,16},{22,20},{26,24},{30,28}} | collective-permute-start | bytes 393224 | tf_op jit(solution)/shard_map/ppermute | solution.py:631
  16.0 0.7 %collective-permute-start.7 = (bf16[2,64,640]{2,1,0:T(8,128)(2,1)S(1)}, bf16[2,64,640]{2,1,0:T(8,128)(2,1)S(1)}, u32[]{:S(2)}, u32[]{:S(2)}) collective-permute-start(bf16[2,64,640]{2,1,0:T(8,128)(2,1)S(1)} %constant_dynamic-update-slice_fusion), channel_id=1, source_target_pairs={{3,11},{7,15},{11,3},{15,7},{19,27},{23,31},{27,19},{31,23}} | collective-permute-start | bytes 491528 | tf_op jit(solution)/shard_map/ppermute | solution.py:504
  16.7 0.7 %collective-permute-start.11 = (f32[432,128]{1,0:T(8,128)S(1)}, f32[432,128]{1,0:T(8,128)S(1)}, u32[]{:S(2)}, u32[]{:S(2)}) collective-permute-start(f32[432,128]{1,0:T(8,128)S(1)} %get-tuple-element.73), channel_id=1, source_target_pairs={{2,6},{6,2},{10,14},{14,10},{18,22},{22,18},{26,30},{30,26}} | collective-permute-start | bytes 663560 | tf_op jit(solution)/shard_map/ppermute | solution.py:504
  17.4 0.0 collective-permute-done.7
  17.4 0.7 %collective-permute-start.14 = (bf16[4,64,640]{2,1,0:T(8,128)(2,1)S(1)}, bf16[4,64,640]{2,1,0:T(8,128)(2,1)S(1)}, u32[]{:S(2)}, u32[]{:S(2)}) collective-permute-start(bf16[4,64,640]{2,1,0:T(8,128)(2,1)S(1)} %constant_dynamic-update-slice_fusion.2), channel_id=1, source_target_pairs={{3,7},{7,3},{11,15},{15,11},{19,23},{23,19},{27,31},{31,27}} | collective-permute-start | bytes 983048 | tf_op jit(solution)/shard_map/ppermute | solution.py:504
  18.1 1.3 %collective-permute-start.6 = (f32[144,128]{1,0:T(8,128)S(1)}, f32[144,128]{1,0:T(8,128)S(1)}, u32[]{:S(2)}, u32[]{:S(2)}) collective-permute-start(f32[144,128]{1,0:T(8,128)S(1)} %get-tuple-element.69), channel_id=1, source_target_pairs={{2,1},{6,5},{10,9},{14,13},{18,17},{22,21},{26,25},{30,29}} | collective-permute-start | bytes 221192 | tf_op jit(solution)/shard_map/ppermute | solution.py:632
  19.4 11.6 %collective-permute-done.6.sum1_ref = f32[144,128]{1,0:T(8,128)S(1)} collective-permute-done((f32[144,128]{1,0:T(8,128)S(1)}, f32[144,128]{1,0:T(8,128)S(1)}, u32[]{:S(2)}, u32[]{:S(2)}) %collective-permute-start.6) | collective-permute-done | bytes 73760 | tf_op jit(solution)/shard_map/ppermute | solution.py:632
  31.0 0.0 collective-permute-done.5.grad0_ref
  31.0 1.9 %collective-permute-start.8 = (f32[144,128]{1,0:T(8,128)S(1)}, f32[144,128]{1,0:T(8,128)S(1)}, u32[]{:S(2)}, u32[]{:S(2)}) collective-permute-start(f32[144,128]{1,0:T(8,128)S(1)} %shard_map.46), channel_id=1, source_target_pairs={{0,4},{1,5},{4,0},{5,1},{8,12},{9,13},{12,8},{13,9},{16,20},{17,21... | collective-permute-start | bytes 221192 | tf_op jit(solution)/shard_map/ppermute | solution.py:504
  32.9 0.0 collective-permute-done.11
  33.0 0.7 %collective-permute-start.12 = (f32[432,128]{1,0:T(8,128)S(1)}, f32[432,128]{1,0:T(8,128)S(1)}, u32[]{:S(2)}, u32[]{:S(2)}) collective-permute-start(f32[432,128]{1,0:T(8,128)S(1)} %add.39), channel_id=1, source_target_pairs={{2,10},{6,14},{10,2},{14,6},{18,26},{22,30},{26,18},{30,22}} | collective-permute-start | bytes 663560 | tf_op jit(solution)/shard_map/ppermute | solution.py:504
  33.7 2.4 %collective-permute-done.8 = f32[144,128]{1,0:T(8,128)S(1)} collective-permute-done((f32[144,128]{1,0:T(8,128)S(1)}, f32[144,128]{1,0:T(8,128)S(1)}, u32[]{:S(2)}, u32[]{:S(2)}) %collective-permute-start.8) | collective-permute-done | bytes 73760 | tf_op jit(solution)/shard_map/ppermute | solution.py:504
  36.1 3.2 %collective-permute-start.9 = (f32[144,128]{1,0:T(8,128)S(1)}, f32[144,128]{1,0:T(8,128)S(1)}, u32[]{:S(2)}, u32[]{:S(2)}) collective-permute-start(f32[144,128]{1,0:T(8,128)S(1)} %add.37), channel_id=1, source_target_pairs={{0,8},{1,9},{4,12},{5,13},{8,0},{9,1},{12,4},{13,5},{16,24},{17,25... | collective-permute-start | bytes 221192 | tf_op jit(solution)/shard_map/ppermute | solution.py:504
  39.3 1.9 %collective-permute-done.9 = f32[144,128]{1,0:T(8,128)S(1)} collective-permute-done((f32[144,128]{1,0:T(8,128)S(1)}, f32[144,128]{1,0:T(8,128)S(1)}, u32[]{:S(2)}, u32[]{:S(2)}) %collective-permute-start.9) | collective-permute-done | bytes 73760 | tf_op jit(solution)/shard_map/ppermute | solution.py:504
  41.2 4.2 %collective-permute-start.10 = (f32[144,128]{1,0:T(8,128)S(1)}, f32[144,128]{1,0:T(8,128)S(1)}, u32[]{:S(2)}, u32[]{:S(2)}) collective-permute-start(f32[144,128]{1,0:T(8,128)S(1)} %add.38), channel_id=1, source_target_pairs={{0,16},{1,17},{4,20},{5,21},{8,24},{9,25},{12,28},{13,29},{16,0},{... | collective-permute-start | bytes 221192 | tf_op jit(solution)/shard_map/ppermute | solution.py:504
  45.5 1.8 %collective-permute-done.10 = f32[144,128]{1,0:T(8,128)S(1)} collective-permute-done((f32[144,128]{1,0:T(8,128)S(1)}, f32[144,128]{1,0:T(8,128)S(1)}, u32[]{:S(2)}, u32[]{:S(2)}) %collective-permute-start.10) | collective-permute-done | bytes 73760 | tf_op jit(solution)/shard_map/ppermute | solution.py:504
  47.2 0.0 collective-permute-done.12
  47.3 0.7 %collective-permute-start.13 = (f32[432,128]{1,0:T(8,128)S(1)}, f32[432,128]{1,0:T(8,128)S(1)}, u32[]{:S(2)}, u32[]{:S(2)}) collective-permute-start(f32[432,128]{1,0:T(8,128)S(1)} %add.40), channel_id=1, source_target_pairs={{2,18},{6,22},{10,26},{14,30},{18,2},{22,6},{26,10},{30,14}} | collective-permute-start | bytes 663560 | tf_op jit(solution)/shard_map/ppermute | solution.py:504
  48.0 0.0 collective-permute-done.14
  48.0 0.1 pad_maximum_fusion.blocks_ref
  48.1 0.0 collective-permute-done.13
  48.1 0.7 %conditional.1 = (f32[1,221184]{1,0:T(1,128)S(1)}) conditional(s32[]{:T(128)} %clamp.3, (f32[144,128]{1,0:T(8,128)S(1)}, f32[144,128]{1,0:T(8,128)S(1)}) %tuple.36, (f32[144,128]{1,0:T(8,128)S(1)}, f32[144,128]{1,0:T(8,128)S(1)}) %tuple.36, (f32[432,128]{1,0:T(8,128)S(1)}, f32[432,128]{1,0:T(8,128)S(1)}) %tuple.37, ...), branch_computations={%region_0.1_spmd, %region_1.2_spmd, %region_2.3_spmd, %region_3.4_... | conditional | flops 55296 | bytes 1769484 | solution.py:687
  48.1 0.2 reshape.25
  48.3 0.2 copy.10
  48.5 0.2 reshape.26
  48.7 0.1 pad.14
  48.8 0.0 copy-start
  48.8 0.9 %copy-done = f32[1,221184]{1,0:T(1,128)} copy-done((f32[1,221184]{1,0:T(1,128)}, f32[1,221184]{1,0:T(1,128)S(1)}, u32[]{:S(2)}) %copy-start) | copy-done | bytes 884760
  (15 shorter events, 0.2 us)
Async XLA Ops:
  2.2 8.0 %collective-permute-start.2 = (bf16[16,5248]{1,0:T(8,128)(2,1)S(1)}, bf16[16,5248]{1,0:T(8,128)(2,1)S(1)}, u32[]{:S(2)}, u32[]{:S(2)}) collective-permute-start(bf16[16,5248]{1,0:T(8,128)(2,1)S(1)} %get-tuple-element.60.own_ref), channel_id=1, source_target_pairs={{1,2},{5,6},{9,10},{13,14},{17,18},{21,22},{25,26},{29,30}} | collective-permute-start | bytes 503816 | tf_op jit(solution)/shard_map/ppermute | solution.py:561
  5.7 4.5 %collective-permute-start = (bf16[64,512]{1,0:T(8,128)(2,1)S(1)}, bf16[64,512]{1,0:T(8,128)(2,1)S(1)}, u32[]{:S(2)}, u32[]{:S(2)}) collective-permute-start(bf16[64,512]{1,0:T(8,128)(2,1)S(1)} %get-tuple-element.55), channel_id=1, source_target_pairs={{0,4},{1,5},{2,6},{3,7},{4,8},{5,9},{6,10},{7,11},{8,12},{9,13},{1... | collective-permute-start | bytes 196616 | tf_op jit(solution)/shard_map/ppermute | solution.py:504
  8.9 5.0 %collective-permute-start.1 = (bf16[64,512]{1,0:T(8,128)(2,1)S(1)}, bf16[64,512]{1,0:T(8,128)(2,1)S(1)}, u32[]{:S(2)}, u32[]{:S(2)}) collective-permute-start(bf16[64,512]{1,0:T(8,128)(2,1)S(1)} %get-tuple-element.56), channel_id=1, source_target_pairs={{4,0},{5,1},{6,2},{7,3},{8,4},{9,5},{10,6},{11,7},{12,8},{13,9},{1... | collective-permute-start | bytes 196616 | tf_op jit(solution)/shard_map/ppermute | solution.py:504
  13.9 1.4 %collective-permute-start.3 = (bf16[64,2048]{1,0:T(8,128)(2,1)S(1)}, bf16[64,2048]{1,0:T(8,128)(2,1)S(1)}, u32[]{:S(2)}, u32[]{:S(2)}) collective-permute-start(bf16[64,2048]{1,0:T(8,128)(2,1)S(1)} %shard_map.43), channel_id=1, source_target_pairs={{3,2},{7,6},{11,10},{15,14},{19,18},{23,22},{27,26},{31,30}} | collective-permute-start | bytes 786440 | tf_op jit(solution)/shard_map/ppermute | solution.py:600
  14.6 0.7 %collective-permute-start.4 = (bf16[1,64,640]{2,1,0:T(8,128)(2,1)S(1)}, bf16[1,64,640]{2,1,0:T(8,128)(2,1)S(1)}, u32[]{:S(2)}, u32[]{:S(2)}) collective-permute-start(bf16[1,64,640]{2,1,0:T(8,128)(2,1)S(1)} %bitcast.21), channel_id=1, source_target_pairs={{3,19},{7,23},{11,27},{15,31},{19,3},{23,7},{27,11},{31,15}} | collective-permute-start | bytes 245768 | tf_op jit(solution)/shard_map/ppermute | solution.py:504
  15.3 15.7 %collective-permute-start.5 = (bf16[16,4096]{1,0:T(8,128)(2,1)S(1)}, bf16[16,4096]{1,0:T(8,128)(2,1)S(1)}, u32[]{:S(2)}, u32[]{:S(2)}) collective-permute-start(bf16[16,4096]{1,0:T(8,128)(2,1)S(1)} %get-tuple-element.66), channel_id=1, source_target_pairs={{2,0},{6,4},{10,8},{14,12},{18,16},{22,20},{26,24},{30,28}} | collective-permute-start | bytes 393224 | tf_op jit(solution)/shard_map/ppermute | solution.py:631
  16.0 1.4 %collective-permute-start.7 = (bf16[2,64,640]{2,1,0:T(8,128)(2,1)S(1)}, bf16[2,64,640]{2,1,0:T(8,128)(2,1)S(1)}, u32[]{:S(2)}, u32[]{:S(2)}) collective-permute-start(bf16[2,64,640]{2,1,0:T(8,128)(2,1)S(1)} %constant_dynamic-update-slice_fusion), channel_id=1, source_target_pairs={{3,11},{7,15},{11,3},{15,7},{19,27},{23,31},{27,19},{31,23}} | collective-permute-start | bytes 491528 | tf_op jit(solution)/shard_map/ppermute | solution.py:504
  16.7 16.3 %collective-permute-start.11 = (f32[432,128]{1,0:T(8,128)S(1)}, f32[432,128]{1,0:T(8,128)S(1)}, u32[]{:S(2)}, u32[]{:S(2)}) collective-permute-start(f32[432,128]{1,0:T(8,128)S(1)} %get-tuple-element.73), channel_id=1, source_target_pairs={{2,6},{6,2},{10,14},{14,10},{18,22},{22,18},{26,30},{30,26}} | collective-permute-start | bytes 663560 | tf_op jit(solution)/shard_map/ppermute | solution.py:504
  17.4 30.5 %collective-permute-start.14 = (bf16[4,64,640]{2,1,0:T(8,128)(2,1)S(1)}, bf16[4,64,640]{2,1,0:T(8,128)(2,1)S(1)}, u32[]{:S(2)}, u32[]{:S(2)}) collective-permute-start(bf16[4,64,640]{2,1,0:T(8,128)(2,1)S(1)} %constant_dynamic-update-slice_fusion.2), channel_id=1, source_target_pairs={{3,7},{7,3},{11,15},{15,11},{19,23},{23,19},{27,31},{31,27}} | collective-permute-start | bytes 983048 | tf_op jit(solution)/shard_map/ppermute | solution.py:504
  18.1 12.9 %collective-permute-start.6 = (f32[144,128]{1,0:T(8,128)S(1)}, f32[144,128]{1,0:T(8,128)S(1)}, u32[]{:S(2)}, u32[]{:S(2)}) collective-permute-start(f32[144,128]{1,0:T(8,128)S(1)} %get-tuple-element.69), channel_id=1, source_target_pairs={{2,1},{6,5},{10,9},{14,13},{18,17},{22,21},{26,25},{30,29}} | collective-permute-start | bytes 221192 | tf_op jit(solution)/shard_map/ppermute | solution.py:632
  31.0 5.1 %collective-permute-start.8 = (f32[144,128]{1,0:T(8,128)S(1)}, f32[144,128]{1,0:T(8,128)S(1)}, u32[]{:S(2)}, u32[]{:S(2)}) collective-permute-start(f32[144,128]{1,0:T(8,128)S(1)} %shard_map.46), channel_id=1, source_target_pairs={{0,4},{1,5},{4,0},{5,1},{8,12},{9,13},{12,8},{13,9},{16,20},{17,21... | collective-permute-start | bytes 221192 | tf_op jit(solution)/shard_map/ppermute | solution.py:504
  33.0 14.2 %collective-permute-start.12 = (f32[432,128]{1,0:T(8,128)S(1)}, f32[432,128]{1,0:T(8,128)S(1)}, u32[]{:S(2)}, u32[]{:S(2)}) collective-permute-start(f32[432,128]{1,0:T(8,128)S(1)} %add.39), channel_id=1, source_target_pairs={{2,10},{6,14},{10,2},{14,6},{18,26},{22,30},{26,18},{30,22}} | collective-permute-start | bytes 663560 | tf_op jit(solution)/shard_map/ppermute | solution.py:504
  36.1 5.1 %collective-permute-start.9 = (f32[144,128]{1,0:T(8,128)S(1)}, f32[144,128]{1,0:T(8,128)S(1)}, u32[]{:S(2)}, u32[]{:S(2)}) collective-permute-start(f32[144,128]{1,0:T(8,128)S(1)} %add.37), channel_id=1, source_target_pairs={{0,8},{1,9},{4,12},{5,13},{8,0},{9,1},{12,4},{13,5},{16,24},{17,25... | collective-permute-start | bytes 221192 | tf_op jit(solution)/shard_map/ppermute | solution.py:504
  41.2 6.0 %collective-permute-start.10 = (f32[144,128]{1,0:T(8,128)S(1)}, f32[144,128]{1,0:T(8,128)S(1)}, u32[]{:S(2)}, u32[]{:S(2)}) collective-permute-start(f32[144,128]{1,0:T(8,128)S(1)} %add.38), channel_id=1, source_target_pairs={{0,16},{1,17},{4,20},{5,21},{8,24},{9,25},{12,28},{13,29},{16,0},{... | collective-permute-start | bytes 221192 | tf_op jit(solution)/shard_map/ppermute | solution.py:504
  47.3 0.8 %collective-permute-start.13 = (f32[432,128]{1,0:T(8,128)S(1)}, f32[432,128]{1,0:T(8,128)S(1)}, u32[]{:S(2)}, u32[]{:S(2)}) collective-permute-start(f32[432,128]{1,0:T(8,128)S(1)} %add.40), channel_id=1, source_target_pairs={{2,18},{6,22},{10,26},{14,30},{18,2},{22,6},{26,10},{30,14}} | collective-permute-start | bytes 663560 | tf_op jit(solution)/shard_map/ppermute | solution.py:504
  48.8 0.9 %copy-start = (f32[1,221184]{1,0:T(1,128)}, f32[1,221184]{1,0:T(1,128)S(1)}, u32[]{:S(2)}) copy-start(f32[1,221184]{1,0:T(1,128)S(1)} %get-tuple-element.111) | copy-start | bytes 2654212

commit v10 on v9

--- a/solution.py
+++ b/solution.py
@@ -634,7 +634,7 @@
         for bit in bits[:0:-1][1:]:
             blocks = gathered(blocks, bit)
             places = places + [place ^ bit for place in places]
-    grad0, sum1 = behind((grad0, sum1), blocks)
+    grad0, sum1 = behind((grad0, sum1), sum2)
     (sum01,) = call(
         functools.partial(weights01_kernel, scales[0]),
         [((144, 128), F32)],

time: 50.1 us -> 50.1 us (level)
  no operation moved by 1% of the time
where the time goes in v10:
time: 50.1 us; the launch traced here: 49.7 us
  starting transfers between devices  23.9 us (48%)
  waiting for transfers between devices  21.4 us (43%)
  Pallas kernels  2.31 us (5%)
  local copies, waits for them, and re-layouts  1.52 us (3%)
    ppermute x11, starting transfers between devices, over_space(): return lax.ppermute(block, ('space', 'segment'), pairs_of(segments, route))  17.8 us
    ppermute x1, waiting for transfers between devices, shards(): sum1 = lax.ppermute(sum1, 'segment', [(2, 1)])  11.6 us
    ppermute x11, waiting for transfers between devices, over_space(): return lax.ppermute(block, ('space', 'segment'), pairs_of(segments, route))  9.77 us
    ppermute x1, starting transfers between devices, shards(): next_own = lax.ppermute(own01, 'segment', [(1, 2)])  3.47 us
    pallas_call x7, Pallas kernels, call(): pl.pallas_call(kernel, out_shape=shapes, in_specs=[far_spec if place in f...  2.31 us
    ppermute x1, starting transfers between devices, shards(): sum1 = lax.ppermute(sum1, 'segment', [(2, 1)])  1.29 us
  transfers between devices with their start and end apart: 15, of which 5 were waited for; matrix products, arithmetic and copies ran while one was open for 0% of the time, Pallas kernels for 0%

profile of v10, /device:TPU:1, one launch (start us, length us, event | category | flops | bytes accessed | tf_op | source)
XLA Modules:
  0.0 49.7 jit_solution(9237474642320312899)
XLA Ops:
  0.0 2.2 %shard_map.41 = (bf16[64,640]{1,0:T(8,128)(2,1)S(1)}, bf16[64,512]{1,0:T(8,128)(2,1)S(1)}, bf16[64,512]{1,0:T(8,128)(2,1)S(1)}, bf16[32,4096]{1,0:T(8,128)(2,1)S(1)}, bf16[16,5248]{1,0:T(8,128)(2,1)S(1)}) custom-call(bf16[1,131072]{1,0:T(2,128)(2,1)} %saved_ref.1, bf16[1,221184]{1,0:T(2,128)(2,1)} %weights_ref.2, bf16[64,128]{1,0:T(8,128)(2,1)} %bitcast.24), custom_call_target="tpu_custom_call" | custom-call | bytes 1363968 | tf_op jit(solution)/shard_map/pallas_call | solution.py:483
  2.2 3.5 %collective-permute-start.2 = (bf16[16,5248]{1,0:T(8,128)(2,1)S(1)}, bf16[16,5248]{1,0:T(8,128)(2,1)S(1)}, u32[]{:S(2)}, u32[]{:S(2)}) collective-permute-start(bf16[16,5248]{1,0:T(8,128)(2,1)S(1)} %get-tuple-element.60.own_ref), channel_id=1, source_target_pairs={{1,2},{5,6},{9,10},{13,14},{17,18},{21,22},{25,26},{29,30}} | collective-permute-start | bytes 503816 | tf_op jit(solution)/shard_map/ppermute | solution.py:561
  5.7 3.1 %collective-permute-start = (bf16[64,512]{1,0:T(8,128)(2,1)S(1)}, bf16[64,512]{1,0:T(8,128)(2,1)S(1)}, u32[]{:S(2)}, u32[]{:S(2)}) collective-permute-start(bf16[64,512]{1,0:T(8,128)(2,1)S(1)} %get-tuple-element.55), channel_id=1, source_target_pairs={{0,4},{1,5},{2,6},{3,7},{4,8},{5,9},{6,10},{7,11},{8,12},{9,13},{1... | collective-permute-start | bytes 196616 | tf_op jit(solution)/shard_map/ppermute | solution.py:504
  8.9 1.3 %collective-permute-start.1 = (bf16[64,512]{1,0:T(8,128)(2,1)S(1)}, bf16[64,512]{1,0:T(8,128)(2,1)S(1)}, u32[]{:S(2)}, u32[]{:S(2)}) collective-permute-start(bf16[64,512]{1,0:T(8,128)(2,1)S(1)} %get-tuple-element.56), channel_id=1, source_target_pairs={{4,0},{5,1},{6,2},{7,3},{8,4},{9,5},{10,6},{11,7},{12,8},{13,9},{1... | collective-permute-start | bytes 196616 | tf_op jit(solution)/shard_map/ppermute | solution.py:504
  10.2 0.0 collective-permute-done.2.next_ref
  10.2 0.0 collective-permute-done.up_ref
  10.2 3.7 %collective-permute-done.1.down_ref = bf16[64,512]{1,0:T(8,128)(2,1)S(1)} collective-permute-done((bf16[64,512]{1,0:T(8,128)(2,1)S(1)}, bf16[64,512]{1,0:T(8,128)(2,1)S(1)}, u32[]{:S(2)}, u32[]{:S(2)}) %collective-permute-start.1) | collective-permute-done | bytes 65568 | tf_op jit(solution)/shard_map/ppermute | solution.py:504
  13.9 0.7 %collective-permute-start.3 = (bf16[64,2048]{1,0:T(8,128)(2,1)S(1)}, bf16[64,2048]{1,0:T(8,128)(2,1)S(1)}, u32[]{:S(2)}, u32[]{:S(2)}) collective-permute-start(bf16[64,2048]{1,0:T(8,128)(2,1)S(1)} %shard_map.43), channel_id=1, source_target_pairs={{3,2},{7,6},{11,10},{15,14},{19,18},{23,22},{27,26},{31,30}} | collective-permute-start | bytes 786440 | tf_op jit(solution)/shard_map/ppermute | solution.py:600
  14.6 0.7 %collective-permute-start.4 = (bf16[1,64,640]{2,1,0:T(8,128)(2,1)S(1)}, bf16[1,64,640]{2,1,0:T(8,128)(2,1)S(1)}, u32[]{:S(2)}, u32[]{:S(2)}) collective-permute-start(bf16[1,64,640]{2,1,0:T(8,128)(2,1)S(1)} %bitcast.21), channel_id=1, source_target_pairs={{3,19},{7,23},{11,27},{15,31},{19,3},{23,7},{27,11},{31,15}} | collective-permute-start | bytes 245768 | tf_op jit(solution)/shard_map/ppermute | solution.py:504
  15.2 0.0 collective-permute-done.4
  15.3 0.0 collective-permute-done.3.grad_ref
  15.3 0.7 %collective-permute-start.5 = (bf16[16,4096]{1,0:T(8,128)(2,1)S(1)}, bf16[16,4096]{1,0:T(8,128)(2,1)S(1)}, u32[]{:S(2)}, u32[]{:S(2)}) collective-permute-start(bf16[16,4096]{1,0:T(8,128)(2,1)S(1)} %get-tuple-element.66), channel_id=1, source_target_pairs={{2,0},{6,4},{10,8},{14,12},{18,16},{22,20},{26,24},{30,28}} | collective-permute-start | bytes 393224 | tf_op jit(solution)/shard_map/ppermute | solution.py:631
  16.0 0.7 %collective-permute-start.13 = (bf16[2,64,640]{2,1,0:T(8,128)(2,1)S(1)}, bf16[2,64,640]{2,1,0:T(8,128)(2,1)S(1)}, u32[]{:S(2)}, u32[]{:S(2)}) collective-permute-start(bf16[2,64,640]{2,1,0:T(8,128)(2,1)S(1)} %constant_dynamic-update-slice_fusion), channel_id=1, source_target_pairs={{3,11},{7,15},{11,3},{15,7},{19,27},{23,31},{27,19},{31,23}} | collective-permute-start | bytes 491528 | tf_op jit(solution)/shard_map/ppermute | solution.py:504
  16.7 0.7 %collective-permute-start.10 = (f32[432,128]{1,0:T(8,128)S(1)}, f32[432,128]{1,0:T(8,128)S(1)}, u32[]{:S(2)}, u32[]{:S(2)}) collective-permute-start(f32[432,128]{1,0:T(8,128)S(1)} %get-tuple-element.70), channel_id=1, source_target_pairs={{2,6},{6,2},{10,14},{14,10},{18,22},{22,18},{26,30},{30,26}} | collective-permute-start | bytes 663560 | tf_op jit(solution)/shard_map/ppermute | solution.py:504
  17.4 0.0 collective-permute-done.13
  17.4 0.7 %collective-permute-start.14 = (bf16[4,64,640]{2,1,0:T(8,128)(2,1)S(1)}, bf16[4,64,640]{2,1,0:T(8,128)(2,1)S(1)}, u32[]{:S(2)}, u32[]{:S(2)}) collective-permute-start(bf16[4,64,640]{2,1,0:T(8,128)(2,1)S(1)} %pad_maximum_fusion.1), channel_id=1, source_target_pairs={{3,7},{7,3},{11,15},{15,11},{19,23},{23,19},{27,31},{31,27}} | collective-permute-start | bytes 983048 | tf_op jit(solution)/shard_map/ppermute | solution.py:504
  18.1 1.3 %collective-permute-start.6 = (f32[144,128]{1,0:T(8,128)S(1)}, f32[144,128]{1,0:T(8,128)S(1)}, u32[]{:S(2)}, u32[]{:S(2)}) collective-permute-start(f32[144,128]{1,0:T(8,128)S(1)} %get-tuple-element.69), channel_id=1, source_target_pairs={{2,1},{6,5},{10,9},{14,13},{18,17},{22,21},{26,25},{30,29}} | collective-permute-start | bytes 221192 | tf_op jit(solution)/shard_map/ppermute | solution.py:632
  19.4 11.6 %collective-permute-done.6.sum1_ref = f32[144,128]{1,0:T(8,128)S(1)} collective-permute-done((f32[144,128]{1,0:T(8,128)S(1)}, f32[144,128]{1,0:T(8,128)S(1)}, u32[]{:S(2)}, u32[]{:S(2)}) %collective-permute-start.6) | collective-permute-done | bytes 73760 | tf_op jit(solution)/shard_map/ppermute | solution.py:632
  31.0 0.0 collective-permute-done.5.grad0_ref
  31.0 1.9 %collective-permute-start.7 = (f32[144,128]{1,0:T(8,128)S(1)}, f32[144,128]{1,0:T(8,128)S(1)}, u32[]{:S(2)}, u32[]{:S(2)}) collective-permute-start(f32[144,128]{1,0:T(8,128)S(1)} %shard_map.46), channel_id=1, source_target_pairs={{0,4},{1,5},{4,0},{5,1},{8,12},{9,13},{12,8},{13,9},{16,20},{17,21... | collective-permute-start | bytes 221192 | tf_op jit(solution)/shard_map/ppermute | solution.py:504
  32.9 0.0 collective-permute-done.10
  33.0 0.7 %collective-permute-start.11 = (f32[432,128]{1,0:T(8,128)S(1)}, f32[432,128]{1,0:T(8,128)S(1)}, u32[]{:S(2)}, u32[]{:S(2)}) collective-permute-start(f32[432,128]{1,0:T(8,128)S(1)} %add.39), channel_id=1, source_target_pairs={{2,10},{6,14},{10,2},{14,6},{18,26},{22,30},{26,18},{30,22}} | collective-permute-start | bytes 663560 | tf_op jit(solution)/shard_map/ppermute | solution.py:504
  33.7 2.4 %collective-permute-done.7 = f32[144,128]{1,0:T(8,128)S(1)} collective-permute-done((f32[144,128]{1,0:T(8,128)S(1)}, f32[144,128]{1,0:T(8,128)S(1)}, u32[]{:S(2)}, u32[]{:S(2)}) %collective-permute-start.7) | collective-permute-done | bytes 73760 | tf_op jit(solution)/shard_map/ppermute | solution.py:504
  36.1 3.2 %collective-permute-start.8 = (f32[144,128]{1,0:T(8,128)S(1)}, f32[144,128]{1,0:T(8,128)S(1)}, u32[]{:S(2)}, u32[]{:S(2)}) collective-permute-start(f32[144,128]{1,0:T(8,128)S(1)} %add.37), channel_id=1, source_target_pairs={{0,8},{1,9},{4,12},{5,13},{8,0},{9,1},{12,4},{13,5},{16,24},{17,25... | collective-permute-start | bytes 221192 | tf_op jit(solution)/shard_map/ppermute | solution.py:504
  39.3 1.9 %collective-permute-done.8 = f32[144,128]{1,0:T(8,128)S(1)} collective-permute-done((f32[144,128]{1,0:T(8,128)S(1)}, f32[144,128]{1,0:T(8,128)S(1)}, u32[]{:S(2)}, u32[]{:S(2)}) %collective-permute-start.8) | collective-permute-done | bytes 73760 | tf_op jit(solution)/shard_map/ppermute | solution.py:504
  41.2 4.2 %collective-permute-start.9 = (f32[144,128]{1,0:T(8,128)S(1)}, f32[144,128]{1,0:T(8,128)S(1)}, u32[]{:S(2)}, u32[]{:S(2)}) collective-permute-start(f32[144,128]{1,0:T(8,128)S(1)} %add.38), channel_id=1, source_target_pairs={{0,16},{1,17},{4,20},{5,21},{8,24},{9,25},{12,28},{13,29},{16,0},{... | collective-permute-start | bytes 221192 | tf_op jit(solution)/shard_map/ppermute | solution.py:504
  45.5 1.8 %collective-permute-done.9 = f32[144,128]{1,0:T(8,128)S(1)} collective-permute-done((f32[144,128]{1,0:T(8,128)S(1)}, f32[144,128]{1,0:T(8,128)S(1)}, u32[]{:S(2)}, u32[]{:S(2)}) %collective-permute-start.9) | collective-permute-done | bytes 73760 | tf_op jit(solution)/shard_map/ppermute | solution.py:504
  47.2 0.0 collective-permute-done.11
  47.3 0.7 %collective-permute-start.12 = (f32[432,128]{1,0:T(8,128)S(1)}, f32[432,128]{1,0:T(8,128)S(1)}, u32[]{:S(2)}, u32[]{:S(2)}) collective-permute-start(f32[432,128]{1,0:T(8,128)S(1)} %add.40), channel_id=1, source_target_pairs={{2,18},{6,22},{10,26},{14,30},{18,2},{22,6},{26,10},{30,14}} | collective-permute-start | bytes 663560 | tf_op jit(solution)/shard_map/ppermute | solution.py:504
  47.9 0.0 collective-permute-done.14
  48.0 0.1 pad_maximum_fusion.blocks_ref
  48.1 0.0 collective-permute-done.12
  48.1 0.7 %conditional.1 = (f32[1,221184]{1,0:T(1,128)S(1)}) conditional(s32[]{:T(128)} %clamp.3, (f32[144,128]{1,0:T(8,128)S(1)}, f32[144,128]{1,0:T(8,128)S(1)}) %tuple.35, (f32[144,128]{1,0:T(8,128)S(1)}, f32[144,128]{1,0:T(8,128)S(1)}) %tuple.35, (f32[432,128]{1,0:T(8,128)S(1)}, f32[432,128]{1,0:T(8,128)S(1)}) %tuple.36, ...), branch_computations={%region_0.1_spmd, %region_1.2_spmd, %region_2.3_spmd, %region_3.4_... | conditional | flops 55296 | bytes 1769484 | solution.py:687
  48.1 0.2 reshape.25
  48.3 0.2 copy.10
  48.5 0.2 reshape.26
  48.7 0.1 pad.14
  48.8 0.0 copy-start
  48.8 0.9 %copy-done = f32[1,221184]{1,0:T(1,128)} copy-done((f32[1,221184]{1,0:T(1,128)}, f32[1,221184]{1,0:T(1,128)S(1)}, u32[]{:S(2)}) %copy-start) | copy-done | bytes 884760
  (14 shorter events, 0.2 us)
Async XLA Ops:
  2.2 8.0 %collective-permute-start.2 = (bf16[16,5248]{1,0:T(8,128)(2,1)S(1)}, bf16[16,5248]{1,0:T(8,128)(2,1)S(1)}, u32[]{:S(2)}, u32[]{:S(2)}) collective-permute-start(bf16[16,5248]{1,0:T(8,128)(2,1)S(1)} %get-tuple-element.60.own_ref), channel_id=1, source_target_pairs={{1,2},{5,6},{9,10},{13,14},{17,18},{21,22},{25,26},{29,30}} | collective-permute-start | bytes 503816 | tf_op jit(solution)/shard_map/ppermute | solution.py:561
  5.7 4.5 %collective-permute-start = (bf16[64,512]{1,0:T(8,128)(2,1)S(1)}, bf16[64,512]{1,0:T(8,128)(2,1)S(1)}, u32[]{:S(2)}, u32[]{:S(2)}) collective-permute-start(bf16[64,512]{1,0:T(8,128)(2,1)S(1)} %get-tuple-element.55), channel_id=1, source_target_pairs={{0,4},{1,5},{2,6},{3,7},{4,8},{5,9},{6,10},{7,11},{8,12},{9,13},{1... | collective-permute-start | bytes 196616 | tf_op jit(solution)/shard_map/ppermute | solution.py:504
  8.9 5.0 %collective-permute-start.1 = (bf16[64,512]{1,0:T(8,128)(2,1)S(1)}, bf16[64,512]{1,0:T(8,128)(2,1)S(1)}, u32[]{:S(2)}, u32[]{:S(2)}) collective-permute-start(bf16[64,512]{1,0:T(8,128)(2,1)S(1)} %get-tuple-element.56), channel_id=1, source_target_pairs={{4,0},{5,1},{6,2},{7,3},{8,4},{9,5},{10,6},{11,7},{12,8},{13,9},{1... | collective-permute-start | bytes 196616 | tf_op jit(solution)/shard_map/ppermute | solution.py:504
  13.9 1.4 %collective-permute-start.3 = (bf16[64,2048]{1,0:T(8,128)(2,1)S(1)}, bf16[64,2048]{1,0:T(8,128)(2,1)S(1)}, u32[]{:S(2)}, u32[]{:S(2)}) collective-permute-start(bf16[64,2048]{1,0:T(8,128)(2,1)S(1)} %shard_map.43), channel_id=1, source_target_pairs={{3,2},{7,6},{11,10},{15,14},{19,18},{23,22},{27,26},{31,30}} | collective-permute-start | bytes 786440 | tf_op jit(solution)/shard_map/ppermute | solution.py:600
  14.6 0.7 %collective-permute-start.4 = (bf16[1,64,640]{2,1,0:T(8,128)(2,1)S(1)}, bf16[1,64,640]{2,1,0:T(8,128)(2,1)S(1)}, u32[]{:S(2)}, u32[]{:S(2)}) collective-permute-start(bf16[1,64,640]{2,1,0:T(8,128)(2,1)S(1)} %bitcast.21), channel_id=1, source_target_pairs={{3,19},{7,23},{11,27},{15,31},{19,3},{23,7},{27,11},{31,15}} | collective-permute-start | bytes 245768 | tf_op jit(solution)/shard_map/ppermute | solution.py:504
  15.3 15.7 %collective-permute-start.5 = (bf16[16,4096]{1,0:T(8,128)(2,1)S(1)}, bf16[16,4096]{1,0:T(8,128)(2,1)S(1)}, u32[]{:S(2)}, u32[]{:S(2)}) collective-permute-start(bf16[16,4096]{1,0:T(8,128)(2,1)S(1)} %get-tuple-element.66), channel_id=1, source_target_pairs={{2,0},{6,4},{10,8},{14,12},{18,16},{22,20},{26,24},{30,28}} | collective-permute-start | bytes 393224 | tf_op jit(solution)/shard_map/ppermute | solution.py:631
  16.0 1.4 %collective-permute-start.13 = (bf16[2,64,640]{2,1,0:T(8,128)(2,1)S(1)}, bf16[2,64,640]{2,1,0:T(8,128)(2,1)S(1)}, u32[]{:S(2)}, u32[]{:S(2)}) collective-permute-start(bf16[2,64,640]{2,1,0:T(8,128)(2,1)S(1)} %constant_dynamic-update-slice_fusion), channel_id=1, source_target_pairs={{3,11},{7,15},{11,3},{15,7},{19,27},{23,31},{27,19},{31,23}} | collective-permute-start | bytes 491528 | tf_op jit(solution)/shard_map/ppermute | solution.py:504
  16.7 16.3 %collective-permute-start.10 = (f32[432,128]{1,0:T(8,128)S(1)}, f32[432,128]{1,0:T(8,128)S(1)}, u32[]{:S(2)}, u32[]{:S(2)}) collective-permute-start(f32[432,128]{1,0:T(8,128)S(1)} %get-tuple-element.70), channel_id=1, source_target_pairs={{2,6},{6,2},{10,14},{14,10},{18,22},{22,18},{26,30},{30,26}} | collective-permute-start | bytes 663560 | tf_op jit(solution)/shard_map/ppermute | solution.py:504
  17.4 30.5 %collective-permute-start.14 = (bf16[4,64,640]{2,1,0:T(8,128)(2,1)S(1)}, bf16[4,64,640]{2,1,0:T(8,128)(2,1)S(1)}, u32[]{:S(2)}, u32[]{:S(2)}) collective-permute-start(bf16[4,64,640]{2,1,0:T(8,128)(2,1)S(1)} %pad_maximum_fusion.1), channel_id=1, source_target_pairs={{3,7},{7,3},{11,15},{15,11},{19,23},{23,19},{27,31},{31,27}} | collective-permute-start | bytes 983048 | tf_op jit(solution)/shard_map/ppermute | solution.py:504
  18.1 12.9 %collective-permute-start.6 = (f32[144,128]{1,0:T(8,128)S(1)}, f32[144,128]{1,0:T(8,128)S(1)}, u32[]{:S(2)}, u32[]{:S(2)}) collective-permute-start(f32[144,128]{1,0:T(8,128)S(1)} %get-tuple-element.69), channel_id=1, source_target_pairs={{2,1},{6,5},{10,9},{14,13},{18,17},{22,21},{26,25},{30,29}} | collective-permute-start | bytes 221192 | tf_op jit(solution)/shard_map/ppermute | solution.py:632
  31.0 5.1 %collective-permute-start.7 = (f32[144,128]{1,0:T(8,128)S(1)}, f32[144,128]{1,0:T(8,128)S(1)}, u32[]{:S(2)}, u32[]{:S(2)}) collective-permute-start(f32[144,128]{1,0:T(8,128)S(1)} %shard_map.46), channel_id=1, source_target_pairs={{0,4},{1,5},{4,0},{5,1},{8,12},{9,13},{12,8},{13,9},{16,20},{17,21... | collective-permute-start | bytes 221192 | tf_op jit(solution)/shard_map/ppermute | solution.py:504
  33.0 14.2 %collective-permute-start.11 = (f32[432,128]{1,0:T(8,128)S(1)}, f32[432,128]{1,0:T(8,128)S(1)}, u32[]{:S(2)}, u32[]{:S(2)}) collective-permute-start(f32[432,128]{1,0:T(8,128)S(1)} %add.39), channel_id=1, source_target_pairs={{2,10},{6,14},{10,2},{14,6},{18,26},{22,30},{26,18},{30,22}} | collective-permute-start | bytes 663560 | tf_op jit(solution)/shard_map/ppermute | solution.py:504
  36.1 5.1 %collective-permute-start.8 = (f32[144,128]{1,0:T(8,128)S(1)}, f32[144,128]{1,0:T(8,128)S(1)}, u32[]{:S(2)}, u32[]{:S(2)}) collective-permute-start(f32[144,128]{1,0:T(8,128)S(1)} %add.37), channel_id=1, source_target_pairs={{0,8},{1,9},{4,12},{5,13},{8,0},{9,1},{12,4},{13,5},{16,24},{17,25... | collective-permute-start | bytes 221192 | tf_op jit(solution)/shard_map/ppermute | solution.py:504
  41.2 6.0 %collective-permute-start.9 = (f32[144,128]{1,0:T(8,128)S(1)}, f32[144,128]{1,0:T(8,128)S(1)}, u32[]{:S(2)}, u32[]{:S(2)}) collective-permute-start(f32[144,128]{1,0:T(8,128)S(1)} %add.38), channel_id=1, source_target_pairs={{0,16},{1,17},{4,20},{5,21},{8,24},{9,25},{12,28},{13,29},{16,0},{... | collective-permute-start | bytes 221192 | tf_op jit(solution)/shard_map/ppermute | solution.py:504
  47.3 0.8 %collective-permute-start.12 = (f32[432,128]{1,0:T(8,128)S(1)}, f32[432,128]{1,0:T(8,128)S(1)}, u32[]{:S(2)}, u32[]{:S(2)}) collective-permute-start(f32[432,128]{1,0:T(8,128)S(1)} %add.40), channel_id=1, source_target_pairs={{2,18},{6,22},{10,26},{14,30},{18,2},{22,6},{26,10},{30,14}} | collective-permute-start | bytes 663560 | tf_op jit(solution)/shard_map/ppermute | solution.py:504
  48.8 0.9 %copy-start = (f32[1,221184]{1,0:T(1,128)}, f32[1,221184]{1,0:T(1,128)S(1)}, u32[]{:S(2)}) copy-start(f32[1,221184]{1,0:T(1,128)S(1)} %get-tuple-element.111) | copy-start | bytes 2654212

commit v11 on v10

--- a/solution.py
+++ b/solution.py
@@ -556,8 +556,8 @@
         flops=0,
         far=(0, 1, 2),
     )
-    up = over_space(up, range(4), later)
-    down = over_space(down, range(4), sooner)
+    up = over_space(up, [0, 2, 3], later)
+    down = over_space(down, [0, 2, 3], sooner)
     next_own = lax.ppermute(own01, "segment", [(1, 2)])
     (weights,) = behind((conv_weights,), deep)
     taps3, taps2 = call(

time: 50.1 us -> 50.1 us (level)
  waiting for transfers between devices: 21.4 us -> 24.5 us
  starting transfers between devices: 23.9 us -> 20.8 us
    ppermute x1, waiting for transfers between devices: 11.6 us -> 17.5 us  [shards(): sum1 = lax.ppermute(sum1, 'segment', [(2, 1)])]
    ppermute x11, waiting for transfers between devices: 9.77 us -> 6.12 us  [over_space(): return lax.ppermute(block, ('space', 'segment'), pairs_of(segments, route))]
    ppermute x11, starting transfers between devices: 17.8 us -> 14.7 us  [over_space(): return lax.ppermute(block, ('space', 'segment'), pairs_of(segments, route))]
    ppermute x1, waiting for transfers between devices: 0.01 us -> 0.9 us  [shards(): next_own = lax.ppermute(own01, 'segment', [(1, 2)])]
where the time goes in v11:
time: 50.1 us; the launch traced here: 49.7 us
  waiting for transfers between devices  24.5 us (49%)
  starting transfers between devices  20.8 us (42%)
  Pallas kernels  2.31 us (5%)
  local copies, waits for them, and re-layouts  1.52 us (3%)
    ppermute x1, waiting for transfers between devices, shards(): sum1 = lax.ppermute(sum1, 'segment', [(2, 1)])  17.5 us
    ppermute x11, starting transfers between devices, over_space(): return lax.ppermute(block, ('space', 'segment'), pairs_of(segments, route))  14.7 us
    ppermute x11, waiting for transfers between devices, over_space(): return lax.ppermute(block, ('space', 'segment'), pairs_of(segments, route))  6.12 us
    ppermute x1, starting transfers between devices, shards(): next_own = lax.ppermute(own01, 'segment', [(1, 2)])  3.47 us
    pallas_call x7, Pallas kernels, call(): pl.pallas_call(kernel, out_shape=shapes, in_specs=[far_spec if place in f...  2.31 us
    ppermute x1, starting transfers between devices, shards(): sum1 = lax.ppermute(sum1, 'segment', [(2, 1)])  1.29 us
  transfers between devices with their start and end apart: 15, of which 5 were waited for; matrix products, arithmetic and copies ran while one was open for 0% of the time, Pallas kernels for 0%

profile of v11, /device:TPU:1, one launch (start us, length us, event | category | flops | bytes accessed | tf_op | source)
XLA Modules:
  0.0 49.7 jit_solution(12913066817471127653)
XLA Ops:
  0.0 2.2 %shard_map.41 = (bf16[64,640]{1,0:T(8,128)(2,1)S(1)}, bf16[64,512]{1,0:T(8,128)(2,1)S(1)}, bf16[64,512]{1,0:T(8,128)(2,1)S(1)}, bf16[32,4096]{1,0:T(8,128)(2,1)S(1)}, bf16[16,5248]{1,0:T(8,128)(2,1)S(1)}) custom-call(bf16[1,131072]{1,0:T(2,128)(2,1)} %saved_ref.1, bf16[1,221184]{1,0:T(2,128)(2,1)} %weights_ref.2, bf16[64,128]{1,0:T(8,128)(2,1)} %bitcast.24), custom_call_target="tpu_custom_call" | custom-call | bytes 1363968 | tf_op jit(solution)/shard_map/pallas_call | solution.py:483
  2.2 3.5 %collective-permute-start.2 = (bf16[16,5248]{1,0:T(8,128)(2,1)S(1)}, bf16[16,5248]{1,0:T(8,128)(2,1)S(1)}, u32[]{:S(2)}, u32[]{:S(2)}) collective-permute-start(bf16[16,5248]{1,0:T(8,128)(2,1)S(1)} %get-tuple-element.60.own_ref), channel_id=1, source_target_pairs={{1,2},{5,6},{9,10},{13,14},{17,18},{21,22},{25,26},{29,30}} | collective-permute-start | bytes 503816 | tf_op jit(solution)/shard_map/ppermute | solution.py:561
  5.7 0.7 %collective-permute-start = (bf16[64,512]{1,0:T(8,128)(2,1)S(1)}, bf16[64,512]{1,0:T(8,128)(2,1)S(1)}, u32[]{:S(2)}, u32[]{:S(2)}) collective-permute-start(bf16[64,512]{1,0:T(8,128)(2,1)S(1)} %get-tuple-element.55), channel_id=1, source_target_pairs={{0,4},{2,6},{3,7},{4,8},{6,10},{7,11},{8,12},{10,14},{11,15},{12,1... | collective-permute-start | bytes 196616 | tf_op jit(solution)/shard_map/ppermute | solution.py:504
  6.4 0.7 %collective-permute-start.1 = (bf16[64,512]{1,0:T(8,128)(2,1)S(1)}, bf16[64,512]{1,0:T(8,128)(2,1)S(1)}, u32[]{:S(2)}, u32[]{:S(2)}) collective-permute-start(bf16[64,512]{1,0:T(8,128)(2,1)S(1)} %get-tuple-element.56), channel_id=1, source_target_pairs={{4,0},{6,2},{7,3},{8,4},{10,6},{11,7},{12,8},{14,10},{15,11},{16,1... | collective-permute-start | bytes 196616 | tf_op jit(solution)/shard_map/ppermute | solution.py:504
  7.1 0.9 %collective-permute-done.2.next_ref = bf16[16,5248]{1,0:T(8,128)(2,1)S(1)} collective-permute-done((bf16[16,5248]{1,0:T(8,128)(2,1)S(1)}, bf16[16,5248]{1,0:T(8,128)(2,1)S(1)}, u32[]{:S(2)}, u32[]{:S(2)}) %collective-permute-start.2) | collective-permute-done | bytes 167968 | tf_op jit(solution)/shard_map/ppermute | solution.py:561
  8.0 0.0 collective-permute-done.up_ref
  8.0 0.0 collective-permute-done.1.down_ref
  8.0 0.7 %collective-permute-start.3 = (bf16[64,2048]{1,0:T(8,128)(2,1)S(1)}, bf16[64,2048]{1,0:T(8,128)(2,1)S(1)}, u32[]{:S(2)}, u32[]{:S(2)}) collective-permute-start(bf16[64,2048]{1,0:T(8,128)(2,1)S(1)} %shard_map.43), channel_id=1, source_target_pairs={{3,2},{7,6},{11,10},{15,14},{19,18},{23,22},{27,26},{31,30}} | collective-permute-start | bytes 786440 | tf_op jit(solution)/shard_map/ppermute | solution.py:600
  8.7 0.7 %collective-permute-start.4 = (bf16[1,64,640]{2,1,0:T(8,128)(2,1)S(1)}, bf16[1,64,640]{2,1,0:T(8,128)(2,1)S(1)}, u32[]{:S(2)}, u32[]{:S(2)}) collective-permute-start(bf16[1,64,640]{2,1,0:T(8,128)(2,1)S(1)} %bitcast.21), channel_id=1, source_target_pairs={{3,19},{7,23},{11,27},{15,31},{19,3},{23,7},{27,11},{31,15}} | collective-permute-start | bytes 245768 | tf_op jit(solution)/shard_map/ppermute | solution.py:504
  9.4 0.0 collective-permute-done.4
  9.4 0.0 collective-permute-done.3.grad_ref
  9.4 0.7 %collective-permute-start.5 = (bf16[16,4096]{1,0:T(8,128)(2,1)S(1)}, bf16[16,4096]{1,0:T(8,128)(2,1)S(1)}, u32[]{:S(2)}, u32[]{:S(2)}) collective-permute-start(bf16[16,4096]{1,0:T(8,128)(2,1)S(1)} %get-tuple-element.66), channel_id=1, source_target_pairs={{2,0},{6,4},{10,8},{14,12},{18,16},{22,20},{26,24},{30,28}} | collective-permute-start | bytes 393224 | tf_op jit(solution)/shard_map/ppermute | solution.py:631
  10.1 0.7 %collective-permute-start.13 = (bf16[2,64,640]{2,1,0:T(8,128)(2,1)S(1)}, bf16[2,64,640]{2,1,0:T(8,128)(2,1)S(1)}, u32[]{:S(2)}, u32[]{:S(2)}) collective-permute-start(bf16[2,64,640]{2,1,0:T(8,128)(2,1)S(1)} %constant_dynamic-update-slice_fusion), channel_id=1, source_target_pairs={{3,11},{7,15},{11,3},{15,7},{19,27},{23,31},{27,19},{31,23}} | collective-permute-start | bytes 491528 | tf_op jit(solution)/shard_map/ppermute | solution.py:504
  10.8 0.7 %collective-permute-start.10 = (f32[432,128]{1,0:T(8,128)S(1)}, f32[432,128]{1,0:T(8,128)S(1)}, u32[]{:S(2)}, u32[]{:S(2)}) collective-permute-start(f32[432,128]{1,0:T(8,128)S(1)} %get-tuple-element.70), channel_id=1, source_target_pairs={{2,6},{6,2},{10,14},{14,10},{18,22},{22,18},{26,30},{30,26}} | collective-permute-start | bytes 663560 | tf_op jit(solution)/shard_map/ppermute | solution.py:504
  11.5 0.0 collective-permute-done.13
  11.5 0.7 %collective-permute-start.14 = (bf16[4,64,640]{2,1,0:T(8,128)(2,1)S(1)}, bf16[4,64,640]{2,1,0:T(8,128)(2,1)S(1)}, u32[]{:S(2)}, u32[]{:S(2)}) collective-permute-start(bf16[4,64,640]{2,1,0:T(8,128)(2,1)S(1)} %pad_maximum_fusion.1), channel_id=1, source_target_pairs={{3,7},{7,3},{11,15},{15,11},{19,23},{23,19},{27,31},{31,27}} | collective-permute-start | bytes 983048 | tf_op jit(solution)/shard_map/ppermute | solution.py:504
  12.2 1.3 %collective-permute-start.6 = (f32[144,128]{1,0:T(8,128)S(1)}, f32[144,128]{1,0:T(8,128)S(1)}, u32[]{:S(2)}, u32[]{:S(2)}) collective-permute-start(f32[144,128]{1,0:T(8,128)S(1)} %get-tuple-element.69), channel_id=1, source_target_pairs={{2,1},{6,5},{10,9},{14,13},{18,17},{22,21},{26,25},{30,29}} | collective-permute-start | bytes 221192 | tf_op jit(solution)/shard_map/ppermute | solution.py:632
  13.5 17.5 %collective-permute-done.6.sum1_ref = f32[144,128]{1,0:T(8,128)S(1)} collective-permute-done((f32[144,128]{1,0:T(8,128)S(1)}, f32[144,128]{1,0:T(8,128)S(1)}, u32[]{:S(2)}, u32[]{:S(2)}) %collective-permute-start.6) | collective-permute-done | bytes 73760 | tf_op jit(solution)/shard_map/ppermute | solution.py:632
  31.0 0.0 collective-permute-done.5.grad0_ref
  31.0 1.9 %collective-permute-start.7 = (f32[144,128]{1,0:T(8,128)S(1)}, f32[144,128]{1,0:T(8,128)S(1)}, u32[]{:S(2)}, u32[]{:S(2)}) collective-permute-start(f32[144,128]{1,0:T(8,128)S(1)} %shard_map.46), channel_id=1, source_target_pairs={{0,4},{1,5},{4,0},{5,1},{8,12},{9,13},{12,8},{13,9},{16,20},{17,21... | collective-permute-start | bytes 221192 | tf_op jit(solution)/shard_map/ppermute | solution.py:504
  32.9 0.0 collective-permute-done.10
  33.0 0.7 %collective-permute-start.11 = (f32[432,128]{1,0:T(8,128)S(1)}, f32[432,128]{1,0:T(8,128)S(1)}, u32[]{:S(2)}, u32[]{:S(2)}) collective-permute-start(f32[432,128]{1,0:T(8,128)S(1)} %add.39), channel_id=1, source_target_pairs={{2,10},{6,14},{10,2},{14,6},{18,26},{22,30},{26,18},{30,22}} | collective-permute-start | bytes 663560 | tf_op jit(solution)/shard_map/ppermute | solution.py:504
  33.7 2.4 %collective-permute-done.7 = f32[144,128]{1,0:T(8,128)S(1)} collective-permute-done((f32[144,128]{1,0:T(8,128)S(1)}, f32[144,128]{1,0:T(8,128)S(1)}, u32[]{:S(2)}, u32[]{:S(2)}) %collective-permute-start.7) | collective-permute-done | bytes 73760 | tf_op jit(solution)/shard_map/ppermute | solution.py:504
  36.1 3.2 %collective-permute-start.8 = (f32[144,128]{1,0:T(8,128)S(1)}, f32[144,128]{1,0:T(8,128)S(1)}, u32[]{:S(2)}, u32[]{:S(2)}) collective-permute-start(f32[144,128]{1,0:T(8,128)S(1)} %add.37), channel_id=1, source_target_pairs={{0,8},{1,9},{4,12},{5,13},{8,0},{9,1},{12,4},{13,5},{16,24},{17,25... | collective-permute-start | bytes 221192 | tf_op jit(solution)/shard_map/ppermute | solution.py:504
  39.3 1.9 %collective-permute-done.8 = f32[144,128]{1,0:T(8,128)S(1)} collective-permute-done((f32[144,128]{1,0:T(8,128)S(1)}, f32[144,128]{1,0:T(8,128)S(1)}, u32[]{:S(2)}, u32[]{:S(2)}) %collective-permute-start.8) | collective-permute-done | bytes 73760 | tf_op jit(solution)/shard_map/ppermute | solution.py:504
  41.2 4.2 %collective-permute-start.9 = (f32[144,128]{1,0:T(8,128)S(1)}, f32[144,128]{1,0:T(8,128)S(1)}, u32[]{:S(2)}, u32[]{:S(2)}) collective-permute-start(f32[144,128]{1,0:T(8,128)S(1)} %add.38), channel_id=1, source_target_pairs={{0,16},{1,17},{4,20},{5,21},{8,24},{9,25},{12,28},{13,29},{16,0},{... | collective-permute-start | bytes 221192 | tf_op jit(solution)/shard_map/ppermute | solution.py:504
  45.5 1.8 %collective-permute-done.9 = f32[144,128]{1,0:T(8,128)S(1)} collective-permute-done((f32[144,128]{1,0:T(8,128)S(1)}, f32[144,128]{1,0:T(8,128)S(1)}, u32[]{:S(2)}, u32[]{:S(2)}) %collective-permute-start.9) | collective-permute-done | bytes 73760 | tf_op jit(solution)/shard_map/ppermute | solution.py:504
  47.2 0.0 collective-permute-done.11
  47.3 0.7 %collective-permute-start.12 = (f32[432,128]{1,0:T(8,128)S(1)}, f32[432,128]{1,0:T(8,128)S(1)}, u32[]{:S(2)}, u32[]{:S(2)}) collective-permute-start(f32[432,128]{1,0:T(8,128)S(1)} %add.40), channel_id=1, source_target_pairs={{2,18},{6,22},{10,26},{14,30},{18,2},{22,6},{26,10},{30,14}} | collective-permute-start | bytes 663560 | tf_op jit(solution)/shard_map/ppermute | solution.py:504
  47.9 0.0 collective-permute-done.14
  48.0 0.1 pad_maximum_fusion.blocks_ref
  48.1 0.0 collective-permute-done.12
  48.1 0.7 %conditional.1 = (f32[1,221184]{1,0:T(1,128)S(1)}) conditional(s32[]{:T(128)} %clamp.3, (f32[144,128]{1,0:T(8,128)S(1)}, f32[144,128]{1,0:T(8,128)S(1)}) %tuple.35, (f32[144,128]{1,0:T(8,128)S(1)}, f32[144,128]{1,0:T(8,128)S(1)}) %tuple.35, (f32[432,128]{1,0:T(8,128)S(1)}, f32[432,128]{1,0:T(8,128)S(1)}) %tuple.36, ...), branch_computations={%region_0.1_spmd, %region_1.2_spmd, %region_2.3_spmd, %region_3.4_... | conditional | flops 55296 | bytes 1769484 | solution.py:687
  48.1 0.2 reshape.25
  48.3 0.2 copy.10
  48.5 0.2 reshape.26
  48.7 0.1 pad.14
  48.8 0.0 copy-start
  48.8 0.9 %copy-done = f32[1,221184]{1,0:T(1,128)} copy-done((f32[1,221184]{1,0:T(1,128)}, f32[1,221184]{1,0:T(1,128)S(1)}, u32[]{:S(2)}) %copy-start) | copy-done | bytes 884760
  (14 shorter events, 0.2 us)
Async XLA Ops:
  2.2 5.8 %collective-permute-start.2 = (bf16[16,5248]{1,0:T(8,128)(2,1)S(1)}, bf16[16,5248]{1,0:T(8,128)(2,1)S(1)}, u32[]{:S(2)}, u32[]{:S(2)}) collective-permute-start(bf16[16,5248]{1,0:T(8,128)(2,1)S(1)} %get-tuple-element.60.own_ref), channel_id=1, source_target_pairs={{1,2},{5,6},{9,10},{13,14},{17,18},{21,22},{25,26},{29,30}} | collective-permute-start | bytes 503816 | tf_op jit(solution)/shard_map/ppermute | solution.py:561
  5.7 2.3 %collective-permute-start = (bf16[64,512]{1,0:T(8,128)(2,1)S(1)}, bf16[64,512]{1,0:T(8,128)(2,1)S(1)}, u32[]{:S(2)}, u32[]{:S(2)}) collective-permute-start(bf16[64,512]{1,0:T(8,128)(2,1)S(1)} %get-tuple-element.55), channel_id=1, source_target_pairs={{0,4},{2,6},{3,7},{4,8},{6,10},{7,11},{8,12},{10,14},{11,15},{12,1... | collective-permute-start | bytes 196616 | tf_op jit(solution)/shard_map/ppermute | solution.py:504
  6.4 1.6 %collective-permute-start.1 = (bf16[64,512]{1,0:T(8,128)(2,1)S(1)}, bf16[64,512]{1,0:T(8,128)(2,1)S(1)}, u32[]{:S(2)}, u32[]{:S(2)}) collective-permute-start(bf16[64,512]{1,0:T(8,128)(2,1)S(1)} %get-tuple-element.56), channel_id=1, source_target_pairs={{4,0},{6,2},{7,3},{8,4},{10,6},{11,7},{12,8},{14,10},{15,11},{16,1... | collective-permute-start | bytes 196616 | tf_op jit(solution)/shard_map/ppermute | solution.py:504
  8.0 1.4 %collective-permute-start.3 = (bf16[64,2048]{1,0:T(8,128)(2,1)S(1)}, bf16[64,2048]{1,0:T(8,128)(2,1)S(1)}, u32[]{:S(2)}, u32[]{:S(2)}) collective-permute-start(bf16[64,2048]{1,0:T(8,128)(2,1)S(1)} %shard_map.43), channel_id=1, source_target_pairs={{3,2},{7,6},{11,10},{15,14},{19,18},{23,22},{27,26},{31,30}} | collective-permute-start | bytes 786440 | tf_op jit(solution)/shard_map/ppermute | solution.py:600
  8.7 0.7 %collective-permute-start.4 = (bf16[1,64,640]{2,1,0:T(8,128)(2,1)S(1)}, bf16[1,64,640]{2,1,0:T(8,128)(2,1)S(1)}, u32[]{:S(2)}, u32[]{:S(2)}) collective-permute-start(bf16[1,64,640]{2,1,0:T(8,128)(2,1)S(1)} %bitcast.21), channel_id=1, source_target_pairs={{3,19},{7,23},{11,27},{15,31},{19,3},{23,7},{27,11},{31,15}} | collective-permute-start | bytes 245768 | tf_op jit(solution)/shard_map/ppermute | solution.py:504
  9.4 21.6 %collective-permute-start.5 = (bf16[16,4096]{1,0:T(8,128)(2,1)S(1)}, bf16[16,4096]{1,0:T(8,128)(2,1)S(1)}, u32[]{:S(2)}, u32[]{:S(2)}) collective-permute-start(bf16[16,4096]{1,0:T(8,128)(2,1)S(1)} %get-tuple-element.66), channel_id=1, source_target_pairs={{2,0},{6,4},{10,8},{14,12},{18,16},{22,20},{26,24},{30,28}} | collective-permute-start | bytes 393224 | tf_op jit(solution)/shard_map/ppermute | solution.py:631
  10.1 1.4 %collective-permute-start.13 = (bf16[2,64,640]{2,1,0:T(8,128)(2,1)S(1)}, bf16[2,64,640]{2,1,0:T(8,128)(2,1)S(1)}, u32[]{:S(2)}, u32[]{:S(2)}) collective-permute-start(bf16[2,64,640]{2,1,0:T(8,128)(2,1)S(1)} %constant_dynamic-update-slice_fusion), channel_id=1, source_target_pairs={{3,11},{7,15},{11,3},{15,7},{19,27},{23,31},{27,19},{31,23}} | collective-permute-start | bytes 491528 | tf_op jit(solution)/shard_map/ppermute | solution.py:504
  10.8 22.1 %collective-permute-start.10 = (f32[432,128]{1,0:T(8,128)S(1)}, f32[432,128]{1,0:T(8,128)S(1)}, u32[]{:S(2)}, u32[]{:S(2)}) collective-permute-start(f32[432,128]{1,0:T(8,128)S(1)} %get-tuple-element.70), channel_id=1, source_target_pairs={{2,6},{6,2},{10,14},{14,10},{18,22},{22,18},{26,30},{30,26}} | collective-permute-start | bytes 663560 | tf_op jit(solution)/shard_map/ppermute | solution.py:504
  11.5 36.4 %collective-permute-start.14 = (bf16[4,64,640]{2,1,0:T(8,128)(2,1)S(1)}, bf16[4,64,640]{2,1,0:T(8,128)(2,1)S(1)}, u32[]{:S(2)}, u32[]{:S(2)}) collective-permute-start(bf16[4,64,640]{2,1,0:T(8,128)(2,1)S(1)} %pad_maximum_fusion.1), channel_id=1, source_target_pairs={{3,7},{7,3},{11,15},{15,11},{19,23},{23,19},{27,31},{31,27}} | collective-permute-start | bytes 983048 | tf_op jit(solution)/shard_map/ppermute | solution.py:504
  12.2 18.8 %collective-permute-start.6 = (f32[144,128]{1,0:T(8,128)S(1)}, f32[144,128]{1,0:T(8,128)S(1)}, u32[]{:S(2)}, u32[]{:S(2)}) collective-permute-start(f32[144,128]{1,0:T(8,128)S(1)} %get-tuple-element.69), channel_id=1, source_target_pairs={{2,1},{6,5},{10,9},{14,13},{18,17},{22,21},{26,25},{30,29}} | collective-permute-start | bytes 221192 | tf_op jit(solution)/shard_map/ppermute | solution.py:632
  31.0 5.1 %collective-permute-start.7 = (f32[144,128]{1,0:T(8,128)S(1)}, f32[144,128]{1,0:T(8,128)S(1)}, u32[]{:S(2)}, u32[]{:S(2)}) collective-permute-start(f32[144,128]{1,0:T(8,128)S(1)} %shard_map.46), channel_id=1, source_target_pairs={{0,4},{1,5},{4,0},{5,1},{8,12},{9,13},{12,8},{13,9},{16,20},{17,21... | collective-permute-start | bytes 221192 | tf_op jit(solution)/shard_map/ppermute | solution.py:504
  33.0 14.2 %collective-permute-start.11 = (f32[432,128]{1,0:T(8,128)S(1)}, f32[432,128]{1,0:T(8,128)S(1)}, u32[]{:S(2)}, u32[]{:S(2)}) collective-permute-start(f32[432,128]{1,0:T(8,128)S(1)} %add.39), channel_id=1, source_target_pairs={{2,10},{6,14},{10,2},{14,6},{18,26},{22,30},{26,18},{30,22}} | collective-permute-start | bytes 663560 | tf_op jit(solution)/shard_map/ppermute | solution.py:504
  36.1 5.1 %collective-permute-start.8 = (f32[144,128]{1,0:T(8,128)S(1)}, f32[144,128]{1,0:T(8,128)S(1)}, u32[]{:S(2)}, u32[]{:S(2)}) collective-permute-start(f32[144,128]{1,0:T(8,128)S(1)} %add.37), channel_id=1, source_target_pairs={{0,8},{1,9},{4,12},{5,13},{8,0},{9,1},{12,4},{13,5},{16,24},{17,25... | collective-permute-start | bytes 221192 | tf_op jit(solution)/shard_map/ppermute | solution.py:504
  41.2 6.0 %collective-permute-start.9 = (f32[144,128]{1,0:T(8,128)S(1)}, f32[144,128]{1,0:T(8,128)S(1)}, u32[]{:S(2)}, u32[]{:S(2)}) collective-permute-start(f32[144,128]{1,0:T(8,128)S(1)} %add.38), channel_id=1, source_target_pairs={{0,16},{1,17},{4,20},{5,21},{8,24},{9,25},{12,28},{13,29},{16,0},{... | collective-permute-start | bytes 221192 | tf_op jit(solution)/shard_map/ppermute | solution.py:504
  47.3 0.8 %collective-permute-start.12 = (f32[432,128]{1,0:T(8,128)S(1)}, f32[432,128]{1,0:T(8,128)S(1)}, u32[]{:S(2)}, u32[]{:S(2)}) collective-permute-start(f32[432,128]{1,0:T(8,128)S(1)} %add.40), channel_id=1, source_target_pairs={{2,18},{6,22},{10,26},{14,30},{18,2},{22,6},{26,10},{30,14}} | collective-permute-start | bytes 663560 | tf_op jit(solution)/shard_map/ppermute | solution.py:504
  48.8 0.9 %copy-start = (f32[1,221184]{1,0:T(1,128)}, f32[1,221184]{1,0:T(1,128)S(1)}, u32[]{:S(2)}) copy-start(f32[1,221184]{1,0:T(1,128)S(1)} %get-tuple-element.111) | copy-start | bytes 2654212
